TPU v7x, 32 devices: a whole 2x2x4 slice. The times are simulated.
32 devices in a mesh: ctx: 16 (over z, y, core), wa: 2 (over x).
Axes of the slice: x: 2, y: 2, z: 4, core: 2. Of those that a mesh axis runs over, the one named last changes fastest.
Arguments:
- tokens: bfloat16 [2, 5120, 768], P('wa', 'ctx'), may hold values from -6 to 6
- segment_ids: int32 [2, 5120], P('wa', 'ctx'), may hold values from 0 to 31, never falling along the last dimension, each value on 1 to 3200 neighbouring positions
- cotangent: bfloat16 [2, 5120, 768], P('wa', 'ctx'), may hold values from -6 to 6
- w_query: bfloat16 [768, 768], P('wa'), may hold values from -0.21875 to 0.21875
- w_key: bfloat16 [768, 768], P('wa'), may hold values from -0.21875 to 0.21875
- w_value: bfloat16 [768, 768], P('wa'), may hold values from -0.21875 to 0.21875
- w_out: bfloat16 [768, 768], P('wa'), may hold values from -4 to 4
- w_up: bfloat16 [768, 3072], P('wa'), may hold values from -0.21875 to 0.21875
- w_down: bfloat16 [3072, 768], P('wa'), may hold values from -0.109375 to 0.109375
- b_query: bfloat16 [768], P('wa'), may hold values from -3 to 3
- b_value: bfloat16 [768], P('wa'), may hold values from -0.119628906 to 0.119628906
- b_out: bfloat16 [768], P('wa'), may hold values from -1.796875 to 1.796875
- gain_one: bfloat16 [768], P('wa'), may hold values from 0.5 to 1.5
- shift_one: bfloat16 [768], P('wa'), may hold values from -1.796875 to 1.796875
- b_up: bfloat16 [3072], P('wa'), may hold values from -1.796875 to 1.796875
- b_down: bfloat16 [768], P('wa'), may hold values from -1.796875 to 1.796875
- gain_two: bfloat16 [768], P('wa'), may hold values from 0.5 to 1.5
- shift_two: bfloat16 [768], P('wa'), may hold values from -1.796875 to 1.796875
Outputs:
- layer_out: bfloat16 [2, 5120, 768], P('wa', 'ctx')
- grad_tokens: float32 [2, 5120, 768], P('wa', 'ctx')
- grad_w_query: float32 [768, 768], P('wa')
- grad_w_key: float32 [768, 768], P('wa')
- grad_w_value: float32 [768, 768], P('wa')
- grad_w_out: float32 [768, 768], P('wa')
- grad_w_up: float32 [768, 3072], P('wa')
- grad_w_down: float32 [3072, 768], P('wa')
- grad_b_query: float32 [768], P('wa')
- grad_b_value: float32 [768], P('wa')
- grad_b_out: float32 [768], P('wa')
- grad_gain_one: float32 [768], P('wa')
- grad_shift_one: float32 [768], P('wa')
- grad_b_up: float32 [3072], P('wa')
- grad_b_down: float32 [768], P('wa')
- grad_gain_two: float32 [768], P('wa')
- grad_shift_two: float32 [768], P('wa')
Inputs may be any that keep to these rules, and one draw needn't show every extreme that they name: `segment_ids`: within each sequence the ids never fall; each of the 32 ids names one document of 1 to 3200 tokens, and some document holds exactly 3200 tokens.
All inputs are finite; a program needn't handle non-finite values.
Results may differ from a plain program's by a relative error of at most 0.025.
Values may be sent and summed in bfloat16 or wider, within the bound.
No kernel may reach another device: no remote copies, remote signals or barrier semaphores. Data moves between devices by JAX's collectives and lax.ppermute only.
A program may use at most 192 MiB of HBM per device.

v0:
```python
import jax
import jax.numpy as jnp
from jax import lax
from jax.sharding import PartitionSpec as P

D = 768
HEADS = 12
HEAD_DIM = 64


epsilon = 1e-05
masked_value = -1e30


def widen(array):
    return array.astype(jnp.float32)


def outer_sum(left, right):
    return lax.dot_general(
        left, right, (((0,), (0,)), ((), ())), preferred_element_type=jnp.float32
    )


def back_product(grad, weight):
    return lax.dot_general(
        grad, weight, (((1,), (1,)), ((), ())), preferred_element_type=jnp.float32
    )


def norm_forward(values, gain, shift):
    centre = values - jnp.mean(values, axis=-1, keepdims=True)
    scale = lax.rsqrt(jnp.mean(centre * centre, axis=-1, keepdims=True) + epsilon)
    unit = centre * scale
    return (unit * gain + shift, unit, scale)


def norm_backward(grad, unit, scale, gain):
    grad_gain = jnp.sum(grad * unit, axis=0)
    grad_shift = jnp.sum(grad, axis=0)
    inner = grad * gain
    grad_in = scale * (
        inner
        - jnp.mean(inner, axis=-1, keepdims=True)
        - unit * jnp.mean(inner * unit, axis=-1, keepdims=True)
    )
    return (grad_in, grad_gain, grad_shift)


def gelu_pair(values):
    cumulative = 0.5 * (1.0 + lax.erf(values * 0.7071067811865476))
    density = jnp.exp(-0.5 * values * values) * 0.3989422804014327
    return (values * cumulative, cumulative + values * density)


def over_blocks(length, block, state):
    rows = 512

    def turn(number, inner):
        return block(inner, number * rows, rows)

    return lax.fori_loop(0, length // rows, turn, state)


def per_device(
    tokens,
    segment_ids,
    cotangent,
    w_query,
    w_key,
    w_value,
    w_out,
    w_up,
    w_down,
    b_query,
    b_value,
    b_out,
    gain_one,
    shift_one,
    b_up,
    b_down,
    gain_two,
    shift_two,
):
    gathered = (
        lax.all_gather(w_query, "wa", axis=0, tiled=True),
        lax.all_gather(w_key, "wa", axis=0, tiled=True),
        lax.all_gather(w_value, "wa", axis=0, tiled=True),
        lax.all_gather(w_out, "wa", axis=0, tiled=True),
        lax.all_gather(w_up, "wa", axis=0, tiled=True),
        lax.all_gather(w_down, "wa", axis=0, tiled=True),
        lax.all_gather(b_query, "wa", axis=0, tiled=True),
        lax.all_gather(b_value, "wa", axis=0, tiled=True),
        lax.all_gather(b_out, "wa", axis=0, tiled=True),
        lax.all_gather(gain_one, "wa", axis=0, tiled=True),
        lax.all_gather(shift_one, "wa", axis=0, tiled=True),
        lax.all_gather(b_up, "wa", axis=0, tiled=True),
        lax.all_gather(b_down, "wa", axis=0, tiled=True),
        lax.all_gather(gain_two, "wa", axis=0, tiled=True),
        lax.all_gather(shift_two, "wa", axis=0, tiled=True),
    )
    full_query, full_key, full_value, full_out, full_up, full_down = gathered[:6]
    (
        bias_query,
        bias_value,
        bias_out,
        gain_attn,
        shift_attn,
        bias_up,
        bias_down,
        gain_ffn,
        shift_ffn,
    ) = [widen(item) for item in gathered[6:]]
    inputs = tokens[0]
    own_segs = segment_ids[0]
    seg_float = widen(own_segs)
    seg_wire = own_segs.astype(jnp.bfloat16)
    count = inputs.shape[0]
    length = count * lax.axis_size("ctx")
    query_rows = (
        jnp.dot(inputs, full_query, preferred_element_type=jnp.float32) + bias_query
    ).astype(jnp.bfloat16)
    key_rows = jnp.dot(inputs, full_key, preferred_element_type=jnp.float32).astype(jnp.bfloat16)
    value_rows = (
        jnp.dot(inputs, full_value, preferred_element_type=jnp.float32) + bias_value
    ).astype(jnp.bfloat16)
    query_heads = query_rows.reshape(count, HEADS, HEAD_DIM)
    first_state = (
        jnp.full((HEADS, count), masked_value, jnp.float32),
        jnp.zeros((HEADS, count), jnp.float32),
        jnp.zeros((HEADS, count, HEAD_DIM), jnp.float32),
    )
    keys_in = lax.all_gather(key_rows, "ctx", axis=0, tiled=True)
    values_in = lax.all_gather(value_rows, "ctx", axis=0, tiled=True)
    segs_in = lax.all_gather(seg_wire, "ctx", axis=0, tiled=True)

    def block(inner, offset, rows):
        key_part = lax.dynamic_slice_in_dim(keys_in, offset, rows, 0).reshape(rows, HEADS, HEAD_DIM)
        value_part = lax.dynamic_slice_in_dim(values_in, offset, rows, 0).reshape(
            rows, HEADS, HEAD_DIM
        )
        seg_part = lax.dynamic_slice_in_dim(segs_in, offset, rows, 0)

        def work(current):
            top, total, accum = current
            scores = (
                jnp.einsum(
                    "qhd,khd->hqk", query_heads, key_part, preferred_element_type=jnp.float32
                )
                * 0.125
            )
            allowed = (seg_float[:, None] == widen(seg_part)[None, :])[None]
            scores = jnp.where(allowed, scores, masked_value)
            new_top = jnp.maximum(top, jnp.max(scores, axis=-1))
            weights = jnp.where(allowed, jnp.exp(scores - new_top[:, :, None]), 0.0)
            factor = jnp.exp(top - new_top)
            total = total * factor + jnp.sum(weights, axis=-1)
            accum = accum * factor[:, :, None] + jnp.einsum(
                "hqk,khd->hqd",
                weights.astype(jnp.bfloat16),
                value_part,
                preferred_element_type=jnp.float32,
            )
            return (new_top, total, accum)

        return work(inner)

    top, total, accum = over_blocks(keys_in.shape[0], block, first_state)
    attn_heads = accum / total[:, :, None]
    log_total = top + jnp.log(total)
    attn_low = jnp.transpose(attn_heads, (1, 0, 2)).reshape(count, D).astype(jnp.bfloat16)
    attended = jnp.dot(attn_low, full_out, preferred_element_type=jnp.float32) + bias_out
    hidden, unit_one, scale_one = norm_forward(widen(inputs) + attended, gain_attn, shift_attn)
    hidden_low = hidden.astype(jnp.bfloat16)
    raised = jnp.dot(hidden_low, full_up, preferred_element_type=jnp.float32) + bias_up
    active, slope = gelu_pair(raised)
    active_low = active.astype(jnp.bfloat16)
    lowered = jnp.dot(active_low, full_down, preferred_element_type=jnp.float32) + bias_down
    result, unit_two, scale_two = norm_forward(hidden + lowered, gain_ffn, shift_ffn)
    grad_sum_two, grad_gain_two, grad_shift_two = norm_backward(
        widen(cotangent[0]), unit_two, scale_two, gain_ffn
    )
    grad_lowered = grad_sum_two.astype(jnp.bfloat16)
    grad_w_down = outer_sum(active_low, grad_lowered)
    grad_b_down = jnp.sum(widen(grad_lowered), axis=0)
    grad_raised = (back_product(grad_lowered, full_down) * slope).astype(jnp.bfloat16)
    grad_w_up = outer_sum(hidden_low, grad_raised)
    grad_b_up = jnp.sum(widen(grad_raised), axis=0)
    grad_hidden = grad_sum_two + back_product(grad_raised, full_up)
    grad_sum_one, grad_gain_one, grad_shift_one = norm_backward(
        grad_hidden, unit_one, scale_one, gain_attn
    )
    grad_attended = grad_sum_one.astype(jnp.bfloat16)
    grad_w_out = outer_sum(attn_low, grad_attended)
    grad_b_out = jnp.sum(widen(grad_attended), axis=0)
    grad_attn = back_product(grad_attended, full_out).astype(jnp.bfloat16)
    grad_heads = grad_attn.reshape(count, HEADS, HEAD_DIM)
    delta = jnp.sum(jnp.transpose(widen(grad_heads), (1, 0, 2)) * attn_heads, axis=-1)
    second_state = (
        jnp.zeros((HEADS, count, HEAD_DIM), jnp.float32),
        jnp.zeros((length, 2 * D), jnp.float32),
    )
    fold_keys_in = lax.all_gather(key_rows, "ctx", axis=0, tiled=True)
    fold_values_in = lax.all_gather(value_rows, "ctx", axis=0, tiled=True)
    fold_segs_in = lax.all_gather(seg_wire, "ctx", axis=0, tiled=True)

    def block(inner, offset, rows):
        key_part = lax.dynamic_slice_in_dim(fold_keys_in, offset, rows, 0).reshape(
            rows, HEADS, HEAD_DIM
        )
        value_part = lax.dynamic_slice_in_dim(fold_values_in, offset, rows, 0).reshape(
            rows, HEADS, HEAD_DIM
        )
        seg_part = lax.dynamic_slice_in_dim(fold_segs_in, offset, rows, 0)

        def work(current):
            grad_query_acc, grad_pairs = current
            scores = (
                jnp.einsum(
                    "qhd,khd->hqk", query_heads, key_part, preferred_element_type=jnp.float32
                )
                * 0.125
            )
            allowed = (seg_float[:, None] == widen(seg_part)[None, :])[None]
            probs = jnp.where(allowed, jnp.exp(scores - log_total[:, :, None]), 0.0)
            grad_probs = jnp.einsum(
                "qhd,khd->hqk", grad_heads, value_part, preferred_element_type=jnp.float32
            )
            grad_scores = (probs * (grad_probs - delta[:, :, None])).astype(jnp.bfloat16)
            grad_query_acc = (
                grad_query_acc
                + jnp.einsum(
                    "hqk,khd->hqd", grad_scores, key_part, preferred_element_type=jnp.float32
                )
                * 0.125
            )
            key_terms = (
                jnp.einsum(
                    "hqk,qhd->khd", grad_scores, query_heads, preferred_element_type=jnp.float32
                ).reshape(rows, D)
                * 0.125
            )
            value_terms = jnp.einsum(
                "hqk,qhd->khd",
                probs.astype(jnp.bfloat16),
                grad_heads,
                preferred_element_type=jnp.float32,
            ).reshape(rows, D)
            grad_pairs = lax.dynamic_update_slice_in_dim(
                grad_pairs, jnp.concatenate([key_terms, value_terms], axis=1), offset, 0
            )
            return (grad_query_acc, grad_pairs)

        return work(inner)

    grad_query_heads, grad_pairs_all = over_blocks(fold_keys_in.shape[0], block, second_state)
    grad_pairs_own = lax.psum_scatter(
        grad_pairs_all.astype(jnp.bfloat16), "ctx", scatter_dimension=0, tiled=True
    ).astype(jnp.float32)
    grad_query = jnp.transpose(grad_query_heads, (1, 0, 2)).reshape(count, D)
    grad_key = grad_pairs_own[:, :D]
    grad_value = grad_pairs_own[:, D:]
    grad_query_low = grad_query.astype(jnp.bfloat16)
    grad_key_low = grad_key.astype(jnp.bfloat16)
    grad_value_low = grad_value.astype(jnp.bfloat16)
    grad_w_query = outer_sum(inputs, grad_query_low)
    grad_b_query = jnp.sum(widen(grad_query_low), axis=0)
    grad_w_key = outer_sum(inputs, grad_key_low)
    grad_w_value = outer_sum(inputs, grad_value_low)
    grad_b_value = jnp.sum(widen(grad_value_low), axis=0)
    grad_inputs = (
        grad_sum_one
        + back_product(grad_query_low, full_query)
        + back_product(grad_key_low, full_key)
        + back_product(grad_value_low, full_value)
    )
    shares = (
        lax.psum_scatter(
            grad_w_query.astype(jnp.bfloat16), "wa", scatter_dimension=0, tiled=True
        ).astype(jnp.float32),
        lax.psum_scatter(
            grad_w_key.astype(jnp.bfloat16), "wa", scatter_dimension=0, tiled=True
        ).astype(jnp.float32),
        lax.psum_scatter(
            grad_w_value.astype(jnp.bfloat16), "wa", scatter_dimension=0, tiled=True
        ).astype(jnp.float32),
        lax.psum_scatter(
            grad_w_out.astype(jnp.bfloat16), "wa", scatter_dimension=0, tiled=True
        ).astype(jnp.float32),
        lax.psum_scatter(
            grad_w_up.astype(jnp.bfloat16), "wa", scatter_dimension=0, tiled=True
        ).astype(jnp.float32),
        lax.psum_scatter(
            grad_w_down.astype(jnp.bfloat16), "wa", scatter_dimension=0, tiled=True
        ).astype(jnp.float32),
        lax.psum_scatter(
            grad_b_query.astype(jnp.bfloat16), "wa", scatter_dimension=0, tiled=True
        ).astype(jnp.float32),
        lax.psum_scatter(
            grad_b_value.astype(jnp.bfloat16), "wa", scatter_dimension=0, tiled=True
        ).astype(jnp.float32),
        lax.psum_scatter(
            grad_b_out.astype(jnp.bfloat16), "wa", scatter_dimension=0, tiled=True
        ).astype(jnp.float32),
        lax.psum_scatter(
            grad_gain_one.astype(jnp.bfloat16), "wa", scatter_dimension=0, tiled=True
        ).astype(jnp.float32),
        lax.psum_scatter(
            grad_shift_one.astype(jnp.bfloat16), "wa", scatter_dimension=0, tiled=True
        ).astype(jnp.float32),
        lax.psum_scatter(
            grad_b_up.astype(jnp.bfloat16), "wa", scatter_dimension=0, tiled=True
        ).astype(jnp.float32),
        lax.psum_scatter(
            grad_b_down.astype(jnp.bfloat16), "wa", scatter_dimension=0, tiled=True
        ).astype(jnp.float32),
        lax.psum_scatter(
            grad_gain_two.astype(jnp.bfloat16), "wa", scatter_dimension=0, tiled=True
        ).astype(jnp.float32),
        lax.psum_scatter(
            grad_shift_two.astype(jnp.bfloat16), "wa", scatter_dimension=0, tiled=True
        ).astype(jnp.float32),
    )
    totals = (
        lax.psum(shares[0].astype(jnp.bfloat16), "ctx").astype(jnp.float32),
        lax.psum(shares[1].astype(jnp.bfloat16), "ctx").astype(jnp.float32),
        lax.psum(shares[2].astype(jnp.bfloat16), "ctx").astype(jnp.float32),
        lax.psum(shares[3].astype(jnp.bfloat16), "ctx").astype(jnp.float32),
        lax.psum(shares[4].astype(jnp.bfloat16), "ctx").astype(jnp.float32),
        lax.psum(shares[5].astype(jnp.bfloat16), "ctx").astype(jnp.float32),
        lax.psum(shares[6].astype(jnp.bfloat16), "ctx").astype(jnp.float32),
        lax.psum(shares[7].astype(jnp.bfloat16), "ctx").astype(jnp.float32),
        lax.psum(shares[8].astype(jnp.bfloat16), "ctx").astype(jnp.float32),
        lax.psum(shares[9].astype(jnp.bfloat16), "ctx").astype(jnp.float32),
        lax.psum(shares[10].astype(jnp.bfloat16), "ctx").astype(jnp.float32),
        lax.psum(shares[11].astype(jnp.bfloat16), "ctx").astype(jnp.float32),
        lax.psum(shares[12].astype(jnp.bfloat16), "ctx").astype(jnp.float32),
        lax.psum(shares[13].astype(jnp.bfloat16), "ctx").astype(jnp.float32),
        lax.psum(shares[14].astype(jnp.bfloat16), "ctx").astype(jnp.float32),
    )
    return (result.astype(jnp.bfloat16)[None], grad_inputs[None]) + tuple(totals)


def solution(mesh):
    placed = (
        P("wa", "ctx", None),
        P("wa", "ctx"),
        P("wa", "ctx", None),
        P("wa", None),
        P("wa", None),
        P("wa", None),
        P("wa", None),
        P("wa", None),
        P("wa", None),
        P("wa"),
        P("wa"),
        P("wa"),
        P("wa"),
        P("wa"),
        P("wa"),
        P("wa"),
        P("wa"),
        P("wa"),
    )
    return jax.shard_map(
        per_device,
        mesh=mesh,
        in_specs=placed,
        out_specs=(
            P("wa", "ctx", None),
            P("wa", "ctx", None),
            P("wa", None),
            P("wa", None),
            P("wa", None),
            P("wa", None),
            P("wa", None),
            P("wa", None),
            P("wa"),
            P("wa"),
            P("wa"),
            P("wa"),
            P("wa"),
            P("wa"),
            P("wa"),
            P("wa"),
            P("wa"),
        ),
        check_vma=False,
    )
```

profile of v0, /device:TPU:0, one launch (start us, length us, event | category | flops | bytes accessed | tf_op | source)
XLA Modules:
  0.0 1106.7 jit_solution(13284803453610989271)
XLA Ops:
  10.1 5.2 all-gather.2
  15.4 19.7 %all-gather.25.cloned.1.call-done = bf16[768,768]{1,0:T(8,128)(2,1)} async-done(((bf16[384,768]{1,0:T(8,128)(2,1)}), bf16[768,768]{1,0:T(8,128)(2,1)}) %all-gather.25.cloned.1.call-update) | async-done | bytes 1179664 | tf_op jit(solution)/shard_map/all_gather | solution.py:88
  35.1 2.8 fusion.33
  38.0 21.4 %all-gather.19.cloned.1.call-done = bf16[768,768]{1,0:T(8,128)(2,1)} async-done(((bf16[384,768]{1,0:T(8,128)(2,1)}), bf16[768,768]{1,0:T(8,128)(2,1)}) %all-gather.19.cloned.1.call-update) | async-done | bytes 1179664 | tf_op jit(solution)/shard_map/all_gather | solution.py:87
  64.3 4.3 all-gather.1
  68.7 4.3 all-gather.3
  73.1 4.3 all-gather.4
  77.5 4.3 all-gather.5
  81.9 4.3 all-gather.7
  86.3 4.3 all-gather.8
  90.7 4.3 all-gather.9
  95.1 4.4 all-gather.6
  101.0 59.6 %all-reduce = bf16[5120]{0:T(1024)(128)(2,1)S(1)} all-reduce(bf16[5120]{0:T(1024)(128)(2,1)S(1)} %dynamic-update-slice), channel_id=2, replica_groups=mesh['ctx'=16,'wa'=2] {'ctx'}, use_global_device_ids=true, to_apply=%add | all-reduce | flops 5120 | bytes 20480 | tf_op jit(solution)/shard_map/all_gather | solution.py:135
  162.7 10.7 copy.57
  173.4 58.5 %all-gather.21.cloned.1.call-done = bf16[5120,768]{1,0:T(8,128)(2,1)} async-done(((bf16[320,768]{1,0:T(8,128)(2,1)}), bf16[5120,768]{1,0:T(8,128)(2,1)}) %all-gather.21.cloned.1.call-update) | async-done | bytes 7864336 | tf_op jit(solution)/shard_map/all_gather | solution.py:133
  231.9 10.5 copy.56
  242.4 94.3 %while.34 = (s32[]{:T(128)}, f32[12,320]{1,0:T(8,128)S(1)}, f32[12,320]{1,0:T(8,128)S(1)}, f32[12,320,64]{1,2,0:T(8,128)}, f32[320]{0:T(512)S(1)}, /*index=5*/bf...) while((s32[]{:T(128)}, f32[12,320]{1,0:T(8,128)S(1)}, ...), condition=%wide.region_3.4_spmd.clone, body=%wide.region_0.3_spmd.clone.sunk | while | flops 529796352 | bytes 39541244 | solution.py:62
  340.8 6.7 multiply_convert_fusion
  347.5 35.4 %all-gather.33.cloned.1.call-done = bf16[3072,768]{1,0:T(8,128)(2,1)} async-done(((bf16[1536,768]{1,0:T(8,128)(2,1)}), bf16[3072,768]{1,0:T(8,128)(2,1)}) %all-gather.33.cloned.1.call-update) | async-done | bytes 4718608 | tf_op jit(solution)/shard_map/all_gather | solution.py:91
  382.9 5.1 fusion.63
  390.3 2.9 fusion.64
  400.9 7.5 broadcast_in_dim.126
  408.4 119.5 %while.35 = (s32[]{:T(128)}, f32[12,320,64]{1,2,0:T(8,128)S(1)}, bf16[5120,1536]{0,1:T(8,128)(2,1)}, f32[320]{0:T(512)S(1)}, bf16[5120]{0:T(1024)(128)(2,1)S(1)}...) while((s32[]{:T(128)}, f32[12,320,64]{1,2,0:T(8,128)S(1)}, ...), condition=%wide.region_14.15_spmd.clone, body=%wide.region_13.14_spmd.clone.sunk | while | flops 1282785792 | bytes 52055540 | solution.py:62
  413.7 3.3 fusion.139
  425.6 3.3 fusion.139
  437.6 3.3 fusion.139
  449.5 3.3 fusion.139
  461.5 3.3 fusion.139
  473.4 3.3 fusion.139
  485.2 3.3 fusion.139
  497.2 3.3 fusion.139
  509.1 3.3 fusion.139
  521.1 3.3 fusion.139
  528.0 20.7 %copy.64 = bf16[5120,1536]{1,0:T(8,128)(2,1)} copy(bf16[5120,1536]{0,1:T(8,128)(2,1)} %get-tuple-element.362) | data formatting | bytes 31457280
  552.2 153.4 %reduce-scatter.22.cloned.1.call-done = bf16[320,1536]{1,0:T(8,128)(2,1)} async-done(((bf16[5120,1536]{1,0:T(8,128)(2,1)}), bf16[320,1536]{1,0:T(8,128)(2,1)}) %reduce-scatter.22.cloned.1.call-update) | async-done | bytes 983056
  705.7 3.1 fusion.28
  711.2 2.8 fusion.27
  716.6 2.9 convolution_convert_fusion.2
  719.5 6.1 convolution_convert_fusion.1
  726.8 6.4 convolution_convert_fusion
  735.5 18.5 %reduce-scatter.28.cloned.1.call-done = bf16[384,768]{1,0:T(8,128)(2,1)} async-done(((bf16[768,768]{1,0:T(8,128)(2,1)}), bf16[384,768]{1,0:T(8,128)(2,1)}) %reduce-scatter.28.cloned.1.call-update) | async-done | bytes 589840
  756.0 22.4 %reduce-scatter.26.cloned.1.call-done = bf16[384,768]{1,0:T(8,128)(2,1)} async-done(((bf16[768,768]{1,0:T(8,128)(2,1)}), bf16[384,768]{1,0:T(8,128)(2,1)}) %reduce-scatter.26.cloned.1.call-update) | async-done | bytes 589840
  780.6 22.5 %reduce-scatter.16.cloned.1.call-done = bf16[384,768]{1,0:T(8,128)(2,1)} async-done(((bf16[768,768]{1,0:T(8,128)(2,1)}), bf16[384,768]{1,0:T(8,128)(2,1)}) %reduce-scatter.16.cloned.1.call-update) | async-done | bytes 589840 | tf_op jit(solution)/shard_map/reduce_scatter | solution.py:287
  803.1 62.9 %reduce-scatter.18.cloned.1.call-done = bf16[384,3072]{1,0:T(8,128)(2,1)} async-done(((bf16[768,3072]{1,0:T(8,128)(2,1)}), bf16[384,3072]{1,0:T(8,128)(2,1)}) %reduce-scatter.18.cloned.1.call-update) | async-done | bytes 2359312 | tf_op jit(solution)/shard_map/reduce_scatter | solution.py:290
  865.9 62.8 %reduce-scatter.20.cloned.1.call-done = bf16[1536,768]{1,0:T(8,128)(2,1)} async-done(((bf16[3072,768]{1,0:T(8,128)(2,1)}), bf16[1536,768]{1,0:T(8,128)(2,1)}) %reduce-scatter.20.cloned.1.call-update) | async-done | bytes 2359312 | tf_op jit(solution)/shard_map/reduce_scatter | solution.py:293
  934.1 7.1 all-reduce.12
  941.8 62.6 %all-reduce.10 = (bf16[384]{0:T(512)(128)(2,1)S(1)}, bf16[384]{0:T(512)(128)(2,1)S(1)}, bf16[384]{0:T(512)(128)(2,1)S(1)}, bf16[384]{0:T(512)(128)(2,1)S(1)}, bf...) all-reduce(bf16[384]{0:T(512)(128)(2,1)S(1)} %dynamic-slice.2, ...), channel_id=1, replica_groups=mesh['ctx'=16,'wa'=2] {'ctx'}, use_global_device_ids=true, to_apply=%region_30.31 | all-reduce | flops 4608 | bytes 18432 | tf_op jit(solution)/shard_map/psum | solution.py:331
  1013.2 74.2 %all-reduce.15.cloned.1.call-done = (bf16[384,768]{0,1:T(8,128)(2,1)}, bf16[384,768]{0,1:T(8,128)(2,1)}, bf16[384,768]{0,1:T(8,128)(2,1)}, bf16[384,768]{1,0:T(8...) async-done(((bf16[384,768]{0,1:T(8,128)(2,1)}, bf16[384,768]{0,1:T(8,128)(2,1)}, bf16[384,768]{0,1:T(8,128)(2,1)}, bf16[384,768]{1,0:T(8,128)(2,1)}, ...) | async-done | bytes 7077904 | tf_op jit(solution)/shard_map/psum | solution.py:325
  (431 shorter events, 246.0 us)
Async XLA Ops:
  7.2 52.3 %copy-start.18 = (bf16[1,320,768]{2,1,0:T(8,128)(2,1)S(1)}, bf16[1,320,768]{2,1,0:T(8,128)(2,1)}, u32[]{:S(2)}) copy-start(bf16[1,320,768]{2,1,0:T(8,128)(2,1)} %param.22) | copy-start | bytes 1474564
  7.2 27.9 %all-gather.25.cloned.1.call-start = ((), (), s32[]{:S(2)}) async-start(), calls=%async_computation.10 | async-start | bytes 1769472 | tf_op jit(solution)/shard_map/all_gather | solution.py:88
  7.9 51.5 %all-gather.19.cloned.1.call-start = ((), (), s32[]{:S(2)}) async-start(), calls=%async_computation.7 | async-start | bytes 1769472 | tf_op jit(solution)/shard_map/all_gather | solution.py:87
  8.7 151.8 %all-gather.23.cloned.1.call-start = ((), (), s32[]{:S(2)}) async-start(), calls=%async_computation.9 | async-start | bytes 1769472 | tf_op jit(solution)/shard_map/all_gather | solution.py:86
  9.4 153.3 %all-gather.27.cloned.1.call-start = ((), (), s32[]{:S(2)}) async-start(), calls=%async_computation.11 | async-start | bytes 8355840 | tf_op jit(solution)/shard_map/all_gather | solution.py:134
  37.9 26.3 %copy-start.19 = (s32[1,320]{1,0:T(1,128)S(1)}, s32[1,320]{1,0:T(1,128)}, u32[]{:S(2)}) copy-start(s32[1,320]{1,0:T(1,128)} %param.23) | copy-start | bytes 3844
  37.9 26.4 %copy-start.21 = (bf16[384]{0:T(512)(128)(2,1)S(1)}, bf16[384]{0:T(512)(128)(2,1)}, u32[]{:S(2)}) copy-start(bf16[384]{0:T(512)(128)(2,1)} %param.31) | copy-start | bytes 2308
  37.9 30.8 %copy-start.22 = (bf16[384]{0:T(512)(128)(2,1)S(1)}, bf16[384]{0:T(512)(128)(2,1)}, u32[]{:S(2)}) copy-start(bf16[384]{0:T(512)(128)(2,1)} %param.33) | copy-start | bytes 2308
  37.9 35.2 %copy-start.23 = (bf16[384]{0:T(512)(128)(2,1)S(1)}, bf16[384]{0:T(512)(128)(2,1)}, u32[]{:S(2)}) copy-start(bf16[384]{0:T(512)(128)(2,1)} %param.34) | copy-start | bytes 2308
  37.9 39.6 %copy-start.24 = (bf16[384]{0:T(512)(128)(2,1)S(1)}, bf16[384]{0:T(512)(128)(2,1)}, u32[]{:S(2)}) copy-start(bf16[384]{0:T(512)(128)(2,1)} %param.35) | copy-start | bytes 2308
  37.9 44.0 %copy-start.25 = (bf16[384]{0:T(512)(128)(2,1)S(1)}, bf16[384]{0:T(512)(128)(2,1)}, u32[]{:S(2)}) copy-start(bf16[384]{0:T(512)(128)(2,1)} %param.37) | copy-start | bytes 2308
  37.9 48.3 %copy-start.26 = (bf16[384]{0:T(512)(128)(2,1)S(1)}, bf16[384]{0:T(512)(128)(2,1)}, u32[]{:S(2)}) copy-start(bf16[384]{0:T(512)(128)(2,1)} %param.38) | copy-start | bytes 2308
  38.0 52.7 %copy-start.27 = (bf16[384]{0:T(512)(128)(2,1)S(1)}, bf16[384]{0:T(512)(128)(2,1)}, u32[]{:S(2)}) copy-start(bf16[384]{0:T(512)(128)(2,1)} %param.39) | copy-start | bytes 2308
  38.0 57.1 %copy-start.20 = (bf16[1536]{0:T(1024)(128)(2,1)S(1)}, bf16[1536]{0:T(1024)(128)(2,1)}, u32[]{:S(2)}) copy-start(bf16[1536]{0:T(1024)(128)(2,1)} %param.36) | copy-start | bytes 9220
  38.0 61.5 %copy-start.29 = (u32[32]{0:T(128)S(1)}, u32[32]{0:T(128)}, u32[]{:S(2)}) copy-start(u32[32]{0:T(128)} %constant.137) | copy-start | bytes 388
  38.0 193.9 %all-gather.21.cloned.1.call-start = ((), (), s32[]{:S(2)}) async-start(), calls=%async_computation.8 | async-start | bytes 8355840 | tf_op jit(solution)/shard_map/all_gather | solution.py:133
  62.1 276.1 %all-gather.29.cloned.1.call-start = ((), (), s32[]{:S(2)}) async-start(), calls=%async_computation.12 | async-start | bytes 1769472 | tf_op jit(solution)/shard_map/all_gather | solution.py:89
  62.7 278.1 %all-gather.31.cloned.1.call-start = ((), (), s32[]{:S(2)}) async-start(), calls=%async_computation.13 | async-start | bytes 7077888 | tf_op jit(solution)/shard_map/all_gather | solution.py:90
  63.4 319.5 %all-gather.33.cloned.1.call-start = ((), (), s32[]{:S(2)}) async-start(), calls=%async_computation.14 | async-start | bytes 7077888 | tf_op jit(solution)/shard_map/all_gather | solution.py:91
  64.2 641.5 %reduce-scatter.22.cloned.1.call-start = ((), (), s32[]{:S(2)}) async-start(), calls=%async_computation.18 | async-start | bytes 16711680
  245.8 2.7 copy-start
  264.8 2.7 copy-start
  283.6 2.7 copy-start
  338.1 9.4 copy-start.9
  340.5 7.0 copy-start.3
  382.9 7.1 slice-start.2
  382.9 5.4 copy-start.2
  382.9 7.1 slice-start.3
  389.6 3.7 slice-start
  390.0 3.3 copy-start.14
  390.3 3.0 copy-start.4
  390.3 3.0 slice-start.1
  548.6 184.7 %reduce-scatter.24.cloned.1.call-start = ((), (), s32[]{:S(2)}) async-start(), calls=%async_computation.19 | async-start | bytes 1769472
  552.2 201.8 %reduce-scatter.28.cloned.1.call-start = ((), (), s32[]{:S(2)}) async-start(), calls=%async_computation.21 | async-start | bytes 1769472
  705.7 5.5 copy-start.10
  711.1 67.3 %reduce-scatter.26.cloned.1.call-start = ((), (), s32[]{:S(2)}) async-start(), calls=%async_computation.20 | async-start | bytes 1769472
  714.1 5.5 copy-start.5
  716.5 86.5 %reduce-scatter.16.cloned.1.call-start = ((), (), s32[]{:S(2)}) async-start(), calls=%async_computation.15 | async-start | bytes 1769472 | tf_op jit(solution)/shard_map/reduce_scatter | solution.py:287
  719.5 146.5 %reduce-scatter.18.cloned.1.call-start = ((), (), s32[]{:S(2)}) async-start(), calls=%async_computation.16 | async-start | bytes 7077888 | tf_op jit(solution)/shard_map/reduce_scatter | solution.py:290
  725.6 203.0 %reduce-scatter.20.cloned.1.call-start = ((), (), s32[]{:S(2)}) async-start(), calls=%async_computation.17 | async-start | bytes 7077888 | tf_op jit(solution)/shard_map/reduce_scatter | solution.py:293
  733.3 354.2 %all-reduce.15.cloned.1.call-start = ((), (), s32[]{:S(2)}) async-start(), calls=%async_computation.22 | async-start | bytes 14155776 | tf_op jit(solution)/shard_map/psum | solution.py:325
  780.6 148.2 %copy-start.28 = (u32[32]{0:T(128)S(1)}, u32[32]{0:T(128)}, u32[]{:S(2)}) copy-start(u32[32]{0:T(128)} %constant.143) | copy-start | bytes 388
  932.8 78.9 %copy-start.11 = (bf16[320,1536]{1,0:T(8,128)(2,1)S(1)}, bf16[320,1536]{1,0:T(8,128)(2,1)}, u32[]{:S(2)}) copy-start(bf16[320,1536]{1,0:T(8,128)(2,1)} %reduce-scatter.22.cloned.1.call-done) | copy-start | bytes 2949124
  932.8 78.9 %copy-start.12 = (bf16[768,768]{1,0:T(8,128)(2,1)S(1)}, bf16[768,768]{1,0:T(8,128)(2,1)}, u32[]{:S(2)}) copy-start(bf16[768,768]{1,0:T(8,128)(2,1)} %all-gather.25.cloned.1.call-done) | copy-start | bytes 3538948
  1087.5 4.8 copy-start.17
  1087.5 6.1 copy-start.16
  1087.5 7.2 copy-start.7
  1094.6 2.8 copy-start.6
  (31 other events, 49.5 us)
Sparse Core Ops, SparseCore 0:
  9.6 25.4 all-gather.24
  36.6 22.7 all-gather.18
  61.0 22.8 all-gather.22
  86.6 72.4 all-gather.26
  161.8 70.0 all-gather.20
  233.3 21.1 all-gather.28
  256.0 62.6 all-gather.30
  320.2 62.6 all-gather.32
  548.8 156.8 reduce-scatter.21
  708.4 20.8 reduce-scatter.23
  732.1 21.7 reduce-scatter.27
  756.7 21.7 reduce-scatter.25
  781.3 21.7 reduce-scatter.15
  805.9 59.9 reduce-scatter.17
  868.7 59.9 reduce-scatter.19
  934.1 153.2 all-reduce.14
where the time goes:
time: 1110 us
  waiting for transfers between devices  556 us (50%)
  matrix products  183 us (16%)
  blocking collectives  169 us (15%)
  local copies, waits for them, and re-layouts  115 us (10%)
  other arithmetic  63.8 us (6%)
  between operations  16.9 us (2%)
    unnamed x20, waiting for transfers between devices  198 us
    psum x1, waiting for transfers between devices, per_device(): lax.psum(shares[0].astype(jnp.bfloat16), 'ctx').astype(jnp.float32)  74.2 us
    unnamed x100, local copies, waits for them, and re-layouts  64.8 us
    reduce_scatter x1, waiting for transfers between devices, per_device(): lax.psum_scatter(grad_w_up.astype(jnp.bfloat16), 'wa', scatter_dimension=...  62.9 us
    reduce_scatter x1, waiting for transfers between devices, per_device(): lax.psum_scatter(grad_w_down.astype(jnp.bfloat16), 'wa', scatter_dimensio...  62.8 us
    psum x1, blocking collectives, per_device(): lax.psum(shares[6].astype(jnp.bfloat16), 'ctx').astype(jnp.float32)  62.6 us
    all_gather x1, blocking collectives, per_device(): segs_in = lax.all_gather(seg_wire, 'ctx', axis=0, tiled=True)  59.6 us
    all_gather x1, waiting for transfers between devices, per_device(): keys_in = lax.all_gather(key_rows, 'ctx', axis=0, tiled=True)  58.5 us
  transfers between devices with their start and end apart: 16, of which 11 were waited for; matrix products, arithmetic and copies ran while one was open for 16% of the time, Pallas kernels for 0%

commit v1 on v0

v1 whole, which is shorter than its diff:
```python
import functools

import jax
import jax.numpy as jnp
from jax import lax
from jax.experimental import pallas as pl
from jax.experimental.pallas import tpu as pltpu
from jax.sharding import Mesh
from jax.sharding import PartitionSpec as P

D = 768
HEADS = 12
HEAD_DIM = 64
FF = 3072
DOCS = 32

GROUPS = 4
OWN = HEADS // GROUPS
WIDTH = OWN * HEAD_DIM
QTILE = 256
KTILE = 512

epsilon = 1e-05
masked_value = -1e30
NT = (((1,), (1,)), ((), ()))
NN = (((1,), (0,)), ((), ()))


def widen(array):
    return array.astype(jnp.float32)


def low(array):
    return array.astype(jnp.bfloat16)


def mm(left, right):
    return jnp.dot(left, right, preferred_element_type=jnp.float32)


def outer_sum(left, right):
    return lax.dot_general(
        left, right, (((0,), (0,)), ((), ())), preferred_element_type=jnp.float32
    )


def back_product(grad, weight):
    return lax.dot_general(grad, weight, NT, preferred_element_type=jnp.float32)


def norm_forward(values, gain, shift):
    centre = values - jnp.mean(values, axis=-1, keepdims=True)
    scale = lax.rsqrt(jnp.mean(centre * centre, axis=-1, keepdims=True) + epsilon)
    unit = centre * scale
    return (unit * gain + shift, unit, scale)


def norm_backward(grad, unit, scale, gain):
    grad_gain = jnp.sum(grad * unit, axis=0)
    grad_shift = jnp.sum(grad, axis=0)
    inner = grad * gain
    grad_in = scale * (
        inner
        - jnp.mean(inner, axis=-1, keepdims=True)
        - unit * jnp.mean(inner * unit, axis=-1, keepdims=True)
    )
    return (grad_in, grad_gain, grad_shift)


def gelu_pair(values):
    cumulative = 0.5 * (1.0 + lax.erf(values * 0.7071067811865476))
    density = jnp.exp(-0.5 * values * values) * 0.3989422804014327
    return (values * cumulative, cumulative + values * density)


def swap(array, axis, bit):
    size = lax.axis_size(axis)
    return lax.ppermute(array, axis, [(i, i ^ bit) for i in range(size)])


K_BLOCK = (0, 0, 1)
V_BLOCK = (2, 2, 1)
K_UPPER = (False, True, True)
V_UPPER = (False, True, False)


def lane_half(array, upper):
    lane = lax.broadcasted_iota(jnp.int32, array.shape, 1)
    keep = (lane >= 64) if upper else (lane < 64)
    return jnp.where(keep, array, jnp.zeros_like(array))


def load_pieces(where, ids, pieces, kv, sem, rows, classes):
    copies = []
    for piece, (mask, flips) in zip(pieces, where):
        for slot, flip in enumerate(flips):
            chunk = (ids[0] ^ flip) * classes + (ids[1] ^ mask)
            start = pl.multiple_of(chunk * rows, 64)
            copies.append(
                pltpu.make_async_copy(
                    piece.at[slot], kv.at[pl.ds(start, rows), :], sem.at[len(copies)]
                )
            )
    for copy in copies:
        copy.start()
    for copy in copies:
        copy.wait()


def forward_kernel(where, rows, classes, ids, flags, q, seg_q, seg_k, *rest):
    count = len(where)
    pieces = rest[:count]
    o_low, o_full, lse, kv, vt, qm, top, total, accum, sem = rest[count:]
    length = kv.shape[0]
    tiles = length // KTILE
    load_pieces(where, ids, pieces, kv, sem, rows, classes)

    @pl.loop(0, tiles)
    def _(t):
        start = pl.multiple_of(t * KTILE, KTILE)
        vt[0:128, pl.ds(start, KTILE)] = kv[pl.ds(start, KTILE), 128:256].T
        vt[128:256, pl.ds(start, KTILE)] = kv[pl.ds(start, KTILE), 256:384].T

    v_row = (128, 192, 0)

    @pl.loop(0, q.shape[0] // QTILE)
    def _(j):
        base = pl.multiple_of(j * QTILE, QTILE)
        for head in range(OWN):
            block = q[pl.ds(base, QTILE), pl.ds(128 * K_BLOCK[head], 128)]
            qm[head] = lane_half(block, K_UPPER[head])
        top[...] = jnp.full_like(top, masked_value)
        total[...] = jnp.zeros_like(total)
        accum[...] = jnp.zeros_like(accum)
        query_ids = seg_q[0:1, pl.ds(base, QTILE)]

        @pl.loop(0, tiles)
        def _(t):
            @pl.when(flags[j * tiles + t] > 0)
            def _():
                start = pl.multiple_of(t * KTILE, KTILE)
                ids_k = seg_k[pl.ds(start, KTILE), :]
                same = jnp.concatenate([ids_k] * (QTILE // 128), axis=1) == query_ids
                for head in range(OWN):
                    keys = kv[pl.ds(start, KTILE), 128 * K_BLOCK[head] : 128 * K_BLOCK[head] + 128]
                    scores = lax.dot_general(
                        keys, qm[head], NT, preferred_element_type=jnp.float32
                    )
                    scores = jnp.where(same, scores, masked_value)
                    old = top[head : head + 1, :]
                    new = jnp.maximum(old, jnp.max(scores, axis=0, keepdims=True))
                    weights = jnp.exp(scores - new)
                    factor = jnp.exp(old - new)
                    top[head : head + 1, :] = new
                    total[head : head + 1, :] = total[head : head + 1, :] * factor + jnp.sum(
                        weights, axis=0, keepdims=True
                    )
                    rows_v = slice(v_row[head], v_row[head] + 64)
                    accum[64 * head : 64 * head + 64, :] = accum[
                        64 * head : 64 * head + 64, :
                    ] * factor + jnp.dot(
                        vt[rows_v, pl.ds(start, KTILE)],
                        weights.astype(jnp.bfloat16),
                        preferred_element_type=jnp.float32,
                    )

        outs = [accum[64 * head : 64 * head + 64, :] / total[head : head + 1, :] for head in range(OWN)]
        lower = jnp.concatenate(outs[:2], axis=0).T
        upper = jnp.concatenate([outs[2], jnp.zeros_like(outs[2])], axis=0).T
        o_full[pl.ds(base, QTILE), 0:128] = lower
        o_full[pl.ds(base, QTILE), 128:256] = upper
        o_low[pl.ds(base, QTILE), 0:128] = lower.astype(jnp.bfloat16)
        o_low[pl.ds(base, QTILE), 128:192] = upper[:, 0:64].astype(jnp.bfloat16)
        lse[:, pl.ds(base, QTILE)] = top[...] + jnp.log(total[...])


def backward_kernel(where, rows, classes, out_where, ids, flags, q, seg_q, seg_k, grad, o_full, lse, *rest):
    count = len(where)
    pieces = rest[:count]
    rest = rest[count:]
    outs = rest[: len(out_where)]
    dq, kv, kt, qm, dom, stats, dqt, dkv, low_kv, sem = rest[len(out_where) :]
    length = kv.shape[0]
    tiles = length // KTILE
    load_pieces(where, ids, pieces, kv, sem, rows, classes)

    @pl.loop(0, tiles)
    def _(t):
        start = pl.multiple_of(t * KTILE, KTILE)
        kt[0:128, pl.ds(start, KTILE)] = kv[pl.ds(start, KTILE), 0:128].T
        kt[128:256, pl.ds(start, KTILE)] = kv[pl.ds(start, KTILE), 128:256].T
        dkv[pl.ds(start, KTILE), :] = jnp.zeros((KTILE, 384), jnp.float32)

    k_row = (0, 64, 192)

    @pl.loop(0, q.shape[0] // QTILE)
    def _(j):
        base = pl.multiple_of(j * QTILE, QTILE)
        for head in range(OWN):
            block = q[pl.ds(base, QTILE), pl.ds(128 * K_BLOCK[head], 128)]
            qm[head] = lane_half(block, K_UPPER[head])
            block = grad[pl.ds(base, QTILE), pl.ds(128 * (2 - V_BLOCK[head]), 128)]
            dom[head] = lane_half(block, V_UPPER[head])
        for part in range(2):
            product = (
                grad[pl.ds(base, QTILE), 128 * part : 128 * part + 128].astype(jnp.float32)
                * o_full[pl.ds(base, QTILE), 128 * part : 128 * part + 128]
            ).T
            for half in range(2):
                head = 2 * part + half
                if head < OWN:
                    stats[head : head + 1, :] = jnp.sum(
                        product[64 * half : 64 * half + 64], axis=0, keepdims=True
                    )
        dqt[...] = jnp.zeros_like(dqt)
        query_ids = seg_q[0:1, pl.ds(base, QTILE)]

        @pl.loop(0, tiles)
        def _(t):
            @pl.when(flags[j * tiles + t] > 0)
            def _():
                start = pl.multiple_of(t * KTILE, KTILE)
                ids_k = seg_k[pl.ds(start, KTILE), :]
                same = jnp.concatenate([ids_k] * (QTILE // 128), axis=1) == query_ids
                sums = [None, None, None]

                def add(block, term):
                    sums[block] = term if sums[block] is None else sums[block] + term

                for head in range(OWN):
                    kb, vb = K_BLOCK[head], V_BLOCK[head]
                    keys = kv[pl.ds(start, KTILE), 128 * kb : 128 * kb + 128]
                    vals = kv[pl.ds(start, KTILE), 128 * vb : 128 * vb + 128]
                    scores = lax.dot_general(
                        keys, qm[head], NT, preferred_element_type=jnp.float32
                    )
                    probs = jnp.where(
                        same, jnp.exp(scores - lse[head : head + 1, pl.ds(base, QTILE)]), 0.0
                    )
                    grad_probs = lax.dot_general(
                        vals, dom[head], NT, preferred_element_type=jnp.float32
                    )
                    grad_scores = (probs * (grad_probs - stats[head : head + 1, :])).astype(
                        jnp.bfloat16
                    )
                    add(vb, jnp.dot(probs.astype(jnp.bfloat16), dom[head], preferred_element_type=jnp.float32))
                    add(kb, jnp.dot(grad_scores, qm[head], preferred_element_type=jnp.float32))
                    rows_k = slice(k_row[head], k_row[head] + 64)
                    dqt[64 * head : 64 * head + 64, :] += jnp.dot(
                        kt[rows_k, pl.ds(start, KTILE)],
                        grad_scores,
                        preferred_element_type=jnp.float32,
                    )
                for block in range(3):
                    dkv[pl.ds(start, KTILE), 128 * block : 128 * block + 128] += sums[block]

        lower = dqt[0:128, :].T * 0.125
        upper = dqt[64:192, :].T * 0.125
        dq[pl.ds(base, QTILE), 0:128] = lower.astype(jnp.bfloat16)
        dq[pl.ds(base, QTILE), 128:192] = upper[:, 64:128].astype(jnp.bfloat16)

    @pl.loop(0, tiles)
    def _(t):
        start = pl.multiple_of(t * KTILE, KTILE)
        low_kv[pl.ds(start, KTILE), :] = dkv[pl.ds(start, KTILE), :].astype(jnp.bfloat16)

    copies = []
    for out, masks in zip(outs, out_where):
        for slot, mask in enumerate(masks):
            for flip in range(GROUPS):
                chunk = (ids[0] ^ flip) * classes + (ids[1] ^ mask)
                start = pl.multiple_of(chunk * rows, 64)
                copies.append(
                    pltpu.make_async_copy(
                        low_kv.at[pl.ds(start, rows), :], out.at[slot, flip], sem.at[len(copies)]
                    )
                )
    for copy in copies:
        copy.start()
    for copy in copies:
        copy.wait()


VMEM_SPEC = pl.BlockSpec(memory_space=pltpu.VMEM)
SMEM_SPEC = pl.BlockSpec(memory_space=pltpu.SMEM)
ANY_SPEC = pl.BlockSpec(memory_space=pl.ANY)
PARAMS = pltpu.CompilerParams(vmem_limit_bytes=56 * 1024 * 1024)


def attend_forward(ids, flags, q, seg_q, seg_k, pieces, where, rows, classes):
    length = seg_k.shape[0]
    queries = q.shape[0]
    copies = sum(len(flips) for _, flips in where)
    return pl.pallas_call(
        functools.partial(forward_kernel, where, rows, classes),
        out_shape=(
            jax.ShapeDtypeStruct((queries, WIDTH), jnp.bfloat16),
            jax.ShapeDtypeStruct((queries, 256), jnp.float32),
            jax.ShapeDtypeStruct((8, queries), jnp.float32),
        ),
        in_specs=[SMEM_SPEC, SMEM_SPEC, VMEM_SPEC, VMEM_SPEC, VMEM_SPEC]
        + [ANY_SPEC] * len(pieces),
        out_specs=(VMEM_SPEC,) * 3,
        scratch_shapes=[
            pltpu.VMEM((length, 384), jnp.bfloat16),
            pltpu.VMEM((256, length), jnp.bfloat16),
            pltpu.VMEM((OWN, QTILE, 128), jnp.bfloat16),
            pltpu.VMEM((8, QTILE), jnp.float32),
            pltpu.VMEM((8, QTILE), jnp.float32),
            pltpu.VMEM((WIDTH, QTILE), jnp.float32),
            pltpu.SemaphoreType.DMA((copies,)),
        ],
        compiler_params=PARAMS,
        cost_estimate=pl.CostEstimate(
            flops=queries * length * WIDTH * 4, bytes_accessed=8 << 20, transcendentals=0
        ),
        name="attend_forward",
    )(ids, flags, q, seg_q, seg_k, *pieces)


def attend_backward(ids, flags, q, seg_q, seg_k, grad, o_full, lse, pieces, where, rows, classes, out_where):
    length = seg_k.shape[0]
    queries = q.shape[0]
    copies = sum(len(flips) for _, flips in where)
    return pl.pallas_call(
        functools.partial(backward_kernel, where, rows, classes, out_where),
        out_shape=tuple(
            jax.ShapeDtypeStruct((len(masks), GROUPS, rows, 384), jnp.bfloat16)
            for masks in out_where
        )
        + (jax.ShapeDtypeStruct((queries, WIDTH), jnp.bfloat16),),
        in_specs=[SMEM_SPEC, SMEM_SPEC] + [VMEM_SPEC] * 6 + [ANY_SPEC] * len(pieces),
        out_specs=(ANY_SPEC,) * len(out_where) + (VMEM_SPEC,),
        scratch_shapes=[
            pltpu.VMEM((length, 384), jnp.bfloat16),
            pltpu.VMEM((256, length), jnp.bfloat16),
            pltpu.VMEM((OWN, QTILE, 128), jnp.bfloat16),
            pltpu.VMEM((OWN, QTILE, 128), jnp.bfloat16),
            pltpu.VMEM((8, QTILE), jnp.float32),
            pltpu.VMEM((WIDTH, QTILE), jnp.float32),
            pltpu.VMEM((length, 384), jnp.float32),
            pltpu.VMEM((length, 384), jnp.bfloat16),
            pltpu.SemaphoreType.DMA((copies,)),
        ],
        compiler_params=PARAMS,
        cost_estimate=pl.CostEstimate(
            flops=queries * length * WIDTH * 10, bytes_accessed=16 << 20, transcendentals=0
        ),
        name="attend_backward",
    )(ids, flags, q, seg_q, seg_k, grad, o_full, lse, *pieces)


def gather_rows(weight, core):
    half = weight.shape[0] // 2
    part = lax.dynamic_slice_in_dim(weight, core * half, half, 0)
    return lax.all_gather(part, ("wa", "c"), axis=0, tiled=True)


def reduce_blocks(grad):
    flat = grad.reshape((-1,) + grad.shape[2:])
    mine = lax.psum_scatter(flat, ("wa", "c"), scatter_dimension=0, tiled=True)
    mine = lax.psum_scatter(mine, "m", scatter_dimension=0, tiled=True)
    mine = lax.psum_scatter(mine, "h", scatter_dimension=0, tiled=True)
    return lax.all_gather(mine, ("c", "m", "h"), axis=0, tiled=True)


def pick_columns(weight, group):
    q, k, v = (lax.dynamic_slice_in_dim(w, group * WIDTH, WIDTH, w.ndim - 1) for w in weight)
    return jnp.concatenate(
        [
            k[..., :128],
            v[..., 128:],
            k[..., 128:],
            v[..., :128],
            q[..., :128],
            jnp.zeros_like(q[..., :64]),
            q[..., 128:],
        ],
        axis=-1,
    )


def per_device(
    tokens,
    segment_ids,
    cotangent,
    w_query,
    w_key,
    w_value,
    w_out,
    w_up,
    w_down,
    b_query,
    b_value,
    b_out,
    gain_one,
    shift_one,
    b_up,
    b_down,
    gain_two,
    shift_two,
):
    mid = lax.axis_size("m")
    wide = lax.axis_size("wa")
    classes = 2 * mid
    group = lax.axis_index("h")
    core = lax.axis_index("c")
    kind = lax.axis_index("m") * 2 + core
    side = lax.axis_index("wa")
    inputs = tokens[0]
    count = inputs.shape[0]
    length = count * GROUPS * classes
    tiles = length // KTILE
    ids = jnp.stack([group, kind]).astype(jnp.int32)
    order = group ^ jnp.arange(GROUPS)

    second = swap(inputs, "h", 1)
    third = swap(inputs, "h", 2)
    fourth = swap(third, "h", 1)

    smalls = [b_query, b_value, b_out, gain_one, shift_one, b_up, b_down, gain_two, shift_two]
    joined = lax.all_gather(jnp.concatenate(smalls), "wa", axis=0)
    full, place = [], 0
    for item in smalls:
        size = item.shape[0]
        full.append(widen(joined[:, place : place + size].reshape(-1)))
        place += size
    bias_query, bias_value, bias_out, gain_attn, shift_attn, bias_up, bias_down, gain_ffn, shift_ffn = full

    segs = lax.all_gather(segment_ids[0], ("h", "m", "c"), axis=0)
    w_group = lax.all_gather(
        pick_columns((w_query, w_key, w_value), group), "wa", axis=0, tiled=True
    )
    zero_bias = jnp.zeros_like(bias_query)
    b_group = pick_columns((bias_query, zero_bias, bias_value), group)

    full_out = gather_rows(w_out, core)
    full_up = gather_rows(w_up, core)
    full_down = gather_rows(w_down, core)
    full_query = gather_rows(w_query, core)
    full_key = gather_rows(w_key, core)
    full_value = gather_rows(w_value, core)

    own_segs = jnp.take(segs.reshape(GROUPS, classes, count), order, axis=0)
    own_segs = lax.dynamic_index_in_dim(own_segs, kind, 1, keepdims=False).reshape(-1)
    names = jnp.arange(DOCS)
    has_q = jnp.any(own_segs.reshape(-1, QTILE, 1) == names, axis=1)
    has_k = jnp.any(segs.reshape(tiles, KTILE, 1) == names, axis=1)
    flags = jnp.any(has_q[:, None, :] & has_k[None, :, :], axis=-1).astype(jnp.int32).reshape(-1)
    seg_q = jnp.broadcast_to(widen(own_segs)[None, :], (8, GROUPS * count))
    seg_k = jnp.broadcast_to(widen(segs).reshape(-1, 1), (length, 128))

    def project(chunks):
        joined = jnp.concatenate(chunks, axis=0)
        kv = low(mm(joined, w_group[:, :384]) + b_group[:384])
        return kv.reshape(len(chunks), count, 384)

    where, pieces = [], []
    for chunks, flips in (((inputs, second, third), (0, 1, 2)), ((fourth,), (3,))):
        have = {0: project(chunks)}
        bit = 1
        while bit < mid:
            for mask in list(have):
                have[mask | (bit << 1)] = swap(have[mask], "m", bit)
            bit *= 2
        for mask in list(have):
            have[mask | 1] = swap(have[mask], "c", 1)
        for mask, piece in have.items():
            where.append((mask, flips))
            pieces.append(piece)
    where = tuple(where)
    group_tokens = jnp.concatenate([inputs, second, third, fourth], axis=0)
    q_rows = low(mm(group_tokens, w_group[:, 384:]) + b_group[384:]) * jnp.bfloat16(0.125)

    o_low, o_full, lse = attend_forward(
        ids, flags, q_rows, seg_q, seg_k, pieces, where, count, classes
    )

    def send_back(rows):
        parts = rows.reshape(GROUPS, count, -1)
        return [parts[0]] + [swap(parts[flip], "h", flip) for flip in range(1, GROUPS)]

    def in_order(parts):
        return jnp.take(jnp.stack(parts), order, axis=0)

    attn_low = jnp.transpose(in_order(send_back(o_low)), (1, 0, 2)).reshape(count, D)
    attended = mm(attn_low, full_out) + bias_out
    hidden, unit_one, scale_one = norm_forward(widen(inputs) + attended, gain_attn, shift_attn)
    hidden_low = low(hidden)
    raised = mm(hidden_low, full_up) + bias_up
    active, slope = gelu_pair(raised)
    active_low = low(active)
    lowered = mm(active_low, full_down) + bias_down
    result, unit_two, scale_two = norm_forward(hidden + lowered, gain_ffn, shift_ffn)
    grad_sum_two, grad_gain_two, grad_shift_two = norm_backward(
        widen(cotangent[0]), unit_two, scale_two, gain_ffn
    )
    grad_lowered = low(grad_sum_two)
    grad_w_down = low(outer_sum(active_low, grad_lowered))
    grad_b_down = jnp.sum(widen(grad_lowered), axis=0)
    grad_raised = low(back_product(grad_lowered, full_down) * slope)
    grad_w_up = low(outer_sum(hidden_low, grad_raised))
    grad_b_up = jnp.sum(widen(grad_raised), axis=0)
    grad_hidden = grad_sum_two + back_product(grad_raised, full_up)
    grad_sum_one, grad_gain_one, grad_shift_one = norm_backward(
        grad_hidden, unit_one, scale_one, gain_attn
    )
    grad_attended = low(grad_sum_one)
    grad_w_out = low(outer_sum(attn_low, grad_attended))
    grad_b_out = jnp.sum(widen(grad_attended), axis=0)
    grad_attn = low(back_product(grad_attended, full_out))

    by_group = jnp.take(
        jnp.transpose(grad_attn.reshape(count, GROUPS, WIDTH), (1, 0, 2)), order, axis=0
    )
    grad_heads = [by_group[0]] + [swap(by_group[flip], "h", flip) for flip in range(1, GROUPS)]
    grad_rows = jnp.pad(jnp.concatenate(grad_heads, axis=0), ((0, 0), (0, 64)))

    keep, give = tuple(range(0, classes, 2)), tuple(range(1, classes, 2))
    kept, given, dq = attend_backward(
        ids, flags, q_rows, seg_q, seg_k, grad_rows, o_full, lse,
        pieces, where, count, classes, (keep, give),
    )

    blocks = 2 * wide
    vectors = jnp.concatenate(
        [grad_b_out, grad_gain_one, grad_shift_one, grad_b_down, grad_gain_two, grad_shift_two, grad_b_up]
    )
    vectors = jnp.pad(low(vectors).reshape(-1, D), ((0, 6), (0, 0)))
    down_rows, up_rows, out_rows = FF // blocks, FF // blocks, D // blocks
    ffn = jnp.concatenate(
        [
            grad_w_down.reshape(blocks, down_rows, D),
            grad_w_up.reshape(blocks, up_rows, D),
            grad_w_out.reshape(blocks, out_rows, D),
            jnp.broadcast_to(vectors[None], (blocks, 16, D)),
        ],
        axis=1,
    )
    ffn_sum = reduce_blocks(ffn).reshape(2, -1, D)
    out_down = widen(ffn_sum[:, :down_rows]).reshape(-1, D)
    out_up = widen(ffn_sum[:, down_rows : down_rows + up_rows]).reshape(-1, FF)
    place = down_rows + up_rows
    out_out = widen(ffn_sum[:, place : place + out_rows]).reshape(-1, D)
    small = widen(ffn_sum[0, place + out_rows :])

    def share(row, rows):
        vector = small[row : row + rows].reshape(-1)
        size = vector.shape[0] // wide
        return lax.dynamic_slice_in_dim(vector, side * size, size, 0)

    partial = widen(kept) + widen(swap(given, "c", 1))
    stay = list(keep)
    bit = mid // 2
    while bit >= 1:
        mask = bit << 1
        near = [i for i, m in enumerate(stay) if not m & mask]
        far = [i for i, m in enumerate(stay) if m & mask]
        sent = swap(low(partial[far[0] : far[-1] + 1]), "m", bit)
        partial = widen(low(partial[near[0] : near[-1] + 1])) + widen(sent)
        stay = [stay[i] for i in near]
        bit //= 2
    dkv = low(partial[0]).reshape(GROUPS * count, 384)
    both = jnp.concatenate([dkv, dq], axis=1)

    width = both.shape[1]
    w_grad = low(outer_sum(group_tokens, both)).reshape(blocks, D // blocks, width)
    b_grad = low(jnp.sum(widen(both), axis=0))
    b_grad = jnp.pad(b_grad[None], ((0, 15), (0, 0)))
    qkv = jnp.concatenate([w_grad, jnp.broadcast_to(b_grad[None], (blocks, 16, width))], axis=1)
    rows = qkv.shape[1]
    mine = lax.psum_scatter(qkv.reshape(blocks * rows, width), ("wa", "c"), scatter_dimension=0, tiled=True)
    mine = lax.psum(mine, "m")
    every = lax.all_gather(mine, ("c", "h"), axis=0).reshape(2, GROUPS, rows, width)
    every = widen(every)

    def columns(block):
        k = jnp.concatenate([block[..., :128], block[..., 192:256]], axis=-1)
        v = jnp.concatenate([block[..., 256:384], block[..., 128:192]], axis=-1)
        q = block[..., 384:576]
        return [
            jnp.transpose(item, (0, 2, 1, 3)).reshape(2, -1, D) for item in (q, k, v)
        ]

    out_query, out_key, out_value = (
        item.reshape(-1, D) for item in columns(every[:, :, : rows - 16])
    )
    bias_rows = columns(every[:, :, rows - 16 : rows - 15])
    part = D // wide
    out_b_query = lax.dynamic_slice_in_dim(bias_rows[0][0, 0], side * part, part, 0)
    out_b_value = lax.dynamic_slice_in_dim(bias_rows[2][0, 0], side * part, part, 0)

    back = in_order(send_back(both))
    own_key = jnp.concatenate([back[..., :128], back[..., 192:256]], axis=-1)
    own_value = jnp.concatenate([back[..., 256:384], back[..., 128:192]], axis=-1)
    own_query = back[..., 384:576]
    natural = [
        jnp.transpose(item, (1, 0, 2)).reshape(count, D) for item in (own_query, own_key, own_value)
    ]
    grad_inputs = (
        grad_sum_one
        + back_product(natural[0], full_query)
        + back_product(natural[1], full_key)
        + back_product(natural[2], full_value)
    )
    return (
        low(result)[None],
        grad_inputs[None],
        out_query,
        out_key,
        out_value,
        out_out,
        out_up,
        out_down,
        out_b_query,
        out_b_value,
        share(0, 1),
        share(1, 1),
        share(2, 1),
        share(6, 4),
        share(3, 1),
        share(4, 1),
        share(5, 1),
    )


def solution(mesh):
    chunks, wide = mesh.devices.shape
    finer = Mesh(
        mesh.devices.reshape(GROUPS, chunks // (2 * GROUPS), 2, wide), ("h", "m", "c", "wa")
    )
    ctx = ("h", "m", "c")
    seq3, seq2 = P("wa", ctx, None), P("wa", ctx)
    matrix, vector = P("wa", None), P("wa")
    return jax.shard_map(
        per_device,
        mesh=finer,
        in_specs=(seq3, seq2, seq3) + (matrix,) * 6 + (vector,) * 9,
        out_specs=(seq3, seq3) + (matrix,) * 6 + (vector,) * 9,
        check_vma=False,
    )
```

time: 1110 us -> 725 us (0.65)
  waiting for transfers between devices: 556 us -> 298 us
  matrix products: 183 us -> 47.3 us
  Pallas kernels: 0 us -> 101 us
  blocking collectives: 169 us -> 82.1 us
  starting transfers between devices: 0.89 us -> 30.6 us
  other arithmetic: 63.8 us -> 42.1 us
  local copies, waits for them, and re-layouts: 115 us -> 95.7 us
    unnamed x20 -> x13, waiting for transfers between devices: 198 us -> 1.04 us
    dot_general x82 -> x12, matrix products: 160 us -> 32 us  [the longest x6 19.2 us: mm(): return jnp.dot(left, right, preferred_element_type=jnp.float32)]
    ppermute x0 -> x20, waiting for transfers between devices: none -> 104 us  [swap(): return lax.ppermute(array, axis, [(i, i ^ bit) for i in range(size)])]
    pallas_call x0 -> x2, Pallas kernels: none -> 101 us  [the longest x1 50.5 us: attend_forward(): pl.pallas_call(functools.partial(forward_kernel, where, rows, classes), o...]
    all_gather x8, waiting for transfers between devices: 135 us -> 37.1 us  [the longest x1 31 us: reduce_blocks(): return lax.all_gather(mine, ('c', 'm', 'h'), axis=0, tiled=True)]
    psum x1 -> x0, blocking collectives: 62.6 us -> none  [per_device(): lax.psum(shares[6].astype(jnp.bfloat16), 'ctx').astype(jnp.float32)]
    psum x1, waiting for transfers between devices: 74.2 us -> 22 us  [per_device(): mine = lax.psum(mine, 'm')]
    unnamed x100 -> x116, local copies, waits for them, and re-layouts: 64.8 us -> 12.7 us
  transfers between devices with their start and end apart: 16 -> 33, of which waited for: 11 -> 16; matrix products, arithmetic and copies ran while one was open for 16% -> 22% of each run, Pallas kernels for 0% -> 7%
where the time goes in v1:
time: 725 us; the launch traced here: 713 us
  waiting for transfers between devices  298 us (41%)
  Pallas kernels  101 us (14%)
  local copies, waits for them, and re-layouts  95.7 us (13%)
  blocking collectives  82.1 us (11%)
  matrix products  47.3 us (7%)
  other arithmetic  42.1 us (6%)
  starting transfers between devices  30.6 us (4%)
  between operations  16.3 us (2%)
    ppermute x20, waiting for transfers between devices, swap(): return lax.ppermute(array, axis, [(i, i ^ bit) for i in range(size)])  104 us
    reduce_scatter x1, waiting for transfers between devices, reduce_blocks(): mine = lax.psum_scatter(flat, ('wa', 'c'), scatter_dimension=0, tiled=True)  93.6 us
    pallas_call x1, Pallas kernels, attend_forward(): pl.pallas_call(functools.partial(forward_kernel, where, rows, classes), o...  50.5 us
    pallas_call x1, Pallas kernels, attend_backward(): pl.pallas_call(functools.partial(backward_kernel, where, rows, classes, o...  50.3 us
    reduce_scatter x1, waiting for transfers between devices, reduce_blocks(): mine = lax.psum_scatter(mine, 'm', scatter_dimension=0, tiled=True)  40.6 us
    unnamed x1, blocking collectives  31.3 us
    all_gather x1, waiting for transfers between devices, reduce_blocks(): return lax.all_gather(mine, ('c', 'm', 'h'), axis=0, tiled=True)  31 us
    ppermute x20, starting transfers between devices, swap(): return lax.ppermute(array, axis, [(i, i ^ bit) for i in range(size)])  28.7 us
  transfers between devices with their start and end apart: 33, of which 16 were waited for; matrix products, arithmetic and copies ran while one was open for 22% of the time, Pallas kernels for 7%

profile of v1, /device:TPU:0, one launch (start us, length us, event | category | flops | bytes accessed | tf_op | source)
XLA Modules:
  0.0 713.1 jit_solution(11001609127826742748)
XLA Ops:
  10.5 2.4 constant_dynamic-slice_fusion.12
  13.0 4.1 collective-permute-start.1
  20.7 4.8 all-gather.2
  31.9 21.7 %all-gather.1 = s32[16,1,320]{2,1,0:T(1,128)S(1)} all-gather(s32[1,1,320]{2,1,0:T(1,128)S(1)} %bitcast.130), channel_id=1, replica_groups=mesh['h'=4,'m'=2,'c'=2,'wa'=2] {'h','m','c'}, dimensions={0}, use_global_device_ids=true | all-gather | bytes 21760 | tf_op jit(solution)/shard_map/all_gather | solution.py:430
  54.8 24.3 %all_gather.40 = bf16[768,640]{1,0:T(8,128)(2,1)S(1)} all-gather(bf16[384,640]{1,0:T(8,128)(2,1)S(1)} %concatenate.51), channel_id=1, replica_groups=mesh['h'=4,'m'=2,'c'=2,'wa'=2] {'wa'}, dimensions={0}, use_global_device_ids=true | all-gather | bytes 1474560 | tf_op jit(solution)/shard_map/all_gather | solution.py:431
  82.5 17.1 %collective-permute-done.3.rest_1_ = bf16[3,320,384]{2,1,0:T(8,128)(2,1)S(1)} collective-permute-done((bf16[3,320,384]{2,1,0:T(8,128)(2,1)S(1)}, bf16[3,320,384]{2,1,0:T(8,128)(2,1)S(1)}, u32[]{:S(2)}, u32[]{:S(2)}) %collective-permute-start.3) | collective-permute-done | bytes 737312 | tf_op jit(solution)/shard_map/ppermute | solution.py:78
  102.5 6.1 collective-permute-done.6.rest_5_
  108.6 3.1 fusion.7.q
  112.5 3.4 broadcast_in_dim.49.seg_k
  115.9 50.5 %attend_forward.1 = (bf16[1280,192]{1,0:T(8,128)(2,1)}, f32[1280,256]{1,0:T(8,128)}, f32[8,1280]{1,0:T(8,128)}) custom-call(s32[2]{0:T(128)} %pad_add_fusion.ids, s32[50]{0:T(128)} %reshape.337.flags, bf16[1280,256]{1,0:T(8,128)(2,1)} %fusion.7.q, f32[8,1280]{1,0:T(8,128)} %broadcast_in_dim.47.seg_q, f32[5120,128]{1,0:T(8,128)} %broadcast_in_dim.49.seg_k, ...), custom_call_target="tpu_custom_call" | custom-call | flops 5033164800 | bytes 8388608 | tf_op jit(solution)/shard_map/attend_forward/pallas_call | solution.py:294
  167.6 8.5 %collective-permute-start.9 = (bf16[320,192]{1,0:T(8,128)(2,1)S(1)}, bf16[320,192]{1,0:T(8,128)(2,1)S(1)}, u32[]{:S(2)}, u32[]{:S(2)}) collective-permute-start(bf16[320,192]{1,0:T(8,128)(2,1)S(1)} %get-tuple-element.65), channel_id=1, source_target_pairs={{0,8},{8,0},{16,24},{24,16},{1,9},{9,1},{17,25},{25,17},{2,10},{10... | collective-permute-start | bytes 368648 | tf_op jit(solution)/shard_map/ppermute | solution.py:78
  176.1 2.4 collective-permute-start.11
  178.7 2.6 collective-permute-done.9
  181.3 9.4 %collective-permute-done.10 = bf16[320,192]{1,0:T(8,128)(2,1)S(1)} collective-permute-done((bf16[320,192]{1,0:T(8,128)(2,1)S(1)}, bf16[320,192]{1,0:T(8,128)(2,1)S(1)}, u32[]{:S(2)}, u32[]{:S(2)}) %collective-permute-start.10) | collective-permute-done | bytes 122912 | tf_op jit(solution)/shard_map/ppermute | solution.py:78
  194.4 6.5 multiply_convert_fusion
  200.9 4.9 fusion.73
  208.4 3.2 fusion.74
  218.9 3.7 collective-permute-start.12
  222.6 2.4 collective-permute-start.14
  225.0 2.8 collective-permute-done.12
  227.8 9.1 %collective-permute-done.13 = bf16[320,192]{1,0:T(8,128)(2,1)S(1)} collective-permute-done((bf16[320,192]{1,0:T(8,128)(2,1)S(1)}, bf16[320,192]{1,0:T(8,128)(2,1)S(1)}, u32[]{:S(2)}, u32[]{:S(2)}) %collective-permute-start.13) | collective-permute-done | bytes 122912 | tf_op jit(solution)/shard_map/ppermute | solution.py:78
  237.9 50.3 %attend_backward.1 = (bf16[2,4,320,384]{3,2,1,0:T(8,128)(2,1)}, bf16[2,4,320,384]{3,2,1,0:T(8,128)(2,1)}, bf16[1280,192]{1,0:T(8,128)(2,1)}) custom-call(s32[2]{0:T(128)} %pad_add_fusion.ids, s32[50]{0:T(128)} %reshape.337.flags, bf16[1280,256]{1,0:T(8,128)(2,1)} %fusion.7.q, f32[8,1280]{1,0:T(8,128)} %broadcast_in_dim.47.seg_q, ...), custom_call_target="tpu_custom_call" | custom-call | flops 12582912000 | bytes 16777216 | tf_op jit(solution)/shard_map/attend_backward/pallas_call | solution.py:325
  288.3 4.2 collective-permute-done.15
  297.0 24.0 %collective-permute-done.16 = bf16[1,4,320,384]{3,2,1,0:T(8,128)(2,1)} collective-permute-done((bf16[1,4,320,384]{3,2,1,0:T(8,128)(2,1)}, bf16[1,4,320,384]{3,2,1,0:T(8,128)(2,1)}, u32[]{:S(2)}, u32[]{:S(2)}) %collective-permute-start.16) | collective-permute-done | bytes 983072 | tf_op jit(solution)/shard_map/ppermute | solution.py:78
  323.1 3.3 convolution_convert_fusion.3
  329.1 6.8 convolution_convert_fusion
  336.0 8.9 %reshape.326 = bf16[4,768,768]{2,1,0:T(8,128)(2,1)} reshape(bf16[768,3072]{1,0:T(8,128)(2,1)} %convolution_convert_fusion) | data formatting | bytes 9437184 | tf_op jit(solution)/shard_map/reshape | solution.py:534
  347.9 4.4 convolution_convert_fusion.1
  352.4 14.5 %pad_maximum_fusion = bf16[4,1744,768]{2,1,0:T(8,128)(2,1)} fusion(bf16[4,16,768]{2,1,0:T(8,128)(2,1)S(1)} %broadcast_in_dim.59, bf16[4,192,768]{2,1,0:T(8,128)(2,1)S(1)} %bitcast.112, bf16[4,768,768]{2,1,0:T(8,128)(2,1)S(1)} %bitcast.107, bf16[4,768,768]{2,1,0:T(8,128)(2,1)S(1)} %bitcast.111), kind=kLoop, calls=%fused_computation.4 | loop fusion | flops 42860544 | bytes 21430272 | tf_op jit(solution)/shard_map/concatenate | solution.py:531
  367.5 93.6 %reduce-scatter.8.cloned.1.call-done = bf16[1744,768]{1,0:T(8,128)(2,1)} async-done(((bf16[6976,768]{1,0:T(8,128)(2,1)}), bf16[1744,768]{1,0:T(8,128)(2,1)}) %reduce-scatter.8.cloned.1.call-update) | async-done | bytes 2678800 | tf_op jit(solution)/shard_map/reduce_scatter | solution.py:361
  464.6 22.0 %all-reduce.7.cloned.1.call-done = bf16[1,208,576]{2,1,0:T(8,128)(2,1)} async-done(((bf16[1,208,576]{2,1,0:T(8,128)(2,1)}), bf16[1,208,576]{2,1,0:T(8,128)(2,1)}) %all-reduce.7.cloned.1.call-update) | async-done | bytes 239632 | tf_op jit(solution)/shard_map/psum | solution.py:573
  486.7 40.6 %reduce-scatter.10.cloned.1.call-done = bf16[872,768]{1,0:T(8,128)(2,1)} async-done(((bf16[1744,768]{1,0:T(8,128)(2,1)}), bf16[872,768]{1,0:T(8,128)(2,1)}) %reduce-scatter.10.cloned.1.call-update) | async-done | bytes 1339408 | tf_op jit(solution)/shard_map/reduce_scatter | solution.py:362
  527.3 31.3 %fusion = bf16[224,768]{1,0:T(8,128)(2,1)S(1)} fusion(bf16[872,768]{1,0:T(8,128)(2,1)} %reduce-scatter.10.cloned.1.call-done), kind=kCustom, calls=%all-reduce-scatter | all-reduce-scatter fusion | flops 688129 | bytes 1683968
  565.1 2.3 collective-permute-start.17
  569.8 11.9 %collective-permute-done.17 = bf16[320,576]{1,0:T(8,128)(2,1)S(1)} collective-permute-done((bf16[320,576]{1,0:T(8,128)(2,1)}, bf16[320,576]{1,0:T(8,128)(2,1)S(1)}, u32[]{:S(2)}, u32[]{:S(2)}) %collective-permute-start.17) | collective-permute-done | bytes 368672 | tf_op jit(solution)/shard_map/ppermute | solution.py:78
  581.7 16.8 %collective-permute-done.18 = bf16[320,576]{1,0:T(8,128)(2,1)S(1)} collective-permute-done((bf16[320,576]{1,0:T(8,128)(2,1)}, bf16[320,576]{1,0:T(8,128)(2,1)S(1)}, u32[]{:S(2)}, u32[]{:S(2)}) %collective-permute-start.18) | collective-permute-done | bytes 368672 | tf_op jit(solution)/shard_map/ppermute | solution.py:78
  600.0 3.3 gather_fusion.1
  613.7 2.9 fusion.16
  616.6 6.0 all-gather.25.cloned.1.call-done
  632.1 3.0 reshape_reshape.12
  637.4 3.0 reshape_reshape.11
  642.0 2.2 copy.66
  644.2 3.2 reshape_reshape.10
  649.6 31.0 %all-gather.27.cloned.1.call-done = bf16[16,218,768]{2,1,0:T(8,128)(2,1)} async-done(((bf16[1,218,768]{2,1,0:T(8,128)(2,1)}), bf16[16,218,768]{2,1,0:T(8,128)(2,1)}) %all-gather.27.cloned.1.call-update) | async-done | bytes 5357584 | tf_op jit(solution)/shard_map/all_gather | solution.py:364
  680.6 5.9 reshape.329
  686.5 5.2 fusion.66
  691.8 2.7 bitcast_convert_fusion
  694.5 6.2 reshape.351
  (320 shorter events, 94.1 us)
Async XLA Ops:
  7.2 184.7 %all-gather.13.cloned.1.call-start = ((), (), s32[]{:S(2)}) async-start(), calls=%async_computation.3 | async-start | bytes 1474560 | tf_op jit(solution)/shard_map/all_gather | solution.py:356
  9.1 185.3 %all-gather.15.cloned.1.call-start = ((), (), s32[]{:S(2)}) async-start(), calls=%async_computation.4 | async-start | bytes 5898240 | tf_op jit(solution)/shard_map/all_gather | solution.py:356
  10.4 190.5 %all-gather.17.cloned.1.call-start = ((), (), s32[]{:S(2)}) async-start(), calls=%async_computation.5 | async-start | bytes 5898240 | tf_op jit(solution)/shard_map/all_gather | solution.py:356
  10.5 21.4 %copy-start.17 = (s32[1,320]{1,0:T(1,128)S(1)}, s32[1,320]{1,0:T(1,128)}, u32[]{:S(2)}) copy-start(s32[1,320]{1,0:T(1,128)} %param.21) | copy-start | bytes 3844
  13.0 354.0 %reduce-scatter.6.cloned.1.call-start = ((), (), s32[]{:S(2)}) async-start(), calls=%async_computation.9 | async-start | bytes 1331200 | tf_op jit(solution)/shard_map/reduce_scatter | solution.py:572
  13.0 66.1 %collective-permute-start.1 = (bf16[320,768]{1,0:T(8,128)(2,1)S(1)}, bf16[320,768]{1,0:T(8,128)(2,1)S(1)}, u32[]{:S(2)}, u32[]{:S(2)}) collective-permute-start(bf16[320,768]{1,0:T(8,128)(2,1)S(1)} %bitcast.138), channel_id=1, source_target_pairs={{0,16},{8,24},{16,0},{24,8},{1,17},{9,25},{17,1},{25,9},{2,18},{10... | collective-permute-start | bytes 1474568 | tf_op jit(solution)/shard_map/ppermute | solution.py:78
  17.1 62.0 %collective-permute-start = (bf16[320,768]{1,0:T(8,128)(2,1)S(1)}, bf16[320,768]{1,0:T(8,128)(2,1)}, u32[]{:S(2)}, u32[]{:S(2)}) collective-permute-start(bf16[320,768]{1,0:T(8,128)(2,1)S(1)} %bitcast.139), channel_id=1, source_target_pairs={{0,8},{8,0},{16,24},{24,16},{1,9},{9,1},{17,25},{25,17},{2,10},{10... | collective-permute-start | bytes 1474568 | tf_op jit(solution)/shard_map/ppermute | solution.py:78
  81.3 30.4 %copy-start.28 = (bf16[960,384]{1,0:T(8,128)(2,1)}, bf16[960,384]{1,0:T(8,128)(2,1)S(1)}, u32[]{:S(2)}) copy-start(bf16[960,384]{1,0:T(8,128)(2,1)S(1)} %add_convert_fusion.2) | copy-start | bytes 2211844
  81.3 18.4 %collective-permute-start.3 = (bf16[3,320,384]{2,1,0:T(8,128)(2,1)S(1)}, bf16[3,320,384]{2,1,0:T(8,128)(2,1)S(1)}, u32[]{:S(2)}, u32[]{:S(2)}) collective-permute-start(bf16[3,320,384]{2,1,0:T(8,128)(2,1)S(1)} %bitcast.133), channel_id=1, source_target_pairs={{0,4},{4,0},{1,5},{5,1},{2,6},{6,2},{3,7},{7,3},{8,12},{12,8},{9,1... | collective-permute-start | bytes 2211848 | tf_op jit(solution)/shard_map/ppermute | solution.py:78
  82.2 17.5 %collective-permute-start.2 = (bf16[320,768]{1,0:T(8,128)(2,1)}, bf16[320,768]{1,0:T(8,128)(2,1)S(1)}, u32[]{:S(2)}, u32[]{:S(2)}) collective-permute-start(bf16[320,768]{1,0:T(8,128)(2,1)} %copy-done.33), channel_id=1, source_target_pairs={{0,8},{8,0},{16,24},{24,16},{1,9},{9,1},{17,25},{25,17},{2,10},{10... | collective-permute-start | bytes 1474568 | tf_op jit(solution)/shard_map/ppermute | solution.py:78
  82.5 29.2 %collective-permute-start.4 = (bf16[3,320,384]{2,1,0:T(8,128)(2,1)S(1)}, bf16[3,320,384]{2,1,0:T(8,128)(2,1)}, u32[]{:S(2)}, u32[]{:S(2)}) collective-permute-start(bf16[3,320,384]{2,1,0:T(8,128)(2,1)S(1)} %bitcast.134), channel_id=1, source_target_pairs={{0,2},{2,0},{1,3},{3,1},{4,6},{6,4},{5,7},{7,5},{8,10},{10,8},{9,1... | collective-permute-start | bytes 2211848 | tf_op jit(solution)/shard_map/ppermute | solution.py:78
  99.7 12.0 %copy-start.29 = (bf16[3,320,384]{2,1,0:T(8,128)(2,1)}, bf16[3,320,384]{2,1,0:T(8,128)(2,1)S(1)}, u32[]{:S(2)}) copy-start(bf16[3,320,384]{2,1,0:T(8,128)(2,1)S(1)} %collective-permute-done.3.rest_1_) | copy-start | bytes 2211844
  99.7 12.1 %collective-permute-start.5 = (bf16[3,320,384]{2,1,0:T(8,128)(2,1)S(1)}, bf16[3,320,384]{2,1,0:T(8,128)(2,1)}, u32[]{:S(2)}, u32[]{:S(2)}) collective-permute-start(bf16[3,320,384]{2,1,0:T(8,128)(2,1)S(1)} %collective-permute-done.3.rest_1_), channel_id=1, source_target_pairs={{0,2},{2,0},{1,3},{3,1},{4,6},{6,4},{5,7},{7,5},{8,10},{10,8},{9,1... | collective-permute-start | bytes 2211848 | tf_op jit(solution)/shard_map/ppermute | solution.py:78
  100.1 11.5 %copy-start.37 = (bf16[1,320,384]{2,1,0:T(8,128)(2,1)}, bf16[1,320,384]{2,1,0:T(8,128)(2,1)S(1)}, u32[]{:S(2)}) copy-start(bf16[1,320,384]{2,1,0:T(8,128)(2,1)S(1)} %fusion.27.rest_4_) | copy-start | bytes 737284
  100.1 8.4 %collective-permute-start.6 = (bf16[1,320,384]{2,1,0:T(8,128)(2,1)S(1)}, bf16[1,320,384]{2,1,0:T(8,128)(2,1)S(1)}, u32[]{:S(2)}, u32[]{:S(2)}) collective-permute-start(bf16[1,320,384]{2,1,0:T(8,128)(2,1)S(1)} %fusion.27.rest_4_), channel_id=1, source_target_pairs={{0,4},{4,0},{1,5},{5,1},{2,6},{6,2},{3,7},{7,3},{8,12},{12,8},{9,1... | collective-permute-start | bytes 737288 | tf_op jit(solution)/shard_map/ppermute | solution.py:78
  102.2 9.5 %collective-permute-start.7 = (bf16[1,320,384]{2,1,0:T(8,128)(2,1)S(1)}, bf16[1,320,384]{2,1,0:T(8,128)(2,1)S(1)}, u32[]{:S(2)}, u32[]{:S(2)}) collective-permute-start(bf16[1,320,384]{2,1,0:T(8,128)(2,1)S(1)} %fusion.27.rest_4_), channel_id=1, source_target_pairs={{0,2},{2,0},{1,3},{3,1},{4,6},{6,4},{5,7},{7,5},{8,10},{10,8},{9,1... | collective-permute-start | bytes 737288 | tf_op jit(solution)/shard_map/ppermute | solution.py:78
  108.6 3.1 collective-permute-start.8
  167.6 13.7 %collective-permute-start.9 = (bf16[320,192]{1,0:T(8,128)(2,1)S(1)}, bf16[320,192]{1,0:T(8,128)(2,1)S(1)}, u32[]{:S(2)}, u32[]{:S(2)}) collective-permute-start(bf16[320,192]{1,0:T(8,128)(2,1)S(1)} %get-tuple-element.65), channel_id=1, source_target_pairs={{0,8},{8,0},{16,24},{24,16},{1,9},{9,1},{17,25},{25,17},{2,10},{10... | collective-permute-start | bytes 368648 | tf_op jit(solution)/shard_map/ppermute | solution.py:78
  176.1 14.5 %collective-permute-start.10 = (bf16[320,192]{1,0:T(8,128)(2,1)S(1)}, bf16[320,192]{1,0:T(8,128)(2,1)S(1)}, u32[]{:S(2)}, u32[]{:S(2)}) collective-permute-start(bf16[320,192]{1,0:T(8,128)(2,1)S(1)} %get-tuple-element.64), channel_id=1, source_target_pairs={{0,16},{8,24},{16,0},{24,8},{1,17},{9,25},{17,1},{25,9},{2,18},{10... | collective-permute-start | bytes 368648 | tf_op jit(solution)/shard_map/ppermute | solution.py:78
  176.1 14.5 %collective-permute-start.11 = (bf16[320,192]{1,0:T(8,128)(2,1)S(1)}, bf16[320,192]{1,0:T(8,128)(2,1)S(1)}, u32[]{:S(2)}, u32[]{:S(2)}) collective-permute-start(bf16[320,192]{1,0:T(8,128)(2,1)S(1)} %get-tuple-element.63), channel_id=1, source_target_pairs={{0,24},{8,16},{16,8},{24,0},{1,25},{9,17},{17,9},{25,1},{2,26},{10... | collective-permute-start | bytes 368648 | tf_op jit(solution)/shard_map/ppermute | solution.py:78
  194.1 19.6 %copy-start.7 = (f32[320,768]{1,0:T(8,128)}, f32[320,768]{1,0:T(8,128)S(1)}, u32[]{:S(2)}) copy-start(f32[320,768]{1,0:T(8,128)S(1)} %get-tuple-element.81) | copy-start | bytes 2949124
  218.9 8.9 %collective-permute-start.12 = (bf16[320,192]{1,0:T(8,128)(2,1)S(1)}, bf16[320,192]{1,0:T(8,128)(2,1)S(1)}, u32[]{:S(2)}, u32[]{:S(2)}) collective-permute-start(bf16[320,192]{1,0:T(8,128)(2,1)S(1)} %get-tuple-element.61), channel_id=1, source_target_pairs={{0,8},{8,0},{16,24},{24,16},{1,9},{9,1},{17,25},{25,17},{2,10},{10... | collective-permute-start | bytes 368648 | tf_op jit(solution)/shard_map/ppermute | solution.py:78
  222.6 14.3 %collective-permute-start.13 = (bf16[320,192]{1,0:T(8,128)(2,1)S(1)}, bf16[320,192]{1,0:T(8,128)(2,1)S(1)}, u32[]{:S(2)}, u32[]{:S(2)}) collective-permute-start(bf16[320,192]{1,0:T(8,128)(2,1)S(1)} %get-tuple-element.60), channel_id=1, source_target_pairs={{0,16},{8,24},{16,0},{24,8},{1,17},{9,25},{17,1},{25,9},{2,18},{10... | collective-permute-start | bytes 368648 | tf_op jit(solution)/shard_map/ppermute | solution.py:78
  222.6 14.3 %collective-permute-start.14 = (bf16[320,192]{1,0:T(8,128)(2,1)S(1)}, bf16[320,192]{1,0:T(8,128)(2,1)S(1)}, u32[]{:S(2)}, u32[]{:S(2)}) collective-permute-start(bf16[320,192]{1,0:T(8,128)(2,1)S(1)} %get-tuple-element.59), channel_id=1, source_target_pairs={{0,24},{8,16},{16,8},{24,0},{1,25},{9,17},{17,9},{25,1},{2,26},{10... | collective-permute-start | bytes 368648 | tf_op jit(solution)/shard_map/ppermute | solution.py:78
  288.2 4.2 collective-permute-start.15
  296.8 25.9 %copy-start.8 = (bf16[1280,192]{1,0:T(8,128)(2,1)S(1)}, bf16[1280,192]{1,0:T(8,128)(2,1)}, u32[]{:S(2)}) copy-start(bf16[1280,192]{1,0:T(8,128)(2,1)} %get-tuple-element.29) | copy-start | bytes 1474564
  296.8 24.1 %collective-permute-start.16 = (bf16[1,4,320,384]{3,2,1,0:T(8,128)(2,1)}, bf16[1,4,320,384]{3,2,1,0:T(8,128)(2,1)}, u32[]{:S(2)}, u32[]{:S(2)}) collective-permute-start(bf16[1,4,320,384]{3,2,1,0:T(8,128)(2,1)} %slice.311), channel_id=1, source_target_pairs={{0,4},{4,0},{1,5},{5,1},{2,6},{6,2},{3,7},{7,3},{8,12},{12,8},{9,1... | collective-permute-start | bytes 2949128 | tf_op jit(solution)/shard_map/ppermute | solution.py:78
  297.0 26.1 %copy-start.32 = (bf16[1,320,768]{2,1,0:T(8,128)(2,1)S(1)}, bf16[1,320,768]{2,1,0:T(8,128)(2,1)}, u32[]{:S(2)}) copy-start(bf16[1,320,768]{2,1,0:T(8,128)(2,1)} %param.20) | copy-start | bytes 1474564
  297.0 26.1 %copy-start.34 = (bf16[320,768]{1,0:T(8,128)(2,1)S(1)}, bf16[320,768]{1,0:T(8,128)(2,1)}, u32[]{:S(2)}) copy-start(bf16[320,768]{1,0:T(8,128)(2,1)} %copy-done.33) | copy-start | bytes 1474564
  297.0 26.1 %copy-start.36 = (bf16[320,768]{1,0:T(8,128)(2,1)S(1)}, bf16[320,768]{1,0:T(8,128)(2,1)}, u32[]{:S(2)}) copy-start(bf16[320,768]{1,0:T(8,128)(2,1)} %copy-done.35) | copy-start | bytes 1474564
  329.1 132.0 %reduce-scatter.8.cloned.1.call-start = ((), (), s32[]{:S(2)}) async-start(), calls=%async_computation.12 | async-start | bytes 13393920 | tf_op jit(solution)/shard_map/reduce_scatter | solution.py:361
  336.0 10.4 %copy-start.11 = (bf16[320,4,192]{0,2,1:T(8,128)(2,1)S(1)}, bf16[320,4,192]{0,2,1:T(8,128)(2,1)}, u32[]{:S(2)}) copy-start(bf16[320,4,192]{0,2,1:T(8,128)(2,1)} %copy-done.10) | copy-start | bytes 1474564
  366.8 94.3 %copy-start.14 = (bf16[384,768]{1,0:T(8,128)(2,1)S(1)}, bf16[384,768]{1,0:T(8,128)(2,1)}, u32[]{:S(2)}) copy-start(bf16[384,768]{1,0:T(8,128)(2,1)} %param.23) | copy-start | bytes 1769476
  366.9 95.2 %copy-start.15 = (bf16[384,768]{1,0:T(8,128)(2,1)S(1)}, bf16[384,768]{1,0:T(8,128)(2,1)}, u32[]{:S(2)}) copy-start(bf16[384,768]{1,0:T(8,128)(2,1)} %param.24) | copy-start | bytes 1769476
  366.9 119.8 %all-reduce.7.cloned.1.call-start = ((), (), s32[]{:S(2)}) async-start(), calls=%async_computation.10 | async-start | bytes 532480 | tf_op jit(solution)/shard_map/psum | solution.py:573
  367.4 159.9 %reduce-scatter.10.cloned.1.call-start = ((), (), s32[]{:S(2)}) async-start(), calls=%async_computation.13 | async-start | bytes 4018176 | tf_op jit(solution)/shard_map/reduce_scatter | solution.py:362
  461.1 148.4 %all-gather.19.cloned.1.call-start = ((), (), s32[]{:S(2)}) async-start(), calls=%async_computation.6 | async-start | bytes 1474560 | tf_op jit(solution)/shard_map/all_gather | solution.py:356
  462.0 98.1 %copy-start.26 = (u32[32]{0:T(128)S(1)}, u32[32]{0:T(128)}, u32[]{:S(2)}) copy-start(u32[32]{0:T(128)} %constant.131) | copy-start | bytes 388
  462.0 149.7 %all-gather.21.cloned.1.call-start = ((), (), s32[]{:S(2)}) async-start(), calls=%async_computation.7 | async-start | bytes 1474560 | tf_op jit(solution)/shard_map/all_gather | solution.py:356
  462.8 150.9 %all-gather.23.cloned.1.call-start = ((), (), s32[]{:S(2)}) async-start(), calls=%async_computation.8 | async-start | bytes 1474560 | tf_op jit(solution)/shard_map/all_gather | solution.py:356
  464.6 99.5 %copy-start.9 = (bf16[1280,192]{1,0:T(8,128)(2,1)S(1)}, bf16[1280,192]{1,0:T(8,128)(2,1)}, u32[]{:S(2)}) copy-start(bf16[1280,192]{1,0:T(8,128)(2,1)} %get-tuple-element.29) | copy-start | bytes 1474564
  464.6 158.0 %all-gather.25.cloned.1.call-start = ((), (), s32[]{:S(2)}) async-start(), calls=%async_computation.11 | async-start | bytes 2396160 | tf_op jit(solution)/shard_map/all_gather | solution.py:574
  486.7 193.9 %all-gather.27.cloned.1.call-start = ((), (), s32[]{:S(2)}) async-start(), calls=%async_computation.14 | async-start | bytes 5849088 | tf_op jit(solution)/shard_map/all_gather | solution.py:364
  558.6 3.0 collective-permute-start.20
  565.1 16.6 %collective-permute-start.17 = (bf16[320,576]{1,0:T(8,128)(2,1)}, bf16[320,576]{1,0:T(8,128)(2,1)S(1)}, u32[]{:S(2)}, u32[]{:S(2)}) collective-permute-start(bf16[320,576]{1,0:T(8,128)(2,1)} %get-tuple-element.54), channel_id=1, source_target_pairs={{0,8},{8,0},{16,24},{24,16},{1,9},{9,1},{17,25},{25,17},{2,10},{10... | collective-permute-start | bytes 1105928 | tf_op jit(solution)/shard_map/ppermute | solution.py:78
  567.5 31.1 %collective-permute-start.18 = (bf16[320,576]{1,0:T(8,128)(2,1)}, bf16[320,576]{1,0:T(8,128)(2,1)S(1)}, u32[]{:S(2)}, u32[]{:S(2)}) collective-permute-start(bf16[320,576]{1,0:T(8,128)(2,1)} %get-tuple-element.55), channel_id=1, source_target_pairs={{0,16},{8,24},{16,0},{24,8},{1,17},{9,25},{17,1},{25,9},{2,18},{10... | collective-permute-start | bytes 1105928 | tf_op jit(solution)/shard_map/ppermute | solution.py:78
  568.1 30.5 %collective-permute-start.19 = (bf16[320,576]{1,0:T(8,128)(2,1)}, bf16[320,576]{1,0:T(8,128)(2,1)S(1)}, u32[]{:S(2)}, u32[]{:S(2)}) collective-permute-start(bf16[320,576]{1,0:T(8,128)(2,1)} %get-tuple-element.56), channel_id=1, source_target_pairs={{0,24},{8,16},{16,8},{24,0},{1,25},{9,17},{17,9},{25,1},{2,26},{10... | collective-permute-start | bytes 1105928 | tf_op jit(solution)/shard_map/ppermute | solution.py:78
  694.5 11.6 %copy-start.1 = (bf16[384,3072]{1,0:T(8,128)(2,1)S(1)}, bf16[384,3072]{1,0:T(8,128)(2,1)}, u32[]{:S(2)}) copy-start(bf16[384,3072]{1,0:T(8,128)(2,1)} %param.27) | copy-start | bytes 7077892
  (34 other events, 162.6 us)
Sparse Core Ops, SparseCore 0:
  10.2 20.5 all-gather.12
  32.9 47.4 all-gather.14
  82.5 38.2 all-gather.16
  329.2 32.3 reduce-scatter.5
  367.0 94.1 reduce-scatter.7
  463.3 23.2 all-reduce.6
  488.9 38.3 reduce-scatter.9
  529.5 17.4 all-gather.18
  549.2 17.4 all-gather.20
  568.2 17.4 all-gather.22
  587.4 35.1 all-gather.24
  625.0 55.5 all-gather.26

commit v2 on v1

v2 whole, which is shorter than its diff:
```python
import functools

import jax
import jax.numpy as jnp
from jax import lax
from jax.experimental import pallas as pl
from jax.experimental.pallas import tpu as pltpu
from jax.sharding import Mesh
from jax.sharding import PartitionSpec as P

D = 768
HEADS = 12
HEAD_DIM = 64
FF = 3072
DOCS = 32

GROUPS = 4
OWN = HEADS // GROUPS
WIDTH = OWN * HEAD_DIM
QTILE = 256
KTILE = 512

epsilon = 1e-05
masked_value = -1e30
NT = (((1,), (1,)), ((), ()))
NN = (((1,), (0,)), ((), ()))


def widen(array):
    return array.astype(jnp.float32)


def low(array):
    return array.astype(jnp.bfloat16)


def mm(left, right):
    return jnp.dot(left, right, preferred_element_type=jnp.float32)


def outer_sum(left, right):
    return lax.dot_general(
        left, right, (((0,), (0,)), ((), ())), preferred_element_type=jnp.float32
    )


def back_product(grad, weight):
    return lax.dot_general(grad, weight, NT, preferred_element_type=jnp.float32)


def norm_forward(values, gain, shift):
    centre = values - jnp.mean(values, axis=-1, keepdims=True)
    scale = lax.rsqrt(jnp.mean(centre * centre, axis=-1, keepdims=True) + epsilon)
    unit = centre * scale
    return (unit * gain + shift, unit, scale)


def norm_backward(grad, unit, scale, gain):
    grad_gain = jnp.sum(grad * unit, axis=0)
    grad_shift = jnp.sum(grad, axis=0)
    inner = grad * gain
    grad_in = scale * (
        inner
        - jnp.mean(inner, axis=-1, keepdims=True)
        - unit * jnp.mean(inner * unit, axis=-1, keepdims=True)
    )
    return (grad_in, grad_gain, grad_shift)


def gelu_pair(values):
    cumulative = 0.5 * (1.0 + lax.erf(values * 0.7071067811865476))
    density = jnp.exp(-0.5 * values * values) * 0.3989422804014327
    return (values * cumulative, cumulative + values * density)


def swap(array, axis, bit):
    size = lax.axis_size(axis)
    return lax.ppermute(array, axis, [(i, i ^ bit) for i in range(size)])


K_BLOCK = (0, 0, 1)
V_BLOCK = (2, 2, 1)
K_UPPER = (False, True, True)
V_UPPER = (False, True, False)


def lane_half(array, upper):
    lane = lax.broadcasted_iota(jnp.int32, array.shape, 1)
    keep = (lane >= 64) if upper else (lane < 64)
    return jnp.where(keep, array, jnp.zeros_like(array))


def piece_copies(where, ids, pieces, kv, sem, rows, classes):
    copies = []
    for piece, (mask, flips) in zip(pieces, where):
        for slot, flip in enumerate(flips):
            chunk = (ids[0] ^ flip) * classes + (ids[1] ^ mask)
            start = pl.multiple_of(chunk * rows, 64)
            copies.append(
                pltpu.make_async_copy(
                    piece.at[slot], kv.at[pl.ds(start, rows), :], sem.at[len(copies)]
                )
            )
    return copies


def allowed(spans, base, start):
    position = lax.broadcasted_iota(jnp.int32, (KTILE, QTILE), 0)
    first = spans[0:1, pl.ds(base, QTILE)] - start
    last = spans[1:2, pl.ds(base, QTILE)] - start
    return (position >= first) & (position < last)


def walk(steps, tiles, j, fetch, work):
    amount = steps[j * (tiles + 1)]

    def tile(i):
        index = steps[j * (tiles + 1) + 1 + jnp.minimum(i, amount - 1)]
        start = pl.multiple_of(index * KTILE, KTILE)
        return start, jnp.where(i < amount, start, -(1 << 24))

    fetch(0, tile(0)[0])

    @pl.loop(0, (amount + 1) // 2)
    def _(i):
        here, there, later = tile(2 * i), tile(2 * i + 1), tile(2 * i + 2)
        fetch(1, there[0])
        work(0, *here)
        fetch(0, later[0])
        work(1, *there)


def forward_kernel(where, rows, classes, ids, flags, q, spans, *rest):
    count = len(where)
    pieces = rest[:count]
    o_low, o_full, lse, kv, vt, qm, top, total, accum, first, second, sem = rest[count:]
    length = kv.shape[0]
    tiles = length // KTILE
    copies = piece_copies(where, ids, pieces, kv, sem, rows, classes)
    for copy in copies:
        copy.start()
    for copy in copies:
        copy.wait()

    @pl.loop(0, tiles)
    def _(t):
        start = pl.multiple_of(t * KTILE, KTILE)
        vt[0:128, pl.ds(start, KTILE)] = kv[pl.ds(start, KTILE), 128:256].T
        vt[128:256, pl.ds(start, KTILE)] = kv[pl.ds(start, KTILE), 256:384].T

    v_row = (128, 192, 0)

    @pl.loop(0, q.shape[0] // QTILE)
    def _(j):
        base = pl.multiple_of(j * QTILE, QTILE)
        for head in range(OWN):
            block = q[pl.ds(base, QTILE), pl.ds(128 * K_BLOCK[head], 128)]
            qm[head] = lane_half(block, K_UPPER[head])
        top[...] = jnp.full_like(top, masked_value)
        total[...] = jnp.zeros_like(total)
        accum[...] = jnp.zeros_like(accum)

        stages = (first, second)

        def fetch(stage, start):
            for head in range(OWN):
                block = 128 * K_BLOCK[head]
                stages[stage][head] = lax.dot_general(
                    kv[pl.ds(start, KTILE), block : block + 128],
                    qm[head],
                    NT,
                    preferred_element_type=jnp.float32,
                )

        def work(stage, start, position):
            same = allowed(spans, base, position)
            for head in range(OWN):
                scores = jnp.where(same, stages[stage][head], masked_value)
                old = top[head : head + 1, :]
                new = jnp.maximum(old, jnp.max(scores, axis=0, keepdims=True))
                weights = jnp.exp(scores - new)
                factor = jnp.exp(old - new)
                top[head : head + 1, :] = new
                total[head : head + 1, :] = total[head : head + 1, :] * factor + jnp.sum(
                    weights, axis=0, keepdims=True
                )
                rows_v = slice(v_row[head], v_row[head] + 64)
                place = slice(64 * head, 64 * head + 64)
                accum[place, :] = accum[place, :] * factor + jnp.dot(
                    vt[rows_v, pl.ds(start, KTILE)],
                    weights.astype(jnp.bfloat16),
                    preferred_element_type=jnp.float32,
                )

        walk(flags, tiles, j, fetch, work)
        outs = [
            accum[64 * head : 64 * head + 64, :] / total[head : head + 1, :] for head in range(OWN)
        ]
        lower = jnp.concatenate(outs[:2], axis=0).T
        upper = jnp.concatenate([outs[2], jnp.zeros_like(outs[2])], axis=0).T
        o_full[pl.ds(base, QTILE), 0:128] = lower
        o_full[pl.ds(base, QTILE), 128:256] = upper
        o_low[pl.ds(base, QTILE), 0:128] = lower.astype(jnp.bfloat16)
        o_low[pl.ds(base, QTILE), 128:192] = upper[:, 0:64].astype(jnp.bfloat16)
        lse[:, pl.ds(base, QTILE)] = top[...] + jnp.log(total[...])


def backward_kernel(where, rows, classes, out_where, extra, ids, flags, q, spans, grad, o_full, lse, *rest):
    count = len(where)
    pieces = rest[:count]
    rest = rest[count + extra :]
    outs = rest[: len(out_where)]
    dq, kv, kt, qm, dom, stats, dqt, dkv, low_kv, sem = rest[len(out_where) :]
    length = kv.shape[0]
    tiles = length // KTILE
    copies = piece_copies(where, ids, pieces, kv, sem, rows, classes)
    for copy in copies:
        copy.start()

    @pl.loop(0, tiles)
    def _(t):
        start = pl.multiple_of(t * KTILE, KTILE)
        dkv[pl.ds(start, KTILE), :] = jnp.zeros((KTILE, 384), jnp.float32)

    for copy in copies:
        copy.wait()

    @pl.loop(0, tiles)
    def _(t):
        start = pl.multiple_of(t * KTILE, KTILE)
        kt[0:128, pl.ds(start, KTILE)] = kv[pl.ds(start, KTILE), 0:128].T
        kt[128:256, pl.ds(start, KTILE)] = kv[pl.ds(start, KTILE), 128:256].T

    k_row = (0, 64, 192)

    @pl.loop(0, q.shape[0] // QTILE)
    def _(j):
        base = pl.multiple_of(j * QTILE, QTILE)
        for head in range(OWN):
            block = q[pl.ds(base, QTILE), pl.ds(128 * K_BLOCK[head], 128)]
            qm[head] = lane_half(block, K_UPPER[head])
            block = grad[pl.ds(base, QTILE), pl.ds(128 * (2 - V_BLOCK[head]), 128)]
            dom[head] = lane_half(block, V_UPPER[head])
        for part in range(2):
            product = (
                grad[pl.ds(base, QTILE), 128 * part : 128 * part + 128].astype(jnp.float32)
                * o_full[pl.ds(base, QTILE), 128 * part : 128 * part + 128]
            ).T
            for half in range(2):
                head = 2 * part + half
                if head < OWN:
                    stats[head : head + 1, :] = jnp.sum(
                        product[64 * half : 64 * half + 64], axis=0, keepdims=True
                    )
        dqt[...] = jnp.zeros_like(dqt)

        def product(place, block, right):
            left = kv[place, 128 * block : 128 * block + 128]
            return lax.dot_general(left, right, NT, preferred_element_type=jnp.float32)

        @pl.loop(0, flags[j * (tiles + 1)])
        def _(i):
            start = pl.multiple_of(flags[j * (tiles + 1) + 1 + i] * KTILE, KTILE)
            place = pl.ds(start, KTILE)
            same = allowed(spans, base, start)
            sums = [None, None, None]

            def add(block, left, right):
                term = jnp.dot(left, right, preferred_element_type=jnp.float32)
                sums[block] = term if sums[block] is None else sums[block] + term

            for head in range(OWN):
                scores = product(place, K_BLOCK[head], qm[head])
                grad_probs = product(place, V_BLOCK[head], dom[head])
                probs = jnp.where(
                    same, jnp.exp(scores - lse[head : head + 1, pl.ds(base, QTILE)]), 0.0
                )
                grad_scores = (probs * (grad_probs - stats[head : head + 1, :])).astype(jnp.bfloat16)
                add(V_BLOCK[head], probs.astype(jnp.bfloat16), dom[head])
                add(K_BLOCK[head], grad_scores, qm[head])
                rows_k = slice(k_row[head], k_row[head] + 64)
                dqt[64 * head : 64 * head + 64, :] += jnp.dot(
                    kt[rows_k, place], grad_scores, preferred_element_type=jnp.float32
                )
            for block in range(3):
                dkv[place, 128 * block : 128 * block + 128] += sums[block]

        lower = dqt[0:128, :].T * 0.125
        upper = dqt[64:192, :].T * 0.125
        dq[pl.ds(base, QTILE), 0:128] = lower.astype(jnp.bfloat16)
        dq[pl.ds(base, QTILE), 128:192] = upper[:, 64:128].astype(jnp.bfloat16)

    @pl.loop(0, tiles)
    def _(t):
        start = pl.multiple_of(t * KTILE, KTILE)
        low_kv[pl.ds(start, KTILE), :] = dkv[pl.ds(start, KTILE), :].astype(jnp.bfloat16)

    copies = []
    for out, masks in zip(outs, out_where):
        for slot, mask in enumerate(masks):
            for flip in range(GROUPS):
                chunk = (ids[0] ^ flip) * classes + (ids[1] ^ mask)
                start = pl.multiple_of(chunk * rows, 64)
                copies.append(
                    pltpu.make_async_copy(
                        low_kv.at[pl.ds(start, rows), :], out.at[slot, flip], sem.at[len(copies)]
                    )
                )
    for copy in copies:
        copy.start()
    for copy in copies:
        copy.wait()


VMEM_SPEC = pl.BlockSpec(memory_space=pltpu.VMEM)
SMEM_SPEC = pl.BlockSpec(memory_space=pltpu.SMEM)
ANY_SPEC = pl.BlockSpec(memory_space=pl.ANY)
PARAMS = pltpu.CompilerParams(vmem_limit_bytes=56 * 1024 * 1024)


def attend_forward(ids, flags, q, spans, pieces, where, rows, classes):
    length = rows * classes * GROUPS
    queries = q.shape[0]
    copies = sum(len(flips) for _, flips in where)
    return pl.pallas_call(
        functools.partial(forward_kernel, where, rows, classes),
        out_shape=(
            jax.ShapeDtypeStruct((queries, WIDTH), jnp.bfloat16),
            jax.ShapeDtypeStruct((queries, 256), jnp.float32),
            jax.ShapeDtypeStruct((8, queries), jnp.float32),
        ),
        in_specs=[SMEM_SPEC, SMEM_SPEC, VMEM_SPEC, VMEM_SPEC]
        + [ANY_SPEC] * len(pieces),
        out_specs=(VMEM_SPEC,) * 3,
        scratch_shapes=[
            pltpu.VMEM((length, 384), jnp.bfloat16),
            pltpu.VMEM((256, length), jnp.bfloat16),
            pltpu.VMEM((OWN, QTILE, 128), jnp.bfloat16),
            pltpu.VMEM((8, QTILE), jnp.float32),
            pltpu.VMEM((8, QTILE), jnp.float32),
            pltpu.VMEM((WIDTH, QTILE), jnp.float32),
            pltpu.VMEM((OWN, KTILE, QTILE), jnp.float32),
            pltpu.VMEM((OWN, KTILE, QTILE), jnp.float32),
            pltpu.SemaphoreType.DMA((copies,)),
        ],
        compiler_params=PARAMS,
        cost_estimate=pl.CostEstimate(
            flops=queries * length * WIDTH * 4, bytes_accessed=8 << 20, transcendentals=0
        ),
        name="attend_forward",
    )(ids, flags, q, spans, *pieces)


def attend_backward(
    ids, flags, q, spans, grad, o_full, lse, pieces, after, where, rows, classes, out_where
):
    length = rows * classes * GROUPS
    queries = q.shape[0]
    copies = sum(len(flips) for _, flips in where)
    return pl.pallas_call(
        functools.partial(backward_kernel, where, rows, classes, out_where, len(after)),
        out_shape=tuple(
            jax.ShapeDtypeStruct((len(masks), GROUPS, rows, 384), jnp.bfloat16)
            for masks in out_where
        )
        + (jax.ShapeDtypeStruct((queries, WIDTH), jnp.bfloat16),),
        in_specs=[SMEM_SPEC, SMEM_SPEC] + [VMEM_SPEC] * 5 + [ANY_SPEC] * (len(pieces) + len(after)),
        out_specs=(ANY_SPEC,) * len(out_where) + (VMEM_SPEC,),
        scratch_shapes=[
            pltpu.VMEM((length, 384), jnp.bfloat16),
            pltpu.VMEM((256, length), jnp.bfloat16),
            pltpu.VMEM((OWN, QTILE, 128), jnp.bfloat16),
            pltpu.VMEM((OWN, QTILE, 128), jnp.bfloat16),
            pltpu.VMEM((8, QTILE), jnp.float32),
            pltpu.VMEM((WIDTH, QTILE), jnp.float32),
            pltpu.VMEM((length, 384), jnp.float32),
            pltpu.VMEM((length, 384), jnp.bfloat16),
            pltpu.SemaphoreType.DMA((copies,)),
        ],
        compiler_params=PARAMS,
        cost_estimate=pl.CostEstimate(
            flops=queries * length * WIDTH * 10, bytes_accessed=16 << 20, transcendentals=0
        ),
        name="attend_backward",
    )(ids, flags, q, spans, grad, o_full, lse, *pieces, *after)


def tn(left, right):
    return lax.dot_general(
        left, right, (((0,), (0,)), ((), ())), preferred_element_type=jnp.float32
    )


def down_grad_kernel(extra, active, g_low, *rest):
    down = rest[extra]

    @pl.loop(0, 8)
    def _(i):
        part = tn(active[:, pl.ds(pl.multiple_of(i * 384, 128), 384)], g_low[...])
        down[pl.ds(pl.multiple_of(i * 384, 16), 384), :] = part.astype(jnp.bfloat16)


def down_grad(active, g_low, after):
    return pl.pallas_call(
        functools.partial(down_grad_kernel, len(after)),
        out_shape=jax.ShapeDtypeStruct((FF, D), jnp.bfloat16),
        in_specs=[VMEM_SPEC] * 2 + [ANY_SPEC] * len(after),
        out_specs=VMEM_SPEC,
        compiler_params=PARAMS,
        cost_estimate=pl.CostEstimate(
            flops=2 * active.shape[0] * D * FF, bytes_accessed=8 << 20, transcendentals=0
        ),
        name="down_grad",
    )(active, g_low, *after)


def upper_grad_kernel(extra, ids, hid, g_raised, attn, g_att, vec, *rest):
    upper = rest[extra]
    x, c, m, h = ids[0], ids[1], ids[2], ids[3]

    @pl.loop(0, 2)
    def _(i):
        left = hid[:, pl.ds(pl.multiple_of(i * 384, 128), 384)]
        attn_left = attn[:, pl.ds(pl.multiple_of(i * 384, 128), 384)]

        @pl.loop(0, 2)
        def _(j):
            outer = tn(attn_left, g_att[:, pl.ds(pl.multiple_of(j * 384, 128), 384)]).astype(jnp.bfloat16)

            for k in range(4):
                unit = j * 4 + k
                part = tn(left, g_raised[:, pl.ds(pl.multiple_of(unit * 384, 128), 384)]).astype(jnp.bfloat16)
                for b in range(2):
                    place = (((b ^ c) * 2 + (j ^ m)) * 2 + (i ^ x)) * 4 + (k ^ h)
                    upper[place, 0:192, :] = part[192 * b : 192 * b + 192]
                    upper[place, 192:240, :] = outer[192 * b + 48 * k : 192 * b + 48 * k + 48]
                    upper[place, 240:256, :] = vec[unit]


def upper_grad(ids, hid, g_raised, attn, g_att, vec, after):
    return pl.pallas_call(
        functools.partial(upper_grad_kernel, len(after)),
        out_shape=jax.ShapeDtypeStruct((32, 256, 384), jnp.bfloat16),
        in_specs=[SMEM_SPEC] + [VMEM_SPEC] * 5 + [ANY_SPEC] * len(after),
        out_specs=VMEM_SPEC,
        compiler_params=PARAMS,
        cost_estimate=pl.CostEstimate(
            flops=2 * hid.shape[0] * D * (FF + D), bytes_accessed=12 << 20, transcendentals=0
        ),
        name="upper_grad",
    )(ids, hid, g_raised, attn, g_att, vec, *after)


def unpack_ffn_kernel(ids, block, up, out, vec):
    up[...] = block[0, 0:192, :].astype(jnp.float32)
    out[...] = block[0, 192:240, :].astype(jnp.float32)
    vec[0] = block[0, 240:256, :].astype(jnp.float32)


def unpack_ffn(ids, pieces):
    def source(b, u, ids):
        j, k = u // 4, u % 4
        return (((b ^ ids[1]) * 2 + (j ^ ids[2])) * 4 + (k ^ ids[3]), 0, 0)

    return pl.pallas_call(
        unpack_ffn_kernel,
        out_shape=(
            jax.ShapeDtypeStruct((384, FF), jnp.float32),
            jax.ShapeDtypeStruct((384, D), jnp.float32),
            jax.ShapeDtypeStruct((8, 16, 384), jnp.float32),
        ),
        grid_spec=pltpu.PrefetchScalarGridSpec(
            num_scalar_prefetch=1,
            grid=(2, 8),
            in_specs=[pl.BlockSpec((1, 256, 384), source)],
            out_specs=(
                pl.BlockSpec((192, 384), lambda b, u, ids: (b, u)),
                pl.BlockSpec((48, 384), lambda b, u, ids: (b * 4 + u % 4, u // 4)),
                pl.BlockSpec((1, 16, 384), lambda b, u, ids: (u, 0, 0)),
            ),
        ),
        name="unpack_ffn",
    )(ids, pieces)


def qkv_grad_kernel(ids, tokens, dkv, dq, out):
    x, c = ids[0], ids[1]
    total = jnp.concatenate(
        [
            jnp.sum(dkv[...].astype(jnp.float32), axis=0, keepdims=True),
            jnp.sum(dq[...].astype(jnp.float32), axis=0, keepdims=True),
        ],
        axis=1,
    )
    first = lax.broadcasted_iota(jnp.int32, (16, 576), 0) == 0
    total = jnp.where(first, jnp.broadcast_to(total, (16, 576)), 0.0).astype(jnp.bfloat16)

    @pl.loop(0, 2)
    def _(i):
        left = tokens[:, pl.ds(pl.multiple_of(i * 384, 128), 384)]
        for right, low_lane, high_lane in ((dkv, 0, 384), (dq, 384, 576)):
            part = lax.dot_general(
                left, right[...], (((0,), (0,)), ((), ())), preferred_element_type=jnp.float32
            ).astype(jnp.bfloat16)
            for b in range(2):
                out[(b ^ c) * 2 + (i ^ x), 0:192, low_lane:high_lane] = part[192 * b : 192 * b + 192]
        for b in range(2):
            out[(b ^ c) * 2 + (i ^ x), 192:208, :] = total


def qkv_grads(ids, tokens, dkv, dq):
    return pl.pallas_call(
        qkv_grad_kernel,
        out_shape=jax.ShapeDtypeStruct((4, 208, 576), jnp.bfloat16),
        in_specs=[SMEM_SPEC] + [VMEM_SPEC] * 3,
        out_specs=VMEM_SPEC,
        compiler_params=PARAMS,
        cost_estimate=pl.CostEstimate(
            flops=2 * tokens.shape[0] * D * 576, bytes_accessed=4 << 20, transcendentals=0
        ),
        name="qkv_grads",
    )(ids, tokens, dkv, dq)


def unpack_qkv_kernel(ids, pieces, out_q, out_k, out_v, vec):
    c, h = ids[1], ids[3]
    for b in range(2):
        q, k, v = [], [], []
        for g in range(GROUPS):
            block = pieces[(b ^ c) * 4 + (g ^ h), 0:192, :].astype(jnp.float32)
            k += [block[:, 0:128], block[:, 192:256]]
            v += [block[:, 256:384], block[:, 128:192]]
            q += [block[:, 384:576]]
        for out, parts in ((out_q, q), (out_k, k), (out_v, v)):
            out[192 * b : 192 * b + 192, :] = jnp.concatenate(parts, axis=1)
    for g in range(GROUPS):
        vec[g] = pieces[c * 4 + (g ^ h), 192:208, :].astype(jnp.float32)


def unpack_qkv(ids, pieces):
    return pl.pallas_call(
        unpack_qkv_kernel,
        out_shape=(jax.ShapeDtypeStruct((384, D), jnp.float32),) * 3
        + (jax.ShapeDtypeStruct((GROUPS, 16, 576), jnp.float32),),
        in_specs=[SMEM_SPEC, VMEM_SPEC],
        out_specs=(VMEM_SPEC,) * 4,
        compiler_params=PARAMS,
        name="unpack_qkv",
    )(ids, pieces)


def token_grad_kernel(base, kv0, kv1, kv2, kv3, q0, q1, q2, q3, w_kv, w_q, out):
    total = base[...]
    for i, (kv, q) in enumerate(((kv0, q0), (kv1, q1), (kv2, q2), (kv3, q3))):
        total = total + lax.dot_general(kv[...], w_kv[i], NT, preferred_element_type=jnp.float32)
        total = total + lax.dot_general(q[...], w_q[i], NT, preferred_element_type=jnp.float32)
    out[...] = total


def token_grads(base, kv, q, w_kv, w_q):
    return pl.pallas_call(
        token_grad_kernel,
        out_shape=jax.ShapeDtypeStruct(base.shape, jnp.float32),
        in_specs=[VMEM_SPEC] * 11,
        out_specs=VMEM_SPEC,
        compiler_params=PARAMS,
        cost_estimate=pl.CostEstimate(
            flops=2 * base.shape[0] * D * 2304, bytes_accessed=8 << 20, transcendentals=0
        ),
        name="token_grads",
    )(base, *kv, *q, w_kv, w_q)


def gather_rows(weight, core):
    half = weight.shape[0] // 2
    part = lax.dynamic_slice_in_dim(weight, core * half, half, 0)
    return lax.all_gather(part, ("wa", "c"), axis=0, tiled=True)


def reduce_blocks(grad):
    flat = grad.reshape((-1,) + grad.shape[2:])
    mine = lax.psum_scatter(flat, ("wa", "c"), scatter_dimension=0, tiled=True)
    mine = lax.psum_scatter(mine, "m", scatter_dimension=0, tiled=True)
    mine = lax.psum_scatter(mine, "h", scatter_dimension=0, tiled=True)
    return lax.all_gather(mine, ("c", "m", "h"), axis=0, tiled=True)


def tie(array, *others):
    return lax.optimization_barrier((array,) + others)[0]


def halve(array, axis, bit):
    return array[0], swap(array[1], axis, bit)


def both_sum(near, far, *others):
    near = tie(near, *others)
    return low(widen(near) + widen(far))


def double(array, axis, bit):
    return jnp.concatenate([array, swap(array, axis, bit)], axis=0)


def reduce_rest(grad):
    mine = lax.psum_scatter(grad, "h", scatter_dimension=0, tiled=True)
    mine = lax.psum_scatter(mine, "m", scatter_dimension=0, tiled=True)
    return lax.all_gather(mine, ("c", "h", "m"), axis=0, tiled=True)


def pick_columns(weight, group):
    q, k, v = (lax.dynamic_slice_in_dim(w, group * WIDTH, WIDTH, w.ndim - 1) for w in weight)
    return jnp.concatenate(
        [
            k[..., :128],
            v[..., 128:],
            k[..., 128:],
            v[..., :128],
            q[..., :128],
            jnp.zeros_like(q[..., :64]),
            q[..., 128:],
        ],
        axis=-1,
    )


def per_device(
    tokens,
    segment_ids,
    cotangent,
    w_query,
    w_key,
    w_value,
    w_out,
    w_up,
    w_down,
    b_query,
    b_value,
    b_out,
    gain_one,
    shift_one,
    b_up,
    b_down,
    gain_two,
    shift_two,
):
    mid = lax.axis_size("m")
    wide = lax.axis_size("wa")
    paired = mid == 2 and wide == 2
    classes = 2 * mid
    group = lax.axis_index("h")
    core = lax.axis_index("c")
    kind = lax.axis_index("m") * 2 + core
    side = lax.axis_index("wa")
    inputs = tokens[0]
    count = inputs.shape[0]
    chunks = GROUPS * classes
    length = count * chunks
    tiles = length // KTILE
    ids = jnp.stack([group, kind]).astype(jnp.int32)
    place_ids = jnp.stack([side, core, lax.axis_index("m"), group]).astype(jnp.int32)
    order = group ^ jnp.arange(GROUPS)

    second = swap(inputs, "h", 1)
    third = swap(inputs, "h", 2)
    w_part = pick_columns((w_query, w_key, w_value), group)
    w_other = swap(w_part, "wa", 1) if wide == 2 else lax.all_gather(w_part, "wa", axis=0, tiled=True)

    segs = segment_ids
    segs = double(segs, "c", 1)
    bit = 1
    while bit < mid:
        segs = double(segs, "m", bit)
        bit *= 2
    segs = double(double(segs, "h", 1), "h", 2)

    smalls = [b_query, b_value, b_out, gain_one, shift_one, b_up, b_down, gain_two, shift_two]
    joined = lax.all_gather(jnp.concatenate(smalls), "wa", axis=0)
    second, third, w_other, segs, joined = lax.optimization_barrier(
        (second, third, w_other, segs, joined)
    )
    fourth = swap(third, "h", 1)
    if wide == 2:
        w_group = jnp.where(
            side == 0,
            jnp.concatenate([w_part, w_other], axis=0),
            jnp.concatenate([w_other, w_part], axis=0),
        )
    else:
        w_group = w_other
    own_segs = segs.reshape(GROUPS, classes, count)[:, 0].reshape(-1)
    segs = jnp.take(segs, (group * classes + kind) ^ jnp.arange(chunks), axis=0)
    full, place = [], 0
    for item in smalls:
        size = item.shape[0]
        full.append(widen(joined[:, place : place + size].reshape(-1)))
        place += size
    bias_query, bias_value, bias_out, gain_attn, shift_attn, bias_up, bias_down, gain_ffn, shift_ffn = full
    b_group = pick_columns((bias_query, jnp.zeros_like(bias_query), bias_value), group)

    w_group, w_out, w_up, w_down, w_query, w_key, w_value = lax.optimization_barrier(
        (w_group, w_out, w_up, w_down, w_query, w_key, w_value)
    )
    full_out = gather_rows(w_out, core)
    full_up = gather_rows(w_up, core)
    full_down = gather_rows(w_down, core)
    by_group = jnp.concatenate(
        [
            jnp.concatenate(
                [
                    w_key[:, 192 * g : 192 * g + 128],
                    w_value[:, 192 * g + 128 : 192 * g + 192],
                    w_key[:, 192 * g + 128 : 192 * g + 192],
                    w_value[:, 192 * g : 192 * g + 128],
                ],
                axis=1,
            )
            for g in range(GROUPS)
        ]
        + [w_query],
        axis=1,
    )
    by_group = gather_rows(by_group, core)
    back_kv = jnp.take(
        jnp.transpose(by_group[:, : 2 * D].reshape(D, GROUPS, 2 * WIDTH), (1, 0, 2)), order, axis=0
    )
    back_q = jnp.take(
        jnp.transpose(by_group[:, 2 * D :].reshape(D, GROUPS, WIDTH), (1, 0, 2)), order, axis=0
    )

    names = jnp.arange(DOCS)
    begins = jnp.sum((segs.reshape(-1, 1) < names).astype(jnp.int32), axis=0)
    ends = jnp.sum((segs.reshape(-1, 1) <= names).astype(jnp.int32), axis=0)
    chosen = own_segs[None, :] == names[:, None]
    begins = jnp.sum(jnp.where(chosen, begins[:, None], 0), axis=0)
    ends = jnp.sum(jnp.where(chosen, ends[:, None], 0), axis=0)
    spans = jnp.concatenate(
        [begins[None], ends[None], jnp.zeros((6, begins.shape[0]), jnp.int32)], axis=0
    )
    edges = (jnp.arange(tiles) * KTILE)[None, :, None]
    meets = (begins.reshape(-1, 1, QTILE) < edges + KTILE) & (ends.reshape(-1, 1, QTILE) > edges)
    meets = jnp.any(meets, axis=-1).astype(jnp.int32)
    rank = jnp.cumsum(meets, axis=1)
    slots = (rank[:, None, :] == jnp.arange(1, tiles + 1)[None, :, None]) & (meets[:, None, :] > 0)
    listed = jnp.sum(jnp.where(slots, jnp.arange(tiles), 0), axis=-1)
    flags = jnp.concatenate([rank[:, -1:], listed], axis=1).astype(jnp.int32).reshape(-1)

    def project(parts):
        joined = jnp.concatenate(parts, axis=0)
        kv = low(mm(joined, w_group[:, :384]) + b_group[:384])
        return kv.reshape(len(parts), count, 384)

    where, pieces = [], []

    def spread(piece, flips):
        have = {0: piece}
        bit = 1
        while bit < mid:
            for mask in list(have):
                have[mask | (bit << 1)] = swap(have[mask], "m", bit)
            bit *= 2
        for mask in list(have):
            have[mask | 1] = swap(have[mask], "c", 1)
        for mask, item in have.items():
            where.append((mask, flips))
            pieces.append(item)

    def queries(rows):
        return low(mm(rows, w_group[:, 384:]) + b_group[384:]) * jnp.bfloat16(0.125)

    first_kv = project((inputs, second, third))
    spread(first_kv, (0, 1, 2))
    first_q = queries(tie(jnp.concatenate([inputs, second, third], axis=0), first_kv))
    fourth, first_q, spans, flags = lax.optimization_barrier((fourth, first_q, spans, flags))
    last_kv = project((fourth,))
    spread(last_kv, (3,))
    where = tuple(where)
    last_q = queries(tie(fourth, last_kv))
    q_rows = jnp.concatenate([first_q, last_q], axis=0)
    group_tokens = jnp.concatenate([inputs, second, third, fourth], axis=0)

    o_low, o_full, lse = attend_forward(
        ids, flags, q_rows, spans, pieces, where, count, classes
    )

    def send_back(rows):
        parts = rows.reshape(GROUPS, count, -1)
        return [parts[0]] + [swap(parts[flip], "h", flip) for flip in range(1, GROUPS)]

    def in_order(parts):
        return jnp.take(jnp.stack(parts), order, axis=0)

    attn_low = jnp.transpose(in_order(send_back(o_low)), (1, 0, 2)).reshape(count, D)
    attended = mm(attn_low, full_out) + bias_out
    hidden, unit_one, scale_one = norm_forward(widen(inputs) + attended, gain_attn, shift_attn)
    hidden_low = low(hidden)
    raised = mm(hidden_low, full_up) + bias_up
    active, slope = gelu_pair(raised)
    active_low = low(active)
    lowered = mm(active_low, full_down) + bias_down
    result, unit_two, scale_two = norm_forward(hidden + lowered, gain_ffn, shift_ffn)
    grad_sum_two, grad_gain_two, grad_shift_two = norm_backward(
        widen(cotangent[0]), unit_two, scale_two, gain_ffn
    )
    grad_lowered = low(grad_sum_two)
    grad_b_down = jnp.sum(widen(grad_lowered), axis=0)
    grad_raised = low(back_product(grad_lowered, full_down) * slope)
    grad_b_up = jnp.sum(widen(grad_raised), axis=0)
    grad_hidden = grad_sum_two + back_product(grad_raised, full_up)
    grad_sum_one, grad_gain_one, grad_shift_one = norm_backward(
        grad_hidden, unit_one, scale_one, gain_attn
    )
    grad_attended = low(grad_sum_one)
    grad_b_out = jnp.sum(widen(grad_attended), axis=0)
    grad_attn = low(back_product(grad_attended, full_out))

    grad_parts = jnp.take(
        jnp.transpose(grad_attn.reshape(count, GROUPS, WIDTH), (1, 0, 2)), order, axis=0
    )
    grad_heads = [grad_parts[0]] + [swap(grad_parts[flip], "h", flip) for flip in range(1, GROUPS)]
    grad_rows = jnp.pad(jnp.concatenate(grad_heads, axis=0), ((0, 0), (0, 64)))

    vectors = jnp.concatenate(
        [grad_b_out, grad_gain_one, grad_shift_one, grad_b_down, grad_gain_two, grad_shift_two, grad_b_up]
    )
    blocks = 2 * wide
    if paired:
        vectors = jnp.pad(low(vectors), (0, 9216 - 7680)).reshape(8, 3, 384)
        vectors = jnp.pad(vectors, ((0, 0), (0, 13), (0, 0)))
        upper = upper_grad(
            place_ids, hidden_low, grad_raised, attn_low, grad_attended, vectors, (grad_parts, by_group)
        )
        upper = upper.reshape(2, 2, 2, 2, 2, 256, 384)
        near, far = halve(upper, "c", 1)
        down_sum = down_grad(active_low, grad_lowered, (upper,))
        upper = both_sum(near, far, down_sum)
        down_sum = lax.psum_scatter(down_sum, ("wa", "c"), scatter_dimension=0, tiled=True)
        upper_pair = halve(upper, "m", 1)
        after = (upper,)
    else:
        grad_w_down = low(outer_sum(active_low, grad_lowered))
        grad_w_up = low(outer_sum(hidden_low, grad_raised))
        grad_w_out = low(outer_sum(attn_low, grad_attended))
        vectors = jnp.pad(low(vectors).reshape(-1, D), ((0, 6), (0, 0)))
        down_rows, out_rows = FF // blocks, D // blocks
        ffn = jnp.concatenate(
            [
                grad_w_down.reshape(blocks, down_rows, D),
                grad_w_up.reshape(blocks, down_rows, D),
                grad_w_out.reshape(blocks, out_rows, D),
                jnp.broadcast_to(vectors[None], (blocks, 16, D)),
            ],
            axis=1,
        )
        after = ()
        ffn_sum = reduce_blocks(ffn).reshape(2, -1, D)
        out_down = widen(ffn_sum[:, :down_rows]).reshape(-1, D)
        out_up = widen(ffn_sum[:, down_rows : 2 * down_rows]).reshape(-1, FF)
        place = 2 * down_rows
        out_out = widen(ffn_sum[:, place : place + out_rows]).reshape(-1, D)
        small = widen(ffn_sum[0, place + out_rows :])

    def share(row, rows):
        vector = small[row : row + rows].reshape(-1)
        size = vector.shape[0] // wide
        return lax.dynamic_slice_in_dim(vector, side * size, size, 0)

    keep, give = tuple(range(0, classes, 2)), tuple(range(1, classes, 2))
    kept, given, dq = attend_backward(
        ids, flags, q_rows, spans, grad_rows, o_full, lse,
        pieces, after, where, count, classes, (keep, give),
    )

    given = swap(given, "c", 1)
    if paired:
        out_down = widen(reduce_rest(tie(down_sum, dq)))
        upper = both_sum(*upper_pair, dq)
        upper_pair = halve(upper, "wa", 1)
        kept = tie(kept, upper)
    partial = widen(kept) + widen(given)
    stay = list(keep)
    bit = mid // 2
    while bit >= 1:
        mask = bit << 1
        near = [i for i, m in enumerate(stay) if not m & mask]
        far = [i for i, m in enumerate(stay) if m & mask]
        sent = swap(low(partial[far[0] : far[-1] + 1]), "m", bit)
        partial = low(partial[near[0] : near[-1] + 1])
        if paired:
            back_q_parts = send_back(tie(dq, partial))
            upper = both_sum(*upper_pair, partial)
            upper_pair = halve(upper, "h", 2)
            partial = tie(partial, upper)
        partial = widen(partial) + widen(sent)
        stay = [stay[i] for i in near]
        bit //= 2
    if not paired:
        back_q_parts = send_back(dq)
    dkv = low(partial[0]).reshape(GROUPS * count, 384)
    back_kv_parts = send_back(dkv)

    part = D // wide
    if paired:
        qkv = qkv_grads(place_ids, group_tokens, dkv, dq)
        qkv_pair = halve(qkv.reshape(2, 2, 208, 576), "c", 1)
        upper = both_sum(*upper_pair, qkv)
        upper_pair = halve(upper, "h", 1)
        qkv = both_sum(*qkv_pair, upper)
        qkv_pair = halve(qkv, "wa", 1)
        upper = both_sum(*upper_pair, qkv)
        other = swap(upper, "h", 1)
        qkv = both_sum(*qkv_pair, upper)
        qkv_other = swap(qkv, "m", 1)
        upper = jnp.stack([tie(upper, qkv), other])
        other = swap(upper, "h", 2)
        qkv = both_sum(qkv, qkv_other, upper)
        qkv_other = swap(qkv, "h", 1)
        upper = jnp.concatenate([tie(upper, qkv), other], axis=0)
        other = swap(upper, "m", 1)
        qkv = jnp.stack([tie(qkv, upper), qkv_other])
        qkv_other = swap(qkv, "h", 2)
        grad_inputs = token_grads(
            tie(grad_sum_one, qkv), back_kv_parts, back_q_parts, back_kv, back_q
        )
        qkv = jnp.concatenate([tie(qkv, grad_inputs), qkv_other], axis=0)
        qkv_other = swap(qkv, "c", 1)
        upper = jnp.concatenate([tie(upper, qkv), other], axis=0)
        other = swap(upper, "c", 1)
        out_query, out_key, out_value, sums = unpack_qkv(
            place_ids, jnp.concatenate([tie(qkv, upper), qkv_other], axis=0)
        )
        sums = sums[:, 0]
        sums_v = jnp.concatenate([sums[:, 256:384], sums[:, 128:192]], axis=1).reshape(-1)
        sums_q = sums[:, 384:576].reshape(-1)
        upper = jnp.concatenate([tie(upper, out_query), other], axis=0)
        out_up, out_out, small = unpack_ffn(place_ids, upper)
        small = small[:, :3].reshape(-1)[:7680].reshape(10, D)
    else:
        both = jnp.concatenate([dkv, dq], axis=1)
        width = both.shape[1]
        w_grad = low(outer_sum(group_tokens, both)).reshape(blocks, D // blocks, width)
        b_grad = low(jnp.sum(widen(both), axis=0))
        b_grad = jnp.pad(b_grad[None], ((0, 15), (0, 0)))
        qkv = jnp.concatenate([w_grad, jnp.broadcast_to(b_grad[None], (blocks, 16, width))], axis=1)
        rows = qkv.shape[1]
        mine = lax.psum_scatter(
            qkv.reshape(blocks * rows, width), ("wa", "c"), scatter_dimension=0, tiled=True
        )
        mine = lax.psum(mine, "m")
        every = widen(lax.all_gather(mine, ("c", "h"), axis=0).reshape(2, GROUPS, rows, width))

        def columns(block):
            k = jnp.concatenate([block[..., :128], block[..., 192:256]], axis=-1)
            v = jnp.concatenate([block[..., 256:384], block[..., 128:192]], axis=-1)
            q = block[..., 384:576]
            return [jnp.transpose(item, (0, 2, 1, 3)).reshape(2, -1, D) for item in (q, k, v)]

        out_query, out_key, out_value = (
            item.reshape(-1, D) for item in columns(every[:, :, : rows - 16])
        )
        sums_q, _, sums_v = (item[0, 0] for item in columns(every[:, :, rows - 16 : rows - 15]))
        grad_inputs = token_grads(grad_sum_one, back_kv_parts, back_q_parts, back_kv, back_q)
    out_b_query = lax.dynamic_slice_in_dim(sums_q, side * part, part, 0)
    out_b_value = lax.dynamic_slice_in_dim(sums_v, side * part, part, 0)

    return (
        low(result)[None],
        grad_inputs[None],
        out_query,
        out_key,
        out_value,
        out_out,
        out_up,
        out_down,
        out_b_query,
        out_b_value,
        share(0, 1),
        share(1, 1),
        share(2, 1),
        share(6, 4),
        share(3, 1),
        share(4, 1),
        share(5, 1),
    )


def solution(mesh):
    chunks, wide = mesh.devices.shape
    finer = Mesh(
        mesh.devices.reshape(GROUPS, chunks // (2 * GROUPS), 2, wide), ("h", "m", "c", "wa")
    )
    ctx = ("h", "m", "c")
    seq3, seq2 = P("wa", ctx, None), P("wa", ctx)
    matrix, vector = P("wa", None), P("wa")
    return jax.shard_map(
        per_device,
        mesh=finer,
        in_specs=(seq3, seq2, seq3) + (matrix,) * 6 + (vector,) * 9,
        out_specs=(seq3, seq3) + (matrix,) * 6 + (vector,) * 9,
        check_vma=False,
    )
```

time: 725 us -> 506 us (0.70)
  waiting for transfers between devices: 298 us -> 141 us
  blocking collectives: 82.1 us -> 4.44 us
  starting transfers between devices: 30.6 us -> 75.5 us
  local copies, waits for them, and re-layouts: 95.7 us -> 65.4 us
  Pallas kernels: 101 us -> 126 us
  matrix products: 47.3 us -> 27.4 us
    reduce_scatter x3, waiting for transfers between devices: 134 us -> 14 us  [the longest x1 9.08 us: reduce_rest(): mine = lax.psum_scatter(mine, 'm', scatter_dimension=0, tiled=True)]
    ppermute x20 -> x43, starting transfers between devices: 28.7 us -> 74.7 us  [swap(): return lax.ppermute(array, axis, [(i, i ^ bit) for i in range(size)])]
    all_gather x2 -> x0, blocking collectives: 46 us -> none  [the longest x1 24.3 us: per_device(): lax.all_gather(pick_columns((w_query, w_key, w_value), group), 'wa', axis...]
    pallas_call x0 -> x6, Pallas kernels: none -> 43.1 us  [the longest x1 11 us: unpack_ffn(): pl.pallas_call(unpack_ffn_kernel, out_shape=(jax.ShapeDtypeStruct((384, F...]
    all_gather x2 -> x1, waiting for transfers between devices: 37 us -> 0.01 us  [reduce_rest(): return lax.all_gather(mine, ('c', 'h', 'm'), axis=0, tiled=True)]
    unnamed x1 -> x0, blocking collectives: 31.3 us -> none
    ppermute x20 -> x43, waiting for transfers between devices: 104 us -> 127 us  [swap(): return lax.ppermute(array, axis, [(i, i ^ bit) for i in range(size)])]
    psum x1 -> x0, waiting for transfers between devices: 22 us -> none  [per_device(): mine = lax.psum(mine, 'm')]
  transfers between devices with their start and end apart: 33 -> 51, of which waited for: 16 -> 20; matrix products, arithmetic and copies ran while one was open for 22% -> 25% of each run, Pallas kernels for 7% -> 22%
where the time goes in v2:
time: 506 us; the launch traced here: 498 us
  waiting for transfers between devices  141 us (28%)
  Pallas kernels  126 us (25%)
  starting transfers between devices  75.5 us (15%)
  local copies, waits for them, and re-layouts  65.4 us (13%)
  other arithmetic  43.2 us (9%)
  matrix products  27.4 us (5%)
  between operations  15.8 us (3%)
    ppermute x43, waiting for transfers between devices, swap(): return lax.ppermute(array, axis, [(i, i ^ bit) for i in range(size)])  127 us
    ppermute x43, starting transfers between devices, swap(): return lax.ppermute(array, axis, [(i, i ^ bit) for i in range(size)])  74.7 us
    pallas_call x1, Pallas kernels, attend_backward(): pl.pallas_call(functools.partial(backward_kernel, where, rows, classes, o...  48.9 us
    pallas_call x1, Pallas kernels, attend_forward(): pl.pallas_call(functools.partial(forward_kernel, where, rows, classes), o...  33.7 us
    dot_general x7, matrix products, mm(): return jnp.dot(left, right, preferred_element_type=jnp.float32)  21.7 us
    pallas_call x1, Pallas kernels, unpack_ffn(): pl.pallas_call(unpack_ffn_kernel, out_shape=(jax.ShapeDtypeStruct((384, F...  11 us
  transfers between devices with their start and end apart: 51, of which 20 were waited for; matrix products, arithmetic and copies ran while one was open for 25% of the time, Pallas kernels for 22%

profile of v2, /device:TPU:0, one launch (start us, length us, event | category | flops | bytes accessed | tf_op | source)
XLA Modules:
  0.0 498.4 jit_solution(15384275704107091001)
XLA Ops:
  7.4 3.1 collective-permute-start
  10.4 2.6 collective-permute-start.1
  28.6 3.8 collective-permute-done.5
  32.4 3.0 collective-permute-start.6
  37.4 4.4 all-gather.1
  42.0 2.6 maximum_select_fusion
  55.0 2.8 add_convert_fusion.5
  68.2 5.7 %collective-permute-done.8.rest_1_ = bf16[3,320,384]{2,1,0:T(8,128)(2,1)} collective-permute-done((bf16[3,320,384]{2,1,0:T(8,128)(2,1)}, bf16[3,320,384]{2,1,0:T(8,128)(2,1)}, u32[]{:S(2)}, u32[]{:S(2)}) %collective-permute-start.8) | collective-permute-done | bytes 737312 | tf_op jit(solution)/shard_map/ppermute | solution.py:78
  81.9 5.1 %collective-permute-done.11.rest_5_ = bf16[1,320,384]{2,1,0:T(8,128)(2,1)S(1)} collective-permute-done((bf16[1,320,384]{2,1,0:T(8,128)(2,1)S(1)}, bf16[1,320,384]{2,1,0:T(8,128)(2,1)S(1)}, u32[]{:S(2)}, u32[]{:S(2)}) %collective-permute-start.11) | collective-permute-done | bytes 245792 | tf_op jit(solution)/shard_map/ppermute | solution.py:78
  89.2 33.7 %attend_forward.1 = (bf16[1280,192]{1,0:T(8,128)(2,1)}, f32[1280,256]{1,0:T(8,128)}, f32[8,1280]{1,0:T(8,128)}) custom-call(s32[2]{0:T(128)} %pad_add_fusion.4.ids, s32[55]{0:T(128)} %reshape.334.flags, bf16[1280,256]{1,0:T(8,128)(2,1)} %pad_maximum_fusion.4.q, s32[8,1280]{1,0:T(8,128)} %add_add_fusion.spans, bf16[3,320,384]{2,1,0:T(8,128)(2,1)} %bitcast.3.rest_0_, ...), custom_call_target="tpu_custom_call" | custom-call | flops 5033164800 | bytes 8388608 | tf_op jit(solution)/shard_map/attend_forward/pallas_call | solution.py:325
  124.2 3.3 collective-permute-start.16
  127.5 5.9 %collective-permute-start.15 = (bf16[320,192]{1,0:T(8,128)(2,1)S(1)}, bf16[320,192]{1,0:T(8,128)(2,1)S(1)}, u32[]{:S(2)}, u32[]{:S(2)}) collective-permute-start(bf16[320,192]{1,0:T(8,128)(2,1)S(1)} %get-tuple-element.163), channel_id=1, source_target_pairs={{0,16},{8,24},{16,0},{24,8},{1,17},{9,25},{17,1},{25,9},{2,18},{10... | collective-permute-start | bytes 368648 | tf_op jit(solution)/shard_map/ppermute | solution.py:78
  134.6 10.3 %collective-permute-done.15 = bf16[320,192]{1,0:T(8,128)(2,1)S(1)} collective-permute-done((bf16[320,192]{1,0:T(8,128)(2,1)S(1)}, bf16[320,192]{1,0:T(8,128)(2,1)S(1)}, u32[]{:S(2)}, u32[]{:S(2)}) %collective-permute-start.15) | collective-permute-done | bytes 122912 | tf_op jit(solution)/shard_map/ppermute | solution.py:78
  149.9 7.3 %multiply_convert_fusion = (bf16[320,3072]{1,0:T(8,128)(2,1)}, f32[320,3072]{1,0:T(8,128)}) fusion(f32[3072]{0:T(1024)S(1)} %reshape.350, bf16[320,768]{1,0:T(8,128)(2,1)S(1)} %fusion.24.hid, bf16[768,3072]{1,0:T(8,128)(2,1)} %all-gather.10.cloned.1.call-done), kind=kOutput, calls=%fused_computation.15 | convolution fusion | flops 1515847680 | bytes 11120640 | tf_op jit(solution)/shard_map/dot_general | solution.py:38
  157.1 4.9 fusion.49
  164.6 2.9 fusion.50
  176.4 9.3 %upper_grad.1 = bf16[32,256,384]{2,1,0:T(8,128)(2,1)} custom-call(s32[4]{0:T(128)} %pad_add_fusion.5.ids, bf16[320,768]{1,0:T(8,128)(2,1)} %copy-done.13, bf16[320,3072]{1,0:T(8,128)(2,1)} %copy-done.8, bf16[320,768]{1,0:T(8,128)(2,1)} %copy.53.attn, bf16[320,768]{1,0:T(8,128)(2,1)} %copy-done.15, bf16[8,16,384]{2,1,0:T(8,128)(2,1)} %pad.14.vec, ...), custom_call_target="tpu_custom_call" | custom-call | flops 1887436800 | bytes 12582912 | tf_op jit(solution)/shard_map/upper_grad/pallas_call | solution.py:441
  185.6 8.0 %down_grad.1 = bf16[3072,768]{1,0:T(8,128)(2,1)} custom-call(bf16[320,3072]{1,0:T(8,128)(2,1)} %get-tuple-element.203.active, bf16[320,768]{1,0:T(8,128)(2,1)} %copy-done.14, bf16[2,2,2,2,2,256,384]{6,5,4,3,2,1,0:T(8,128)(2,1)} %bitcast.114), custom_call_target="tpu_custom_call" | custom-call | flops 1509949440 | bytes 8388608 | tf_op jit(solution)/shard_map/down_grad/pallas_call | solution.py:404
  193.9 3.5 fusion.39
  199.3 3.2 collective-permute-start.17
  202.5 4.6 collective-permute-done.19
  207.1 6.4 %collective-permute-done.18 = bf16[320,192]{1,0:T(8,128)(2,1)S(1)} collective-permute-done((bf16[320,192]{1,0:T(8,128)(2,1)S(1)}, bf16[320,192]{1,0:T(8,128)(2,1)S(1)}, u32[]{:S(2)}, u32[]{:S(2)}) %collective-permute-start.18) | collective-permute-done | bytes 122912 | tf_op jit(solution)/shard_map/ppermute | solution.py:78
  219.6 48.9 %attend_backward.1 = (bf16[2,4,320,384]{3,2,1,0:T(8,128)(2,1)}, bf16[2,4,320,384]{3,2,1,0:T(8,128)(2,1)}, bf16[1280,192]{1,0:T(8,128)(2,1)}) custom-call(s32[2]{0:T(128)} %pad_add_fusion.4.ids, s32[55]{0:T(128)} %reshape.334.flags, bf16[1280,256]{1,0:T(8,128)(2,1)} %pad_maximum_fusion.4.q, s32[8,1280]{1,0:T(8,128)} %add_add_fusion.spans, ...), custom_call_target="tpu_custom_call" | custom-call | flops 12582912000 | bytes 16777216 | tf_op jit(solution)/shard_map/attend_backward/pallas_call | solution.py:360
  269.0 2.6 pad_maximum_fusion.2.tokens
  276.8 2.7 gather_fusion.1
  281.2 2.5 copy.56
  287.0 5.4 %collective-permute-start.23 = (bf16[2,2,256,384]{3,2,1,0:T(8,128)(2,1)}, bf16[2,2,256,384]{3,2,1,0:T(8,128)(2,1)}, u32[]{:S(2)}, u32[]{:S(2)}) collective-permute-start(bf16[2,2,256,384]{3,2,1,0:T(8,128)(2,1)} %get-tuple-element.143), channel_id=1, source_target_pairs={{0,1},{1,0},{2,3},{3,2},{4,5},{5,4},{6,7},{7,6},{8,9},{9,8},{10,11... | collective-permute-start | bytes 2359304 | tf_op jit(solution)/shard_map/ppermute | solution.py:78
  292.5 2.6 add_convert_fusion.1
  300.0 8.9 %collective-permute-start.36 = (bf16[320,192]{1,0:T(8,128)(2,1)}, bf16[320,192]{1,0:T(8,128)(2,1)}, u32[]{:S(2)}, u32[]{:S(2)}) collective-permute-start(bf16[320,192]{1,0:T(8,128)(2,1)} %get-tuple-element.155), channel_id=1, source_target_pairs={{0,8},{8,0},{16,24},{24,16},{1,9},{9,1},{17,25},{25,17},{2,10},{10... | collective-permute-start | bytes 368648 | tf_op jit(solution)/shard_map/ppermute | solution.py:78
  312.6 10.3 %collective-permute-start.25 = (bf16[2,256,384]{2,1,0:T(8,128)(2,1)}, bf16[2,256,384]{2,1,0:T(8,128)(2,1)S(1)}, u32[]{:S(2)}, u32[]{:S(2)}) collective-permute-start(bf16[2,256,384]{2,1,0:T(8,128)(2,1)} %get-tuple-element.152), channel_id=1, source_target_pairs={{0,16},{8,24},{16,0},{24,8},{1,17},{9,25},{17,1},{25,9},{2,18},{10... | collective-permute-start | bytes 1179656 | tf_op jit(solution)/shard_map/ppermute | solution.py:78
  324.2 5.3 %qkv_grads.1 = bf16[4,208,576]{2,1,0:T(8,128)(2,1)} custom-call(s32[4]{0:T(128)} %pad_add_fusion.5.ids, bf16[1280,768]{1,0:T(8,128)(2,1)} %pad_maximum_fusion.2.tokens, bf16[1280,384]{1,0:T(8,128)(2,1)} %bitcast.118, bf16[1280,192]{1,0:T(8,128)(2,1)} %get-tuple-element.107.dq), custom_call_target="tpu_custom_call" | custom-call | flops 1132462080 | bytes 4194304 | tf_op jit(solution)/shard_map/qkv_grads/pallas_call | solution.py:512
  330.8 4.9 reduce-scatter.6.cloned.1.call-done
  336.1 10.3 %collective-permute-done.25 = bf16[2,256,384]{2,1,0:T(8,128)(2,1)S(1)} collective-permute-done((bf16[2,256,384]{2,1,0:T(8,128)(2,1)}, bf16[2,256,384]{2,1,0:T(8,128)(2,1)S(1)}, u32[]{:S(2)}, u32[]{:S(2)}) %collective-permute-start.25) | collective-permute-done | bytes 393248 | tf_op jit(solution)/shard_map/ppermute | solution.py:78
  347.3 9.1 %reduce-scatter.8.cloned.1.call-done = bf16[96,768]{1,0:T(8,128)(2,1)} async-done(((bf16[192,768]{1,0:T(8,128)(2,1)}), bf16[96,768]{1,0:T(8,128)(2,1)}) %reduce-scatter.8.cloned.1.call-update) | async-done | bytes 147472 | tf_op jit(solution)/shard_map/reduce_scatter | solution.py:607
  365.2 12.7 %collective-permute-done.29 = bf16[256,384]{1,0:T(8,128)(2,1)S(1)} collective-permute-done((bf16[256,384]{1,0:T(8,128)(2,1)S(1)}, bf16[256,384]{1,0:T(8,128)(2,1)S(1)}, u32[]{:S(2)}, u32[]{:S(2)}) %collective-permute-start.29) | collective-permute-done | bytes 196640 | tf_op jit(solution)/shard_map/ppermute | solution.py:78
  380.9 2.5 collective-permute-start.32
  383.5 20.9 %collective-permute-done.31 = bf16[2,256,384]{2,1,0:T(8,128)(2,1)S(1)} collective-permute-done((bf16[2,256,384]{2,1,0:T(8,128)(2,1)S(1)}, bf16[2,256,384]{2,1,0:T(8,128)(2,1)S(1)}, u32[]{:S(2)}, u32[]{:S(2)}) %collective-permute-start.31) | collective-permute-done | bytes 393248 | tf_op jit(solution)/shard_map/ppermute | solution.py:78
  404.5 3.0 collective-permute-start.34
  410.6 7.4 %collective-permute-done.33.kv1 = bf16[320,384]{1,0:T(8,128)(2,1)S(1)} collective-permute-done((bf16[320,384]{1,0:T(8,128)(2,1)S(1)}, bf16[320,384]{1,0:T(8,128)(2,1)S(1)}, u32[]{:S(2)}, u32[]{:S(2)}) %collective-permute-start.33) | collective-permute-done | bytes 245792 | tf_op jit(solution)/shard_map/ppermute | solution.py:78
  418.1 18.5 %collective-permute-done.34.kv2 = bf16[320,384]{1,0:T(8,128)(2,1)S(1)} collective-permute-done((bf16[320,384]{1,0:T(8,128)(2,1)S(1)}, bf16[320,384]{1,0:T(8,128)(2,1)S(1)}, u32[]{:S(2)}, u32[]{:S(2)}) %collective-permute-start.34) | collective-permute-done | bytes 245792 | tf_op jit(solution)/shard_map/ppermute | solution.py:78
  437.3 5.7 %token_grads.1 = f32[320,768]{1,0:T(8,128)} custom-call(f32[320,768]{1,0:T(8,128)} %get-tuple-element.106.base, bf16[320,384]{1,0:T(8,128)(2,1)} %get-tuple-element.150.kv0, bf16[320,384]{1,0:T(8,128)(2,1)} %copy-done.20, bf16[320,384]{1,0:T(8,128)(2,1)} %copy-done.21, bf16[320,384]{1,0:T(8,128)(2,1)} %copy-done.22, bf16[320,192]{1,0:T(8,128)(2,1)} %get-tuple-element.156.q0, ...), custom_call_target="tpu_custom_call" | custom-call | flops 1132462080 | bytes 8388608 | tf_op jit(solution)/shard_map/token_grads/pallas_call | solution.py:561
  443.1 9.3 %collective-permute-done.39 = bf16[2,208,576]{2,1,0:T(8,128)(2,1)S(1)} collective-permute-done((bf16[2,208,576]{2,1,0:T(8,128)(2,1)S(1)}, bf16[2,208,576]{2,1,0:T(8,128)(2,1)S(1)}, u32[]{:S(2)}, u32[]{:S(2)}) %collective-permute-start.39) | collective-permute-done | bytes 479264 | tf_op jit(solution)/shard_map/ppermute | solution.py:78
  453.3 4.6 collective-permute-done.41
  457.8 2.9 pad_maximum_fusion.1.pieces
  460.7 3.8 unpack_qkv.1
  466.9 3.4 pad_maximum_fusion.block
  470.4 11.0 %unpack_ffn.1 = (f32[384,3072]{1,0:T(8,128)}, f32[384,768]{1,0:T(8,128)}, f32[8,16,384]{2,1,0:T(8,128)}) custom-call(s32[4]{0:T(128)} %pad_add_fusion.5.ids, bf16[16,256,384]{2,1,0:T(8,128)(2,1)} %pad_maximum_fusion.block), custom_call_target="tpu_custom_call" | custom-call | tf_op jit(solution)/shard_map/unpack_ffn/pallas_call | solution.py:465
  486.9 4.2 convert_element_type.318
  (390 shorter events, 122.6 us)
Async XLA Ops:
  7.3 139.9 %all-gather.8.cloned.1.call-start = ((), (), s32[]{:S(2)}) async-start(), calls=%async_computation.3 | async-start | bytes 1474560 | tf_op jit(solution)/shard_map/all_gather | solution.py:577
  7.4 34.6 %collective-permute-start = (bf16[320,768]{1,0:T(8,128)(2,1)}, bf16[320,768]{1,0:T(8,128)(2,1)S(1)}, u32[]{:S(2)}, u32[]{:S(2)}) collective-permute-start(bf16[320,768]{1,0:T(8,128)(2,1)} %bitcast.124), channel_id=1, source_target_pairs={{0,8},{8,0},{16,24},{24,16},{1,9},{9,1},{17,25},{25,17},{2,10},{10... | collective-permute-start | bytes 1474568 | tf_op jit(solution)/shard_map/ppermute | solution.py:78
  10.4 31.6 %collective-permute-start.1 = (bf16[320,768]{1,0:T(8,128)(2,1)}, bf16[320,768]{1,0:T(8,128)(2,1)}, u32[]{:S(2)}, u32[]{:S(2)}) collective-permute-start(bf16[320,768]{1,0:T(8,128)(2,1)} %bitcast.125), channel_id=1, source_target_pairs={{0,16},{8,24},{16,0},{24,8},{1,17},{9,25},{17,1},{25,9},{2,18},{10... | collective-permute-start | bytes 1474568 | tf_op jit(solution)/shard_map/ppermute | solution.py:78
  21.7 20.3 %collective-permute-start.2 = (bf16[384,640]{1,0:T(8,128)(2,1)S(1)}, bf16[384,640]{1,0:T(8,128)(2,1)}, u32[]{:S(2)}, u32[]{:S(2)}) collective-permute-start(bf16[384,640]{1,0:T(8,128)(2,1)S(1)} %concatenate.78), channel_id=1, source_target_pairs={{0,1},{1,0},{2,3},{3,2},{4,5},{5,4},{6,7},{7,6},{8,9},{9,8},{10,11... | collective-permute-start | bytes 1474568 | tf_op jit(solution)/shard_map/ppermute | solution.py:78
  28.1 4.3 collective-permute-start.5
  32.4 9.5 %collective-permute-start.6 = (s32[8,320]{1,0:T(8,128)S(1)}, s32[8,320]{1,0:T(8,128)S(1)}, u32[]{:S(2)}, u32[]{:S(2)}) collective-permute-start(s32[8,320]{1,0:T(8,128)S(1)} %pad_add_fusion), channel_id=1, source_target_pairs={{0,16},{8,24},{16,0},{24,8},{1,17},{9,25},{17,1},{25,9},{2,18},{10... | collective-permute-start | bytes 30728 | tf_op jit(solution)/shard_map/ppermute | solution.py:78
  45.4 104.5 %all-gather.10.cloned.1.call-start = ((), (), s32[]{:S(2)}) async-start(), calls=%async_computation.4 | async-start | bytes 5898240 | tf_op jit(solution)/shard_map/all_gather | solution.py:577
  46.6 110.5 %all-gather.12.cloned.1.call-start = ((), (), s32[]{:S(2)}) async-start(), calls=%async_computation.5 | async-start | bytes 5898240 | tf_op jit(solution)/shard_map/all_gather | solution.py:577
  49.2 127.2 %all-gather.14.cloned.1.call-start = ((), (), s32[]{:S(2)}) async-start(), calls=%async_computation.6 | async-start | bytes 4423680 | tf_op jit(solution)/shard_map/all_gather | solution.py:577
  54.5 22.4 %collective-permute-start.7 = (bf16[320,768]{1,0:T(8,128)(2,1)}, bf16[320,768]{1,0:T(8,128)(2,1)}, u32[]{:S(2)}, u32[]{:S(2)}) collective-permute-start(bf16[320,768]{1,0:T(8,128)(2,1)} %collective-permute-done.1), channel_id=1, source_target_pairs={{0,8},{8,0},{16,24},{24,16},{1,9},{9,1},{17,25},{25,17},{2,10},{10... | collective-permute-start | bytes 1474568 | tf_op jit(solution)/shard_map/ppermute | solution.py:78
  57.8 16.1 %collective-permute-start.8 = (bf16[3,320,384]{2,1,0:T(8,128)(2,1)}, bf16[3,320,384]{2,1,0:T(8,128)(2,1)}, u32[]{:S(2)}, u32[]{:S(2)}) collective-permute-start(bf16[3,320,384]{2,1,0:T(8,128)(2,1)} %bitcast.3.rest_0_), channel_id=1, source_target_pairs={{0,4},{4,0},{1,5},{5,1},{2,6},{6,2},{3,7},{7,3},{8,12},{12,8},{9,1... | collective-permute-start | bytes 2211848 | tf_op jit(solution)/shard_map/ppermute | solution.py:78
  59.4 28.5 %collective-permute-start.9 = (bf16[3,320,384]{2,1,0:T(8,128)(2,1)}, bf16[3,320,384]{2,1,0:T(8,128)(2,1)}, u32[]{:S(2)}, u32[]{:S(2)}) collective-permute-start(bf16[3,320,384]{2,1,0:T(8,128)(2,1)} %bitcast.3.rest_0_), channel_id=1, source_target_pairs={{0,2},{2,0},{1,3},{3,1},{4,6},{6,4},{5,7},{7,5},{8,10},{10,8},{9,1... | collective-permute-start | bytes 2211848 | tf_op jit(solution)/shard_map/ppermute | solution.py:78
  74.0 14.6 %collective-permute-start.10 = (bf16[3,320,384]{2,1,0:T(8,128)(2,1)}, bf16[3,320,384]{2,1,0:T(8,128)(2,1)}, u32[]{:S(2)}, u32[]{:S(2)}) collective-permute-start(bf16[3,320,384]{2,1,0:T(8,128)(2,1)} %collective-permute-done.8.rest_1_), channel_id=1, source_target_pairs={{0,2},{2,0},{1,3},{3,1},{4,6},{6,4},{5,7},{7,5},{8,10},{10,8},{9,1... | collective-permute-start | bytes 2211848 | tf_op jit(solution)/shard_map/ppermute | solution.py:78
  78.6 8.4 %collective-permute-start.11 = (bf16[1,320,384]{2,1,0:T(8,128)(2,1)S(1)}, bf16[1,320,384]{2,1,0:T(8,128)(2,1)S(1)}, u32[]{:S(2)}, u32[]{:S(2)}) collective-permute-start(bf16[1,320,384]{2,1,0:T(8,128)(2,1)S(1)} %fusion.18.rest_4_), channel_id=1, source_target_pairs={{0,4},{4,0},{1,5},{5,1},{2,6},{6,2},{3,7},{7,3},{8,12},{12,8},{9,1... | collective-permute-start | bytes 737288 | tf_op jit(solution)/shard_map/ppermute | solution.py:78
  80.2 7.7 %collective-permute-start.12 = (bf16[1,320,384]{2,1,0:T(8,128)(2,1)S(1)}, bf16[1,320,384]{2,1,0:T(8,128)(2,1)S(1)}, u32[]{:S(2)}, u32[]{:S(2)}) collective-permute-start(bf16[1,320,384]{2,1,0:T(8,128)(2,1)S(1)} %fusion.18.rest_4_), channel_id=1, source_target_pairs={{0,2},{2,0},{1,3},{3,1},{4,6},{6,4},{5,7},{7,5},{8,10},{10,8},{9,1... | collective-permute-start | bytes 737288 | tf_op jit(solution)/shard_map/ppermute | solution.py:78
  124.2 10.4 %collective-permute-start.16 = (bf16[320,192]{1,0:T(8,128)(2,1)S(1)}, bf16[320,192]{1,0:T(8,128)(2,1)S(1)}, u32[]{:S(2)}, u32[]{:S(2)}) collective-permute-start(bf16[320,192]{1,0:T(8,128)(2,1)S(1)} %get-tuple-element.162), channel_id=1, source_target_pairs={{0,24},{8,16},{16,8},{24,0},{1,25},{9,17},{17,9},{25,1},{2,26},{10... | collective-permute-start | bytes 368648 | tf_op jit(solution)/shard_map/ppermute | solution.py:78
  127.5 17.3 %collective-permute-start.15 = (bf16[320,192]{1,0:T(8,128)(2,1)S(1)}, bf16[320,192]{1,0:T(8,128)(2,1)S(1)}, u32[]{:S(2)}, u32[]{:S(2)}) collective-permute-start(bf16[320,192]{1,0:T(8,128)(2,1)S(1)} %get-tuple-element.163), channel_id=1, source_target_pairs={{0,16},{8,24},{16,0},{24,8},{1,17},{9,25},{17,1},{25,9},{2,18},{10... | collective-permute-start | bytes 368648 | tf_op jit(solution)/shard_map/ppermute | solution.py:78
  133.4 11.5 %collective-permute-start.14 = (bf16[320,192]{1,0:T(8,128)(2,1)S(1)}, bf16[320,192]{1,0:T(8,128)(2,1)S(1)}, u32[]{:S(2)}, u32[]{:S(2)}) collective-permute-start(bf16[320,192]{1,0:T(8,128)(2,1)S(1)} %get-tuple-element.164), channel_id=1, source_target_pairs={{0,8},{8,0},{16,24},{24,16},{1,9},{9,1},{17,25},{25,17},{2,10},{10... | collective-permute-start | bytes 368648 | tf_op jit(solution)/shard_map/ppermute | solution.py:78
  134.5 157.9 %reduce-scatter.4.cloned.1.call-start = ((), (), s32[]{:S(2)}) async-start(), calls=%async_computation.7 | async-start | bytes 5898240 | tf_op jit(solution)/shard_map/reduce_scatter | solution.py:837
  193.7 142.1 %reduce-scatter.6.cloned.1.call-start = ((), (), s32[]{:S(2)}) async-start(), calls=%async_computation.8 | async-start | bytes 1474560 | tf_op jit(solution)/shard_map/reduce_scatter | solution.py:606
  197.5 17.0 %collective-permute-start.20 = (bf16[2,2,2,2,256,384]{5,4,3,2,1,0:T(8,128)(2,1)S(1)}, bf16[2,2,2,2,256,384]{5,4,3,2,1,0:T(8,128)(2,1)S(1)}, u32[]{:S(2)}, u32[]{:S(2)}) collective-permute-start(bf16[2,2,2,2,256,384]{5,4,3,2,1,0:T(8,128)(2,1)S(1)} %bitcast.120), channel_id=1, source_target_pairs={{0,2},{2,0},{1,3},{3,1},{4,6},{6,4},{5,7},{7,5},{8,10},{10,8},{9,1... | collective-permute-start | bytes 9437192 | tf_op jit(solution)/shard_map/ppermute | solution.py:78
  198.0 9.1 %collective-permute-start.19 = (bf16[320,192]{1,0:T(8,128)(2,1)S(1)}, bf16[320,192]{1,0:T(8,128)(2,1)S(1)}, u32[]{:S(2)}, u32[]{:S(2)}) collective-permute-start(bf16[320,192]{1,0:T(8,128)(2,1)S(1)} %get-tuple-element.158), channel_id=1, source_target_pairs={{0,24},{8,16},{16,8},{24,0},{1,25},{9,17},{17,9},{25,1},{2,26},{10... | collective-permute-start | bytes 368648 | tf_op jit(solution)/shard_map/ppermute | solution.py:78
  199.3 14.2 %collective-permute-start.18 = (bf16[320,192]{1,0:T(8,128)(2,1)S(1)}, bf16[320,192]{1,0:T(8,128)(2,1)S(1)}, u32[]{:S(2)}, u32[]{:S(2)}) collective-permute-start(bf16[320,192]{1,0:T(8,128)(2,1)S(1)} %get-tuple-element.159), channel_id=1, source_target_pairs={{0,16},{8,24},{16,0},{24,8},{1,17},{9,25},{17,1},{25,9},{2,18},{10... | collective-permute-start | bytes 368648 | tf_op jit(solution)/shard_map/ppermute | solution.py:78
  199.3 14.2 %collective-permute-start.17 = (bf16[320,192]{1,0:T(8,128)(2,1)S(1)}, bf16[320,192]{1,0:T(8,128)(2,1)S(1)}, u32[]{:S(2)}, u32[]{:S(2)}) collective-permute-start(bf16[320,192]{1,0:T(8,128)(2,1)S(1)} %get-tuple-element.160), channel_id=1, source_target_pairs={{0,8},{8,0},{16,24},{24,16},{1,9},{9,1},{17,25},{25,17},{2,10},{10... | collective-permute-start | bytes 368648 | tf_op jit(solution)/shard_map/ppermute | solution.py:78
  218.1 65.6 %collective-permute-start.21 = (bf16[2,2,2,256,384]{4,3,2,1,0:T(8,128)(2,1)}, bf16[2,2,2,256,384]{4,3,2,1,0:T(8,128)(2,1)}, u32[]{:S(2)}, u32[]{:S(2)}) collective-permute-start(bf16[2,2,2,256,384]{4,3,2,1,0:T(8,128)(2,1)} %get-tuple-element.139), channel_id=1, source_target_pairs={{0,4},{4,0},{1,5},{5,1},{2,6},{6,2},{3,7},{7,3},{8,12},{12,8},{9,1... | collective-permute-start | bytes 4718600 | tf_op jit(solution)/shard_map/ppermute | solution.py:78
  268.5 24.0 %collective-permute-start.22 = (bf16[2,4,320,384]{3,2,1,0:T(8,128)(2,1)}, bf16[2,4,320,384]{3,2,1,0:T(8,128)(2,1)}, u32[]{:S(2)}, u32[]{:S(2)}) collective-permute-start(bf16[2,4,320,384]{3,2,1,0:T(8,128)(2,1)} %get-tuple-element.95), channel_id=1, source_target_pairs={{0,2},{2,0},{1,3},{3,1},{4,6},{6,4},{5,7},{7,5},{8,10},{10,8},{9,1... | collective-permute-start | bytes 5898248 | tf_op jit(solution)/shard_map/ppermute | solution.py:78
  287.0 23.5 %collective-permute-start.23 = (bf16[2,2,256,384]{3,2,1,0:T(8,128)(2,1)}, bf16[2,2,256,384]{3,2,1,0:T(8,128)(2,1)}, u32[]{:S(2)}, u32[]{:S(2)}) collective-permute-start(bf16[2,2,256,384]{3,2,1,0:T(8,128)(2,1)} %get-tuple-element.143), channel_id=1, source_target_pairs={{0,1},{1,0},{2,3},{3,2},{4,5},{5,4},{6,7},{7,6},{8,9},{9,8},{10,11... | collective-permute-start | bytes 2359304 | tf_op jit(solution)/shard_map/ppermute | solution.py:78
  292.5 63.9 %reduce-scatter.8.cloned.1.call-start = ((), (), s32[]{:S(2)}) async-start(), calls=%async_computation.9 | async-start | bytes 442368 | tf_op jit(solution)/shard_map/reduce_scatter | solution.py:607
  295.4 27.6 %collective-permute-start.24 = (bf16[1,4,320,384]{3,2,1,0:T(8,128)(2,1)S(1)}, bf16[1,4,320,384]{3,2,1,0:T(8,128)(2,1)S(1)}, u32[]{:S(2)}, u32[]{:S(2)}) collective-permute-start(bf16[1,4,320,384]{3,2,1,0:T(8,128)(2,1)S(1)} %get-tuple-element.141), channel_id=1, source_target_pairs={{0,4},{4,0},{1,5},{5,1},{2,6},{6,2},{3,7},{7,3},{8,12},{12,8},{9,1... | collective-permute-start | bytes 2949128 | tf_op jit(solution)/shard_map/ppermute | solution.py:78
  300.0 107.6 %collective-permute-start.36 = (bf16[320,192]{1,0:T(8,128)(2,1)}, bf16[320,192]{1,0:T(8,128)(2,1)}, u32[]{:S(2)}, u32[]{:S(2)}) collective-permute-start(bf16[320,192]{1,0:T(8,128)(2,1)} %get-tuple-element.155), channel_id=1, source_target_pairs={{0,8},{8,0},{16,24},{24,16},{1,9},{9,1},{17,25},{25,17},{2,10},{10... | collective-permute-start | bytes 368648 | tf_op jit(solution)/shard_map/ppermute | solution.py:78
  312.6 33.7 %collective-permute-start.25 = (bf16[2,256,384]{2,1,0:T(8,128)(2,1)}, bf16[2,256,384]{2,1,0:T(8,128)(2,1)S(1)}, u32[]{:S(2)}, u32[]{:S(2)}) collective-permute-start(bf16[2,256,384]{2,1,0:T(8,128)(2,1)} %get-tuple-element.152), channel_id=1, source_target_pairs={{0,16},{8,24},{16,0},{24,8},{1,17},{9,25},{17,1},{25,9},{2,18},{10... | collective-permute-start | bytes 1179656 | tf_op jit(solution)/shard_map/ppermute | solution.py:78
  330.7 16.4 %collective-permute-start.26 = (bf16[2,208,576]{2,1,0:T(8,128)(2,1)S(1)}, bf16[2,208,576]{2,1,0:T(8,128)(2,1)S(1)}, u32[]{:S(2)}, u32[]{:S(2)}) collective-permute-start(bf16[2,208,576]{2,1,0:T(8,128)(2,1)S(1)} %get-tuple-element.145), channel_id=1, source_target_pairs={{0,2},{2,0},{1,3},{3,1},{4,6},{6,4},{5,7},{7,5},{8,10},{10,8},{9,1... | collective-permute-start | bytes 1437704 | tf_op jit(solution)/shard_map/ppermute | solution.py:78
  335.8 151.2 %all-gather.16.cloned.1.call-start = ((), (), s32[]{:S(2)}) async-start(), calls=%async_computation.10 | async-start | bytes 2506752 | tf_op jit(solution)/shard_map/all_gather | solution.py:608
  347.1 14.7 %collective-permute-start.27 = (bf16[256,384]{1,0:T(8,128)(2,1)}, bf16[256,384]{1,0:T(8,128)(2,1)}, u32[]{:S(2)}, u32[]{:S(2)}) collective-permute-start(bf16[256,384]{1,0:T(8,128)(2,1)} %get-tuple-element.184), channel_id=1, source_target_pairs={{0,8},{8,0},{16,24},{24,16},{1,9},{9,1},{17,25},{25,17},{2,10},{10... | collective-permute-start | bytes 589832 | tf_op jit(solution)/shard_map/ppermute | solution.py:78
  356.4 8.2 %collective-permute-start.28 = (bf16[208,576]{1,0:T(8,128)(2,1)S(1)}, bf16[208,576]{1,0:T(8,128)(2,1)S(1)}, u32[]{:S(2)}, u32[]{:S(2)}) collective-permute-start(bf16[208,576]{1,0:T(8,128)(2,1)S(1)} %get-tuple-element.182), channel_id=1, source_target_pairs={{0,1},{1,0},{2,3},{3,2},{4,5},{5,4},{6,7},{7,6},{8,9},{9,8},{10,11... | collective-permute-start | bytes 718856 | tf_op jit(solution)/shard_map/ppermute | solution.py:78
  358.0 51.2 %collective-permute-start.37 = (bf16[320,192]{1,0:T(8,128)(2,1)}, bf16[320,192]{1,0:T(8,128)(2,1)S(1)}, u32[]{:S(2)}, u32[]{:S(2)}) collective-permute-start(bf16[320,192]{1,0:T(8,128)(2,1)} %get-tuple-element.154), channel_id=1, source_target_pairs={{0,16},{8,24},{16,0},{24,8},{1,17},{9,25},{17,1},{25,9},{2,18},{10... | collective-permute-start | bytes 368648 | tf_op jit(solution)/shard_map/ppermute | solution.py:78
  360.4 48.8 %collective-permute-start.38 = (bf16[320,192]{1,0:T(8,128)(2,1)}, bf16[320,192]{1,0:T(8,128)(2,1)S(1)}, u32[]{:S(2)}, u32[]{:S(2)}) collective-permute-start(bf16[320,192]{1,0:T(8,128)(2,1)} %get-tuple-element.153), channel_id=1, source_target_pairs={{0,24},{8,16},{16,8},{24,0},{1,25},{9,17},{17,9},{25,1},{2,26},{10... | collective-permute-start | bytes 368648 | tf_op jit(solution)/shard_map/ppermute | solution.py:78
  362.8 15.2 %collective-permute-start.29 = (bf16[256,384]{1,0:T(8,128)(2,1)S(1)}, bf16[256,384]{1,0:T(8,128)(2,1)S(1)}, u32[]{:S(2)}, u32[]{:S(2)}) collective-permute-start(bf16[256,384]{1,0:T(8,128)(2,1)S(1)} %add_convert_fusion.11), channel_id=1, source_target_pairs={{0,8},{8,0},{16,24},{24,16},{1,9},{9,1},{17,25},{25,17},{2,10},{10... | collective-permute-start | bytes 589832 | tf_op jit(solution)/shard_map/ppermute | solution.py:78
  364.7 16.1 %collective-permute-start.30 = (bf16[208,576]{1,0:T(8,128)(2,1)S(1)}, bf16[208,576]{1,0:T(8,128)(2,1)S(1)}, u32[]{:S(2)}, u32[]{:S(2)}) collective-permute-start(bf16[208,576]{1,0:T(8,128)(2,1)S(1)} %add_convert_fusion.10), channel_id=1, source_target_pairs={{0,4},{4,0},{1,5},{5,1},{2,6},{6,2},{3,7},{7,3},{8,12},{12,8},{9,1... | collective-permute-start | bytes 718856 | tf_op jit(solution)/shard_map/ppermute | solution.py:78
  378.0 26.4 %collective-permute-start.31 = (bf16[2,256,384]{2,1,0:T(8,128)(2,1)S(1)}, bf16[2,256,384]{2,1,0:T(8,128)(2,1)S(1)}, u32[]{:S(2)}, u32[]{:S(2)}) collective-permute-start(bf16[2,256,384]{2,1,0:T(8,128)(2,1)S(1)} %pad_maximum_fusion.7), channel_id=1, source_target_pairs={{0,16},{8,24},{16,0},{24,8},{1,17},{9,25},{17,1},{25,9},{2,18},{10... | collective-permute-start | bytes 1179656 | tf_op jit(solution)/shard_map/ppermute | solution.py:78
  380.9 23.6 %collective-permute-start.32 = (bf16[208,576]{1,0:T(8,128)(2,1)S(1)}, bf16[208,576]{1,0:T(8,128)(2,1)S(1)}, u32[]{:S(2)}, u32[]{:S(2)}) collective-permute-start(bf16[208,576]{1,0:T(8,128)(2,1)S(1)} %add_convert_fusion.9), channel_id=1, source_target_pairs={{0,8},{8,0},{16,24},{24,16},{1,9},{9,1},{17,25},{25,17},{2,10},{10... | collective-permute-start | bytes 718856 | tf_op jit(solution)/shard_map/ppermute | solution.py:78
  404.4 13.6 %collective-permute-start.33 = (bf16[320,384]{1,0:T(8,128)(2,1)S(1)}, bf16[320,384]{1,0:T(8,128)(2,1)S(1)}, u32[]{:S(2)}, u32[]{:S(2)}) collective-permute-start(bf16[320,384]{1,0:T(8,128)(2,1)S(1)} %get-tuple-element.149), channel_id=1, source_target_pairs={{0,8},{8,0},{16,24},{24,16},{1,9},{9,1},{17,25},{25,17},{2,10},{10... | collective-permute-start | bytes 737288 | tf_op jit(solution)/shard_map/ppermute | solution.py:78
  404.5 32.0 %collective-permute-start.34 = (bf16[320,384]{1,0:T(8,128)(2,1)S(1)}, bf16[320,384]{1,0:T(8,128)(2,1)S(1)}, u32[]{:S(2)}, u32[]{:S(2)}) collective-permute-start(bf16[320,384]{1,0:T(8,128)(2,1)S(1)} %get-tuple-element.148), channel_id=1, source_target_pairs={{0,16},{8,24},{16,0},{24,8},{1,17},{9,25},{17,1},{25,9},{2,18},{10... | collective-permute-start | bytes 737288 | tf_op jit(solution)/shard_map/ppermute | solution.py:78
  407.7 28.9 %collective-permute-start.35 = (bf16[320,384]{1,0:T(8,128)(2,1)S(1)}, bf16[320,384]{1,0:T(8,128)(2,1)S(1)}, u32[]{:S(2)}, u32[]{:S(2)}) collective-permute-start(bf16[320,384]{1,0:T(8,128)(2,1)S(1)} %get-tuple-element.147), channel_id=1, source_target_pairs={{0,24},{8,16},{16,8},{24,0},{1,25},{9,17},{17,9},{25,1},{2,26},{10... | collective-permute-start | bytes 737288 | tf_op jit(solution)/shard_map/ppermute | solution.py:78
  409.1 43.4 %collective-permute-start.40 = (bf16[4,256,384]{2,1,0:T(8,128)(2,1)S(1)}, bf16[4,256,384]{2,1,0:T(8,128)(2,1)S(1)}, u32[]{:S(2)}, u32[]{:S(2)}) collective-permute-start(bf16[4,256,384]{2,1,0:T(8,128)(2,1)S(1)} %constant_dynamic-update-slice_fusion), channel_id=1, source_target_pairs={{0,4},{4,0},{1,5},{5,1},{2,6},{6,2},{3,7},{7,3},{8,12},{12,8},{9,1... | collective-permute-start | bytes 2359304 | tf_op jit(solution)/shard_map/ppermute | solution.py:78
  409.2 43.2 %collective-permute-start.39 = (bf16[2,208,576]{2,1,0:T(8,128)(2,1)S(1)}, bf16[2,208,576]{2,1,0:T(8,128)(2,1)S(1)}, u32[]{:S(2)}, u32[]{:S(2)}) collective-permute-start(bf16[2,208,576]{2,1,0:T(8,128)(2,1)S(1)} %pad_maximum_fusion.6), channel_id=1, source_target_pairs={{0,16},{8,24},{16,0},{24,8},{1,17},{9,25},{17,1},{25,9},{2,18},{10... | collective-permute-start | bytes 1437704 | tf_op jit(solution)/shard_map/ppermute | solution.py:78
  452.7 14.2 %collective-permute-start.42 = (bf16[8,256,384]{2,1,0:T(8,128)(2,1)S(1)}, bf16[8,256,384]{2,1,0:T(8,128)(2,1)}, u32[]{:S(2)}, u32[]{:S(2)}) collective-permute-start(bf16[8,256,384]{2,1,0:T(8,128)(2,1)S(1)} %constant_dynamic-update-slice_fusion.4), channel_id=1, source_target_pairs={{0,2},{2,0},{1,3},{3,1},{4,6},{6,4},{5,7},{7,5},{8,10},{10,8},{9,1... | collective-permute-start | bytes 4718600 | tf_op jit(solution)/shard_map/ppermute | solution.py:78
  452.8 5.0 %collective-permute-start.41 = (bf16[4,208,576]{2,1,0:T(8,128)(2,1)S(1)}, bf16[4,208,576]{2,1,0:T(8,128)(2,1)}, u32[]{:S(2)}, u32[]{:S(2)}) collective-permute-start(bf16[4,208,576]{2,1,0:T(8,128)(2,1)S(1)} %constant_dynamic-update-slice_fusion.2), channel_id=1, source_target_pairs={{0,2},{2,0},{1,3},{3,1},{4,6},{6,4},{5,7},{7,5},{8,10},{10,8},{9,1... | collective-permute-start | bytes 2875400 | tf_op jit(solution)/shard_map/ppermute | solution.py:78
  (64 other events, 775.5 us)
Sparse Core Ops, SparseCore 0:
  45.5 16.4 all-gather.7
  64.1 37.4 all-gather.9
  103.8 37.4 all-gather.11
  143.3 30.7 all-gather.13
  193.8 49.5 reduce-scatter.3
  292.6 43.1 reduce-scatter.5
  338.0 18.2 reduce-scatter.7
  358.8 56.4 all-gather.15

commit v3 on v2

--- a/solution.py
+++ b/solution.py
@@ -133,7 +133,7 @@
 def forward_kernel(where, rows, classes, ids, flags, q, spans, *rest):
     count = len(where)
     pieces = rest[:count]
-    o_low, o_full, lse, kv, vt, qm, top, total, accum, first, second, sem = rest[count:]
+    o_parts, o_first, o_second, lse, o_low, kv, vt, qm, top, total, accum, first, second, sem = rest[count:]
     length = kv.shape[0]
     tiles = length // KTILE
     copies = piece_copies(where, ids, pieces, kv, sem, rows, classes)
@@ -198,19 +198,22 @@
         ]
         lower = jnp.concatenate(outs[:2], axis=0).T
         upper = jnp.concatenate([outs[2], jnp.zeros_like(outs[2])], axis=0).T
-        o_full[pl.ds(base, QTILE), 0:128] = lower
-        o_full[pl.ds(base, QTILE), 128:256] = upper
+        o_first[pl.ds(base, QTILE), :] = lower
+        o_second[pl.ds(base, QTILE), :] = upper
         o_low[pl.ds(base, QTILE), 0:128] = lower.astype(jnp.bfloat16)
         o_low[pl.ds(base, QTILE), 128:192] = upper[:, 0:64].astype(jnp.bfloat16)
         lse[:, pl.ds(base, QTILE)] = top[...] + jnp.log(total[...])
 
-
-def backward_kernel(where, rows, classes, out_where, extra, ids, flags, q, spans, grad, o_full, lse, *rest):
+    for flip in range(GROUPS):
+        o_parts[flip ^ ids[0]] = o_low[rows * flip : rows * flip + rows, :]
+
+
+def backward_kernel(where, rows, classes, out_where, extra, ids, flags, q, spans, o_first, o_second, lse, *rest):
     count = len(where)
-    pieces = rest[:count]
-    rest = rest[count + extra :]
+    grads, pieces = rest[0], rest[1 : 1 + count]
+    rest = rest[1 + count + extra :]
     outs = rest[: len(out_where)]
-    dq, kv, kt, qm, dom, stats, dqt, dkv, low_kv, sem = rest[len(out_where) :]
+    dq, grad, kv, kt, qm, dom, stats, dqt, dkv, low_kv, sem = rest[len(out_where) :]
     length = kv.shape[0]
     tiles = length // KTILE
     copies = piece_copies(where, ids, pieces, kv, sem, rows, classes)
@@ -221,6 +224,11 @@
     def _(t):
         start = pl.multiple_of(t * KTILE, KTILE)
         dkv[pl.ds(start, KTILE), :] = jnp.zeros((KTILE, 384), jnp.float32)
+
+    for flip in range(GROUPS):
+        grad[rows * flip : rows * flip + rows, :] = jnp.concatenate(
+            [grads[flip ^ ids[0]], jnp.zeros((rows, 64), jnp.bfloat16)], axis=1
+        )
 
     for copy in copies:
         copy.wait()
@@ -244,7 +252,7 @@
         for part in range(2):
             product = (
                 grad[pl.ds(base, QTILE), 128 * part : 128 * part + 128].astype(jnp.float32)
-                * o_full[pl.ds(base, QTILE), 128 * part : 128 * part + 128]
+                * (o_first, o_second)[part][pl.ds(base, QTILE), :]
             ).T
             for half in range(2):
                 head = 2 * part + half
@@ -325,14 +333,16 @@
     return pl.pallas_call(
         functools.partial(forward_kernel, where, rows, classes),
         out_shape=(
-            jax.ShapeDtypeStruct((queries, WIDTH), jnp.bfloat16),
-            jax.ShapeDtypeStruct((queries, 256), jnp.float32),
+            jax.ShapeDtypeStruct((GROUPS, rows, WIDTH), jnp.bfloat16),
+            jax.ShapeDtypeStruct((queries, 128), jnp.float32),
+            jax.ShapeDtypeStruct((queries, 128), jnp.float32),
             jax.ShapeDtypeStruct((8, queries), jnp.float32),
         ),
         in_specs=[SMEM_SPEC, SMEM_SPEC, VMEM_SPEC, VMEM_SPEC]
         + [ANY_SPEC] * len(pieces),
-        out_specs=(VMEM_SPEC,) * 3,
+        out_specs=(VMEM_SPEC,) * 4,
         scratch_shapes=[
+            pltpu.VMEM((queries, WIDTH), jnp.bfloat16),
             pltpu.VMEM((length, 384), jnp.bfloat16),
             pltpu.VMEM((256, length), jnp.bfloat16),
             pltpu.VMEM((OWN, QTILE, 128), jnp.bfloat16),
@@ -352,7 +362,7 @@
 
 
 def attend_backward(
-    ids, flags, q, spans, grad, o_full, lse, pieces, after, where, rows, classes, out_where
+    ids, flags, q, spans, grads, outputs, lse, pieces, after, where, rows, classes, out_where
 ):
     length = rows * classes * GROUPS
     queries = q.shape[0]
@@ -364,9 +374,10 @@
             for masks in out_where
         )
         + (jax.ShapeDtypeStruct((queries, WIDTH), jnp.bfloat16),),
-        in_specs=[SMEM_SPEC, SMEM_SPEC] + [VMEM_SPEC] * 5 + [ANY_SPEC] * (len(pieces) + len(after)),
+        in_specs=[SMEM_SPEC, SMEM_SPEC] + [VMEM_SPEC] * 6 + [ANY_SPEC] * (len(pieces) + len(after)),
         out_specs=(ANY_SPEC,) * len(out_where) + (VMEM_SPEC,),
         scratch_shapes=[
+            pltpu.VMEM((queries, 256), jnp.bfloat16),
             pltpu.VMEM((length, 384), jnp.bfloat16),
             pltpu.VMEM((256, length), jnp.bfloat16),
             pltpu.VMEM((OWN, QTILE, 128), jnp.bfloat16),
@@ -382,7 +393,66 @@
             flops=queries * length * WIDTH * 10, bytes_accessed=16 << 20, transcendentals=0
         ),
         name="attend_backward",
-    )(ids, flags, q, spans, grad, o_full, lse, *pieces, *after)
+    )(ids, flags, q, spans, *outputs, lse, grads, *pieces, *after)
+
+
+def pick_kernel(ids, w_q, w_k, w_v, out):
+    odd = (ids[3] & 1) == 1
+    start = pl.multiple_of((ids[3] // 2) * 384 + (ids[3] & 1) * 128, 128)
+
+    def take(weight):
+        both = weight[:, pl.ds(start, 256)]
+        return jnp.where(odd, both[:, 64:256], both[:, 0:192])
+
+    q, k, v = take(w_q), take(w_k), take(w_v)
+    out[...] = jnp.concatenate(
+        [k[:, :128], v[:, 128:], k[:, 128:], v[:, :128], q[:, :128], jnp.zeros_like(q[:, :64]), q[:, 128:]],
+        axis=1,
+    )
+
+
+def pick_weights(ids, w_q, w_k, w_v):
+    return pl.pallas_call(
+        pick_kernel,
+        out_shape=jax.ShapeDtypeStruct((w_q.shape[0], 640), jnp.bfloat16),
+        in_specs=[SMEM_SPEC] + [VMEM_SPEC] * 3,
+        out_specs=VMEM_SPEC,
+        compiler_params=PARAMS,
+        name="pick_weights",
+    )(ids, w_q, w_k, w_v)
+
+
+def project_kernel(count, parts, ids, bias, *rest):
+    tokens, weights, (kv, q) = rest[:count], rest[count : count + parts], rest[count + parts :]
+    rows = weights[0].shape[0]
+    for i, chunk in enumerate(tokens):
+        total = bias[...]
+        for part, weight in enumerate(weights):
+            lanes = (0 if parts == 1 else ids[0] ^ part) * rows
+            left = chunk[:, pl.ds(pl.multiple_of(lanes, 128), rows)]
+            total = total + jnp.dot(left, weight[...], preferred_element_type=jnp.float32)
+        kv[i] = total[:, :384].astype(jnp.bfloat16)
+        q[chunk.shape[0] * i : chunk.shape[0] * (i + 1), :] = (
+            total[:, 384:].astype(jnp.bfloat16) * jnp.bfloat16(0.125)
+        )
+
+
+def project(ids, bias, chunks, weights):
+    count, rows = len(chunks), chunks[0].shape[0]
+    return pl.pallas_call(
+        functools.partial(project_kernel, count, len(weights)),
+        out_shape=(
+            jax.ShapeDtypeStruct((count, rows, 384), jnp.bfloat16),
+            jax.ShapeDtypeStruct((count * rows, 256), jnp.bfloat16),
+        ),
+        in_specs=[SMEM_SPEC] + [VMEM_SPEC] * (1 + count + len(weights)),
+        out_specs=(VMEM_SPEC, VMEM_SPEC),
+        compiler_params=PARAMS,
+        cost_estimate=pl.CostEstimate(
+            flops=2 * count * rows * D * 640, bytes_accessed=2 << 20, transcendentals=0
+        ),
+        name="project",
+    )(ids, bias, *chunks, *weights)
 
 
 def tn(left, right):
@@ -396,14 +466,18 @@
 
     @pl.loop(0, 8)
     def _(i):
-        part = tn(active[:, pl.ds(pl.multiple_of(i * 384, 128), 384)], g_low[...])
-        down[pl.ds(pl.multiple_of(i * 384, 16), 384), :] = part.astype(jnp.bfloat16)
+        part = tn(active[:, pl.ds(pl.multiple_of(i * 384, 128), 384)], g_low[...]).astype(jnp.bfloat16)
+        for unit in range(4):
+            for half in range(2):
+                place = (((i % 2) * 2 + unit // 2) * 2 + (i // 2) % 2) * 4 + (i // 4) * 2 + unit % 2
+                start = pl.multiple_of(place * 192, 192) + 96 * half
+                down[pl.ds(start, 96), :] = part[96 * unit : 96 * unit + 96, 384 * half : 384 * half + 384]
 
 
 def down_grad(active, g_low, after):
     return pl.pallas_call(
         functools.partial(down_grad_kernel, len(after)),
-        out_shape=jax.ShapeDtypeStruct((FF, D), jnp.bfloat16),
+        out_shape=jax.ShapeDtypeStruct((2 * FF, D // 2), jnp.bfloat16),
         in_specs=[VMEM_SPEC] * 2 + [ANY_SPEC] * len(after),
         out_specs=VMEM_SPEC,
         compiler_params=PARAMS,
@@ -414,8 +488,12 @@
     )(active, g_low, *after)
 
 
+def turn(index):
+    return (index & 1) * 2 + index // 2
+
+
 def upper_grad_kernel(extra, ids, hid, g_raised, attn, g_att, vec, *rest):
-    upper = rest[extra]
+    near, far = rest[extra:]
     x, c, m, h = ids[0], ids[1], ids[2], ids[3]
 
     @pl.loop(0, 2)
@@ -431,18 +509,23 @@
                 unit = j * 4 + k
                 part = tn(left, g_raised[:, pl.ds(pl.multiple_of(unit * 384, 128), 384)]).astype(jnp.bfloat16)
                 for b in range(2):
-                    place = (((b ^ c) * 2 + (j ^ m)) * 2 + (i ^ x)) * 4 + (k ^ h)
-                    upper[place, 0:192, :] = part[192 * b : 192 * b + 192]
-                    upper[place, 192:240, :] = outer[192 * b + 48 * k : 192 * b + 48 * k + 48]
-                    upper[place, 240:256, :] = vec[unit]
+                    place = ((j ^ m) * 2 + (i ^ x)) * 4 + turn(k ^ h)
+
+                    def store(target):
+                        target[place, 0:192, :] = part[192 * b : 192 * b + 192]
+                        target[place, 192:240, :] = outer[192 * b + 48 * k : 192 * b + 48 * k + 48]
+                        target[place, 240:256, :] = vec[unit]
+
+                    pl.when(c == b)(functools.partial(store, near))
+                    pl.when(c != b)(functools.partial(store, far))
 
 
 def upper_grad(ids, hid, g_raised, attn, g_att, vec, after):
     return pl.pallas_call(
         functools.partial(upper_grad_kernel, len(after)),
-        out_shape=jax.ShapeDtypeStruct((32, 256, 384), jnp.bfloat16),
+        out_shape=(jax.ShapeDtypeStruct((16, 256, 384), jnp.bfloat16),) * 2,
         in_specs=[SMEM_SPEC] + [VMEM_SPEC] * 5 + [ANY_SPEC] * len(after),
-        out_specs=VMEM_SPEC,
+        out_specs=(VMEM_SPEC,) * 2,
         compiler_params=PARAMS,
         cost_estimate=pl.CostEstimate(
             flops=2 * hid.shape[0] * D * (FF + D), bytes_accessed=12 << 20, transcendentals=0
@@ -451,129 +534,176 @@
     )(ids, hid, g_raised, attn, g_att, vec, *after)
 
 
-def unpack_ffn_kernel(ids, block, up, out, vec):
-    up[...] = block[0, 0:192, :].astype(jnp.float32)
-    out[...] = block[0, 192:240, :].astype(jnp.float32)
-    vec[0] = block[0, 240:256, :].astype(jnp.float32)
-
-
-def unpack_ffn(ids, pieces):
-    def source(b, u, ids):
-        j, k = u // 4, u % 4
-        return (((b ^ ids[1]) * 2 + (j ^ ids[2])) * 4 + (k ^ ids[3]), 0, 0)
-
+def unpack_ffn_kernel(ids, block_own, block_other, up, out, down, *vecs):
+    side, core, mid, group = ids[0], ids[1], ids[2], ids[3]
+    b, j = pl.program_id(0) ^ core, pl.program_id(1)
+    own = pl.program_id(0) == 0
+    for k in range(GROUPS):
+        place = turn(k ^ group)
+        part = jnp.where(own, block_own[place], block_other[place]).astype(jnp.float32)
+        up[:, 384 * k : 384 * k + 384] = part[0:192]
+        out[48 * k : 48 * k + 48, :] = part[192:240]
+        rows = pl.ds(pl.multiple_of(96 * j, 32) + 192 * k, 96)
+        down[rows, 0:384] = part[256:352]
+        down[rows, 384:768] = part[352:448]
+
+    @pl.when(b == 0)
+    def _():
+        for u in range(8):
+            place = turn((u % 4) ^ group)
+            rows = jnp.where(own, block_own[place, 240:256, :], block_other[place, 240:256, :])
+            rows = rows.astype(jnp.float32)
+            for r in range(3):
+                row = 3 * u + r
+                if row < 12:
+                    target, where, half = vecs[row // 2], 0, row % 2
+                elif row < 20:
+                    target, where, half = vecs[6], (row - 12) % 4, (row - 12) // 4
+                else:
+                    continue
+
+                @pl.when((j == u // 4) & (side == half))
+                def _():
+                    target[384 * where : 384 * where + 384] = rows[r]
+
+
+def unpack_ffn(ids, own, other):
+    def source_own(d, j, ids):
+        return (jnp.where(d == 0, j, 1) ^ ids[2], 0, 0)
+
+    def source_other(d, j, ids):
+        return (jnp.where(d == 0, 0, j) ^ ids[2], 0, 0)
+
+    sizes = [384] * 6 + [1536]
     return pl.pallas_call(
         unpack_ffn_kernel,
         out_shape=(
             jax.ShapeDtypeStruct((384, FF), jnp.float32),
             jax.ShapeDtypeStruct((384, D), jnp.float32),
-            jax.ShapeDtypeStruct((8, 16, 384), jnp.float32),
-        ),
+            jax.ShapeDtypeStruct((FF // 2, D), jnp.float32),
+        )
+        + tuple(jax.ShapeDtypeStruct((size,), jnp.float32) for size in sizes),
         grid_spec=pltpu.PrefetchScalarGridSpec(
             num_scalar_prefetch=1,
-            grid=(2, 8),
-            in_specs=[pl.BlockSpec((1, 256, 384), source)],
+            grid=(2, 2),
+            in_specs=[pl.BlockSpec((4, 448, 384), source_own), pl.BlockSpec((4, 448, 384), source_other)],
             out_specs=(
-                pl.BlockSpec((192, 384), lambda b, u, ids: (b, u)),
-                pl.BlockSpec((48, 384), lambda b, u, ids: (b * 4 + u % 4, u // 4)),
-                pl.BlockSpec((1, 16, 384), lambda b, u, ids: (u, 0, 0)),
-            ),
+                pl.BlockSpec((192, 1536), lambda d, j, ids: (d ^ ids[1], j)),
+                pl.BlockSpec((192, 384), lambda d, j, ids: (d ^ ids[1], j)),
+                pl.BlockSpec((FF // 4, D), lambda d, j, ids: (d ^ ids[1], 0)),
+            )
+            + tuple(pl.BlockSpec((size,), lambda d, j, ids: (0,)) for size in sizes),
         ),
+        compiler_params=PARAMS,
         name="unpack_ffn",
-    )(ids, pieces)
-
-
-def qkv_grad_kernel(ids, tokens, dkv, dq, out):
+    )(ids, own, other)
+
+
+def qkv_grad_kernel(ids, t0, t1, t2, t3, *rest):
+    kept, given, sent, dq, near, far, both, whole = rest
     x, c = ids[0], ids[1]
-    total = jnp.concatenate(
-        [
-            jnp.sum(dkv[...].astype(jnp.float32), axis=0, keepdims=True),
-            jnp.sum(dq[...].astype(jnp.float32), axis=0, keepdims=True),
-        ],
-        axis=1,
-    )
+    rows = dq.shape[0] // GROUPS
+    total = jnp.zeros((1, 576), jnp.float32)
+    for flip in range(GROUPS):
+        term = (
+            kept[0, flip].astype(jnp.float32)
+            + given[0, flip].astype(jnp.float32)
+            + sent[flip].astype(jnp.float32)
+        ).astype(jnp.bfloat16)
+        own = slice(rows * flip, rows * flip + rows)
+        block = jnp.concatenate([term, dq[own, :]], axis=1)
+        both[flip ^ ids[3]] = block
+        whole[own, :] = block
+        total = total + jnp.sum(block.astype(jnp.float32), axis=0, keepdims=True)
     first = lax.broadcasted_iota(jnp.int32, (16, 576), 0) == 0
     total = jnp.where(first, jnp.broadcast_to(total, (16, 576)), 0.0).astype(jnp.bfloat16)
 
     @pl.loop(0, 2)
     def _(i):
-        left = tokens[:, pl.ds(pl.multiple_of(i * 384, 128), 384)]
-        for right, low_lane, high_lane in ((dkv, 0, 384), (dq, 384, 576)):
-            part = lax.dot_general(
-                left, right[...], (((0,), (0,)), ((), ())), preferred_element_type=jnp.float32
-            ).astype(jnp.bfloat16)
-            for b in range(2):
-                out[(b ^ c) * 2 + (i ^ x), 0:192, low_lane:high_lane] = part[192 * b : 192 * b + 192]
+        lanes = pl.ds(pl.multiple_of(i * 384, 128), 384)
+        left = jnp.concatenate([t[:, lanes] for t in (t0, t1, t2, t3)], axis=0)
+        part = tn(left, whole[...]).astype(jnp.bfloat16)
         for b in range(2):
-            out[(b ^ c) * 2 + (i ^ x), 192:208, :] = total
-
-
-def qkv_grads(ids, tokens, dkv, dq):
+
+            def store(target):
+                target[i ^ x, 0:192, :] = part[192 * b : 192 * b + 192]
+
+            pl.when(c == b)(functools.partial(store, near))
+            pl.when(c != b)(functools.partial(store, far))
+        near[i ^ x, 192:208, :] = total
+        far[i ^ x, 192:208, :] = total
+
+
+def qkv_grads(ids, tokens, kept, given, sent, dq):
+    queries = dq.shape[0]
+    rows = queries // GROUPS
     return pl.pallas_call(
         qkv_grad_kernel,
-        out_shape=jax.ShapeDtypeStruct((4, 208, 576), jnp.bfloat16),
-        in_specs=[SMEM_SPEC] + [VMEM_SPEC] * 3,
-        out_specs=VMEM_SPEC,
+        out_shape=(jax.ShapeDtypeStruct((2, 208, 576), jnp.bfloat16),) * 2
+        + (jax.ShapeDtypeStruct((GROUPS, rows, 576), jnp.bfloat16),),
+        in_specs=[SMEM_SPEC] + [VMEM_SPEC] * 8,
+        out_specs=(VMEM_SPEC,) * 3,
+        scratch_shapes=[pltpu.VMEM((queries, 576), jnp.bfloat16)],
         compiler_params=PARAMS,
         cost_estimate=pl.CostEstimate(
-            flops=2 * tokens.shape[0] * D * 576, bytes_accessed=4 << 20, transcendentals=0
+            flops=2 * queries * D * 576, bytes_accessed=4 << 20, transcendentals=0
         ),
         name="qkv_grads",
-    )(ids, tokens, dkv, dq)
-
-
-def unpack_qkv_kernel(ids, pieces, out_q, out_k, out_v, vec):
+    )(ids, *tokens, kept, given, sent, dq)
+
+
+def unpack_qkv_kernel(ids, own, other, out_q, out_k, out_v, vec):
     c, h = ids[1], ids[3]
     for b in range(2):
         q, k, v = [], [], []
         for g in range(GROUPS):
-            block = pieces[(b ^ c) * 4 + (g ^ h), 0:192, :].astype(jnp.float32)
+            block = jnp.where(c == b, own[turn(g ^ h), 0:192, :], other[turn(g ^ h), 0:192, :]).astype(jnp.float32)
             k += [block[:, 0:128], block[:, 192:256]]
             v += [block[:, 256:384], block[:, 128:192]]
             q += [block[:, 384:576]]
         for out, parts in ((out_q, q), (out_k, k), (out_v, v)):
             out[192 * b : 192 * b + 192, :] = jnp.concatenate(parts, axis=1)
     for g in range(GROUPS):
-        vec[g] = pieces[c * 4 + (g ^ h), 192:208, :].astype(jnp.float32)
-
-
-def unpack_qkv(ids, pieces):
+        vec[g] = jnp.where(c == 0, own[turn(g ^ h), 192:208, :], other[turn(g ^ h), 192:208, :]).astype(jnp.float32)
+
+
+def unpack_qkv(ids, own, other):
     return pl.pallas_call(
         unpack_qkv_kernel,
         out_shape=(jax.ShapeDtypeStruct((384, D), jnp.float32),) * 3
         + (jax.ShapeDtypeStruct((GROUPS, 16, 576), jnp.float32),),
-        in_specs=[SMEM_SPEC, VMEM_SPEC],
+        in_specs=[SMEM_SPEC, VMEM_SPEC, VMEM_SPEC],
         out_specs=(VMEM_SPEC,) * 4,
         compiler_params=PARAMS,
         name="unpack_qkv",
-    )(ids, pieces)
-
-
-def token_grad_kernel(base, kv0, kv1, kv2, kv3, q0, q1, q2, q3, w_kv, w_q, out):
+    )(ids, own, other)
+
+
+def token_grad_kernel(base, both, weight, out):
     total = base[...]
-    for i, (kv, q) in enumerate(((kv0, q0), (kv1, q1), (kv2, q2), (kv3, q3))):
-        total = total + lax.dot_general(kv[...], w_kv[i], NT, preferred_element_type=jnp.float32)
-        total = total + lax.dot_general(q[...], w_q[i], NT, preferred_element_type=jnp.float32)
+    for g in range(GROUPS):
+        w = weight[:, 640 * g : 640 * g + 576]
+        total = total + lax.dot_general(both[g], w, NT, preferred_element_type=jnp.float32)
     out[...] = total
 
 
-def token_grads(base, kv, q, w_kv, w_q):
+def token_grads(base, both, weight):
     return pl.pallas_call(
         token_grad_kernel,
         out_shape=jax.ShapeDtypeStruct(base.shape, jnp.float32),
-        in_specs=[VMEM_SPEC] * 11,
+        in_specs=[VMEM_SPEC] * 3,
         out_specs=VMEM_SPEC,
         compiler_params=PARAMS,
         cost_estimate=pl.CostEstimate(
             flops=2 * base.shape[0] * D * 2304, bytes_accessed=8 << 20, transcendentals=0
         ),
         name="token_grads",
-    )(base, *kv, *q, w_kv, w_q)
-
-
-def gather_rows(weight, core):
+    )(base, both, weight)
+
+
+def gather_rows(weight, core, *others):
     half = weight.shape[0] // 2
-    part = lax.dynamic_slice_in_dim(weight, core * half, half, 0)
+    part = tie(lax.dynamic_slice_in_dim(weight, core * half, half, 0), *others)
     return lax.all_gather(part, ("wa", "c"), axis=0, tiled=True)
 
 
@@ -589,23 +719,18 @@
     return lax.optimization_barrier((array,) + others)[0]
 
 
-def halve(array, axis, bit):
-    return array[0], swap(array[1], axis, bit)
-
-
 def both_sum(near, far, *others):
     near = tie(near, *others)
     return low(widen(near) + widen(far))
 
 
+def fold(near, far, *others):
+    near = tie(near, *others)
+    return [low(widen(near[i]) + widen(far[i])) for i in range(2)]
+
+
 def double(array, axis, bit):
     return jnp.concatenate([array, swap(array, axis, bit)], axis=0)
-
-
-def reduce_rest(grad):
-    mine = lax.psum_scatter(grad, "h", scatter_dimension=0, tiled=True)
-    mine = lax.psum_scatter(mine, "m", scatter_dimension=0, tiled=True)
-    return lax.all_gather(mine, ("c", "h", "m"), axis=0, tiled=True)
 
 
 def pick_columns(weight, group):
@@ -663,93 +788,31 @@
 
     second = swap(inputs, "h", 1)
     third = swap(inputs, "h", 2)
-    w_part = pick_columns((w_query, w_key, w_value), group)
-    w_other = swap(w_part, "wa", 1) if wide == 2 else lax.all_gather(w_part, "wa", axis=0, tiled=True)
-
-    segs = segment_ids
-    segs = double(segs, "c", 1)
-    bit = 1
-    while bit < mid:
-        segs = double(segs, "m", bit)
-        bit *= 2
-    segs = double(double(segs, "h", 1), "h", 2)
+    if wide == 2:
+        w_own = pick_weights(place_ids, w_query, w_key, w_value)
+        w_other = swap(w_own, "wa", 1)
+    else:
+        w_own = None
+        w_other = lax.all_gather(
+            pick_columns((w_query, w_key, w_value), group), "wa", axis=0, tiled=True
+        )
 
     smalls = [b_query, b_value, b_out, gain_one, shift_one, b_up, b_down, gain_two, shift_two]
     joined = lax.all_gather(jnp.concatenate(smalls), "wa", axis=0)
-    second, third, w_other, segs, joined = lax.optimization_barrier(
-        (second, third, w_other, segs, joined)
-    )
+    second, third, w_other, joined = lax.optimization_barrier((second, third, w_other, joined))
     fourth = swap(third, "h", 1)
-    if wide == 2:
-        w_group = jnp.where(
-            side == 0,
-            jnp.concatenate([w_part, w_other], axis=0),
-            jnp.concatenate([w_other, w_part], axis=0),
-        )
-    else:
-        w_group = w_other
-    own_segs = segs.reshape(GROUPS, classes, count)[:, 0].reshape(-1)
-    segs = jnp.take(segs, (group * classes + kind) ^ jnp.arange(chunks), axis=0)
     full, place = [], 0
     for item in smalls:
         size = item.shape[0]
         full.append(widen(joined[:, place : place + size].reshape(-1)))
         place += size
     bias_query, bias_value, bias_out, gain_attn, shift_attn, bias_up, bias_down, gain_ffn, shift_ffn = full
-    b_group = pick_columns((bias_query, jnp.zeros_like(bias_query), bias_value), group)
-
-    w_group, w_out, w_up, w_down, w_query, w_key, w_value = lax.optimization_barrier(
-        (w_group, w_out, w_up, w_down, w_query, w_key, w_value)
-    )
-    full_out = gather_rows(w_out, core)
-    full_up = gather_rows(w_up, core)
-    full_down = gather_rows(w_down, core)
-    by_group = jnp.concatenate(
-        [
-            jnp.concatenate(
-                [
-                    w_key[:, 192 * g : 192 * g + 128],
-                    w_value[:, 192 * g + 128 : 192 * g + 192],
-                    w_key[:, 192 * g + 128 : 192 * g + 192],
-                    w_value[:, 192 * g : 192 * g + 128],
-                ],
-                axis=1,
-            )
-            for g in range(GROUPS)
-        ]
-        + [w_query],
-        axis=1,
-    )
-    by_group = gather_rows(by_group, core)
-    back_kv = jnp.take(
-        jnp.transpose(by_group[:, : 2 * D].reshape(D, GROUPS, 2 * WIDTH), (1, 0, 2)), order, axis=0
-    )
-    back_q = jnp.take(
-        jnp.transpose(by_group[:, 2 * D :].reshape(D, GROUPS, WIDTH), (1, 0, 2)), order, axis=0
-    )
-
-    names = jnp.arange(DOCS)
-    begins = jnp.sum((segs.reshape(-1, 1) < names).astype(jnp.int32), axis=0)
-    ends = jnp.sum((segs.reshape(-1, 1) <= names).astype(jnp.int32), axis=0)
-    chosen = own_segs[None, :] == names[:, None]
-    begins = jnp.sum(jnp.where(chosen, begins[:, None], 0), axis=0)
-    ends = jnp.sum(jnp.where(chosen, ends[:, None], 0), axis=0)
-    spans = jnp.concatenate(
-        [begins[None], ends[None], jnp.zeros((6, begins.shape[0]), jnp.int32)], axis=0
-    )
-    edges = (jnp.arange(tiles) * KTILE)[None, :, None]
-    meets = (begins.reshape(-1, 1, QTILE) < edges + KTILE) & (ends.reshape(-1, 1, QTILE) > edges)
-    meets = jnp.any(meets, axis=-1).astype(jnp.int32)
-    rank = jnp.cumsum(meets, axis=1)
-    slots = (rank[:, None, :] == jnp.arange(1, tiles + 1)[None, :, None]) & (meets[:, None, :] > 0)
-    listed = jnp.sum(jnp.where(slots, jnp.arange(tiles), 0), axis=-1)
-    flags = jnp.concatenate([rank[:, -1:], listed], axis=1).astype(jnp.int32).reshape(-1)
-
-    def project(parts):
-        joined = jnp.concatenate(parts, axis=0)
-        kv = low(mm(joined, w_group[:, :384]) + b_group[:384])
-        return kv.reshape(len(parts), count, 384)
-
+    b_group = pick_columns((bias_query, jnp.zeros_like(bias_query), bias_value), group)[None]
+
+    w_group = (w_own, w_other) if wide == 2 else (w_other,)
+    full_out = gather_rows(w_out, core, w_other)
+    full_up = gather_rows(w_up, core, w_other)
+    full_down = gather_rows(w_down, core, w_other)
     where, pieces = [], []
 
     def spread(piece, flips):
@@ -765,32 +828,57 @@
             where.append((mask, flips))
             pieces.append(item)
 
-    def queries(rows):
-        return low(mm(rows, w_group[:, 384:]) + b_group[384:]) * jnp.bfloat16(0.125)
-
-    first_kv = project((inputs, second, third))
+    first_kv, first_q = project(place_ids, b_group, (inputs, second, third), w_group)
     spread(first_kv, (0, 1, 2))
-    first_q = queries(tie(jnp.concatenate([inputs, second, third], axis=0), first_kv))
-    fourth, first_q, spans, flags = lax.optimization_barrier((fourth, first_q, spans, flags))
-    last_kv = project((fourth,))
+
+    segs = double(tie(segment_ids, first_kv), "c", 1)
+    bit = 1
+    while bit < mid:
+        segs = double(segs, "m", bit)
+        bit *= 2
+    segs = double(double(segs, "h", 1), "h", 2)
+    own_segs = segs.reshape(GROUPS, classes, count)[:, 0].reshape(-1)
+    segs = jnp.take(segs, (group * classes + kind) ^ jnp.arange(chunks), axis=0)
+
+    names = jnp.arange(DOCS)
+    begins = jnp.sum((segs.reshape(-1, 1) < names).astype(jnp.int32), axis=0)
+    ends = jnp.sum((segs.reshape(-1, 1) <= names).astype(jnp.int32), axis=0)
+    chosen = own_segs[None, :] == names[:, None]
+    begins = jnp.sum(jnp.where(chosen, begins[:, None], 0), axis=0)
+    ends = jnp.sum(jnp.where(chosen, ends[:, None], 0), axis=0)
+    spans = jnp.concatenate(
+        [begins[None], ends[None], jnp.zeros((6, begins.shape[0]), jnp.int32)], axis=0
+    )
+    edges = (jnp.arange(tiles) * KTILE)[None, :, None]
+    meets = (begins.reshape(-1, 1, QTILE) < edges + KTILE) & (ends.reshape(-1, 1, QTILE) > edges)
+    meets = jnp.any(meets, axis=-1).astype(jnp.int32)
+    rank = jnp.cumsum(meets, axis=1)
+    slots = (rank[:, None, :] == jnp.arange(1, tiles + 1)[None, :, None]) & (meets[:, None, :] > 0)
+    listed = jnp.sum(jnp.where(slots, jnp.arange(tiles), 0), axis=-1)
+    flags = jnp.concatenate([rank[:, -1:], listed], axis=1).astype(jnp.int32).reshape(-1)
+
+    last_kv, last_q = project(place_ids, b_group, (fourth,), w_group)
     spread(last_kv, (3,))
     where = tuple(where)
-    last_q = queries(tie(fourth, last_kv))
     q_rows = jnp.concatenate([first_q, last_q], axis=0)
-    group_tokens = jnp.concatenate([inputs, second, third, fourth], axis=0)
-
-    o_low, o_full, lse = attend_forward(
+    group_tokens = [inputs, second, third, fourth]
+
+    o_parts, o_first, o_second, lse = attend_forward(
         ids, flags, q_rows, spans, pieces, where, count, classes
     )
 
-    def send_back(rows):
-        parts = rows.reshape(GROUPS, count, -1)
-        return [parts[0]] + [swap(parts[flip], "h", flip) for flip in range(1, GROUPS)]
-
-    def in_order(parts):
-        return jnp.take(jnp.stack(parts), order, axis=0)
-
-    attn_low = jnp.transpose(in_order(send_back(o_low)), (1, 0, 2)).reshape(count, D)
+    w_query, w_key, w_value = (tie(item, lse) for item in (w_query, w_key, w_value))
+    columns = []
+    for g in range(GROUPS):
+        low_part, high_part = slice(192 * g, 192 * g + 128), slice(192 * g + 128, 192 * g + 192)
+        columns += [w_key[:, low_part], w_value[:, high_part], w_key[:, high_part], w_value[:, low_part]]
+        columns += [w_query[:, 192 * g : 192 * g + 192], jnp.zeros_like(w_query[:, :64])]
+    by_group = gather_rows(jnp.concatenate(columns, axis=1), core)
+
+    def send_back(parts):
+        return lax.all_to_all(parts, "h", 0, 0, tiled=True)
+
+    attn_low = jnp.transpose(send_back(o_parts), (1, 0, 2)).reshape(count, D)
     attended = mm(attn_low, full_out) + bias_out
     hidden, unit_one, scale_one = norm_forward(widen(inputs) + attended, gain_attn, shift_attn)
     hidden_low = low(hidden)
@@ -814,11 +902,7 @@
     grad_b_out = jnp.sum(widen(grad_attended), axis=0)
     grad_attn = low(back_product(grad_attended, full_out))
 
-    grad_parts = jnp.take(
-        jnp.transpose(grad_attn.reshape(count, GROUPS, WIDTH), (1, 0, 2)), order, axis=0
-    )
-    grad_heads = [grad_parts[0]] + [swap(grad_parts[flip], "h", flip) for flip in range(1, GROUPS)]
-    grad_rows = jnp.pad(jnp.concatenate(grad_heads, axis=0), ((0, 0), (0, 64)))
+    grad_rows = send_back(jnp.transpose(grad_attn.reshape(count, GROUPS, WIDTH), (1, 0, 2)))
 
     vectors = jnp.concatenate(
         [grad_b_out, grad_gain_one, grad_shift_one, grad_b_down, grad_gain_two, grad_shift_two, grad_b_up]
@@ -827,16 +911,18 @@
     if paired:
         vectors = jnp.pad(low(vectors), (0, 9216 - 7680)).reshape(8, 3, 384)
         vectors = jnp.pad(vectors, ((0, 0), (0, 13), (0, 0)))
-        upper = upper_grad(
-            place_ids, hidden_low, grad_raised, attn_low, grad_attended, vectors, (grad_parts, by_group)
+        near, far = upper_grad(
+            place_ids, hidden_low, grad_raised, attn_low, grad_attended, vectors, (by_group,)
         )
-        upper = upper.reshape(2, 2, 2, 2, 2, 256, 384)
-        near, far = halve(upper, "c", 1)
-        down_sum = down_grad(active_low, grad_lowered, (upper,))
-        upper = both_sum(near, far, down_sum)
-        down_sum = lax.psum_scatter(down_sum, ("wa", "c"), scatter_dimension=0, tiled=True)
-        upper_pair = halve(upper, "m", 1)
-        after = (upper,)
+        shape = (2, 2, 2, 2, 256, 384)
+        near, far = near.reshape(shape), swap(far, "c", 1).reshape(shape)
+        grad_rows = tie(grad_rows, near)
+        down_sum = down_grad(active_low, grad_lowered, (near,))
+        upper, give = fold(near, far, down_sum)
+        after = (give,)
+        give = swap(give, "m", 1)
+        down_sum = tie(down_sum, grad_rows)
+        down_sum = lax.psum_scatter(down_sum, ("h", "c"), scatter_dimension=0, tiled=True)
     else:
         grad_w_down = low(outer_sum(active_low, grad_lowered))
         grad_w_up = low(outer_sum(hidden_low, grad_raised))
@@ -860,85 +946,88 @@
         out_out = widen(ffn_sum[:, place : place + out_rows]).reshape(-1, D)
         small = widen(ffn_sum[0, place + out_rows :])
 
-    def share(row, rows):
-        vector = small[row : row + rows].reshape(-1)
-        size = vector.shape[0] // wide
-        return lax.dynamic_slice_in_dim(vector, side * size, size, 0)
-
-    keep, give = tuple(range(0, classes, 2)), tuple(range(1, classes, 2))
-    kept, given, dq = attend_backward(
-        ids, flags, q_rows, spans, grad_rows, o_full, lse,
-        pieces, after, where, count, classes, (keep, give),
-    )
-
-    given = swap(given, "c", 1)
+        def share(row, rows):
+            vector = small[row : row + rows].reshape(-1)
+            size = vector.shape[0] // wide
+            return lax.dynamic_slice_in_dim(vector, side * size, size, 0)
+
+        vectors = [share(row, 1) for row in range(6)] + [share(6, 4)]
+
+    stay_masks, leave_masks = tuple(range(0, classes, 2)), tuple(range(1, classes, 2))
+    out_where = (stay_masks,) + tuple((mask,) for mask in leave_masks)
+
+    kept, *given, dq = attend_backward(
+        ids, flags, q_rows, spans, grad_rows, (o_first, o_second), lse,
+        pieces, after, where, count, classes, out_where,
+    )
+
+    given = [swap(item, "c", 1) for item in given]
     if paired:
-        out_down = widen(reduce_rest(tie(down_sum, dq)))
-        upper = both_sum(*upper_pair, dq)
-        upper_pair = halve(upper, "wa", 1)
-        kept = tie(kept, upper)
-    partial = widen(kept) + widen(given)
-    stay = list(keep)
-    bit = mid // 2
-    while bit >= 1:
-        mask = bit << 1
-        near = [i for i, m in enumerate(stay) if not m & mask]
-        far = [i for i, m in enumerate(stay) if m & mask]
-        sent = swap(low(partial[far[0] : far[-1] + 1]), "m", bit)
-        partial = low(partial[near[0] : near[-1] + 1])
-        if paired:
-            back_q_parts = send_back(tie(dq, partial))
-            upper = both_sum(*upper_pair, partial)
-            upper_pair = halve(upper, "h", 2)
-            partial = tie(partial, upper)
-        partial = widen(partial) + widen(sent)
-        stay = [stay[i] for i in near]
-        bit //= 2
-    if not paired:
-        back_q_parts = send_back(dq)
-    dkv = low(partial[0]).reshape(GROUPS * count, 384)
-    back_kv_parts = send_back(dkv)
+        upper, give = fold(upper, give, dq)
+        kept = tie(kept, give)
+        sent = low(widen(kept[1]) + widen(given[1][0]))
+        down_sum = lax.psum_scatter(tie(down_sum, sent), "wa", scatter_dimension=0, tiled=True)
+        give = swap(give, "wa", 1)
+        upper = tie(upper, sent)
+        sent = swap(sent, "m", 1)
+        upper, give = fold(upper, give)
+        kept = tie(kept, give)
+        give = swap(give, "h", 1)
+    else:
+        partial = widen(kept) + widen(jnp.concatenate(given, axis=0))
+        stay = list(stay_masks)
+        bit = mid // 2
+        while bit >= 1:
+            mask = bit << 1
+            near = [i for i, m in enumerate(stay) if not m & mask]
+            far = [i for i, m in enumerate(stay) if m & mask]
+            sent = swap(low(partial[far[0] : far[-1] + 1]), "m", bit)
+            partial = widen(low(partial[near[0] : near[-1] + 1])) + widen(sent)
+            stay = [stay[i] for i in near]
+            bit //= 2
+        dkv = low(partial[0]).reshape(GROUPS * count, 384)
 
     part = D // wide
     if paired:
-        qkv = qkv_grads(place_ids, group_tokens, dkv, dq)
-        qkv_pair = halve(qkv.reshape(2, 2, 208, 576), "c", 1)
-        upper = both_sum(*upper_pair, qkv)
-        upper_pair = halve(upper, "h", 1)
-        qkv = both_sum(*qkv_pair, upper)
-        qkv_pair = halve(qkv, "wa", 1)
-        upper = both_sum(*upper_pair, qkv)
-        other = swap(upper, "h", 1)
-        qkv = both_sum(*qkv_pair, upper)
-        qkv_other = swap(qkv, "m", 1)
-        upper = jnp.stack([tie(upper, qkv), other])
-        other = swap(upper, "h", 2)
-        qkv = both_sum(qkv, qkv_other, upper)
-        qkv_other = swap(qkv, "h", 1)
-        upper = jnp.concatenate([tie(upper, qkv), other], axis=0)
-        other = swap(upper, "m", 1)
-        qkv = jnp.stack([tie(qkv, upper), qkv_other])
-        qkv_other = swap(qkv, "h", 2)
-        grad_inputs = token_grads(
-            tie(grad_sum_one, qkv), back_kv_parts, back_q_parts, back_kv, back_q
-        )
-        qkv = jnp.concatenate([tie(qkv, grad_inputs), qkv_other], axis=0)
-        qkv_other = swap(qkv, "c", 1)
-        upper = jnp.concatenate([tie(upper, qkv), other], axis=0)
-        other = swap(upper, "c", 1)
-        out_query, out_key, out_value, sums = unpack_qkv(
-            place_ids, jnp.concatenate([tie(qkv, upper), qkv_other], axis=0)
-        )
+        near, far, parts = qkv_grads(place_ids, group_tokens, kept, given[0], sent, dq)
+        far = swap(far, "c", 1)
+        down_sum = lax.psum_scatter(tie(down_sum, near), "m", scatter_dimension=0, tiled=True)
+        upper, give = fold(upper, give, near)
+        near = tie(near, give)
+        give = swap(give, "h", 2)
+        qkv, other = fold(near, far)
+        other = swap(other, "wa", 1)
+        upper = both_sum(upper, give, qkv)
+        joint = jnp.concatenate([upper, down_sum], axis=0)
+        joint_other = swap(joint, "h", 2)
+        qkv = both_sum(qkv, other, joint)
+        other = swap(qkv, "m", 1)
+        qkv = both_sum(qkv, other)
+        other = swap(qkv, "h", 2)
+        joint = jnp.stack([tie(joint, qkv), joint_other])
+        joint_other = swap(joint, "h", 1)
+        qkv = jnp.stack([tie(qkv, joint), other])
+        other = swap(qkv, "h", 1)
+        joint = jnp.stack([tie(joint, qkv), joint_other])
+        joint_other = swap(joint, "m", 1)
+        parts = send_back(tie(parts, joint))
+        qkv = jnp.concatenate([tie(qkv, joint), other], axis=0)
+        other = swap(qkv, "c", 1)
+        grad_inputs = token_grads(tie(grad_sum_one, qkv), parts, by_group)
+        joint = jnp.stack([tie(joint, grad_inputs), joint_other])
+        joint_other = swap(joint, "c", 1)
+        out_query, out_key, out_value, sums = unpack_qkv(place_ids, tie(qkv, joint), other)
+        joint = tie(joint, out_query)
+        joint, joint_other = (item.reshape(8, 448, 384) for item in (tie(joint, out_query), joint_other))
+        out_up, out_out, out_down, *vectors = unpack_ffn(place_ids, joint, joint_other)
         sums = sums[:, 0]
         sums_v = jnp.concatenate([sums[:, 256:384], sums[:, 128:192]], axis=1).reshape(-1)
         sums_q = sums[:, 384:576].reshape(-1)
-        upper = jnp.concatenate([tie(upper, out_query), other], axis=0)
-        out_up, out_out, small = unpack_ffn(place_ids, upper)
-        small = small[:, :3].reshape(-1)[:7680].reshape(10, D)
     else:
         both = jnp.concatenate([dkv, dq], axis=1)
         width = both.shape[1]
-        w_grad = low(outer_sum(group_tokens, both)).reshape(blocks, D // blocks, width)
+        parts = send_back(jnp.take(both.reshape(GROUPS, count, width), order, axis=0))
+        w_grad = low(outer_sum(jnp.concatenate(group_tokens, axis=0), both)).reshape(blocks, D // blocks, width)
         b_grad = low(jnp.sum(widen(both), axis=0))
         b_grad = jnp.pad(b_grad[None], ((0, 15), (0, 0)))
         qkv = jnp.concatenate([w_grad, jnp.broadcast_to(b_grad[None], (blocks, 16, width))], axis=1)
@@ -959,7 +1048,7 @@
             item.reshape(-1, D) for item in columns(every[:, :, : rows - 16])
         )
         sums_q, _, sums_v = (item[0, 0] for item in columns(every[:, :, rows - 16 : rows - 15]))
-        grad_inputs = token_grads(grad_sum_one, back_kv_parts, back_q_parts, back_kv, back_q)
+        grad_inputs = token_grads(grad_sum_one, parts, by_group)
     out_b_query = lax.dynamic_slice_in_dim(sums_q, side * part, part, 0)
     out_b_value = lax.dynamic_slice_in_dim(sums_v, side * part, part, 0)
 
@@ -974,13 +1063,13 @@
         out_down,
         out_b_query,
         out_b_value,
-        share(0, 1),
-        share(1, 1),
-        share(2, 1),
-        share(6, 4),
-        share(3, 1),
-        share(4, 1),
-        share(5, 1),
+        vectors[0],
+        vectors[1],
+        vectors[2],
+        vectors[6],
+        vectors[3],
+        vectors[4],
+        vectors[5],
     )
 
 

time: 506 us -> 441 us (0.87); the launches traced: 498 us -> 444 us
  other arithmetic: 43.2 us -> 15.4 us
  local copies, waits for them, and re-layouts: 65.4 us -> 42.1 us
  matrix products: 27.4 us -> 19 us
  waiting for transfers between devices: 141 us -> 133 us
    all_to_all x0 -> x3, starting transfers between devices: none -> 17.5 us  [send_back(): return lax.all_to_all(parts, 'h', 0, 0, tiled=True)]
    ppermute x43 -> x32, starting transfers between devices: 74.7 us -> 60.5 us  [swap(): return lax.ppermute(array, axis, [(i, i ^ bit) for i in range(size)])]
    reduce_scatter x3, waiting for transfers between devices: 14 us -> 0.03 us  [the longest x1 0.02 us: per_device(): lax.psum_scatter(tie(down_sum, near), 'm', scatter_dimension=0, tiled=True)]
    slice x18 -> x6, local copies, waits for them, and re-layouts: 16.4 us -> 3.81 us  [the longest x1 0.87 us: per_device(): w_value[:, low_part]]
    pallas_call x1 -> x4, Pallas kernels: 5.27 us -> 17.1 us  [the longest x1 7.42 us: qkv_grads(): pl.pallas_call(qkv_grad_kernel, out_shape=(jax.ShapeDtypeStruct((2, 208,...]
    concatenate x8 -> x1, other arithmetic: 12.1 us -> 0.95 us  [per_device(): joint = jnp.concatenate([upper, down_sum], axis=0)]
    gather x6 -> x0, local copies, waits for them, and re-layouts: 8.66 us -> none  [the longest x2 4.14 us: per_device(): jnp.take(jnp.transpose(by_group[:, 2 * D:].reshape(D, GROUPS, WIDTH), (1,...]
    dot_general x7 -> x3, matrix products: 21.7 us -> 13.2 us  [mm(): return jnp.dot(left, right, preferred_element_type=jnp.float32)]
  transfers between devices with their start and end apart: 51 -> 42, of which waited for: 20 -> 21; matrix products, arithmetic and copies ran while one was open for 25% -> 15% of each run, Pallas kernels for 22% -> 28%
where the time goes in v3:
time: 441 us; the launch traced here: 444 us
  waiting for transfers between devices  133 us (30%)
  Pallas kernels  131 us (30%)
  starting transfers between devices  78.7 us (18%)
  local copies, waits for them, and re-layouts  42.1 us (10%)
  matrix products  19 us (4%)
  other arithmetic  15.4 us (3%)
  between operations  15 us (3%)
  blocking collectives  9.49 us (2%)
    ppermute x32, waiting for transfers between devices, swap(): return lax.ppermute(array, axis, [(i, i ^ bit) for i in range(size)])  125 us
    ppermute x32, starting transfers between devices, swap(): return lax.ppermute(array, axis, [(i, i ^ bit) for i in range(size)])  60.5 us
    pallas_call x1, Pallas kernels, attend_backward(): pl.pallas_call(functools.partial(backward_kernel, where, rows, classes, o...  45.1 us
    pallas_call x1, Pallas kernels, attend_forward(): pl.pallas_call(functools.partial(forward_kernel, where, rows, classes), o...  30.7 us
    all_to_all x3, starting transfers between devices, send_back(): return lax.all_to_all(parts, 'h', 0, 0, tiled=True)  17.5 us
    dot_general x3, matrix products, mm(): return jnp.dot(left, right, preferred_element_type=jnp.float32)  13.2 us
    pallas_call x1, Pallas kernels, upper_grad(): pl.pallas_call(functools.partial(upper_grad_kernel, len(after)), out_shap...  12.2 us
    unnamed x113, local copies, waits for them, and re-layouts  12.1 us
  transfers between devices with their start and end apart: 42, of which 21 were waited for; matrix products, arithmetic and copies ran while one was open for 15% of the time, Pallas kernels for 28%

profile of v3, /device:TPU:0, one launch (start us, length us, event | category | flops | bytes accessed | tf_op | source)
XLA Modules:
  0.0 443.7 jit_solution(5350975952950889298)
XLA Ops:
  7.3 3.1 collective-permute-start
  10.4 2.6 collective-permute-start.1
  13.7 2.6 pick_weights.1.rest_3_.rest_1_
  19.8 9.5 %all-gather.1 = bf16[2,1,4608]{2,1,0:T(2,128)(2,1)S(1)} all-gather(bf16[1,1,4608]{2,1,0:T(2,128)(2,1)S(1)} %reshape.309), channel_id=2, replica_groups=mesh['h'=4,'m'=2,'c'=2,'wa'=2] {'wa'}, dimensions={0}, use_global_device_ids=true | all-gather | bytes 27648 | tf_op jit(solution)/shard_map/all_gather | solution.py:801
  29.3 1.7 constant_dynamic-slice_fusion.3
  32.3 2.7 collective-permute-done.1.rest_2_.t2
  36.2 2.4 constant_dynamic-slice_fusion.1
  39.6 4.2 project.2
  56.3 4.7 %collective-permute-done.6 = s32[8,320]{1,0:T(8,128)S(1)} collective-permute-done((s32[8,320]{1,0:T(8,128)S(1)}, s32[8,320]{1,0:T(8,128)S(1)}, u32[]{:S(2)}, u32[]{:S(2)}) %collective-permute-start.6) | collective-permute-done | bytes 10272 | tf_op jit(solution)/shard_map/ppermute | solution.py:78
  63.6 2.8 project.3
  70.0 3.4 collective-permute-done.11.rest_5_.rest_6_
  76.7 30.7 %attend_forward.1 = (bf16[4,320,192]{2,1,0:T(8,128)(2,1)}, f32[1280,128]{1,0:T(8,128)}, f32[1280,128]{1,0:T(8,128)}, f32[8,1280]{1,0:T(8,128)}) custom-call(s32[2]{0:T(128)} %pad_add_fusion.4.ids, s32[55]{0:T(128)} %reshape.278.flags, bf16[1280,256]{1,0:T(8,128)(2,1)} %copy-done.23, s32[8,1280]{1,0:T(8,128)} %add_add_fusion.spans, ...), custom_call_target="tpu_custom_call" | custom-call | flops 5033164800 | bytes 8388608 | tf_op jit(solution)/shard_map/attend_forward/pallas_call | solution.py:333
  107.5 2.3 copy.44
  109.7 10.3 %all-to-all-start = ((bf16[4,320,192]{1,2,0:T(8,128)(2,1)}), bf16[4,320,192]{1,2,0:T(8,128)(2,1)S(1)}, u32[]{:S(2)}, u32[]{:S(2)}) async-start(bf16[4,320,192]{1,2,0:T(8,128)(2,1)} %copy.44), calls=%async_computation | async-start | bytes 1179648 | tf_op jit(solution)/shard_map/all_to_all | solution.py:879
  123.5 3.8 concatenate.56
  128.5 7.0 %all-to-all-done = bf16[4,320,192]{1,2,0:T(8,128)(2,1)S(1)} async-done(((bf16[4,320,192]{1,2,0:T(8,128)(2,1)}), bf16[4,320,192]{1,2,0:T(8,128)(2,1)S(1)}, u32[]{:S(2)}, u32[]{:S(2)}) %all-to-all-start) | async-done | bytes 491552 | tf_op jit(solution)/shard_map/all_to_all | solution.py:879
  135.5 2.0 fusion.38
  138.2 6.4 %multiply_convert_fusion = (bf16[320,3072]{1,0:T(8,128)(2,1)}, f32[320,3072]{1,0:T(8,128)}) fusion(f32[3072]{0:T(1024)S(1)} %copy-done.25, bf16[320,768]{1,0:T(8,128)(2,1)S(1)} %fusion.17.hid, bf16[768,3072]{1,0:T(8,128)(2,1)} %all-gather.9.cloned.1.call-done), kind=kOutput, calls=%fused_computation.9 | convolution fusion | flops 1515847680 | bytes 11120640 | tf_op jit(solution)/shard_map/dot_general | solution.py:38
  144.6 4.9 %fusion.39 = (f32[320]{0:T(512)S(1)}, f32[320,768]{1,0:T(8,128)S(1)}) fusion(f32[768]{0:T(1024)S(1)} %copy-done.27, bf16[320,3072]{1,0:T(8,128)(2,1)} %get-tuple-element.208.active, bf16[3072,768]{1,0:T(8,128)(2,1)} %all-gather.11.cloned.1.call-done, f32[768]{0:T(1024)S(1)} %reshape.291, f32[768]{0:T(1024)S(1)} %reshape.290, f32[320]{0:T(512)S(1)} %add_rsqrt_fusion.1, ...), kind=kOutput, calls=%fused_computation.133 | convolution fusion | flops 1511669504 | bytes 8663808 | tf_op jit(solution)/shard_map/dot_general | solution.py:38
  152.1 2.9 fusion.40
  155.0 2.3 multiply_reduce_fusion
  160.3 3.5 all-to-all-start.1
  167.8 12.2 %upper_grad.1 = (bf16[16,256,384]{2,1,0:T(8,128)(2,1)}, bf16[16,256,384]{2,1,0:T(8,128)(2,1)}) custom-call(s32[4]{0:T(128)} %pad_add_fusion.5.ids, bf16[320,768]{1,0:T(8,128)(2,1)} %copy-done.13, bf16[320,3072]{1,0:T(8,128)(2,1)} %copy-done.16, bf16[320,768]{1,0:T(8,128)(2,1)} %copy.46.attn, bf16[320,768]{1,0:T(8,128)(2,1)} %copy-done.15, ...), custom_call_target="tpu_custom_call" | custom-call | flops 1887436800 | bytes 12582912 | tf_op jit(solution)/shard_map/upper_grad/pallas_call | solution.py:524
  180.1 8.0 %down_grad.1 = bf16[6144,384]{1,0:T(8,128)(2,1)} custom-call(bf16[320,3072]{1,0:T(8,128)(2,1)} %get-tuple-element.208.active, bf16[320,768]{1,0:T(8,128)(2,1)} %copy-done.14, bf16[2,2,2,2,256,384]{5,4,3,2,1,0:T(8,128)(2,1)} %bitcast.86), custom_call_target="tpu_custom_call" | custom-call | flops 1509949440 | bytes 8388608 | tf_op jit(solution)/shard_map/down_grad/pallas_call | solution.py:478
  190.5 2.2 copy.47.rest_0_
  192.7 3.3 collective-permute-done.14
  197.4 5.9 %collective-permute-start.15 = (bf16[2,2,2,256,384]{4,3,2,1,0:T(8,128)(2,1)S(1)}, bf16[2,2,2,256,384]{4,3,2,1,0:T(8,128)(2,1)S(1)}, u32[]{:S(2)}, u32[]{:S(2)}) collective-permute-start(bf16[2,2,2,256,384]{4,3,2,1,0:T(8,128)(2,1)S(1)} %get-tuple-element.166.rest_9_), channel_id=1, source_target_pairs={{0,4},{4,0},{1,5},{5,1},{2,6},{6,2},{3,7},{7,3},{8,12},{12,8},{9,1... | collective-permute-start | bytes 4718600 | tf_op jit(solution)/shard_map/ppermute | solution.py:78
  203.4 45.1 %attend_backward.1 = (bf16[2,4,320,384]{3,2,1,0:T(8,128)(2,1)}, bf16[1,4,320,384]{3,2,1,0:T(8,128)(2,1)}, bf16[1,4,320,384]{3,2,1,0:T(8,128)(2,1)}, bf16[1280,192]{1,0:T(8,128)(2,1)}) custom-call(s32[2]{0:T(128)} %pad_add_fusion.4.ids, s32[55]{0:T(128)} %reshape.278.flags, bf16[1280,256]{1,0:T(8,128)(2,1)} %copy-done.23, s32[8,1280]{1,0:T(8,128)} %add_add_fusion.spans, ...), custom_call_target="tpu_custom_call" | custom-call | flops 12582912000 | bytes 16777216 | tf_op jit(solution)/shard_map/attend_backward/pallas_call | solution.py:370
  248.5 8.7 %collective-permute-start.16 = (bf16[1,4,320,384]{3,2,1,0:T(8,128)(2,1)}, bf16[1,4,320,384]{3,2,1,0:T(8,128)(2,1)S(1)}, u32[]{:S(2)}, u32[]{:S(2)}) collective-permute-start(bf16[1,4,320,384]{3,2,1,0:T(8,128)(2,1)} %get-tuple-element.109), channel_id=1, source_target_pairs={{0,2},{2,0},{1,3},{3,1},{4,6},{6,4},{5,7},{7,5},{8,10},{10,8},{9,1... | collective-permute-start | bytes 2949128 | tf_op jit(solution)/shard_map/ppermute | solution.py:78
  257.7 2.3 collective-permute-done.16
  262.6 15.1 %collective-permute-done.17 = bf16[2,2,256,384]{3,2,1,0:T(8,128)(2,1)} collective-permute-done((bf16[2,2,256,384]{3,2,1,0:T(8,128)(2,1)S(1)}, bf16[2,2,256,384]{3,2,1,0:T(8,128)(2,1)}, u32[]{:S(2)}, u32[]{:S(2)}) %collective-permute-start.17) | collective-permute-done | bytes 786464 | tf_op jit(solution)/shard_map/ppermute | solution.py:78
  279.0 16.6 %collective-permute-start.20 = (bf16[2,256,384]{2,1,0:T(8,128)(2,1)S(1)}, bf16[2,256,384]{2,1,0:T(8,128)(2,1)S(1)}, u32[]{:S(2)}, u32[]{:S(2)}) collective-permute-start(bf16[2,256,384]{2,1,0:T(8,128)(2,1)S(1)} %get-tuple-element.170), channel_id=1, source_target_pairs={{0,8},{8,0},{16,24},{24,16},{1,9},{9,1},{17,25},{25,17},{2,10},{10... | collective-permute-start | bytes 1179656 | tf_op jit(solution)/shard_map/ppermute | solution.py:78
  296.6 7.4 %qkv_grads.1 = (bf16[2,208,576]{2,1,0:T(8,128)(2,1)}, bf16[2,208,576]{2,1,0:T(8,128)(2,1)}, bf16[4,320,576]{2,1,0:T(8,128)(2,1)}) custom-call(s32[4]{0:T(128)} %pad_add_fusion.5.ids, bf16[320,768]{1,0:T(8,128)(2,1)} %bitcast.102, bf16[320,768]{1,0:T(8,128)(2,1)} %copy-done.22, bf16[320,768]{1,0:T(8,128)(2,1)} %collective-permute-done.1.rest_2_.t2, ...), custom_call_target="tpu_custom_call" | custom-call | flops 1132462080 | bytes 4194304 | tf_op jit(solution)/shard_map/qkv_grads/pallas_call | solution.py:640
  307.7 9.0 %collective-permute-done.22 = bf16[256,384]{1,0:T(8,128)(2,1)S(1)} collective-permute-done((bf16[256,384]{1,0:T(8,128)(2,1)S(1)}, bf16[256,384]{1,0:T(8,128)(2,1)S(1)}, u32[]{:S(2)}, u32[]{:S(2)}) %collective-permute-start.22) | collective-permute-done | bytes 196640 | tf_op jit(solution)/shard_map/ppermute | solution.py:78
  317.8 3.5 collective-permute-start.24
  321.3 6.6 %collective-permute-done.24 = bf16[208,576]{1,0:T(8,128)(2,1)S(1)} collective-permute-done((bf16[208,576]{1,0:T(8,128)(2,1)S(1)}, bf16[208,576]{1,0:T(8,128)(2,1)S(1)}, u32[]{:S(2)}, u32[]{:S(2)}) %collective-permute-start.24) | collective-permute-done | bytes 239648 | tf_op jit(solution)/shard_map/ppermute | solution.py:78
  328.0 10.1 %collective-permute-done.25 = bf16[448,384]{1,0:T(8,128)(2,1)S(1)} collective-permute-done((bf16[448,384]{1,0:T(8,128)(2,1)S(1)}, bf16[448,384]{1,0:T(8,128)(2,1)S(1)}, u32[]{:S(2)}, u32[]{:S(2)}) %collective-permute-start.25) | collective-permute-done | bytes 344096 | tf_op jit(solution)/shard_map/ppermute | solution.py:78
  338.3 2.9 collective-permute-start.26
  341.2 17.9 %collective-permute-done.26 = bf16[208,576]{1,0:T(8,128)(2,1)S(1)} collective-permute-done((bf16[208,576]{1,0:T(8,128)(2,1)S(1)}, bf16[208,576]{1,0:T(8,128)(2,1)S(1)}, u32[]{:S(2)}, u32[]{:S(2)}) %collective-permute-start.26) | collective-permute-done | bytes 239648 | tf_op jit(solution)/shard_map/ppermute | solution.py:78
  359.2 2.1 collective-permute-done.27
  361.5 3.7 all-to-all-start.2
  365.5 2.0 collective-permute-start.28
  368.4 36.4 %collective-permute-done.28 = bf16[2,208,576]{2,1,0:T(8,128)(2,1)S(1)} collective-permute-done((bf16[2,208,576]{2,1,0:T(8,128)(2,1)S(1)}, bf16[2,208,576]{2,1,0:T(8,128)(2,1)S(1)}, u32[]{:S(2)}, u32[]{:S(2)}) %collective-permute-start.28) | collective-permute-done | bytes 479264 | tf_op jit(solution)/shard_map/ppermute | solution.py:78
  406.8 5.7 %token_grads.1 = f32[320,768]{1,0:T(8,128)} custom-call(f32[320,768]{1,0:T(8,128)} %get-tuple-element.126.base, bf16[4,320,576]{2,1,0:T(8,128)(2,1)} %copy-done.4, bf16[768,2560]{1,0:T(8,128)(2,1)} %all-gather.13.cloned.1.call-done.rest_0_.weight), custom_call_target="tpu_custom_call" | custom-call | flops 1132462080 | bytes 8388608 | tf_op jit(solution)/shard_map/token_grads/pallas_call | solution.py:691
  412.4 1.6 pad_maximum_fusion
  416.1 6.1 %collective-permute-done.30.other = bf16[4,208,576]{2,1,0:T(8,128)(2,1)} collective-permute-done((bf16[4,208,576]{2,1,0:T(8,128)(2,1)}, bf16[4,208,576]{2,1,0:T(8,128)(2,1)}, u32[]{:S(2)}, u32[]{:S(2)}) %collective-permute-start.30) | collective-permute-done | bytes 958496 | tf_op jit(solution)/shard_map/ppermute | solution.py:78
  422.2 3.8 unpack_qkv.1
  428.4 8.4 %unpack_ffn.1 = (f32[384,3072]{1,0:T(8,128)}, f32[384,768]{1,0:T(8,128)}, f32[1536,768]{1,0:T(8,128)}, f32[384]{0:T(512)}, f32[384]{0:T(512)}, /*index=5*/f32[38...) custom-call(s32[4]{0:T(128)} %pad_add_fusion.5.ids, bf16[8,448,384]{2,1,0:T(8,128)(2,1)} %bitcast.88, ...), custom_call_target="tpu_custom_call" | custom-call | tf_op jit(solution)/shard_map/unpack_ffn/pallas_call | solution.py:578
  (292 shorter events, 66.0 us)
Async XLA Ops:
  7.2 27.8 %copy-start = (bf16[384,3072]{1,0:T(8,128)(2,1)S(1)}, bf16[384,3072]{1,0:T(8,128)(2,1)}, u32[]{:S(2)}) copy-start(bf16[384,3072]{1,0:T(8,128)(2,1)} %param.25) | copy-start | bytes 7077892
  7.3 12.1 %copy-start.35 = (bf16[384]{0:T(512)(128)(2,1)S(1)}, bf16[384]{0:T(512)(128)(2,1)}, u32[]{:S(2)}) copy-start(bf16[384]{0:T(512)(128)(2,1)} %param.34) | copy-start | bytes 2308
  7.3 12.3 %copy-start.36 = (bf16[384]{0:T(512)(128)(2,1)S(1)}, bf16[384]{0:T(512)(128)(2,1)}, u32[]{:S(2)}) copy-start(bf16[384]{0:T(512)(128)(2,1)} %param.35) | copy-start | bytes 2308
  7.3 121.2 %all-gather.7.cloned.1.call-start = ((), (), s32[]{:S(2)}) async-start(), calls=%async_computation.6 | async-start | bytes 1474560 | tf_op jit(solution)/shard_map/all_gather | solution.py:707
  7.3 24.9 %collective-permute-start = (bf16[320,768]{1,0:T(8,128)(2,1)}, bf16[320,768]{1,0:T(8,128)(2,1)S(1)}, u32[]{:S(2)}, u32[]{:S(2)}) collective-permute-start(bf16[320,768]{1,0:T(8,128)(2,1)} %bitcast.99), channel_id=1, source_target_pairs={{0,8},{8,0},{16,24},{24,16},{1,9},{9,1},{17,25},{25,17},{2,10},{10... | collective-permute-start | bytes 1474568 | tf_op jit(solution)/shard_map/ppermute | solution.py:78
  10.4 24.5 %collective-permute-start.1 = (bf16[320,768]{1,0:T(8,128)(2,1)}, bf16[320,768]{1,0:T(8,128)(2,1)}, u32[]{:S(2)}, u32[]{:S(2)}) collective-permute-start(bf16[320,768]{1,0:T(8,128)(2,1)} %bitcast.100), channel_id=1, source_target_pairs={{0,16},{8,24},{16,0},{24,8},{1,17},{9,25},{17,1},{25,9},{2,18},{10... | collective-permute-start | bytes 1474568 | tf_op jit(solution)/shard_map/ppermute | solution.py:78
  16.3 18.7 %collective-permute-start.2 = (bf16[384,640]{1,0:T(8,128)(2,1)}, bf16[384,640]{1,0:T(8,128)(2,1)S(1)}, u32[]{:S(2)}, u32[]{:S(2)}) collective-permute-start(bf16[384,640]{1,0:T(8,128)(2,1)} %pick_weights.1.rest_3_.rest_1_), channel_id=1, source_target_pairs={{0,1},{1,0},{2,3},{3,2},{4,5},{5,4},{6,7},{7,6},{8,9},{9,8},{10,11... | collective-permute-start | bytes 1474568 | tf_op jit(solution)/shard_map/ppermute | solution.py:78
  35.0 103.1 %all-gather.9.cloned.1.call-start = ((), (), s32[]{:S(2)}) async-start(), calls=%async_computation.7 | async-start | bytes 5898240 | tf_op jit(solution)/shard_map/all_gather | solution.py:707
  36.1 108.4 %all-gather.11.cloned.1.call-start = ((), (), s32[]{:S(2)}) async-start(), calls=%async_computation.8 | async-start | bytes 5898240 | tf_op jit(solution)/shard_map/all_gather | solution.py:707
  43.8 1.2 collective-permute-start.3
  45.0 3.7 collective-permute-start.4
  48.6 3.8 collective-permute-start.5
  49.1 13.7 %collective-permute-start.7 = (bf16[320,768]{1,0:T(8,128)(2,1)}, bf16[320,768]{1,0:T(8,128)(2,1)S(1)}, u32[]{:S(2)}, u32[]{:S(2)}) collective-permute-start(bf16[320,768]{1,0:T(8,128)(2,1)} %collective-permute-done.1.rest_2_.t2), channel_id=1, source_target_pairs={{0,8},{8,0},{16,24},{24,16},{1,9},{9,1},{17,25},{25,17},{2,10},{10... | collective-permute-start | bytes 1474568 | tf_op jit(solution)/shard_map/ppermute | solution.py:78
  50.7 18.1 %collective-permute-start.8 = (bf16[3,320,384]{2,1,0:T(8,128)(2,1)}, bf16[3,320,384]{2,1,0:T(8,128)(2,1)S(1)}, u32[]{:S(2)}, u32[]{:S(2)}) collective-permute-start(bf16[3,320,384]{2,1,0:T(8,128)(2,1)} %get-tuple-element.86.rest_0_.rest_1_), channel_id=1, source_target_pairs={{0,4},{4,0},{1,5},{5,1},{2,6},{6,2},{3,7},{7,3},{8,12},{12,8},{9,1... | collective-permute-start | bytes 2211848 | tf_op jit(solution)/shard_map/ppermute | solution.py:78
  52.2 23.2 %collective-permute-start.9 = (bf16[3,320,384]{2,1,0:T(8,128)(2,1)}, bf16[3,320,384]{2,1,0:T(8,128)(2,1)S(1)}, u32[]{:S(2)}, u32[]{:S(2)}) collective-permute-start(bf16[3,320,384]{2,1,0:T(8,128)(2,1)} %get-tuple-element.86.rest_0_.rest_1_), channel_id=1, source_target_pairs={{0,2},{2,0},{1,3},{3,1},{4,6},{6,4},{5,7},{7,5},{8,10},{10,8},{9,1... | collective-permute-start | bytes 2211848 | tf_op jit(solution)/shard_map/ppermute | solution.py:78
  52.4 8.6 %collective-permute-start.6 = (s32[8,320]{1,0:T(8,128)S(1)}, s32[8,320]{1,0:T(8,128)S(1)}, u32[]{:S(2)}, u32[]{:S(2)}) collective-permute-start(s32[8,320]{1,0:T(8,128)S(1)} %pad_add_fusion), channel_id=1, source_target_pairs={{0,16},{8,24},{16,0},{24,8},{1,17},{9,25},{17,1},{25,9},{2,18},{10... | collective-permute-start | bytes 30728 | tf_op jit(solution)/shard_map/ppermute | solution.py:78
  66.4 7.0 %collective-permute-start.11 = (bf16[1,320,384]{2,1,0:T(8,128)(2,1)}, bf16[1,320,384]{2,1,0:T(8,128)(2,1)S(1)}, u32[]{:S(2)}, u32[]{:S(2)}) collective-permute-start(bf16[1,320,384]{2,1,0:T(8,128)(2,1)} %get-tuple-element.90.rest_4_.rest_5_), channel_id=1, source_target_pairs={{0,4},{4,0},{1,5},{5,1},{2,6},{6,2},{3,7},{7,3},{8,12},{12,8},{9,1... | collective-permute-start | bytes 737288 | tf_op jit(solution)/shard_map/ppermute | solution.py:78
  68.8 6.6 %collective-permute-start.10 = (bf16[3,320,384]{2,1,0:T(8,128)(2,1)S(1)}, bf16[3,320,384]{2,1,0:T(8,128)(2,1)}, u32[]{:S(2)}, u32[]{:S(2)}) collective-permute-start(bf16[3,320,384]{2,1,0:T(8,128)(2,1)S(1)} %collective-permute-done.8.rest_1_.rest_2_), channel_id=1, source_target_pairs={{0,2},{2,0},{1,3},{3,1},{4,6},{6,4},{5,7},{7,5},{8,10},{10,8},{9,1... | collective-permute-start | bytes 2211848 | tf_op jit(solution)/shard_map/ppermute | solution.py:78
  69.6 5.8 %collective-permute-start.12 = (bf16[1,320,384]{2,1,0:T(8,128)(2,1)}, bf16[1,320,384]{2,1,0:T(8,128)(2,1)S(1)}, u32[]{:S(2)}, u32[]{:S(2)}) collective-permute-start(bf16[1,320,384]{2,1,0:T(8,128)(2,1)} %get-tuple-element.90.rest_4_.rest_5_), channel_id=1, source_target_pairs={{0,2},{2,0},{1,3},{3,1},{4,6},{6,4},{5,7},{7,5},{8,10},{10,8},{9,1... | collective-permute-start | bytes 737288 | tf_op jit(solution)/shard_map/ppermute | solution.py:78
  73.5 2.0 collective-permute-start.13
  107.4 12.6 %copy-start.9 = (bf16[384,768]{1,0:T(8,128)(2,1)S(1)}, bf16[384,768]{1,0:T(8,128)(2,1)}, u32[]{:S(2)}) copy-start(bf16[384,768]{1,0:T(8,128)(2,1)} %w_k.1) | copy-start | bytes 1769476
  107.5 14.2 %copy-start.10 = (bf16[384,768]{1,0:T(8,128)(2,1)S(1)}, bf16[384,768]{1,0:T(8,128)(2,1)}, u32[]{:S(2)}) copy-start(bf16[384,768]{1,0:T(8,128)(2,1)} %w_v.1) | copy-start | bytes 1769476
  109.7 13.6 %copy-start.11 = (bf16[384,768]{1,0:T(8,128)(2,1)S(1)}, bf16[384,768]{1,0:T(8,128)(2,1)}, u32[]{:S(2)}) copy-start(bf16[384,768]{1,0:T(8,128)(2,1)} %w_q.1) | copy-start | bytes 1769476
  109.7 25.8 %all-to-all-start = ((bf16[4,320,192]{1,2,0:T(8,128)(2,1)}), bf16[4,320,192]{1,2,0:T(8,128)(2,1)S(1)}, u32[]{:S(2)}, u32[]{:S(2)}) async-start(bf16[4,320,192]{1,2,0:T(8,128)(2,1)} %copy.44), calls=%async_computation | async-start | bytes 1179648 | tf_op jit(solution)/shard_map/all_to_all | solution.py:879
  120.0 47.8 %all-gather.13.cloned.1.call-start = ((), (), s32[]{:S(2)}) async-start(), calls=%async_computation.9 | async-start | bytes 4915200 | tf_op jit(solution)/shard_map/all_gather | solution.py:707
  160.3 27.8 %all-to-all-start.1 = ((bf16[4,320,192]{1,2,0:T(8,128)(2,1)}), bf16[4,320,192]{1,2,0:T(8,128)(2,1)S(1)}, u32[]{:S(2)}, u32[]{:S(2)}) async-start(bf16[4,320,192]{1,2,0:T(8,128)(2,1)} %bitcast.12), calls=%async_computation.1 | async-start | bytes 1179648 | tf_op jit(solution)/shard_map/all_to_all | solution.py:879
  163.8 98.5 %reduce-scatter.4.cloned.1.call-start = ((), (), s32[]{:S(2)}) async-start(), calls=%async_computation.10 | async-start | bytes 5308416 | tf_op jit(solution)/shard_map/reduce_scatter | solution.py:925
  188.1 116.0 %reduce-scatter.6.cloned.1.call-start = ((), (), s32[]{:S(2)}) async-start(), calls=%async_computation.11 | async-start | bytes 884736 | tf_op jit(solution)/shard_map/reduce_scatter | solution.py:969
  188.9 7.1 %collective-permute-start.14 = (bf16[16,256,384]{2,1,0:T(8,128)(2,1)}, bf16[16,256,384]{2,1,0:T(8,128)(2,1)S(1)}, u32[]{:S(2)}, u32[]{:S(2)}) collective-permute-start(bf16[16,256,384]{2,1,0:T(8,128)(2,1)} %get-tuple-element.104), channel_id=1, source_target_pairs={{0,2},{2,0},{1,3},{3,1},{4,6},{6,4},{5,7},{7,5},{8,10},{10,8},{9,1... | collective-permute-start | bytes 9437192 | tf_op jit(solution)/shard_map/ppermute | solution.py:78
  197.4 59.8 %collective-permute-start.15 = (bf16[2,2,2,256,384]{4,3,2,1,0:T(8,128)(2,1)S(1)}, bf16[2,2,2,256,384]{4,3,2,1,0:T(8,128)(2,1)S(1)}, u32[]{:S(2)}, u32[]{:S(2)}) collective-permute-start(bf16[2,2,2,256,384]{4,3,2,1,0:T(8,128)(2,1)S(1)} %get-tuple-element.166.rest_9_), channel_id=1, source_target_pairs={{0,4},{4,0},{1,5},{5,1},{2,6},{6,2},{3,7},{7,3},{8,12},{12,8},{9,1... | collective-permute-start | bytes 4718600 | tf_op jit(solution)/shard_map/ppermute | solution.py:78
  248.5 11.6 %collective-permute-start.16 = (bf16[1,4,320,384]{3,2,1,0:T(8,128)(2,1)}, bf16[1,4,320,384]{3,2,1,0:T(8,128)(2,1)S(1)}, u32[]{:S(2)}, u32[]{:S(2)}) collective-permute-start(bf16[1,4,320,384]{3,2,1,0:T(8,128)(2,1)} %get-tuple-element.109), channel_id=1, source_target_pairs={{0,2},{2,0},{1,3},{3,1},{4,6},{6,4},{5,7},{7,5},{8,10},{10,8},{9,1... | collective-permute-start | bytes 2949128 | tf_op jit(solution)/shard_map/ppermute | solution.py:78
  257.2 38.5 %collective-permute-start.18 = (bf16[1,4,320,384]{3,2,1,0:T(8,128)(2,1)}, bf16[1,4,320,384]{3,2,1,0:T(8,128)(2,1)}, u32[]{:S(2)}, u32[]{:S(2)}) collective-permute-start(bf16[1,4,320,384]{3,2,1,0:T(8,128)(2,1)} %get-tuple-element.112), channel_id=1, source_target_pairs={{0,2},{2,0},{1,3},{3,1},{4,6},{6,4},{5,7},{7,5},{8,10},{10,8},{9,1... | collective-permute-start | bytes 2949128 | tf_op jit(solution)/shard_map/ppermute | solution.py:78
  257.7 20.1 %collective-permute-start.17 = (bf16[2,2,256,384]{3,2,1,0:T(8,128)(2,1)S(1)}, bf16[2,2,256,384]{3,2,1,0:T(8,128)(2,1)}, u32[]{:S(2)}, u32[]{:S(2)}) collective-permute-start(bf16[2,2,256,384]{3,2,1,0:T(8,128)(2,1)S(1)} %get-tuple-element.164), channel_id=1, source_target_pairs={{0,1},{1,0},{2,3},{3,2},{4,5},{5,4},{6,7},{7,6},{8,9},{9,8},{10,11... | collective-permute-start | bytes 2359304 | tf_op jit(solution)/shard_map/ppermute | solution.py:78
  261.3 34.4 %collective-permute-start.19 = (bf16[4,320,384]{2,1,0:T(8,128)(2,1)}, bf16[4,320,384]{2,1,0:T(8,128)(2,1)S(1)}, u32[]{:S(2)}, u32[]{:S(2)}) collective-permute-start(bf16[4,320,384]{2,1,0:T(8,128)(2,1)} %fusion.16), channel_id=1, source_target_pairs={{0,4},{4,0},{1,5},{5,1},{2,6},{6,2},{3,7},{7,3},{8,12},{12,8},{9,1... | collective-permute-start | bytes 2949128 | tf_op jit(solution)/shard_map/ppermute | solution.py:78
  262.3 54.4 %reduce-scatter.8.cloned.1.call-start = ((), (), s32[]{:S(2)}) async-start(), calls=%async_computation.12 | async-start | bytes 442368 | tf_op jit(solution)/shard_map/reduce_scatter | solution.py:994
  279.0 25.5 %collective-permute-start.20 = (bf16[2,256,384]{2,1,0:T(8,128)(2,1)S(1)}, bf16[2,256,384]{2,1,0:T(8,128)(2,1)S(1)}, u32[]{:S(2)}, u32[]{:S(2)}) collective-permute-start(bf16[2,256,384]{2,1,0:T(8,128)(2,1)S(1)} %get-tuple-element.170), channel_id=1, source_target_pairs={{0,8},{8,0},{16,24},{24,16},{1,9},{9,1},{17,25},{25,17},{2,10},{10... | collective-permute-start | bytes 1179656 | tf_op jit(solution)/shard_map/ppermute | solution.py:78
  304.0 2.1 collective-permute-start.21
  304.6 12.1 %collective-permute-start.22 = (bf16[256,384]{1,0:T(8,128)(2,1)S(1)}, bf16[256,384]{1,0:T(8,128)(2,1)S(1)}, u32[]{:S(2)}, u32[]{:S(2)}) collective-permute-start(bf16[256,384]{1,0:T(8,128)(2,1)S(1)} %get-tuple-element.175), channel_id=1, source_target_pairs={{0,16},{8,24},{16,0},{24,8},{1,17},{9,25},{17,1},{25,9},{2,18},{10... | collective-permute-start | bytes 589832 | tf_op jit(solution)/shard_map/ppermute | solution.py:78
  307.3 10.4 %collective-permute-start.23 = (bf16[208,576]{1,0:T(8,128)(2,1)S(1)}, bf16[208,576]{1,0:T(8,128)(2,1)S(1)}, u32[]{:S(2)}, u32[]{:S(2)}) collective-permute-start(bf16[208,576]{1,0:T(8,128)(2,1)S(1)} %get-tuple-element.172), channel_id=1, source_target_pairs={{0,1},{1,0},{2,3},{3,2},{4,5},{5,4},{6,7},{7,6},{8,9},{9,8},{10,11... | collective-permute-start | bytes 718856 | tf_op jit(solution)/shard_map/ppermute | solution.py:78
  317.8 10.1 %collective-permute-start.24 = (bf16[208,576]{1,0:T(8,128)(2,1)S(1)}, bf16[208,576]{1,0:T(8,128)(2,1)S(1)}, u32[]{:S(2)}, u32[]{:S(2)}) collective-permute-start(bf16[208,576]{1,0:T(8,128)(2,1)S(1)} %add_convert_fusion.7), channel_id=1, source_target_pairs={{0,4},{4,0},{1,5},{5,1},{2,6},{6,2},{3,7},{7,3},{8,12},{12,8},{9,1... | collective-permute-start | bytes 718856 | tf_op jit(solution)/shard_map/ppermute | solution.py:78
  321.3 16.8 %collective-permute-start.25 = (bf16[448,384]{1,0:T(8,128)(2,1)S(1)}, bf16[448,384]{1,0:T(8,128)(2,1)S(1)}, u32[]{:S(2)}, u32[]{:S(2)}) collective-permute-start(bf16[448,384]{1,0:T(8,128)(2,1)S(1)} %pad_maximum_fusion.4), channel_id=1, source_target_pairs={{0,16},{8,24},{16,0},{24,8},{1,17},{9,25},{17,1},{25,9},{2,18},{10... | collective-permute-start | bytes 1032200 | tf_op jit(solution)/shard_map/ppermute | solution.py:78
  338.2 23.1 %collective-permute-start.27 = (bf16[2,448,384]{2,1,0:T(8,128)(2,1)S(1)}, bf16[2,448,384]{2,1,0:T(8,128)(2,1)S(1)}, u32[]{:S(2)}, u32[]{:S(2)}) collective-permute-start(bf16[2,448,384]{2,1,0:T(8,128)(2,1)S(1)} %pad_maximum_fusion.2), channel_id=1, source_target_pairs={{0,8},{8,0},{16,24},{24,16},{1,9},{9,1},{17,25},{25,17},{2,10},{10... | collective-permute-start | bytes 2064392 | tf_op jit(solution)/shard_map/ppermute | solution.py:78
  338.3 20.9 %collective-permute-start.26 = (bf16[208,576]{1,0:T(8,128)(2,1)S(1)}, bf16[208,576]{1,0:T(8,128)(2,1)S(1)}, u32[]{:S(2)}, u32[]{:S(2)}) collective-permute-start(bf16[208,576]{1,0:T(8,128)(2,1)S(1)} %add_convert_fusion.6), channel_id=1, source_target_pairs={{0,16},{8,24},{16,0},{24,8},{1,17},{9,25},{17,1},{25,9},{2,18},{10... | collective-permute-start | bytes 718856 | tf_op jit(solution)/shard_map/ppermute | solution.py:78
  361.5 44.1 %all-to-all-start.2 = ((bf16[4,320,576]{2,1,0:T(8,128)(2,1)}), bf16[4,320,576]{2,1,0:T(8,128)(2,1)S(1)}, u32[]{:S(2)}, u32[]{:S(2)}) async-start(bf16[4,320,576]{2,1,0:T(8,128)(2,1)} %get-tuple-element.128), calls=%async_computation.5 | async-start | bytes 3276800 | tf_op jit(solution)/shard_map/all_to_all | solution.py:879
  365.1 47.3 %collective-permute-start.29 = (bf16[2,2,448,384]{3,2,1,0:T(8,128)(2,1)S(1)}, bf16[2,2,448,384]{3,2,1,0:T(8,128)(2,1)}, u32[]{:S(2)}, u32[]{:S(2)}) collective-permute-start(bf16[2,2,448,384]{3,2,1,0:T(8,128)(2,1)S(1)} %pad_maximum_fusion.1), channel_id=1, source_target_pairs={{0,4},{4,0},{1,5},{5,1},{2,6},{6,2},{3,7},{7,3},{8,12},{12,8},{9,1... | collective-permute-start | bytes 4128776 | tf_op jit(solution)/shard_map/ppermute | solution.py:78
  365.5 39.2 %collective-permute-start.28 = (bf16[2,208,576]{2,1,0:T(8,128)(2,1)S(1)}, bf16[2,208,576]{2,1,0:T(8,128)(2,1)S(1)}, u32[]{:S(2)}, u32[]{:S(2)}) collective-permute-start(bf16[2,208,576]{2,1,0:T(8,128)(2,1)S(1)} %pad_maximum_fusion.3), channel_id=1, source_target_pairs={{0,8},{8,0},{16,24},{24,16},{1,9},{9,1},{17,25},{25,17},{2,10},{10... | collective-permute-start | bytes 1437704 | tf_op jit(solution)/shard_map/ppermute | solution.py:78
  415.6 12.8 %collective-permute-start.31 = (bf16[2,2,2,448,384]{4,3,2,1,0:T(8,128)(2,1)S(1)}, bf16[2,2,2,448,384]{4,3,2,1,0:T(8,128)(2,1)}, u32[]{:S(2)}, u32[]{:S(2)}) collective-permute-start(bf16[2,2,2,448,384]{4,3,2,1,0:T(8,128)(2,1)S(1)} %pad_maximum_fusion), channel_id=1, source_target_pairs={{0,2},{2,0},{1,3},{3,1},{4,6},{6,4},{5,7},{7,5},{8,10},{10,8},{9,1... | collective-permute-start | bytes 8257544 | tf_op jit(solution)/shard_map/ppermute | solution.py:78
  415.6 6.6 %collective-permute-start.30 = (bf16[4,208,576]{2,1,0:T(8,128)(2,1)}, bf16[4,208,576]{2,1,0:T(8,128)(2,1)}, u32[]{:S(2)}, u32[]{:S(2)}) collective-permute-start(bf16[4,208,576]{2,1,0:T(8,128)(2,1)} %constant_dynamic-update-slice_fusion.2.own), channel_id=1, source_target_pairs={{0,2},{2,0},{1,3},{3,1},{4,6},{6,4},{5,7},{7,5},{8,10},{10,8},{9,1... | collective-permute-start | bytes 2875400 | tf_op jit(solution)/shard_map/ppermute | solution.py:78
  (41 other events, 205.6 us)
Sparse Core Ops, SparseCore 0:
  35.1 17.5 all-gather.6
  54.8 38.2 all-gather.8
  95.2 37.4 all-gather.10
  134.7 33.0 all-gather.12
  188.2 60.8 reduce-scatter.3
  262.4 24.3 reduce-scatter.5
  304.2 12.3 reduce-scatter.7

commit v4 on v3

--- a/solution.py
+++ b/solution.py
@@ -104,6 +104,13 @@
     return copies
 
 
+def order_queries(ids, first_q, last_q, q, rows):
+    for flip in range(GROUPS):
+        part, place = (last_q, 0) if flip == 3 else (first_q, rows * flip)
+        start = pl.multiple_of((ids[0] ^ flip) * rows, 64)
+        q[pl.ds(start, rows), :] = part[place : place + rows, :]
+
+
 def allowed(spans, base, start):
     position = lax.broadcasted_iota(jnp.int32, (KTILE, QTILE), 0)
     first = spans[0:1, pl.ds(base, QTILE)] - start
@@ -130,15 +137,18 @@
         work(1, *there)
 
 
-def forward_kernel(where, rows, classes, ids, flags, q, spans, *rest):
+def forward_kernel(where, rows, classes, ids, flags, first_q, last_q, spans, *rest):
     count = len(where)
     pieces = rest[:count]
-    o_parts, o_first, o_second, lse, o_low, kv, vt, qm, top, total, accum, first, second, sem = rest[count:]
+    o_parts, o_first, o_second, lse, q, o_low, kv, vt, qm, top, total, accum, first, second, sem = rest[
+        count:
+    ]
     length = kv.shape[0]
     tiles = length // KTILE
     copies = piece_copies(where, ids, pieces, kv, sem, rows, classes)
     for copy in copies:
         copy.start()
+    order_queries(ids, first_q, last_q, q, rows)
     for copy in copies:
         copy.wait()
 
@@ -204,16 +214,16 @@
         o_low[pl.ds(base, QTILE), 128:192] = upper[:, 0:64].astype(jnp.bfloat16)
         lse[:, pl.ds(base, QTILE)] = top[...] + jnp.log(total[...])
 
-    for flip in range(GROUPS):
-        o_parts[flip ^ ids[0]] = o_low[rows * flip : rows * flip + rows, :]
-
-
-def backward_kernel(where, rows, classes, out_where, extra, ids, flags, q, spans, o_first, o_second, lse, *rest):
+    for chunk in range(GROUPS):
+        o_parts[chunk] = o_low[rows * chunk : rows * chunk + rows, :]
+
+
+def backward_kernel(where, rows, classes, out_where, extra, ids, flags, first_q, last_q, spans, o_first, o_second, lse, *rest):
     count = len(where)
     grads, pieces = rest[0], rest[1 : 1 + count]
     rest = rest[1 + count + extra :]
     outs = rest[: len(out_where)]
-    dq, grad, kv, kt, qm, dom, stats, dqt, dkv, low_kv, sem = rest[len(out_where) :]
+    dq, q, grad, kv, kt, qm, dom, stats, dqt, dkv, low_kv, sem = rest[len(out_where) :]
     length = kv.shape[0]
     tiles = length // KTILE
     copies = piece_copies(where, ids, pieces, kv, sem, rows, classes)
@@ -225,9 +235,10 @@
         start = pl.multiple_of(t * KTILE, KTILE)
         dkv[pl.ds(start, KTILE), :] = jnp.zeros((KTILE, 384), jnp.float32)
 
-    for flip in range(GROUPS):
-        grad[rows * flip : rows * flip + rows, :] = jnp.concatenate(
-            [grads[flip ^ ids[0]], jnp.zeros((rows, 64), jnp.bfloat16)], axis=1
+    order_queries(ids, first_q, last_q, q, rows)
+    for chunk in range(GROUPS):
+        grad[rows * chunk : rows * chunk + rows, :] = jnp.concatenate(
+            [grads[chunk], jnp.zeros((rows, 64), jnp.bfloat16)], axis=1
         )
 
     for copy in copies:
@@ -326,9 +337,9 @@
 PARAMS = pltpu.CompilerParams(vmem_limit_bytes=56 * 1024 * 1024)
 
 
-def attend_forward(ids, flags, q, spans, pieces, where, rows, classes):
+def attend_forward(ids, flags, first_q, last_q, spans, pieces, where, rows, classes):
     length = rows * classes * GROUPS
-    queries = q.shape[0]
+    queries = GROUPS * rows
     copies = sum(len(flips) for _, flips in where)
     return pl.pallas_call(
         functools.partial(forward_kernel, where, rows, classes),
@@ -338,10 +349,11 @@
             jax.ShapeDtypeStruct((queries, 128), jnp.float32),
             jax.ShapeDtypeStruct((8, queries), jnp.float32),
         ),
-        in_specs=[SMEM_SPEC, SMEM_SPEC, VMEM_SPEC, VMEM_SPEC]
+        in_specs=[SMEM_SPEC, SMEM_SPEC, VMEM_SPEC, VMEM_SPEC, VMEM_SPEC]
         + [ANY_SPEC] * len(pieces),
         out_specs=(VMEM_SPEC,) * 4,
         scratch_shapes=[
+            pltpu.VMEM((queries, 256), jnp.bfloat16),
             pltpu.VMEM((queries, WIDTH), jnp.bfloat16),
             pltpu.VMEM((length, 384), jnp.bfloat16),
             pltpu.VMEM((256, length), jnp.bfloat16),
@@ -358,14 +370,14 @@
             flops=queries * length * WIDTH * 4, bytes_accessed=8 << 20, transcendentals=0
         ),
         name="attend_forward",
-    )(ids, flags, q, spans, *pieces)
+    )(ids, flags, first_q, last_q, spans, *pieces)
 
 
 def attend_backward(
-    ids, flags, q, spans, grads, outputs, lse, pieces, after, where, rows, classes, out_where
+    ids, flags, first_q, last_q, spans, grads, outputs, lse, pieces, after, where, rows, classes, out_where
 ):
     length = rows * classes * GROUPS
-    queries = q.shape[0]
+    queries = GROUPS * rows
     copies = sum(len(flips) for _, flips in where)
     return pl.pallas_call(
         functools.partial(backward_kernel, where, rows, classes, out_where, len(after)),
@@ -374,9 +386,10 @@
             for masks in out_where
         )
         + (jax.ShapeDtypeStruct((queries, WIDTH), jnp.bfloat16),),
-        in_specs=[SMEM_SPEC, SMEM_SPEC] + [VMEM_SPEC] * 6 + [ANY_SPEC] * (len(pieces) + len(after)),
+        in_specs=[SMEM_SPEC, SMEM_SPEC] + [VMEM_SPEC] * 7 + [ANY_SPEC] * (len(pieces) + len(after)),
         out_specs=(ANY_SPEC,) * len(out_where) + (VMEM_SPEC,),
         scratch_shapes=[
+            pltpu.VMEM((queries, 256), jnp.bfloat16),
             pltpu.VMEM((queries, 256), jnp.bfloat16),
             pltpu.VMEM((length, 384), jnp.bfloat16),
             pltpu.VMEM((256, length), jnp.bfloat16),
@@ -393,7 +406,7 @@
             flops=queries * length * WIDTH * 10, bytes_accessed=16 << 20, transcendentals=0
         ),
         name="attend_backward",
-    )(ids, flags, q, spans, *outputs, lse, grads, *pieces, *after)
+    )(ids, flags, first_q, last_q, spans, *outputs, lse, grads, *pieces, *after)
 
 
 def pick_kernel(ids, w_q, w_k, w_v, out):
@@ -461,77 +474,84 @@
     )
 
 
-def down_grad_kernel(extra, active, g_low, *rest):
-    down = rest[extra]
-
-    @pl.loop(0, 8)
-    def _(i):
-        part = tn(active[:, pl.ds(pl.multiple_of(i * 384, 128), 384)], g_low[...]).astype(jnp.bfloat16)
-        for unit in range(4):
-            for half in range(2):
-                place = (((i % 2) * 2 + unit // 2) * 2 + (i // 2) % 2) * 4 + (i // 4) * 2 + unit % 2
-                start = pl.multiple_of(place * 192, 192) + 96 * half
-                down[pl.ds(start, 96), :] = part[96 * unit : 96 * unit + 96, 384 * half : 384 * half + 384]
+def down_grad_kernel(active, g_low, after, down):
+    part = tn(active[...], g_low[...]).astype(jnp.bfloat16)
+    for unit in range(4):
+        for half in range(2):
+            row = (unit % 2) * 192 + 96 * half
+            down[unit // 2, 0, row : row + 96, :] = part[
+                96 * unit : 96 * unit + 96, 384 * half : 384 * half + 384
+            ]
 
 
 def down_grad(active, g_low, after):
+    rows = active.shape[0]
     return pl.pallas_call(
-        functools.partial(down_grad_kernel, len(after)),
-        out_shape=jax.ShapeDtypeStruct((2 * FF, D // 2), jnp.bfloat16),
-        in_specs=[VMEM_SPEC] * 2 + [ANY_SPEC] * len(after),
-        out_specs=VMEM_SPEC,
+        down_grad_kernel,
+        out_shape=jax.ShapeDtypeStruct((4, 4, 384, 384), jnp.bfloat16),
+        grid=(8,),
+        in_specs=[
+            pl.BlockSpec((rows, 384), lambda i: (0, i)),
+            pl.BlockSpec((rows, D), lambda i: (0, 0)),
+            ANY_SPEC,
+        ],
+        out_specs=pl.BlockSpec((2, 1, 384, 384), lambda i: (i % 2, (i // 2) % 2 * 2 + i // 4, 0, 0)),
         compiler_params=PARAMS,
         cost_estimate=pl.CostEstimate(
-            flops=2 * active.shape[0] * D * FF, bytes_accessed=8 << 20, transcendentals=0
+            flops=2 * rows * D * FF, bytes_accessed=8 << 20, transcendentals=0
         ),
         name="down_grad",
-    )(active, g_low, *after)
+    )(active, g_low, after).reshape(2 * FF, D // 2)
 
 
 def turn(index):
     return (index & 1) * 2 + index // 2
 
 
-def upper_grad_kernel(extra, ids, hid, g_raised, attn, g_att, vec, *rest):
-    near, far = rest[extra:]
-    x, c, m, h = ids[0], ids[1], ids[2], ids[3]
-
-    @pl.loop(0, 2)
-    def _(i):
-        left = hid[:, pl.ds(pl.multiple_of(i * 384, 128), 384)]
-        attn_left = attn[:, pl.ds(pl.multiple_of(i * 384, 128), 384)]
-
-        @pl.loop(0, 2)
-        def _(j):
-            outer = tn(attn_left, g_att[:, pl.ds(pl.multiple_of(j * 384, 128), 384)]).astype(jnp.bfloat16)
-
-            for k in range(4):
-                unit = j * 4 + k
-                part = tn(left, g_raised[:, pl.ds(pl.multiple_of(unit * 384, 128), 384)]).astype(jnp.bfloat16)
-                for b in range(2):
-                    place = ((j ^ m) * 2 + (i ^ x)) * 4 + turn(k ^ h)
-
-                    def store(target):
-                        target[place, 0:192, :] = part[192 * b : 192 * b + 192]
-                        target[place, 192:240, :] = outer[192 * b + 48 * k : 192 * b + 48 * k + 48]
-                        target[place, 240:256, :] = vec[unit]
-
-                    pl.when(c == b)(functools.partial(store, near))
-                    pl.when(c != b)(functools.partial(store, far))
+def upper_grad_kernel(ids, hid, g_raised, attn, g_att, vec, after, near, far):
+    core, group = ids[1], ids[3]
+    outer = tn(attn[...], g_att[...]).astype(jnp.bfloat16)
+    left = hid[...].T
+    for k in range(GROUPS):
+        lanes = slice(384 * k, 384 * k + 384)
+        part = jnp.dot(left, g_raised[:, lanes], preferred_element_type=jnp.float32)
+        part = part.astype(jnp.bfloat16)
+        place = turn(k ^ group)
+        for target, own in ((near, core == 0), (far, core != 0)):
+            target[place, 0:192, :] = jnp.where(own, part[:192], part[192:])
+            first, second = (outer[192 * b + 48 * k : 192 * b + 48 * k + 48] for b in range(2))
+            target[place, 192:240, :] = jnp.where(own, first, second)
+            target[place, 240:256, :] = vec[k]
 
 
 def upper_grad(ids, hid, g_raised, attn, g_att, vec, after):
+    rows = hid.shape[0]
+
+    def place(i, j, ids):
+        return ((j ^ ids[2]) * 2 + (i ^ ids[0]), 0, 0)
+
     return pl.pallas_call(
-        functools.partial(upper_grad_kernel, len(after)),
+        upper_grad_kernel,
         out_shape=(jax.ShapeDtypeStruct((16, 256, 384), jnp.bfloat16),) * 2,
-        in_specs=[SMEM_SPEC] + [VMEM_SPEC] * 5 + [ANY_SPEC] * len(after),
-        out_specs=(VMEM_SPEC,) * 2,
+        grid_spec=pltpu.PrefetchScalarGridSpec(
+            num_scalar_prefetch=1,
+            grid=(2, 2),
+            in_specs=[
+                pl.BlockSpec((rows, 384), lambda i, j, ids: (0, i)),
+                pl.BlockSpec((rows, 1536), lambda i, j, ids: (0, j)),
+                pl.BlockSpec((rows, 384), lambda i, j, ids: (0, i)),
+                pl.BlockSpec((rows, 384), lambda i, j, ids: (0, j)),
+                pl.BlockSpec((4, 16, 384), lambda i, j, ids: (j, 0, 0)),
+                ANY_SPEC,
+            ],
+            out_specs=(pl.BlockSpec((4, 256, 384), place),) * 2,
+        ),
         compiler_params=PARAMS,
         cost_estimate=pl.CostEstimate(
-            flops=2 * hid.shape[0] * D * (FF + D), bytes_accessed=12 << 20, transcendentals=0
+            flops=2 * rows * D * (FF + D), bytes_accessed=12 << 20, transcendentals=0
         ),
         name="upper_grad",
-    )(ids, hid, g_raised, attn, g_att, vec, *after)
+    )(ids, hid, g_raised, attn, g_att, vec, after)
 
 
 def unpack_ffn_kernel(ids, block_own, block_other, up, out, down, *vecs):
@@ -611,7 +631,8 @@
             + sent[flip].astype(jnp.float32)
         ).astype(jnp.bfloat16)
         own = slice(rows * flip, rows * flip + rows)
-        block = jnp.concatenate([term, dq[own, :]], axis=1)
+        start = pl.multiple_of((flip ^ ids[3]) * rows, 64)
+        block = jnp.concatenate([term, dq[pl.ds(start, rows), :]], axis=1)
         both[flip ^ ids[3]] = block
         whole[own, :] = block
         total = total + jnp.sum(block.astype(jnp.float32), axis=0, keepdims=True)
@@ -837,8 +858,11 @@
         segs = double(segs, "m", bit)
         bit *= 2
     segs = double(double(segs, "h", 1), "h", 2)
-    own_segs = segs.reshape(GROUPS, classes, count)[:, 0].reshape(-1)
     segs = jnp.take(segs, (group * classes + kind) ^ jnp.arange(chunks), axis=0)
+
+    own_segs = lax.dynamic_index_in_dim(
+        segs.reshape(GROUPS, classes, count), kind, 1, keepdims=False
+    ).reshape(-1)
 
     names = jnp.arange(DOCS)
     begins = jnp.sum((segs.reshape(-1, 1) < names).astype(jnp.int32), axis=0)
@@ -860,11 +884,10 @@
     last_kv, last_q = project(place_ids, b_group, (fourth,), w_group)
     spread(last_kv, (3,))
     where = tuple(where)
-    q_rows = jnp.concatenate([first_q, last_q], axis=0)
     group_tokens = [inputs, second, third, fourth]
 
     o_parts, o_first, o_second, lse = attend_forward(
-        ids, flags, q_rows, spans, pieces, where, count, classes
+        ids, flags, first_q, last_q, spans, pieces, where, count, classes
     )
 
     w_query, w_key, w_value = (tie(item, lse) for item in (w_query, w_key, w_value))
@@ -912,12 +935,12 @@
         vectors = jnp.pad(low(vectors), (0, 9216 - 7680)).reshape(8, 3, 384)
         vectors = jnp.pad(vectors, ((0, 0), (0, 13), (0, 0)))
         near, far = upper_grad(
-            place_ids, hidden_low, grad_raised, attn_low, grad_attended, vectors, (by_group,)
+            place_ids, hidden_low, grad_raised, attn_low, grad_attended, vectors, by_group
         )
         shape = (2, 2, 2, 2, 256, 384)
         near, far = near.reshape(shape), swap(far, "c", 1).reshape(shape)
         grad_rows = tie(grad_rows, near)
-        down_sum = down_grad(active_low, grad_lowered, (near,))
+        down_sum = down_grad(active_low, grad_lowered, near)
         upper, give = fold(near, far, down_sum)
         after = (give,)
         give = swap(give, "m", 1)
@@ -957,7 +980,7 @@
     out_where = (stay_masks,) + tuple((mask,) for mask in leave_masks)
 
     kept, *given, dq = attend_backward(
-        ids, flags, q_rows, spans, grad_rows, (o_first, o_second), lse,
+        ids, flags, first_q, last_q, spans, grad_rows, (o_first, o_second), lse,
         pieces, after, where, count, classes, out_where,
     )
 
@@ -1024,6 +1047,7 @@
         sums_v = jnp.concatenate([sums[:, 256:384], sums[:, 128:192]], axis=1).reshape(-1)
         sums_q = sums[:, 384:576].reshape(-1)
     else:
+        dq = jnp.take(dq.reshape(GROUPS, count, WIDTH), order, axis=0).reshape(-1, WIDTH)
         both = jnp.concatenate([dkv, dq], axis=1)
         width = both.shape[1]
         parts = send_back(jnp.take(both.reshape(GROUPS, count, width), order, axis=0))

time: 441 us -> 422 us (0.957)
  starting transfers between devices: 78.7 us -> 49 us
  waiting for transfers between devices: 133 us -> 138 us
    ppermute x32, starting transfers between devices: 60.5 us -> 37.3 us  [swap(): return lax.ppermute(array, axis, [(i, i ^ bit) for i in range(size)])]
    all_to_all x3, starting transfers between devices: 17.5 us -> 11 us  [send_back(): return lax.all_to_all(parts, 'h', 0, 0, tiled=True)]
    unnamed x113 -> x112, local copies, waits for them, and re-layouts: 12.1 us -> 10.8 us
  transfers between devices with their start and end apart: 42 -> 42, of which waited for: 21 -> 22; matrix products, arithmetic and copies ran while one was open for 15% -> 16% of each run, Pallas kernels for 28% -> 30%
where the time goes in v4:
time: 422 us; the launch traced here: 421 us
  waiting for transfers between devices  138 us (33%)
  Pallas kernels  134 us (32%)
  starting transfers between devices  49 us (12%)
  local copies, waits for them, and re-layouts  39.9 us (9%)
  matrix products  19.6 us (5%)
  other arithmetic  15.5 us (4%)
  between operations  15 us (4%)
  blocking collectives  9.49 us (2%)
    ppermute x32, waiting for transfers between devices, swap(): return lax.ppermute(array, axis, [(i, i ^ bit) for i in range(size)])  129 us
    pallas_call x1, Pallas kernels, attend_backward(): pl.pallas_call(functools.partial(backward_kernel, where, rows, classes, o...  48.9 us
    ppermute x32, starting transfers between devices, swap(): return lax.ppermute(array, axis, [(i, i ^ bit) for i in range(size)])  37.3 us
    pallas_call x1, Pallas kernels, attend_forward(): pl.pallas_call(functools.partial(forward_kernel, where, rows, classes), o...  33.8 us
    dot_general x3, matrix products, mm(): return jnp.dot(left, right, preferred_element_type=jnp.float32)  13.8 us
    all_to_all x3, starting transfers between devices, send_back(): return lax.all_to_all(parts, 'h', 0, 0, tiled=True)  11 us
    unnamed x112, local copies, waits for them, and re-layouts  10.8 us
    all_gather x1, blocking collectives, per_device(): joined = lax.all_gather(jnp.concatenate(smalls), 'wa', axis=0)  9.49 us
  transfers between devices with their start and end apart: 42, of which 22 were waited for; matrix products, arithmetic and copies ran while one was open for 16% of the time, Pallas kernels for 30%

profile of v4, /device:TPU:0, one launch (start us, length us, event | category | flops | bytes accessed | tf_op | source)
XLA Modules:
  0.0 420.6 jit_solution(16718363914761494092)
XLA Ops:
  7.3 3.1 collective-permute-start
  10.4 2.6 collective-permute-start.1
  13.7 2.6 pick_weights.1.rest_3_.rest_1_
  19.8 9.5 %all-gather.1 = bf16[2,1,4608]{2,1,0:T(2,128)(2,1)S(1)} all-gather(bf16[1,1,4608]{2,1,0:T(2,128)(2,1)S(1)} %reshape.317), channel_id=2, replica_groups=mesh['h'=4,'m'=2,'c'=2,'wa'=2] {'wa'}, dimensions={0}, use_global_device_ids=true | all-gather | bytes 27648 | tf_op jit(solution)/shard_map/all_gather | solution.py:822
  29.3 1.7 constant_dynamic-slice_fusion.3
  32.3 2.7 collective-permute-done.1.rest_2_.t2
  36.2 2.4 constant_dynamic-slice_fusion.1
  39.6 4.3 %project.2 = (bf16[3,320,384]{2,1,0:T(8,128)(2,1)}, bf16[960,256]{1,0:T(8,128)(2,1)}) custom-call(s32[4]{0:T(128)} %pad_add_fusion.5.ids, f32[1,640]{1,0:T(1,128)} %broadcast_in_dim.85.bias, bf16[320,768]{1,0:T(8,128)(2,1)} %bitcast.103, bf16[320,768]{1,0:T(8,128)(2,1)} %copy-done.22, bf16[320,768]{1,0:T(8,128)(2,1)} %collective-permute-done.1.rest_2_.t2, ...), custom_call_target="tpu_custom_call" | custom-call | flops 943718400 | bytes 2097152 | tf_op jit(solution)/shard_map/project/pallas_call | solution.py:455
  53.5 2.0 collective-permute-start.7
  58.9 6.6 %collective-permute-done.7.rest_0_.t3 = bf16[320,768]{1,0:T(8,128)(2,1)S(1)} collective-permute-done((bf16[320,768]{1,0:T(8,128)(2,1)}, bf16[320,768]{1,0:T(8,128)(2,1)S(1)}, u32[]{:S(2)}, u32[]{:S(2)}) %collective-permute-start.7) | collective-permute-done | bytes 491552 | tf_op jit(solution)/shard_map/ppermute | solution.py:78
  66.3 2.7 project.3
  72.3 3.2 collective-permute-done.11.rest_5_.rest_6_
  78.0 33.8 %attend_forward.1 = (bf16[4,320,192]{2,1,0:T(8,128)(2,1)}, f32[1280,128]{1,0:T(8,128)}, f32[1280,128]{1,0:T(8,128)}, f32[8,1280]{1,0:T(8,128)}) custom-call(s32[2]{0:T(128)} %pad_add_fusion.4.ids, s32[55]{0:T(128)} %reshape.285.flags, bf16[960,256]{1,0:T(8,128)(2,1)} %get-tuple-element.88.first_q, bf16[320,256]{1,0:T(8,128)(2,1)} %get-tuple-element.89.last_q, ...), custom_call_target="tpu_custom_call" | custom-call | flops 5033164800 | bytes 8388608 | tf_op jit(solution)/shard_map/attend_forward/pallas_call | solution.py:344
  111.8 2.3 copy.44
  114.1 3.6 all-to-all-start
  121.5 3.8 concatenate.52
  126.4 3.4 all-to-all-done
  129.8 2.0 fusion.39
  132.5 6.4 %multiply_convert_fusion = (bf16[320,3072]{1,0:T(8,128)(2,1)}, f32[320,3072]{1,0:T(8,128)}) fusion(f32[3072]{0:T(1024)S(1)} %copy-done.24, bf16[320,768]{1,0:T(8,128)(2,1)S(1)} %fusion.17.hid, bf16[768,3072]{1,0:T(8,128)(2,1)} %all-gather.9.cloned.1.call-done), kind=kOutput, calls=%fused_computation.9 | convolution fusion | flops 1515847680 | bytes 11120640 | tf_op jit(solution)/shard_map/dot_general | solution.py:38
  138.9 5.5 %fusion.40 = (f32[320]{0:T(512)S(1)}, f32[320,768]{1,0:T(8,128)S(1)}) fusion(f32[768]{0:T(1024)S(1)} %copy-done.26, bf16[320,3072]{1,0:T(8,128)(2,1)} %get-tuple-element.208.active, bf16[3072,768]{1,0:T(8,128)(2,1)} %all-gather.11.cloned.1.call-done, f32[768]{0:T(1024)S(1)} %reshape.299, f32[768]{0:T(1024)S(1)} %reshape.298, f32[320]{0:T(512)S(1)} %add_rsqrt_fusion.1, ...), kind=kOutput, calls=%fused_computation.135 | convolution fusion | flops 1511669504 | bytes 8663808 | tf_op jit(solution)/shard_map/dot_general | solution.py:38
  146.9 2.9 fusion.41
  149.9 2.3 multiply_reduce_fusion
  155.1 3.5 all-to-all-start.1
  162.1 4.8 %all-gather.13.cloned.1.call-done.after.weight = bf16[768,2560]{1,0:T(8,128)(2,1)} async-done(((bf16[192,2560]{1,0:T(8,128)(2,1)}), bf16[768,2560]{1,0:T(8,128)(2,1)}) %all-gather.13.cloned.1.call-update) | async-done | bytes 3932176 | tf_op jit(solution)/shard_map/all_gather | solution.py:728
  167.0 8.6 %upper_grad.1 = (bf16[16,256,384]{2,1,0:T(8,128)(2,1)}, bf16[16,256,384]{2,1,0:T(8,128)(2,1)}) custom-call(s32[4]{0:T(128)} %pad_add_fusion.5.ids, bf16[320,768]{1,0:T(8,128)(2,1)} %copy-done.13, bf16[320,3072]{1,0:T(8,128)(2,1)} %copy-done.16, bf16[320,768]{1,0:T(8,128)(2,1)} %copy.46.attn, bf16[320,768]{1,0:T(8,128)(2,1)} %copy-done.15, ...), custom_call_target="tpu_custom_call" | custom-call | flops 1887436800 | bytes 12582912 | tf_op jit(solution)/shard_map/upper_grad/pallas_call | solution.py:533
  175.6 8.2 %down_grad.1 = bf16[4,4,384,384]{3,2,1,0:T(8,128)(2,1)} custom-call(bf16[320,3072]{1,0:T(8,128)(2,1)} %get-tuple-element.208.active, bf16[320,768]{1,0:T(8,128)(2,1)} %copy-done.14, bf16[2,2,2,2,256,384]{5,4,3,2,1,0:T(8,128)(2,1)} %bitcast.88), custom_call_target="tpu_custom_call" | custom-call | flops 1509949440 | bytes 8388608 | tf_op jit(solution)/shard_map/down_grad/pallas_call | solution.py:489
  184.9 2.2 copy.47.rest_0_
  187.1 3.4 collective-permute-done.14
  193.5 48.9 %attend_backward.1 = (bf16[2,4,320,384]{3,2,1,0:T(8,128)(2,1)}, bf16[1,4,320,384]{3,2,1,0:T(8,128)(2,1)}, bf16[1,4,320,384]{3,2,1,0:T(8,128)(2,1)}, bf16[1280,192]{1,0:T(8,128)(2,1)}) custom-call(s32[2]{0:T(128)} %pad_add_fusion.4.ids, s32[55]{0:T(128)} %reshape.285.flags, bf16[960,256]{1,0:T(8,128)(2,1)} %get-tuple-element.88.first_q, ...), custom_call_target="tpu_custom_call" | custom-call | flops 12582912000 | bytes 16777216 | tf_op jit(solution)/shard_map/attend_backward/pallas_call | solution.py:382
  243.9 1.7 collective-permute-done.16
  246.9 3.6 collective-permute-start.19
  250.5 18.4 %collective-permute-done.17 = bf16[2,2,256,384]{3,2,1,0:T(8,128)(2,1)} collective-permute-done((bf16[2,2,256,384]{3,2,1,0:T(8,128)(2,1)S(1)}, bf16[2,2,256,384]{3,2,1,0:T(8,128)(2,1)}, u32[]{:S(2)}, u32[]{:S(2)}) %collective-permute-start.17) | collective-permute-done | bytes 786464 | tf_op jit(solution)/shard_map/ppermute | solution.py:78
  273.6 7.4 %qkv_grads.1 = (bf16[2,208,576]{2,1,0:T(8,128)(2,1)}, bf16[2,208,576]{2,1,0:T(8,128)(2,1)}, bf16[4,320,576]{2,1,0:T(8,128)(2,1)}) custom-call(s32[4]{0:T(128)} %pad_add_fusion.5.ids, bf16[320,768]{1,0:T(8,128)(2,1)} %bitcast.104, bf16[320,768]{1,0:T(8,128)(2,1)} %copy-done.22, bf16[320,768]{1,0:T(8,128)(2,1)} %collective-permute-done.1.rest_2_.t2, ...), custom_call_target="tpu_custom_call" | custom-call | flops 1132462080 | bytes 4194304 | tf_op jit(solution)/shard_map/qkv_grads/pallas_call | solution.py:661
  281.2 2.5 collective-permute-start.22
  285.6 8.1 %collective-permute-done.22 = bf16[256,384]{1,0:T(8,128)(2,1)S(1)} collective-permute-done((bf16[256,384]{1,0:T(8,128)(2,1)S(1)}, bf16[256,384]{1,0:T(8,128)(2,1)S(1)}, u32[]{:S(2)}, u32[]{:S(2)}) %collective-permute-start.22) | collective-permute-done | bytes 196640 | tf_op jit(solution)/shard_map/ppermute | solution.py:78
  295.2 2.7 collective-permute-start.24
  298.5 6.0 %collective-permute-done.24 = bf16[208,576]{1,0:T(8,128)(2,1)S(1)} collective-permute-done((bf16[208,576]{1,0:T(8,128)(2,1)S(1)}, bf16[208,576]{1,0:T(8,128)(2,1)S(1)}, u32[]{:S(2)}, u32[]{:S(2)}) %collective-permute-start.24) | collective-permute-done | bytes 239648 | tf_op jit(solution)/shard_map/ppermute | solution.py:78
  304.6 10.1 %collective-permute-done.25 = bf16[448,384]{1,0:T(8,128)(2,1)S(1)} collective-permute-done((bf16[448,384]{1,0:T(8,128)(2,1)S(1)}, bf16[448,384]{1,0:T(8,128)(2,1)S(1)}, u32[]{:S(2)}, u32[]{:S(2)}) %collective-permute-start.25) | collective-permute-done | bytes 344096 | tf_op jit(solution)/shard_map/ppermute | solution.py:78
  314.9 2.9 collective-permute-start.26
  317.8 17.9 %collective-permute-done.26 = bf16[208,576]{1,0:T(8,128)(2,1)S(1)} collective-permute-done((bf16[208,576]{1,0:T(8,128)(2,1)S(1)}, bf16[208,576]{1,0:T(8,128)(2,1)S(1)}, u32[]{:S(2)}, u32[]{:S(2)}) %collective-permute-start.26) | collective-permute-done | bytes 239648 | tf_op jit(solution)/shard_map/ppermute | solution.py:78
  335.8 2.1 collective-permute-done.27
  338.1 3.9 all-to-all-start.2
  343.4 2.0 collective-permute-start.28
  346.2 35.4 %collective-permute-done.28 = bf16[2,208,576]{2,1,0:T(8,128)(2,1)S(1)} collective-permute-done((bf16[2,208,576]{2,1,0:T(8,128)(2,1)S(1)}, bf16[2,208,576]{2,1,0:T(8,128)(2,1)S(1)}, u32[]{:S(2)}, u32[]{:S(2)}) %collective-permute-start.28) | collective-permute-done | bytes 479264 | tf_op jit(solution)/shard_map/ppermute | solution.py:78
  383.7 5.6 %token_grads.1 = f32[320,768]{1,0:T(8,128)} custom-call(f32[320,768]{1,0:T(8,128)} %get-tuple-element.126.base, bf16[4,320,576]{2,1,0:T(8,128)(2,1)} %copy-done.4, bf16[768,2560]{1,0:T(8,128)(2,1)} %all-gather.13.cloned.1.call-done.after.weight), custom_call_target="tpu_custom_call" | custom-call | flops 1132462080 | bytes 8388608 | tf_op jit(solution)/shard_map/token_grads/pallas_call | solution.py:712
  393.0 6.1 %collective-permute-done.30.other = bf16[4,208,576]{2,1,0:T(8,128)(2,1)} collective-permute-done((bf16[4,208,576]{2,1,0:T(8,128)(2,1)}, bf16[4,208,576]{2,1,0:T(8,128)(2,1)}, u32[]{:S(2)}, u32[]{:S(2)}) %collective-permute-start.30) | collective-permute-done | bytes 958496 | tf_op jit(solution)/shard_map/ppermute | solution.py:78
  399.1 3.8 unpack_qkv.1
  405.3 8.4 %unpack_ffn.1 = (f32[384,3072]{1,0:T(8,128)}, f32[384,768]{1,0:T(8,128)}, f32[1536,768]{1,0:T(8,128)}, f32[384]{0:T(512)}, f32[384]{0:T(512)}, /*index=5*/f32[38...) custom-call(s32[4]{0:T(128)} %pad_add_fusion.5.ids, bf16[8,448,384]{2,1,0:T(8,128)(2,1)} %bitcast.90, ...), custom_call_target="tpu_custom_call" | custom-call | tf_op jit(solution)/shard_map/unpack_ffn/pallas_call | solution.py:598
  (292 shorter events, 67.9 us)
Async XLA Ops:
  7.2 27.8 %copy-start = (bf16[384,3072]{1,0:T(8,128)(2,1)S(1)}, bf16[384,3072]{1,0:T(8,128)(2,1)}, u32[]{:S(2)}) copy-start(bf16[384,3072]{1,0:T(8,128)(2,1)} %param.25) | copy-start | bytes 7077892
  7.2 11.4 %copy-start.32 = (bf16[384]{0:T(512)(128)(2,1)S(1)}, bf16[384]{0:T(512)(128)(2,1)}, u32[]{:S(2)}) copy-start(bf16[384]{0:T(512)(128)(2,1)} %param.31) | copy-start | bytes 2308
  7.3 11.6 %copy-start.25 = (bf16[1536]{0:T(1024)(128)(2,1)S(1)}, bf16[1536]{0:T(1024)(128)(2,1)}, u32[]{:S(2)}) copy-start(bf16[1536]{0:T(1024)(128)(2,1)} %param.32) | copy-start | bytes 9220
  7.3 11.8 %copy-start.33 = (bf16[384]{0:T(512)(128)(2,1)S(1)}, bf16[384]{0:T(512)(128)(2,1)}, u32[]{:S(2)}) copy-start(bf16[384]{0:T(512)(128)(2,1)} %param.33) | copy-start | bytes 2308
  7.3 12.1 %copy-start.34 = (bf16[384]{0:T(512)(128)(2,1)S(1)}, bf16[384]{0:T(512)(128)(2,1)}, u32[]{:S(2)}) copy-start(bf16[384]{0:T(512)(128)(2,1)} %param.34) | copy-start | bytes 2308
  7.3 12.3 %copy-start.35 = (bf16[384]{0:T(512)(128)(2,1)S(1)}, bf16[384]{0:T(512)(128)(2,1)}, u32[]{:S(2)}) copy-start(bf16[384]{0:T(512)(128)(2,1)} %param.35) | copy-start | bytes 2308
  7.3 119.1 %all-gather.7.cloned.1.call-start = ((), (), s32[]{:S(2)}) async-start(), calls=%async_computation.6 | async-start | bytes 1474560 | tf_op jit(solution)/shard_map/all_gather | solution.py:728
  7.3 24.9 %collective-permute-start = (bf16[320,768]{1,0:T(8,128)(2,1)}, bf16[320,768]{1,0:T(8,128)(2,1)S(1)}, u32[]{:S(2)}, u32[]{:S(2)}) collective-permute-start(bf16[320,768]{1,0:T(8,128)(2,1)} %bitcast.101), channel_id=1, source_target_pairs={{0,8},{8,0},{16,24},{24,16},{1,9},{9,1},{17,25},{25,17},{2,10},{10... | collective-permute-start | bytes 1474568 | tf_op jit(solution)/shard_map/ppermute | solution.py:78
  10.4 24.5 %collective-permute-start.1 = (bf16[320,768]{1,0:T(8,128)(2,1)}, bf16[320,768]{1,0:T(8,128)(2,1)}, u32[]{:S(2)}, u32[]{:S(2)}) collective-permute-start(bf16[320,768]{1,0:T(8,128)(2,1)} %bitcast.102), channel_id=1, source_target_pairs={{0,16},{8,24},{16,0},{24,8},{1,17},{9,25},{17,1},{25,9},{2,18},{10... | collective-permute-start | bytes 1474568 | tf_op jit(solution)/shard_map/ppermute | solution.py:78
  16.3 18.7 %collective-permute-start.2 = (bf16[384,640]{1,0:T(8,128)(2,1)}, bf16[384,640]{1,0:T(8,128)(2,1)S(1)}, u32[]{:S(2)}, u32[]{:S(2)}) collective-permute-start(bf16[384,640]{1,0:T(8,128)(2,1)} %pick_weights.1.rest_3_.rest_1_), channel_id=1, source_target_pairs={{0,1},{1,0},{2,3},{3,2},{4,5},{5,4},{6,7},{7,6},{8,9},{9,8},{10,11... | collective-permute-start | bytes 1474568 | tf_op jit(solution)/shard_map/ppermute | solution.py:78
  35.0 97.4 %all-gather.9.cloned.1.call-start = ((), (), s32[]{:S(2)}) async-start(), calls=%async_computation.7 | async-start | bytes 5898240 | tf_op jit(solution)/shard_map/all_gather | solution.py:728
  36.1 102.7 %all-gather.11.cloned.1.call-start = ((), (), s32[]{:S(2)}) async-start(), calls=%async_computation.8 | async-start | bytes 5898240 | tf_op jit(solution)/shard_map/all_gather | solution.py:728
  43.8 1.2 collective-permute-start.3
  45.0 3.7 collective-permute-start.4
  48.7 3.7 collective-permute-start.5
  49.3 21.3 %collective-permute-start.8 = (bf16[3,320,384]{2,1,0:T(8,128)(2,1)}, bf16[3,320,384]{2,1,0:T(8,128)(2,1)S(1)}, u32[]{:S(2)}, u32[]{:S(2)}) collective-permute-start(bf16[3,320,384]{2,1,0:T(8,128)(2,1)} %get-tuple-element.86.rest_0_.rest_1_), channel_id=1, source_target_pairs={{0,4},{4,0},{1,5},{5,1},{2,6},{6,2},{3,7},{7,3},{8,12},{12,8},{9,1... | collective-permute-start | bytes 2211848 | tf_op jit(solution)/shard_map/ppermute | solution.py:78
  52.4 4.9 %collective-permute-start.6 = (s32[8,320]{1,0:T(8,128)S(1)}, s32[8,320]{1,0:T(8,128)S(1)}, u32[]{:S(2)}, u32[]{:S(2)}) collective-permute-start(s32[8,320]{1,0:T(8,128)S(1)} %pad_add_fusion), channel_id=1, source_target_pairs={{0,16},{8,24},{16,0},{24,8},{1,17},{9,25},{17,1},{25,9},{2,18},{10... | collective-permute-start | bytes 30728 | tf_op jit(solution)/shard_map/ppermute | solution.py:78
  53.5 12.1 %collective-permute-start.7 = (bf16[320,768]{1,0:T(8,128)(2,1)}, bf16[320,768]{1,0:T(8,128)(2,1)S(1)}, u32[]{:S(2)}, u32[]{:S(2)}) collective-permute-start(bf16[320,768]{1,0:T(8,128)(2,1)} %collective-permute-done.1.rest_2_.t2), channel_id=1, source_target_pairs={{0,8},{8,0},{16,24},{24,16},{1,9},{9,1},{17,25},{25,17},{2,10},{10... | collective-permute-start | bytes 1474568 | tf_op jit(solution)/shard_map/ppermute | solution.py:78
  55.4 20.8 %collective-permute-start.9 = (bf16[3,320,384]{2,1,0:T(8,128)(2,1)}, bf16[3,320,384]{2,1,0:T(8,128)(2,1)S(1)}, u32[]{:S(2)}, u32[]{:S(2)}) collective-permute-start(bf16[3,320,384]{2,1,0:T(8,128)(2,1)} %get-tuple-element.86.rest_0_.rest_1_), channel_id=1, source_target_pairs={{0,2},{2,0},{1,3},{3,1},{4,6},{6,4},{5,7},{7,5},{8,10},{10,8},{9,1... | collective-permute-start | bytes 2211848 | tf_op jit(solution)/shard_map/ppermute | solution.py:78
  69.1 6.4 %collective-permute-start.11 = (bf16[1,320,384]{2,1,0:T(8,128)(2,1)}, bf16[1,320,384]{2,1,0:T(8,128)(2,1)S(1)}, u32[]{:S(2)}, u32[]{:S(2)}) collective-permute-start(bf16[1,320,384]{2,1,0:T(8,128)(2,1)} %get-tuple-element.90.rest_4_.rest_5_), channel_id=1, source_target_pairs={{0,4},{4,0},{1,5},{5,1},{2,6},{6,2},{3,7},{7,3},{8,12},{12,8},{9,1... | collective-permute-start | bytes 737288 | tf_op jit(solution)/shard_map/ppermute | solution.py:78
  70.6 6.4 %collective-permute-start.10 = (bf16[3,320,384]{2,1,0:T(8,128)(2,1)S(1)}, bf16[3,320,384]{2,1,0:T(8,128)(2,1)S(1)}, u32[]{:S(2)}, u32[]{:S(2)}) collective-permute-start(bf16[3,320,384]{2,1,0:T(8,128)(2,1)S(1)} %collective-permute-done.8.rest_1_.rest_2_), channel_id=1, source_target_pairs={{0,2},{2,0},{1,3},{3,1},{4,6},{6,4},{5,7},{7,5},{8,10},{10,8},{9,1... | collective-permute-start | bytes 2211848 | tf_op jit(solution)/shard_map/ppermute | solution.py:78
  71.8 4.4 %collective-permute-start.12 = (bf16[1,320,384]{2,1,0:T(8,128)(2,1)}, bf16[1,320,384]{2,1,0:T(8,128)(2,1)S(1)}, u32[]{:S(2)}, u32[]{:S(2)}) collective-permute-start(bf16[1,320,384]{2,1,0:T(8,128)(2,1)} %get-tuple-element.90.rest_4_.rest_5_), channel_id=1, source_target_pairs={{0,2},{2,0},{1,3},{3,1},{4,6},{6,4},{5,7},{7,5},{8,10},{10,8},{9,1... | collective-permute-start | bytes 737288 | tf_op jit(solution)/shard_map/ppermute | solution.py:78
  75.5 1.5 collective-permute-start.13
  114.1 15.7 %all-to-all-start = ((bf16[4,320,192]{1,2,0:T(8,128)(2,1)}), bf16[4,320,192]{1,2,0:T(8,128)(2,1)S(1)}, u32[]{:S(2)}, u32[]{:S(2)}) async-start(bf16[4,320,192]{1,2,0:T(8,128)(2,1)} %copy.44), calls=%async_computation | async-start | bytes 1179648 | tf_op jit(solution)/shard_map/all_to_all | solution.py:902
  117.7 49.2 %all-gather.13.cloned.1.call-start = ((), (), s32[]{:S(2)}) async-start(), calls=%async_computation.9 | async-start | bytes 4915200 | tf_op jit(solution)/shard_map/all_gather | solution.py:728
  155.1 28.7 %all-to-all-start.1 = ((bf16[4,320,192]{1,2,0:T(8,128)(2,1)}), bf16[4,320,192]{1,2,0:T(8,128)(2,1)S(1)}, u32[]{:S(2)}, u32[]{:S(2)}) async-start(bf16[4,320,192]{1,2,0:T(8,128)(2,1)} %bitcast.12), calls=%async_computation.1 | async-start | bytes 1179648 | tf_op jit(solution)/shard_map/all_to_all | solution.py:902
  158.6 91.9 %reduce-scatter.4.cloned.1.call-start = ((), (), s32[]{:S(2)}) async-start(), calls=%async_computation.10 | async-start | bytes 5308416 | tf_op jit(solution)/shard_map/reduce_scatter | solution.py:948
  183.8 97.2 %reduce-scatter.6.cloned.1.call-start = ((), (), s32[]{:S(2)}) async-start(), calls=%async_computation.11 | async-start | bytes 884736 | tf_op jit(solution)/shard_map/reduce_scatter | solution.py:992
  184.6 5.9 %collective-permute-start.14 = (bf16[16,256,384]{2,1,0:T(8,128)(2,1)}, bf16[16,256,384]{2,1,0:T(8,128)(2,1)S(1)}, u32[]{:S(2)}, u32[]{:S(2)}) collective-permute-start(bf16[16,256,384]{2,1,0:T(8,128)(2,1)} %get-tuple-element.104), channel_id=1, source_target_pairs={{0,2},{2,0},{1,3},{3,1},{4,6},{6,4},{5,7},{7,5},{8,10},{10,8},{9,1... | collective-permute-start | bytes 9437192 | tf_op jit(solution)/shard_map/ppermute | solution.py:78
  191.9 51.0 %collective-permute-start.15 = (bf16[2,2,2,256,384]{4,3,2,1,0:T(8,128)(2,1)S(1)}, bf16[2,2,2,256,384]{4,3,2,1,0:T(8,128)(2,1)S(1)}, u32[]{:S(2)}, u32[]{:S(2)}) collective-permute-start(bf16[2,2,2,256,384]{4,3,2,1,0:T(8,128)(2,1)S(1)} %get-tuple-element.166.rest_9_), channel_id=1, source_target_pairs={{0,4},{4,0},{1,5},{5,1},{2,6},{6,2},{3,7},{7,3},{8,12},{12,8},{9,1... | collective-permute-start | bytes 4718600 | tf_op jit(solution)/shard_map/ppermute | solution.py:78
  242.3 3.3 collective-permute-start.16
  242.4 29.4 %collective-permute-start.18 = (bf16[1,4,320,384]{3,2,1,0:T(8,128)(2,1)}, bf16[1,4,320,384]{3,2,1,0:T(8,128)(2,1)}, u32[]{:S(2)}, u32[]{:S(2)}) collective-permute-start(bf16[1,4,320,384]{3,2,1,0:T(8,128)(2,1)} %get-tuple-element.112), channel_id=1, source_target_pairs={{0,2},{2,0},{1,3},{3,1},{4,6},{6,4},{5,7},{7,5},{8,10},{10,8},{9,1... | collective-permute-start | bytes 2949128 | tf_op jit(solution)/shard_map/ppermute | solution.py:78
  243.3 25.6 %collective-permute-start.17 = (bf16[2,2,256,384]{3,2,1,0:T(8,128)(2,1)S(1)}, bf16[2,2,256,384]{3,2,1,0:T(8,128)(2,1)}, u32[]{:S(2)}, u32[]{:S(2)}) collective-permute-start(bf16[2,2,256,384]{3,2,1,0:T(8,128)(2,1)S(1)} %get-tuple-element.164), channel_id=1, source_target_pairs={{0,1},{1,0},{2,3},{3,2},{4,5},{5,4},{6,7},{7,6},{8,9},{9,8},{10,11... | collective-permute-start | bytes 2359304 | tf_op jit(solution)/shard_map/ppermute | solution.py:78
  246.9 25.8 %collective-permute-start.19 = (bf16[4,320,384]{2,1,0:T(8,128)(2,1)}, bf16[4,320,384]{2,1,0:T(8,128)(2,1)S(1)}, u32[]{:S(2)}, u32[]{:S(2)}) collective-permute-start(bf16[4,320,384]{2,1,0:T(8,128)(2,1)} %fusion.16), channel_id=1, source_target_pairs={{0,4},{4,0},{1,5},{5,1},{2,6},{6,2},{3,7},{7,3},{8,12},{12,8},{9,1... | collective-permute-start | bytes 2949128 | tf_op jit(solution)/shard_map/ppermute | solution.py:78
  250.5 43.7 %reduce-scatter.8.cloned.1.call-start = ((), (), s32[]{:S(2)}) async-start(), calls=%async_computation.12 | async-start | bytes 442368 | tf_op jit(solution)/shard_map/reduce_scatter | solution.py:1017
  270.2 10.9 %collective-permute-start.20 = (bf16[2,256,384]{2,1,0:T(8,128)(2,1)S(1)}, bf16[2,256,384]{2,1,0:T(8,128)(2,1)S(1)}, u32[]{:S(2)}, u32[]{:S(2)}) collective-permute-start(bf16[2,256,384]{2,1,0:T(8,128)(2,1)S(1)} %get-tuple-element.170), channel_id=1, source_target_pairs={{0,8},{8,0},{16,24},{24,16},{1,9},{9,1},{17,25},{25,17},{2,10},{10... | collective-permute-start | bytes 1179656 | tf_op jit(solution)/shard_map/ppermute | solution.py:78
  281.1 2.7 collective-permute-start.21
  281.2 12.5 %collective-permute-start.22 = (bf16[256,384]{1,0:T(8,128)(2,1)S(1)}, bf16[256,384]{1,0:T(8,128)(2,1)S(1)}, u32[]{:S(2)}, u32[]{:S(2)}) collective-permute-start(bf16[256,384]{1,0:T(8,128)(2,1)S(1)} %get-tuple-element.175), channel_id=1, source_target_pairs={{0,16},{8,24},{16,0},{24,8},{1,17},{9,25},{17,1},{25,9},{2,18},{10... | collective-permute-start | bytes 589832 | tf_op jit(solution)/shard_map/ppermute | solution.py:78
  284.9 10.2 %collective-permute-start.23 = (bf16[208,576]{1,0:T(8,128)(2,1)S(1)}, bf16[208,576]{1,0:T(8,128)(2,1)S(1)}, u32[]{:S(2)}, u32[]{:S(2)}) collective-permute-start(bf16[208,576]{1,0:T(8,128)(2,1)S(1)} %get-tuple-element.172), channel_id=1, source_target_pairs={{0,1},{1,0},{2,3},{3,2},{4,5},{5,4},{6,7},{7,6},{8,9},{9,8},{10,11... | collective-permute-start | bytes 718856 | tf_op jit(solution)/shard_map/ppermute | solution.py:78
  295.2 9.3 %collective-permute-start.24 = (bf16[208,576]{1,0:T(8,128)(2,1)S(1)}, bf16[208,576]{1,0:T(8,128)(2,1)S(1)}, u32[]{:S(2)}, u32[]{:S(2)}) collective-permute-start(bf16[208,576]{1,0:T(8,128)(2,1)S(1)} %add_convert_fusion.7), channel_id=1, source_target_pairs={{0,4},{4,0},{1,5},{5,1},{2,6},{6,2},{3,7},{7,3},{8,12},{12,8},{9,1... | collective-permute-start | bytes 718856 | tf_op jit(solution)/shard_map/ppermute | solution.py:78
  297.9 16.8 %collective-permute-start.25 = (bf16[448,384]{1,0:T(8,128)(2,1)S(1)}, bf16[448,384]{1,0:T(8,128)(2,1)S(1)}, u32[]{:S(2)}, u32[]{:S(2)}) collective-permute-start(bf16[448,384]{1,0:T(8,128)(2,1)S(1)} %pad_maximum_fusion.4), channel_id=1, source_target_pairs={{0,16},{8,24},{16,0},{24,8},{1,17},{9,25},{17,1},{25,9},{2,18},{10... | collective-permute-start | bytes 1032200 | tf_op jit(solution)/shard_map/ppermute | solution.py:78
  314.8 23.1 %collective-permute-start.27 = (bf16[2,448,384]{2,1,0:T(8,128)(2,1)S(1)}, bf16[2,448,384]{2,1,0:T(8,128)(2,1)S(1)}, u32[]{:S(2)}, u32[]{:S(2)}) collective-permute-start(bf16[2,448,384]{2,1,0:T(8,128)(2,1)S(1)} %pad_maximum_fusion.2), channel_id=1, source_target_pairs={{0,8},{8,0},{16,24},{24,16},{1,9},{9,1},{17,25},{25,17},{2,10},{10... | collective-permute-start | bytes 2064392 | tf_op jit(solution)/shard_map/ppermute | solution.py:78
  314.9 20.9 %collective-permute-start.26 = (bf16[208,576]{1,0:T(8,128)(2,1)S(1)}, bf16[208,576]{1,0:T(8,128)(2,1)S(1)}, u32[]{:S(2)}, u32[]{:S(2)}) collective-permute-start(bf16[208,576]{1,0:T(8,128)(2,1)S(1)} %add_convert_fusion.6), channel_id=1, source_target_pairs={{0,16},{8,24},{16,0},{24,8},{1,17},{9,25},{17,1},{25,9},{2,18},{10... | collective-permute-start | bytes 718856 | tf_op jit(solution)/shard_map/ppermute | solution.py:78
  338.1 44.4 %all-to-all-start.2 = ((bf16[4,320,576]{2,1,0:T(8,128)(2,1)}), bf16[4,320,576]{2,1,0:T(8,128)(2,1)S(1)}, u32[]{:S(2)}, u32[]{:S(2)}) async-start(bf16[4,320,576]{2,1,0:T(8,128)(2,1)} %get-tuple-element.128), calls=%async_computation.5 | async-start | bytes 3276800 | tf_op jit(solution)/shard_map/all_to_all | solution.py:902
  342.0 47.3 %collective-permute-start.29 = (bf16[2,2,448,384]{3,2,1,0:T(8,128)(2,1)S(1)}, bf16[2,2,448,384]{3,2,1,0:T(8,128)(2,1)}, u32[]{:S(2)}, u32[]{:S(2)}) collective-permute-start(bf16[2,2,448,384]{3,2,1,0:T(8,128)(2,1)S(1)} %pad_maximum_fusion.1), channel_id=1, source_target_pairs={{0,4},{4,0},{1,5},{5,1},{2,6},{6,2},{3,7},{7,3},{8,12},{12,8},{9,1... | collective-permute-start | bytes 4128776 | tf_op jit(solution)/shard_map/ppermute | solution.py:78
  343.4 38.3 %collective-permute-start.28 = (bf16[2,208,576]{2,1,0:T(8,128)(2,1)S(1)}, bf16[2,208,576]{2,1,0:T(8,128)(2,1)S(1)}, u32[]{:S(2)}, u32[]{:S(2)}) collective-permute-start(bf16[2,208,576]{2,1,0:T(8,128)(2,1)S(1)} %pad_maximum_fusion.3), channel_id=1, source_target_pairs={{0,8},{8,0},{16,24},{24,16},{1,9},{9,1},{17,25},{25,17},{2,10},{10... | collective-permute-start | bytes 1437704 | tf_op jit(solution)/shard_map/ppermute | solution.py:78
  392.5 12.8 %collective-permute-start.31 = (bf16[2,2,2,448,384]{4,3,2,1,0:T(8,128)(2,1)S(1)}, bf16[2,2,2,448,384]{4,3,2,1,0:T(8,128)(2,1)}, u32[]{:S(2)}, u32[]{:S(2)}) collective-permute-start(bf16[2,2,2,448,384]{4,3,2,1,0:T(8,128)(2,1)S(1)} %pad_maximum_fusion), channel_id=1, source_target_pairs={{0,2},{2,0},{1,3},{3,1},{4,6},{6,4},{5,7},{7,5},{8,10},{10,8},{9,1... | collective-permute-start | bytes 8257544 | tf_op jit(solution)/shard_map/ppermute | solution.py:78
  392.5 6.6 %collective-permute-start.30 = (bf16[4,208,576]{2,1,0:T(8,128)(2,1)}, bf16[4,208,576]{2,1,0:T(8,128)(2,1)}, u32[]{:S(2)}, u32[]{:S(2)}) collective-permute-start(bf16[4,208,576]{2,1,0:T(8,128)(2,1)} %constant_dynamic-update-slice_fusion.own), channel_id=1, source_target_pairs={{0,2},{2,0},{1,3},{3,1},{4,6},{6,4},{5,7},{7,5},{8,10},{10,8},{9,1... | collective-permute-start | bytes 2875400 | tf_op jit(solution)/shard_map/ppermute | solution.py:78
  (41 other events, 181.3 us)
Sparse Core Ops, SparseCore 0:
  35.1 17.5 all-gather.6
  54.8 37.4 all-gather.8
  94.5 37.4 all-gather.10
  133.9 32.9 all-gather.12
  184.0 54.9 reduce-scatter.3
  250.6 19.5 reduce-scatter.5
  281.2 12.9 reduce-scatter.7

commit v5 on v4

--- a/solution.py
+++ b/solution.py
@@ -554,7 +554,15 @@
     )(ids, hid, g_raised, attn, g_att, vec, after)
 
 
-def unpack_ffn_kernel(ids, block_own, block_other, up, out, down, *vecs):
+def own_source(d, j, ids):
+    return (jnp.where(d == 0, j, 1) ^ ids[2], 0, 0)
+
+
+def other_source(d, j, ids):
+    return (jnp.where(d == 0, 0, j) ^ ids[2], 0, 0)
+
+
+def unpack_upper_kernel(ids, block_own, block_other, up, out, *vecs):
     side, core, mid, group = ids[0], ids[1], ids[2], ids[3]
     b, j = pl.program_id(0) ^ core, pl.program_id(1)
     own = pl.program_id(0) == 0
@@ -563,9 +571,6 @@
         part = jnp.where(own, block_own[place], block_other[place]).astype(jnp.float32)
         up[:, 384 * k : 384 * k + 384] = part[0:192]
         out[48 * k : 48 * k + 48, :] = part[192:240]
-        rows = pl.ds(pl.multiple_of(96 * j, 32) + 192 * k, 96)
-        down[rows, 0:384] = part[256:352]
-        down[rows, 384:768] = part[352:448]
 
     @pl.when(b == 0)
     def _():
@@ -587,35 +592,58 @@
                     target[384 * where : 384 * where + 384] = rows[r]
 
 
-def unpack_ffn(ids, own, other):
-    def source_own(d, j, ids):
-        return (jnp.where(d == 0, j, 1) ^ ids[2], 0, 0)
-
-    def source_other(d, j, ids):
-        return (jnp.where(d == 0, 0, j) ^ ids[2], 0, 0)
-
+def unpack_upper(ids, own, other):
     sizes = [384] * 6 + [1536]
     return pl.pallas_call(
-        unpack_ffn_kernel,
+        unpack_upper_kernel,
         out_shape=(
             jax.ShapeDtypeStruct((384, FF), jnp.float32),
             jax.ShapeDtypeStruct((384, D), jnp.float32),
-            jax.ShapeDtypeStruct((FF // 2, D), jnp.float32),
         )
         + tuple(jax.ShapeDtypeStruct((size,), jnp.float32) for size in sizes),
         grid_spec=pltpu.PrefetchScalarGridSpec(
             num_scalar_prefetch=1,
             grid=(2, 2),
-            in_specs=[pl.BlockSpec((4, 448, 384), source_own), pl.BlockSpec((4, 448, 384), source_other)],
+            in_specs=[
+                pl.BlockSpec((4, 256, 384), own_source),
+                pl.BlockSpec((4, 256, 384), other_source),
+            ],
             out_specs=(
                 pl.BlockSpec((192, 1536), lambda d, j, ids: (d ^ ids[1], j)),
                 pl.BlockSpec((192, 384), lambda d, j, ids: (d ^ ids[1], j)),
-                pl.BlockSpec((FF // 4, D), lambda d, j, ids: (d ^ ids[1], 0)),
             )
             + tuple(pl.BlockSpec((size,), lambda d, j, ids: (0,)) for size in sizes),
         ),
         compiler_params=PARAMS,
-        name="unpack_ffn",
+        name="unpack_upper",
+    )(ids, own, other)
+
+
+def unpack_down_kernel(ids, block_own, block_other, down):
+    own, j = pl.program_id(0) == 0, pl.program_id(1)
+    for k in range(GROUPS):
+        place = turn(k ^ ids[3])
+        part = jnp.where(own, block_own[place], block_other[place]).astype(jnp.float32)
+        rows = pl.ds(pl.multiple_of(96 * j, 32) + 192 * k, 96)
+        down[rows, 0:384] = part[0:96]
+        down[rows, 384:768] = part[96:192]
+
+
+def unpack_down(ids, own, other):
+    return pl.pallas_call(
+        unpack_down_kernel,
+        out_shape=jax.ShapeDtypeStruct((FF // 2, D), jnp.float32),
+        grid_spec=pltpu.PrefetchScalarGridSpec(
+            num_scalar_prefetch=1,
+            grid=(2, 2),
+            in_specs=[
+                pl.BlockSpec((4, 192, 384), own_source),
+                pl.BlockSpec((4, 192, 384), other_source),
+            ],
+            out_specs=pl.BlockSpec((FF // 4, D), lambda d, j, ids: (d ^ ids[1], 0)),
+        ),
+        compiler_params=PARAMS,
+        name="unpack_down",
     )(ids, own, other)
 
 
@@ -722,10 +750,9 @@
     )(base, both, weight)
 
 
-def gather_rows(weight, core, *others):
+def own_part(weight, core):
     half = weight.shape[0] // 2
-    part = tie(lax.dynamic_slice_in_dim(weight, core * half, half, 0), *others)
-    return lax.all_gather(part, ("wa", "c"), axis=0, tiled=True)
+    return lax.dynamic_slice_in_dim(weight, core * half, half, 0)
 
 
 def reduce_blocks(grad):
@@ -819,7 +846,8 @@
         )
 
     smalls = [b_query, b_value, b_out, gain_one, shift_one, b_up, b_down, gain_two, shift_two]
-    joined = lax.all_gather(jnp.concatenate(smalls), "wa", axis=0)
+    w_parts = [own_part(item, core) for item in (w_out, w_up, w_down)]
+    joined = lax.all_gather(tie(jnp.concatenate(smalls), *w_parts), "wa", axis=0)
     second, third, w_other, joined = lax.optimization_barrier((second, third, w_other, joined))
     fourth = swap(third, "h", 1)
     full, place = [], 0
@@ -831,9 +859,9 @@
     b_group = pick_columns((bias_query, jnp.zeros_like(bias_query), bias_value), group)[None]
 
     w_group = (w_own, w_other) if wide == 2 else (w_other,)
-    full_out = gather_rows(w_out, core, w_other)
-    full_up = gather_rows(w_up, core, w_other)
-    full_down = gather_rows(w_down, core, w_other)
+    full_out, full_up, full_down = (
+        lax.all_gather(tie(part, w_other), ("wa", "c"), axis=0, tiled=True) for part in w_parts
+    )
     where, pieces = [], []
 
     def spread(piece, flips):
@@ -896,7 +924,8 @@
         low_part, high_part = slice(192 * g, 192 * g + 128), slice(192 * g + 128, 192 * g + 192)
         columns += [w_key[:, low_part], w_value[:, high_part], w_key[:, high_part], w_value[:, low_part]]
         columns += [w_query[:, 192 * g : 192 * g + 192], jnp.zeros_like(w_query[:, :64])]
-    by_group = gather_rows(jnp.concatenate(columns, axis=1), core)
+    by_group = own_part(jnp.concatenate(columns, axis=1), core)
+    by_group = lax.all_gather(by_group, ("wa", "c"), axis=0, tiled=True)
 
     def send_back(parts):
         return lax.all_to_all(parts, "h", 0, 0, tiled=True)
@@ -1020,29 +1049,36 @@
         give = swap(give, "h", 2)
         qkv, other = fold(near, far)
         other = swap(other, "wa", 1)
+        down_other = swap(down_sum, "h", 2)
         upper = both_sum(upper, give, qkv)
-        joint = jnp.concatenate([upper, down_sum], axis=0)
-        joint_other = swap(joint, "h", 2)
-        qkv = both_sum(qkv, other, joint)
+        upper_other = swap(upper, "h", 2)
+        qkv = both_sum(qkv, other, upper)
         other = swap(qkv, "m", 1)
-        qkv = both_sum(qkv, other)
+        down_sum = jnp.stack([tie(down_sum, qkv), down_other])
+        down_other = swap(down_sum, "h", 1)
+        upper = jnp.stack([tie(upper, down_sum), upper_other])
+        upper_other = swap(upper, "h", 1)
+        qkv = both_sum(qkv, other, upper)
         other = swap(qkv, "h", 2)
-        joint = jnp.stack([tie(joint, qkv), joint_other])
-        joint_other = swap(joint, "h", 1)
-        qkv = jnp.stack([tie(qkv, joint), other])
+        down_sum = jnp.stack([tie(down_sum, qkv), down_other])
+        down_other = swap(down_sum, "m", 1)
+        upper = jnp.stack([tie(upper, down_sum), upper_other])
+        upper_other = swap(upper, "m", 1)
+        parts = send_back(tie(parts, upper))
+        qkv = jnp.stack([tie(qkv, upper), other])
         other = swap(qkv, "h", 1)
-        joint = jnp.stack([tie(joint, qkv), joint_other])
-        joint_other = swap(joint, "m", 1)
-        parts = send_back(tie(parts, joint))
-        qkv = jnp.concatenate([tie(qkv, joint), other], axis=0)
+        down_sum = jnp.stack([tie(down_sum, qkv), down_other])
+        down_other = swap(down_sum, "c", 1)
+        qkv = jnp.concatenate([tie(qkv, down_sum), other], axis=0)
         other = swap(qkv, "c", 1)
-        grad_inputs = token_grads(tie(grad_sum_one, qkv), parts, by_group)
-        joint = jnp.stack([tie(joint, grad_inputs), joint_other])
-        joint_other = swap(joint, "c", 1)
-        out_query, out_key, out_value, sums = unpack_qkv(place_ids, tie(qkv, joint), other)
-        joint = tie(joint, out_query)
-        joint, joint_other = (item.reshape(8, 448, 384) for item in (tie(joint, out_query), joint_other))
-        out_up, out_out, out_down, *vectors = unpack_ffn(place_ids, joint, joint_other)
+        down_sum, down_other = (item.reshape(8, 192, 384) for item in (tie(down_sum, qkv), down_other))
+        out_down = unpack_down(place_ids, down_sum, down_other)
+        upper = jnp.stack([tie(upper, out_down), upper_other])
+        upper_other = swap(upper, "c", 1)
+        out_query, out_key, out_value, sums = unpack_qkv(place_ids, tie(qkv, upper), other)
+        upper, upper_other = (item.reshape(8, 256, 384) for item in (tie(upper, out_query), upper_other))
+        out_up, out_out, *vectors = unpack_upper(place_ids, upper, upper_other)
+        grad_inputs = token_grads(tie(grad_sum_one, out_up), parts, by_group)
         sums = sums[:, 0]
         sums_v = jnp.concatenate([sums[:, 256:384], sums[:, 128:192]], axis=1).reshape(-1)
         sums_q = sums[:, 384:576].reshape(-1)

time: 422 us -> 402 us (0.953)
  waiting for transfers between devices: 138 us -> 125 us
  starting transfers between devices: 49 us -> 56.8 us
  Pallas kernels: 134 us -> 128 us
  blocking collectives: 9.49 us -> 4.44 us
    ppermute x32 -> x36, waiting for transfers between devices: 129 us -> 110 us  [swap(): return lax.ppermute(array, axis, [(i, i ^ bit) for i in range(size)])]
    ppermute x32 -> x36, starting transfers between devices: 37.3 us -> 44.4 us  [swap(): return lax.ppermute(array, axis, [(i, i ^ bit) for i in range(size)])]
    pallas_call x1, Pallas kernels: 48.9 us -> 42.7 us  [attend_backward(): pl.pallas_call(functools.partial(backward_kernel, where, rows, classes, o...]
    all_gather x1, blocking collectives: 9.49 us -> 4.44 us  [per_device(): lax.all_gather(tie(jnp.concatenate(smalls), *w_parts), 'wa', axis=0)]
    all_to_all x3, waiting for transfers between devices: 3.36 us -> 7.81 us  [send_back(): return lax.all_to_all(parts, 'h', 0, 0, tiled=True)]
    pallas_call x1 -> x2, Pallas kernels: 8.44 us -> 11.2 us  [the longest x1 5.97 us: unpack_upper(): pl.pallas_call(unpack_upper_kernel, out_shape=(jax.ShapeDtypeStruct((384,...]
    unnamed x112 -> x110, local copies, waits for them, and re-layouts: 10.8 us -> 8.54 us
  transfers between devices with their start and end apart: 42 -> 46, of which waited for: 22 -> 19; matrix products, arithmetic and copies ran while one was open for 16% -> 17% of each run, Pallas kernels for 30% -> 30%
where the time goes in v5:
time: 402 us; the launch traced here: 403 us
  Pallas kernels  128 us (32%)
  waiting for transfers between devices  125 us (31%)
  starting transfers between devices  56.8 us (14%)
  local copies, waits for them, and re-layouts  37.8 us (9%)
  matrix products  19.2 us (5%)
  other arithmetic  16 us (4%)
  between operations  15 us (4%)
  blocking collectives  4.44 us (1%)
    ppermute x36, waiting for transfers between devices, swap(): return lax.ppermute(array, axis, [(i, i ^ bit) for i in range(size)])  110 us
    ppermute x36, starting transfers between devices, swap(): return lax.ppermute(array, axis, [(i, i ^ bit) for i in range(size)])  44.4 us
    pallas_call x1, Pallas kernels, attend_backward(): pl.pallas_call(functools.partial(backward_kernel, where, rows, classes, o...  42.7 us
    pallas_call x1, Pallas kernels, attend_forward(): pl.pallas_call(functools.partial(forward_kernel, where, rows, classes), o...  30.8 us
    dot_general x3, matrix products, mm(): return jnp.dot(left, right, preferred_element_type=jnp.float32)  13.5 us
    all_to_all x3, starting transfers between devices, send_back(): return lax.all_to_all(parts, 'h', 0, 0, tiled=True)  11.5 us
    pallas_call x1, Pallas kernels, upper_grad(): pl.pallas_call(upper_grad_kernel, out_shape=(jax.ShapeDtypeStruct((16, 25...  8.63 us
    unnamed x110, local copies, waits for them, and re-layouts  8.54 us
  transfers between devices with their start and end apart: 46, of which 19 were waited for; matrix products, arithmetic and copies ran while one was open for 17% of the time, Pallas kernels for 30%

profile of v5, /device:TPU:0, one launch (start us, length us, event | category | flops | bytes accessed | tf_op | source)
XLA Modules:
  0.0 403.3 jit_solution(14028708562179379291)
XLA Ops:
  7.3 3.1 collective-permute-start
  10.3 2.6 collective-permute-start.1
  13.6 2.7 pick_weights.1.rest_3_.rest_1_
  22.5 2.4 constant_dynamic-slice_fusion.3
  24.9 4.4 %all-gather.1 = bf16[2,1,4608]{2,1,0:T(2,128)(2,1)S(1)} all-gather(bf16[1,1,4608]{2,1,0:T(2,128)(2,1)S(1)} %reshape.325), channel_id=2, replica_groups=mesh['h'=4,'m'=2,'c'=2,'wa'=2] {'wa'}, dimensions={0}, use_global_device_ids=true | all-gather | bytes 27648 | tf_op jit(solution)/shard_map/all_gather | solution.py:850
  29.4 2.8 collective-permute-done.rest_1_.t1
  32.2 2.7 collective-permute-done.1.rest_2_.t2
  37.3 4.2 %project.2 = (bf16[3,320,384]{2,1,0:T(8,128)(2,1)}, bf16[960,256]{1,0:T(8,128)(2,1)}) custom-call(s32[4]{0:T(128)} %pad_add_fusion.5.ids, f32[1,640]{1,0:T(1,128)} %broadcast_in_dim.85.bias, bf16[320,768]{1,0:T(8,128)(2,1)} %bitcast.114, bf16[320,768]{1,0:T(8,128)(2,1)} %copy-done.21, bf16[320,768]{1,0:T(8,128)(2,1)} %collective-permute-done.1.rest_2_.t2, ...), custom_call_target="tpu_custom_call" | custom-call | flops 943718400 | bytes 2097152 | tf_op jit(solution)/shard_map/project/pallas_call | solution.py:455
  51.2 2.0 collective-permute-start.7
  56.7 6.4 %collective-permute-done.7.rest_0_.t3 = bf16[320,768]{1,0:T(8,128)(2,1)S(1)} collective-permute-done((bf16[320,768]{1,0:T(8,128)(2,1)}, bf16[320,768]{1,0:T(8,128)(2,1)S(1)}, u32[]{:S(2)}, u32[]{:S(2)}) %collective-permute-start.7) | collective-permute-done | bytes 491552 | tf_op jit(solution)/shard_map/ppermute | solution.py:78
  63.8 3.0 project.3
  69.9 3.4 collective-permute-done.11.rest_5_.rest_6_
  75.8 30.8 %attend_forward.1 = (bf16[4,320,192]{2,1,0:T(8,128)(2,1)}, f32[1280,128]{1,0:T(8,128)}, f32[1280,128]{1,0:T(8,128)}, f32[8,1280]{1,0:T(8,128)}) custom-call(s32[2]{0:T(128)} %pad_add_fusion.4.ids, s32[55]{0:T(128)} %reshape.291.flags, bf16[960,256]{1,0:T(8,128)(2,1)} %get-tuple-element.93.first_q, bf16[320,256]{1,0:T(8,128)(2,1)} %get-tuple-element.94.last_q, ...), custom_call_target="tpu_custom_call" | custom-call | flops 5033164800 | bytes 8388608 | tf_op jit(solution)/shard_map/attend_forward/pallas_call | solution.py:344
  106.6 2.3 copy.44
  108.9 3.6 all-to-all-start
  116.2 3.9 concatenate.49
  121.2 7.8 %all-to-all-done = bf16[4,320,192]{1,2,0:T(8,128)(2,1)S(1)} async-done(((bf16[4,320,192]{1,2,0:T(8,128)(2,1)}), bf16[4,320,192]{1,2,0:T(8,128)(2,1)S(1)}, u32[]{:S(2)}, u32[]{:S(2)}) %all-to-all-start) | async-done | bytes 491552 | tf_op jit(solution)/shard_map/all_to_all | solution.py:931
  129.0 2.0 fusion.39
  131.7 6.4 %multiply_convert_fusion = (bf16[320,3072]{1,0:T(8,128)(2,1)}, f32[320,3072]{1,0:T(8,128)}) fusion(f32[3072]{0:T(1024)S(1)} %copy-done.23, bf16[320,768]{1,0:T(8,128)(2,1)S(1)} %fusion.17.hid, bf16[768,3072]{1,0:T(8,128)(2,1)} %all-gather.9.cloned.1.call-done), kind=kOutput, calls=%fused_computation.9 | convolution fusion | flops 1515847680 | bytes 11120640 | tf_op jit(solution)/shard_map/dot_general | solution.py:38
  138.1 5.1 %fusion.40 = (f32[320]{0:T(512)S(1)}, f32[320,768]{1,0:T(8,128)S(1)}) fusion(f32[768]{0:T(1024)S(1)} %copy-done.25, bf16[320,3072]{1,0:T(8,128)(2,1)} %get-tuple-element.216.active, bf16[3072,768]{1,0:T(8,128)(2,1)} %all-gather.11.cloned.1.call-done, f32[768]{0:T(1024)S(1)} %reshape.307, f32[768]{0:T(1024)S(1)} %reshape.306, f32[320]{0:T(512)S(1)} %add_rsqrt_fusion.1, ...), kind=kOutput, calls=%fused_computation.137 | convolution fusion | flops 1511669504 | bytes 8663808 | tf_op jit(solution)/shard_map/dot_general | solution.py:38
  145.9 2.9 fusion.41
  148.9 2.3 multiply_reduce_fusion
  154.2 3.5 all-to-all-start.1
  161.2 6.5 %all-gather.13.cloned.1.call-done.after.weight = bf16[768,2560]{1,0:T(8,128)(2,1)} async-done(((bf16[192,2560]{1,0:T(8,128)(2,1)}), bf16[768,2560]{1,0:T(8,128)(2,1)}) %all-gather.13.cloned.1.call-update) | async-done | bytes 3932176 | tf_op jit(solution)/shard_map/all_gather | solution.py:928
  167.7 8.6 %upper_grad.1 = (bf16[16,256,384]{2,1,0:T(8,128)(2,1)}, bf16[16,256,384]{2,1,0:T(8,128)(2,1)}) custom-call(s32[4]{0:T(128)} %pad_add_fusion.5.ids, bf16[320,768]{1,0:T(8,128)(2,1)} %copy-done.12, bf16[320,3072]{1,0:T(8,128)(2,1)} %copy-done.15, bf16[320,768]{1,0:T(8,128)(2,1)} %copy.45.attn, bf16[320,768]{1,0:T(8,128)(2,1)} %copy-done.14, ...), custom_call_target="tpu_custom_call" | custom-call | flops 1887436800 | bytes 12582912 | tf_op jit(solution)/shard_map/upper_grad/pallas_call | solution.py:533
  176.3 8.2 %down_grad.1 = bf16[4,4,384,384]{3,2,1,0:T(8,128)(2,1)} custom-call(bf16[320,3072]{1,0:T(8,128)(2,1)} %get-tuple-element.216.active, bf16[320,768]{1,0:T(8,128)(2,1)} %copy-done.13, bf16[2,2,2,2,256,384]{5,4,3,2,1,0:T(8,128)(2,1)} %bitcast.96), custom_call_target="tpu_custom_call" | custom-call | flops 1509949440 | bytes 8388608 | tf_op jit(solution)/shard_map/down_grad/pallas_call | solution.py:489
  185.6 2.2 copy.47.rest_0_
  187.8 3.4 collective-permute-done.14
  194.2 42.7 %attend_backward.1 = (bf16[2,4,320,384]{3,2,1,0:T(8,128)(2,1)}, bf16[1,4,320,384]{3,2,1,0:T(8,128)(2,1)}, bf16[1,4,320,384]{3,2,1,0:T(8,128)(2,1)}, bf16[1280,192]{1,0:T(8,128)(2,1)}) custom-call(s32[2]{0:T(128)} %pad_add_fusion.4.ids, s32[55]{0:T(128)} %reshape.291.flags, bf16[960,256]{1,0:T(8,128)(2,1)} %get-tuple-element.93.first_q, ...), custom_call_target="tpu_custom_call" | custom-call | flops 12582912000 | bytes 16777216 | tf_op jit(solution)/shard_map/attend_backward/pallas_call | solution.py:382
  238.7 10.5 %collective-permute-start.17 = (bf16[2,2,256,384]{3,2,1,0:T(8,128)(2,1)S(1)}, bf16[2,2,256,384]{3,2,1,0:T(8,128)(2,1)}, u32[]{:S(2)}, u32[]{:S(2)}) collective-permute-start(bf16[2,2,256,384]{3,2,1,0:T(8,128)(2,1)S(1)} %get-tuple-element.172), channel_id=1, source_target_pairs={{0,1},{1,0},{2,3},{3,2},{4,5},{5,4},{6,7},{7,6},{8,9},{9,8},{10,11... | collective-permute-start | bytes 2359304 | tf_op jit(solution)/shard_map/ppermute | solution.py:78
  251.0 22.7 %collective-permute-done.17 = bf16[2,2,256,384]{3,2,1,0:T(8,128)(2,1)} collective-permute-done((bf16[2,2,256,384]{3,2,1,0:T(8,128)(2,1)S(1)}, bf16[2,2,256,384]{3,2,1,0:T(8,128)(2,1)}, u32[]{:S(2)}, u32[]{:S(2)}) %collective-permute-start.17) | collective-permute-done | bytes 786464 | tf_op jit(solution)/shard_map/ppermute | solution.py:78
  277.6 7.5 %qkv_grads.1 = (bf16[2,208,576]{2,1,0:T(8,128)(2,1)}, bf16[2,208,576]{2,1,0:T(8,128)(2,1)}, bf16[4,320,576]{2,1,0:T(8,128)(2,1)}) custom-call(s32[4]{0:T(128)} %pad_add_fusion.5.ids, bf16[320,768]{1,0:T(8,128)(2,1)} %bitcast.115, bf16[320,768]{1,0:T(8,128)(2,1)} %copy-done.21, bf16[320,768]{1,0:T(8,128)(2,1)} %collective-permute-done.1.rest_2_.t2, ...), custom_call_target="tpu_custom_call" | custom-call | flops 1132462080 | bytes 4194304 | tf_op jit(solution)/shard_map/qkv_grads/pallas_call | solution.py:689
  285.8 2.5 collective-permute-start.22
  289.4 1.9 collective-permute-start.23
  291.3 6.3 %collective-permute-done.22 = bf16[256,384]{1,0:T(8,128)(2,1)S(1)} collective-permute-done((bf16[256,384]{1,0:T(8,128)(2,1)S(1)}, bf16[256,384]{1,0:T(8,128)(2,1)S(1)}, u32[]{:S(2)}, u32[]{:S(2)}) %collective-permute-start.22) | collective-permute-done | bytes 196640 | tf_op jit(solution)/shard_map/ppermute | solution.py:78
  297.8 2.9 collective-permute-start.24
  300.9 13.9 %collective-permute-done.24 = bf16[192,384]{1,0:T(8,128)(2,1)S(1)} collective-permute-done((bf16[192,384]{1,0:T(8,128)(2,1)}, bf16[192,384]{1,0:T(8,128)(2,1)S(1)}, u32[]{:S(2)}, u32[]{:S(2)}) %collective-permute-start.24) | collective-permute-done | bytes 147488 | tf_op jit(solution)/shard_map/ppermute | solution.py:78
  315.9 2.1 collective-permute-start.28
  318.0 7.6 %collective-permute-done.27 = bf16[2,192,384]{2,1,0:T(8,128)(2,1)S(1)} collective-permute-done((bf16[2,192,384]{2,1,0:T(8,128)(2,1)S(1)}, bf16[2,192,384]{2,1,0:T(8,128)(2,1)S(1)}, u32[]{:S(2)}, u32[]{:S(2)}) %collective-permute-start.27) | collective-permute-done | bytes 294944 | tf_op jit(solution)/shard_map/ppermute | solution.py:78
  326.8 12.0 %collective-permute-done.28 = bf16[2,256,384]{2,1,0:T(8,128)(2,1)S(1)} collective-permute-done((bf16[2,256,384]{2,1,0:T(8,128)(2,1)S(1)}, bf16[2,256,384]{2,1,0:T(8,128)(2,1)S(1)}, u32[]{:S(2)}, u32[]{:S(2)}) %collective-permute-start.28) | collective-permute-done | bytes 393248 | tf_op jit(solution)/shard_map/ppermute | solution.py:78
  340.1 1.9 collective-permute-start.33
  342.0 4.4 %all-to-all-start.2 = ((bf16[4,320,576]{2,1,0:T(8,128)(2,1)}), bf16[4,320,576]{2,1,0:T(8,128)(2,1)}, u32[]{:S(2)}, u32[]{:S(2)}) async-start(bf16[4,320,576]{2,1,0:T(8,128)(2,1)} %get-tuple-element.143), calls=%async_computation.5 | async-start | bytes 3276800 | tf_op jit(solution)/shard_map/all_to_all | solution.py:931
  347.5 18.2 %collective-permute-done.31 = bf16[2,208,576]{2,1,0:T(8,128)(2,1)} collective-permute-done((bf16[2,208,576]{2,1,0:T(8,128)(2,1)}, bf16[2,208,576]{2,1,0:T(8,128)(2,1)}, u32[]{:S(2)}, u32[]{:S(2)}) %collective-permute-start.31) | collective-permute-done | bytes 479264 | tf_op jit(solution)/shard_map/ppermute | solution.py:78
  366.9 5.2 %unpack_down.1 = f32[1536,768]{1,0:T(8,128)} custom-call(s32[4]{0:T(128)} %pad_add_fusion.5.ids, bf16[8,192,384]{2,1,0:T(8,128)(2,1)} %bitcast.101, bf16[8,192,384]{2,1,0:T(8,128)(2,1)} %bitcast.43.block_other), custom_call_target="tpu_custom_call" | custom-call | tf_op jit(solution)/shard_map/unpack_down/pallas_call | solution.py:633
  374.0 4.6 %collective-permute-done.34.other = bf16[4,208,576]{2,1,0:T(8,128)(2,1)} collective-permute-done((bf16[4,208,576]{2,1,0:T(8,128)(2,1)S(1)}, bf16[4,208,576]{2,1,0:T(8,128)(2,1)}, u32[]{:S(2)}, u32[]{:S(2)}) %collective-permute-start.34) | collective-permute-done | bytes 958496 | tf_op jit(solution)/shard_map/ppermute | solution.py:78
  378.6 3.8 unpack_qkv.1
  384.8 6.0 %unpack_upper.1 = (f32[384,3072]{1,0:T(8,128)}, f32[384,768]{1,0:T(8,128)}, f32[384]{0:T(512)}, f32[384]{0:T(512)}, f32[384]{0:T(512)}, /*index=5*/f32[384]{0:T(...) custom-call(s32[4]{0:T(128)} %pad_add_fusion.5.ids, bf16[8,256,384]{2,1,0:T(8,128)(2,1)} %bitcast.100, ...), custom_call_target="tpu_custom_call" | custom-call | tf_op jit(solution)/shard_map/unpack_upper/pallas_call | solution.py:597
  390.8 5.7 %token_grads.1 = f32[320,768]{1,0:T(8,128)} custom-call(f32[320,768]{1,0:T(8,128)} %get-tuple-element.141.base, bf16[4,320,576]{2,1,0:T(8,128)(2,1)} %all-to-all-done.2.both, bf16[768,2560]{1,0:T(8,128)(2,1)} %all-gather.13.cloned.1.call-done.after.weight), custom_call_target="tpu_custom_call" | custom-call | flops 1132462080 | bytes 8388608 | tf_op jit(solution)/shard_map/token_grads/pallas_call | solution.py:740
  (301 shorter events, 66.8 us)
Async XLA Ops:
  7.2 114.0 %all-gather.7.cloned.1.call-start = ((), (), s32[]{:S(2)}) async-start(), calls=%async_computation.6 | async-start | bytes 1474560 | tf_op jit(solution)/shard_map/all_gather | solution.py:863
  7.3 24.9 %collective-permute-start = (bf16[320,768]{1,0:T(8,128)(2,1)}, bf16[320,768]{1,0:T(8,128)(2,1)S(1)}, u32[]{:S(2)}, u32[]{:S(2)}) collective-permute-start(bf16[320,768]{1,0:T(8,128)(2,1)} %bitcast.112), channel_id=1, source_target_pairs={{0,8},{8,0},{16,24},{24,16},{1,9},{9,1},{17,25},{25,17},{2,10},{10... | collective-permute-start | bytes 1474568 | tf_op jit(solution)/shard_map/ppermute | solution.py:78
  10.3 24.5 %collective-permute-start.1 = (bf16[320,768]{1,0:T(8,128)(2,1)}, bf16[320,768]{1,0:T(8,128)(2,1)}, u32[]{:S(2)}, u32[]{:S(2)}) collective-permute-start(bf16[320,768]{1,0:T(8,128)(2,1)} %bitcast.113), channel_id=1, source_target_pairs={{0,16},{8,24},{16,0},{24,8},{1,17},{9,25},{17,1},{25,9},{2,18},{10... | collective-permute-start | bytes 1474568 | tf_op jit(solution)/shard_map/ppermute | solution.py:78
  16.2 18.6 %collective-permute-start.2 = (bf16[384,640]{1,0:T(8,128)(2,1)}, bf16[384,640]{1,0:T(8,128)(2,1)S(1)}, u32[]{:S(2)}, u32[]{:S(2)}) collective-permute-start(bf16[384,640]{1,0:T(8,128)(2,1)} %pick_weights.1.rest_3_.rest_1_), channel_id=1, source_target_pairs={{0,1},{1,0},{2,3},{3,2},{4,5},{5,4},{6,7},{7,6},{8,9},{9,8},{10,11... | collective-permute-start | bytes 1474568 | tf_op jit(solution)/shard_map/ppermute | solution.py:78
  34.9 96.7 %all-gather.9.cloned.1.call-start = ((), (), s32[]{:S(2)}) async-start(), calls=%async_computation.7 | async-start | bytes 5898240 | tf_op jit(solution)/shard_map/all_gather | solution.py:863
  35.6 102.5 %all-gather.11.cloned.1.call-start = ((), (), s32[]{:S(2)}) async-start(), calls=%async_computation.8 | async-start | bytes 5898240 | tf_op jit(solution)/shard_map/all_gather | solution.py:863
  41.6 1.2 collective-permute-start.3
  42.7 3.7 collective-permute-start.4
  46.4 3.7 collective-permute-start.5
  47.0 21.2 %collective-permute-start.8 = (bf16[3,320,384]{2,1,0:T(8,128)(2,1)}, bf16[3,320,384]{2,1,0:T(8,128)(2,1)S(1)}, u32[]{:S(2)}, u32[]{:S(2)}) collective-permute-start(bf16[3,320,384]{2,1,0:T(8,128)(2,1)} %get-tuple-element.91.rest_0_.rest_1_), channel_id=1, source_target_pairs={{0,4},{4,0},{1,5},{5,1},{2,6},{6,2},{3,7},{7,3},{8,12},{12,8},{9,1... | collective-permute-start | bytes 2211848 | tf_op jit(solution)/shard_map/ppermute | solution.py:78
  50.1 4.9 %collective-permute-start.6 = (s32[8,320]{1,0:T(8,128)S(1)}, s32[8,320]{1,0:T(8,128)S(1)}, u32[]{:S(2)}, u32[]{:S(2)}) collective-permute-start(s32[8,320]{1,0:T(8,128)S(1)} %pad_add_fusion), channel_id=1, source_target_pairs={{0,16},{8,24},{16,0},{24,8},{1,17},{9,25},{17,1},{25,9},{2,18},{10... | collective-permute-start | bytes 30728 | tf_op jit(solution)/shard_map/ppermute | solution.py:78
  51.2 11.8 %collective-permute-start.7 = (bf16[320,768]{1,0:T(8,128)(2,1)}, bf16[320,768]{1,0:T(8,128)(2,1)S(1)}, u32[]{:S(2)}, u32[]{:S(2)}) collective-permute-start(bf16[320,768]{1,0:T(8,128)(2,1)} %collective-permute-done.1.rest_2_.t2), channel_id=1, source_target_pairs={{0,8},{8,0},{16,24},{24,16},{1,9},{9,1},{17,25},{25,17},{2,10},{10... | collective-permute-start | bytes 1474568 | tf_op jit(solution)/shard_map/ppermute | solution.py:78
  53.2 20.8 %collective-permute-start.9 = (bf16[3,320,384]{2,1,0:T(8,128)(2,1)}, bf16[3,320,384]{2,1,0:T(8,128)(2,1)S(1)}, u32[]{:S(2)}, u32[]{:S(2)}) collective-permute-start(bf16[3,320,384]{2,1,0:T(8,128)(2,1)} %get-tuple-element.91.rest_0_.rest_1_), channel_id=1, source_target_pairs={{0,2},{2,0},{1,3},{3,1},{4,6},{6,4},{5,7},{7,5},{8,10},{10,8},{9,1... | collective-permute-start | bytes 2211848 | tf_op jit(solution)/shard_map/ppermute | solution.py:78
  66.9 6.4 %collective-permute-start.11 = (bf16[1,320,384]{2,1,0:T(8,128)(2,1)}, bf16[1,320,384]{2,1,0:T(8,128)(2,1)S(1)}, u32[]{:S(2)}, u32[]{:S(2)}) collective-permute-start(bf16[1,320,384]{2,1,0:T(8,128)(2,1)} %get-tuple-element.95.rest_4_.rest_5_), channel_id=1, source_target_pairs={{0,4},{4,0},{1,5},{5,1},{2,6},{6,2},{3,7},{7,3},{8,12},{12,8},{9,1... | collective-permute-start | bytes 737288 | tf_op jit(solution)/shard_map/ppermute | solution.py:78
  68.2 6.6 %collective-permute-start.10 = (bf16[3,320,384]{2,1,0:T(8,128)(2,1)S(1)}, bf16[3,320,384]{2,1,0:T(8,128)(2,1)S(1)}, u32[]{:S(2)}, u32[]{:S(2)}) collective-permute-start(bf16[3,320,384]{2,1,0:T(8,128)(2,1)S(1)} %collective-permute-done.8.rest_1_.rest_2_), channel_id=1, source_target_pairs={{0,2},{2,0},{1,3},{3,1},{4,6},{6,4},{5,7},{7,5},{8,10},{10,8},{9,1... | collective-permute-start | bytes 2211848 | tf_op jit(solution)/shard_map/ppermute | solution.py:78
  69.4 4.6 %collective-permute-start.12 = (bf16[1,320,384]{2,1,0:T(8,128)(2,1)}, bf16[1,320,384]{2,1,0:T(8,128)(2,1)S(1)}, u32[]{:S(2)}, u32[]{:S(2)}) collective-permute-start(bf16[1,320,384]{2,1,0:T(8,128)(2,1)} %get-tuple-element.95.rest_4_.rest_5_), channel_id=1, source_target_pairs={{0,2},{2,0},{1,3},{3,1},{4,6},{6,4},{5,7},{7,5},{8,10},{10,8},{9,1... | collective-permute-start | bytes 737288 | tf_op jit(solution)/shard_map/ppermute | solution.py:78
  73.3 1.5 collective-permute-start.13
  108.9 20.1 %all-to-all-start = ((bf16[4,320,192]{1,2,0:T(8,128)(2,1)}), bf16[4,320,192]{1,2,0:T(8,128)(2,1)S(1)}, u32[]{:S(2)}, u32[]{:S(2)}) async-start(bf16[4,320,192]{1,2,0:T(8,128)(2,1)} %copy.44), calls=%async_computation | async-start | bytes 1179648 | tf_op jit(solution)/shard_map/all_to_all | solution.py:931
  112.5 55.2 %all-gather.13.cloned.1.call-start = ((), (), s32[]{:S(2)}) async-start(), calls=%async_computation.9 | async-start | bytes 4915200 | tf_op jit(solution)/shard_map/all_gather | solution.py:928
  154.2 30.3 %all-to-all-start.1 = ((bf16[4,320,192]{1,2,0:T(8,128)(2,1)}), bf16[4,320,192]{1,2,0:T(8,128)(2,1)S(1)}, u32[]{:S(2)}, u32[]{:S(2)}) async-start(bf16[4,320,192]{1,2,0:T(8,128)(2,1)} %bitcast.18), calls=%async_computation.1 | async-start | bytes 1179648 | tf_op jit(solution)/shard_map/all_to_all | solution.py:931
  157.7 93.0 %reduce-scatter.4.cloned.1.call-start = ((), (), s32[]{:S(2)}) async-start(), calls=%async_computation.10 | async-start | bytes 5308416 | tf_op jit(solution)/shard_map/reduce_scatter | solution.py:977
  184.6 100.4 %reduce-scatter.6.cloned.1.call-start = ((), (), s32[]{:S(2)}) async-start(), calls=%async_computation.11 | async-start | bytes 884736 | tf_op jit(solution)/shard_map/reduce_scatter | solution.py:1021
  185.4 5.9 %collective-permute-start.14 = (bf16[16,256,384]{2,1,0:T(8,128)(2,1)}, bf16[16,256,384]{2,1,0:T(8,128)(2,1)S(1)}, u32[]{:S(2)}, u32[]{:S(2)}) collective-permute-start(bf16[16,256,384]{2,1,0:T(8,128)(2,1)} %get-tuple-element.106), channel_id=1, source_target_pairs={{0,2},{2,0},{1,3},{3,1},{4,6},{6,4},{5,7},{7,5},{8,10},{10,8},{9,1... | collective-permute-start | bytes 9437192 | tf_op jit(solution)/shard_map/ppermute | solution.py:78
  192.7 45.6 %collective-permute-start.15 = (bf16[2,2,2,256,384]{4,3,2,1,0:T(8,128)(2,1)S(1)}, bf16[2,2,2,256,384]{4,3,2,1,0:T(8,128)(2,1)S(1)}, u32[]{:S(2)}, u32[]{:S(2)}) collective-permute-start(bf16[2,2,2,256,384]{4,3,2,1,0:T(8,128)(2,1)S(1)} %get-tuple-element.174.rest_9_), channel_id=1, source_target_pairs={{0,4},{4,0},{1,5},{5,1},{2,6},{6,2},{3,7},{7,3},{8,12},{12,8},{9,1... | collective-permute-start | bytes 4718600 | tf_op jit(solution)/shard_map/ppermute | solution.py:78
  236.9 12.3 %collective-permute-start.16 = (bf16[1,4,320,384]{3,2,1,0:T(8,128)(2,1)}, bf16[1,4,320,384]{3,2,1,0:T(8,128)(2,1)S(1)}, u32[]{:S(2)}, u32[]{:S(2)}) collective-permute-start(bf16[1,4,320,384]{3,2,1,0:T(8,128)(2,1)} %get-tuple-element.114), channel_id=1, source_target_pairs={{0,2},{2,0},{1,3},{3,1},{4,6},{6,4},{5,7},{7,5},{8,10},{10,8},{9,1... | collective-permute-start | bytes 2949128 | tf_op jit(solution)/shard_map/ppermute | solution.py:78
  238.2 11.0 %copy-start.6 = (bf16[2,4,320,384]{3,2,1,0:T(8,128)(2,1)S(1)}, bf16[2,4,320,384]{3,2,1,0:T(8,128)(2,1)}, u32[]{:S(2)}) copy-start(bf16[2,4,320,384]{3,2,1,0:T(8,128)(2,1)} %get-tuple-element.116.rest_0_) | copy-start | bytes 5898244
  238.2 38.4 %collective-permute-start.18 = (bf16[1,4,320,384]{3,2,1,0:T(8,128)(2,1)}, bf16[1,4,320,384]{3,2,1,0:T(8,128)(2,1)}, u32[]{:S(2)}, u32[]{:S(2)}) collective-permute-start(bf16[1,4,320,384]{3,2,1,0:T(8,128)(2,1)} %get-tuple-element.117), channel_id=1, source_target_pairs={{0,2},{2,0},{1,3},{3,1},{4,6},{6,4},{5,7},{7,5},{8,10},{10,8},{9,1... | collective-permute-start | bytes 2949128 | tf_op jit(solution)/shard_map/ppermute | solution.py:78
  238.7 35.1 %collective-permute-start.17 = (bf16[2,2,256,384]{3,2,1,0:T(8,128)(2,1)S(1)}, bf16[2,2,256,384]{3,2,1,0:T(8,128)(2,1)}, u32[]{:S(2)}, u32[]{:S(2)}) collective-permute-start(bf16[2,2,256,384]{3,2,1,0:T(8,128)(2,1)S(1)} %get-tuple-element.172), channel_id=1, source_target_pairs={{0,1},{1,0},{2,3},{3,2},{4,5},{5,4},{6,7},{7,6},{8,9},{9,8},{10,11... | collective-permute-start | bytes 2359304 | tf_op jit(solution)/shard_map/ppermute | solution.py:78
  250.4 26.2 %collective-permute-start.19 = (bf16[4,320,384]{2,1,0:T(8,128)(2,1)}, bf16[4,320,384]{2,1,0:T(8,128)(2,1)S(1)}, u32[]{:S(2)}, u32[]{:S(2)}) collective-permute-start(bf16[4,320,384]{2,1,0:T(8,128)(2,1)} %fusion.16), channel_id=1, source_target_pairs={{0,4},{4,0},{1,5},{5,1},{2,6},{6,2},{3,7},{7,3},{8,12},{12,8},{9,1... | collective-permute-start | bytes 2949128 | tf_op jit(solution)/shard_map/ppermute | solution.py:78
  250.7 47.1 %reduce-scatter.8.cloned.1.call-start = ((), (), s32[]{:S(2)}) async-start(), calls=%async_computation.12 | async-start | bytes 442368 | tf_op jit(solution)/shard_map/reduce_scatter | solution.py:1046
  275.1 10.6 %collective-permute-start.20 = (bf16[2,256,384]{2,1,0:T(8,128)(2,1)S(1)}, bf16[2,256,384]{2,1,0:T(8,128)(2,1)S(1)}, u32[]{:S(2)}, u32[]{:S(2)}) collective-permute-start(bf16[2,256,384]{2,1,0:T(8,128)(2,1)S(1)} %get-tuple-element.178), channel_id=1, source_target_pairs={{0,8},{8,0},{16,24},{24,16},{1,9},{9,1},{17,25},{25,17},{2,10},{10... | collective-permute-start | bytes 1179656 | tf_op jit(solution)/shard_map/ppermute | solution.py:78
  285.0 3.2 collective-permute-start.21
  285.8 11.9 %collective-permute-start.22 = (bf16[256,384]{1,0:T(8,128)(2,1)S(1)}, bf16[256,384]{1,0:T(8,128)(2,1)S(1)}, u32[]{:S(2)}, u32[]{:S(2)}) collective-permute-start(bf16[256,384]{1,0:T(8,128)(2,1)S(1)} %get-tuple-element.183), channel_id=1, source_target_pairs={{0,16},{8,24},{16,0},{24,8},{1,17},{9,25},{17,1},{25,9},{2,18},{10... | collective-permute-start | bytes 589832 | tf_op jit(solution)/shard_map/ppermute | solution.py:78
  289.4 11.3 %collective-permute-start.23 = (bf16[208,576]{1,0:T(8,128)(2,1)S(1)}, bf16[208,576]{1,0:T(8,128)(2,1)S(1)}, u32[]{:S(2)}, u32[]{:S(2)}) collective-permute-start(bf16[208,576]{1,0:T(8,128)(2,1)S(1)} %get-tuple-element.179), channel_id=1, source_target_pairs={{0,1},{1,0},{2,3},{3,2},{4,5},{5,4},{6,7},{7,6},{8,9},{9,8},{10,11... | collective-permute-start | bytes 718856 | tf_op jit(solution)/shard_map/ppermute | solution.py:78
  297.7 18.1 %collective-permute-start.25 = (bf16[256,384]{1,0:T(8,128)(2,1)S(1)}, bf16[256,384]{1,0:T(8,128)(2,1)S(1)}, u32[]{:S(2)}, u32[]{:S(2)}) collective-permute-start(bf16[256,384]{1,0:T(8,128)(2,1)S(1)} %add_convert_fusion.10), channel_id=1, source_target_pairs={{0,16},{8,24},{16,0},{24,8},{1,17},{9,25},{17,1},{25,9},{2,18},{10... | collective-permute-start | bytes 589832 | tf_op jit(solution)/shard_map/ppermute | solution.py:78
  297.8 17.0 %collective-permute-start.24 = (bf16[192,384]{1,0:T(8,128)(2,1)}, bf16[192,384]{1,0:T(8,128)(2,1)S(1)}, u32[]{:S(2)}, u32[]{:S(2)}) collective-permute-start(bf16[192,384]{1,0:T(8,128)(2,1)} %reduce-scatter.8.cloned.1.call-done), channel_id=1, source_target_pairs={{0,16},{8,24},{16,0},{24,8},{1,17},{9,25},{17,1},{25,9},{2,18},{10... | collective-permute-start | bytes 442376 | tf_op jit(solution)/shard_map/ppermute | solution.py:78
  300.8 17.1 %collective-permute-start.26 = (bf16[208,576]{1,0:T(8,128)(2,1)S(1)}, bf16[208,576]{1,0:T(8,128)(2,1)S(1)}, u32[]{:S(2)}, u32[]{:S(2)}) collective-permute-start(bf16[208,576]{1,0:T(8,128)(2,1)S(1)} %add_convert_fusion.7), channel_id=1, source_target_pairs={{0,4},{4,0},{1,5},{5,1},{2,6},{6,2},{3,7},{7,3},{8,12},{12,8},{9,1... | collective-permute-start | bytes 718856 | tf_op jit(solution)/shard_map/ppermute | solution.py:78
  315.7 9.9 %collective-permute-start.27 = (bf16[2,192,384]{2,1,0:T(8,128)(2,1)S(1)}, bf16[2,192,384]{2,1,0:T(8,128)(2,1)S(1)}, u32[]{:S(2)}, u32[]{:S(2)}) collective-permute-start(bf16[2,192,384]{2,1,0:T(8,128)(2,1)S(1)} %pad_maximum_fusion.6), channel_id=1, source_target_pairs={{0,8},{8,0},{16,24},{24,16},{1,9},{9,1},{17,25},{25,17},{2,10},{10... | collective-permute-start | bytes 884744 | tf_op jit(solution)/shard_map/ppermute | solution.py:78
  315.9 23.0 %collective-permute-start.28 = (bf16[2,256,384]{2,1,0:T(8,128)(2,1)S(1)}, bf16[2,256,384]{2,1,0:T(8,128)(2,1)S(1)}, u32[]{:S(2)}, u32[]{:S(2)}) collective-permute-start(bf16[2,256,384]{2,1,0:T(8,128)(2,1)S(1)} %pad_maximum_fusion.5), channel_id=1, source_target_pairs={{0,8},{8,0},{16,24},{24,16},{1,9},{9,1},{17,25},{25,17},{2,10},{10... | collective-permute-start | bytes 1179656 | tf_op jit(solution)/shard_map/ppermute | solution.py:78
  325.7 14.1 %collective-permute-start.30 = (bf16[2,2,192,384]{3,2,1,0:T(8,128)(2,1)S(1)}, bf16[2,2,192,384]{3,2,1,0:T(8,128)(2,1)S(1)}, u32[]{:S(2)}, u32[]{:S(2)}) collective-permute-start(bf16[2,2,192,384]{3,2,1,0:T(8,128)(2,1)S(1)} %pad_maximum_fusion.3), channel_id=1, source_target_pairs={{0,4},{4,0},{1,5},{5,1},{2,6},{6,2},{3,7},{7,3},{8,12},{12,8},{9,1... | collective-permute-start | bytes 1769480 | tf_op jit(solution)/shard_map/ppermute | solution.py:78
  325.8 13.1 %collective-permute-start.29 = (bf16[208,576]{1,0:T(8,128)(2,1)S(1)}, bf16[208,576]{1,0:T(8,128)(2,1)S(1)}, u32[]{:S(2)}, u32[]{:S(2)}) collective-permute-start(bf16[208,576]{1,0:T(8,128)(2,1)S(1)} %add_convert_fusion.6), channel_id=1, source_target_pairs={{0,16},{8,24},{16,0},{24,8},{1,17},{9,25},{17,1},{25,9},{2,18},{10... | collective-permute-start | bytes 718856 | tf_op jit(solution)/shard_map/ppermute | solution.py:78
  340.0 26.9 %collective-permute-start.32 = (bf16[2,2,2,192,384]{4,3,2,1,0:T(8,128)(2,1)S(1)}, bf16[2,2,2,192,384]{4,3,2,1,0:T(8,128)(2,1)}, u32[]{:S(2)}, u32[]{:S(2)}) collective-permute-start(bf16[2,2,2,192,384]{4,3,2,1,0:T(8,128)(2,1)S(1)} %pad_maximum_fusion.1), channel_id=1, source_target_pairs={{0,2},{2,0},{1,3},{3,1},{4,6},{6,4},{5,7},{7,5},{8,10},{10,8},{9,1... | collective-permute-start | bytes 3538952 | tf_op jit(solution)/shard_map/ppermute | solution.py:78
  340.1 32.1 %collective-permute-start.33 = (bf16[2,2,256,384]{3,2,1,0:T(8,128)(2,1)S(1)}, bf16[2,2,256,384]{3,2,1,0:T(8,128)(2,1)}, u32[]{:S(2)}, u32[]{:S(2)}) collective-permute-start(bf16[2,2,256,384]{3,2,1,0:T(8,128)(2,1)S(1)} %pad_maximum_fusion.2), channel_id=1, source_target_pairs={{0,4},{4,0},{1,5},{5,1},{2,6},{6,2},{3,7},{7,3},{8,12},{12,8},{9,1... | collective-permute-start | bytes 2359304 | tf_op jit(solution)/shard_map/ppermute | solution.py:78
  342.0 23.7 %collective-permute-start.31 = (bf16[2,208,576]{2,1,0:T(8,128)(2,1)}, bf16[2,208,576]{2,1,0:T(8,128)(2,1)}, u32[]{:S(2)}, u32[]{:S(2)}) collective-permute-start(bf16[2,208,576]{2,1,0:T(8,128)(2,1)} %pad_maximum_fusion.4), channel_id=1, source_target_pairs={{0,8},{8,0},{16,24},{24,16},{1,9},{9,1},{17,25},{25,17},{2,10},{10... | collective-permute-start | bytes 1437704 | tf_op jit(solution)/shard_map/ppermute | solution.py:78
  342.0 48.8 %all-to-all-start.2 = ((bf16[4,320,576]{2,1,0:T(8,128)(2,1)}), bf16[4,320,576]{2,1,0:T(8,128)(2,1)}, u32[]{:S(2)}, u32[]{:S(2)}) async-start(bf16[4,320,576]{2,1,0:T(8,128)(2,1)} %get-tuple-element.143), calls=%async_computation.5 | async-start | bytes 3276800 | tf_op jit(solution)/shard_map/all_to_all | solution.py:931
  373.4 11.4 %copy-start.3 = (bf16[2,2,2,256,384]{4,3,2,1,0:T(8,128)(2,1)}, bf16[2,2,2,256,384]{4,3,2,1,0:T(8,128)(2,1)S(1)}, u32[]{:S(2)}) copy-start(bf16[2,2,2,256,384]{4,3,2,1,0:T(8,128)(2,1)S(1)} %pad_maximum_fusion) | copy-start | bytes 4718596
  373.4 11.4 %collective-permute-start.35 = (bf16[2,2,2,256,384]{4,3,2,1,0:T(8,128)(2,1)S(1)}, bf16[2,2,2,256,384]{4,3,2,1,0:T(8,128)(2,1)}, u32[]{:S(2)}, u32[]{:S(2)}) collective-permute-start(bf16[2,2,2,256,384]{4,3,2,1,0:T(8,128)(2,1)S(1)} %pad_maximum_fusion), channel_id=1, source_target_pairs={{0,2},{2,0},{1,3},{3,1},{4,6},{6,4},{5,7},{7,5},{8,10},{10,8},{9,1... | collective-permute-start | bytes 4718600 | tf_op jit(solution)/shard_map/ppermute | solution.py:78
  373.5 5.0 %collective-permute-start.34 = (bf16[4,208,576]{2,1,0:T(8,128)(2,1)S(1)}, bf16[4,208,576]{2,1,0:T(8,128)(2,1)}, u32[]{:S(2)}, u32[]{:S(2)}) collective-permute-start(bf16[4,208,576]{2,1,0:T(8,128)(2,1)S(1)} %constant_dynamic-update-slice_fusion.own), channel_id=1, source_target_pairs={{0,2},{2,0},{1,3},{3,1},{4,6},{6,4},{5,7},{7,5},{8,10},{10,8},{9,1... | collective-permute-start | bytes 2875400 | tf_op jit(solution)/shard_map/ppermute | solution.py:78
  (44 other events, 202.3 us)
Sparse Core Ops, SparseCore 0:
  35.0 17.5 all-gather.6
  54.7 38.2 all-gather.8
  95.2 37.4 all-gather.10
  134.7 32.9 all-gather.12
  184.7 54.9 reduce-scatter.3
  250.8 23.6 reduce-scatter.5
  285.2 11.5 reduce-scatter.7

commit v6 on v5

--- a/solution.py
+++ b/solution.py
@@ -19,6 +19,7 @@
 WIDTH = OWN * HEAD_DIM
 QTILE = 256
 KTILE = 512
+KSTEP = 128
 
 epsilon = 1e-05
 masked_value = -1e30
@@ -90,18 +91,40 @@
     return jnp.where(keep, array, jnp.zeros_like(array))
 
 
-def piece_copies(where, ids, pieces, kv, sem, rows, classes):
-    copies = []
+def start_pieces(where, ids, pieces, kv, sem, rows, classes):
     for piece, (mask, flips) in zip(pieces, where):
         for slot, flip in enumerate(flips):
             chunk = (ids[0] ^ flip) * classes + (ids[1] ^ mask)
             start = pl.multiple_of(chunk * rows, 64)
-            copies.append(
-                pltpu.make_async_copy(
-                    piece.at[slot], kv.at[pl.ds(start, rows), :], sem.at[len(copies)]
-                )
-            )
-    return copies
+            pltpu.make_async_copy(
+                piece.at[slot], kv.at[pl.ds(start, rows), :], sem.at[chunk]
+            ).start()
+
+
+def turn_pieces(pieces, kv, turned, blocks, sem, rows):
+    @pl.loop(0, kv.shape[0] // (2 * rows))
+    def _(t):
+        for half in range(2):
+            start = pl.multiple_of((2 * t + half) * rows, 64)
+            pltpu.make_async_copy(
+                pieces[0].at[0], kv.at[pl.ds(start, rows), :], sem.at[2 * t + half]
+            ).wait()
+        both = pl.ds(pl.multiple_of(t * 2 * rows, 128), 2 * rows)
+        for n, block in enumerate(blocks):
+            turned[128 * n : 128 * n + 128, both] = kv[both, 128 * block : 128 * block + 128].T
+
+
+def pack(part):
+    half = part.shape[0] // 2
+    return jnp.concatenate(
+        [part[:, :128], jnp.concatenate([part[:half, 128:], part[half:, 128:]], axis=1)], axis=0
+    )
+
+
+def unpack(packed):
+    rows = packed.shape[0] // 3 * 2
+    rest = packed[rows:]
+    return packed[:rows], jnp.concatenate([rest[:, :64], rest[:, 64:]], axis=0)
 
 
 def order_queries(ids, first_q, last_q, q, rows):
@@ -111,30 +134,47 @@
         q[pl.ds(start, rows), :] = part[place : place + rows, :]
 
 
-def allowed(spans, base, start):
+def allowed(spans, base, start, floor):
     position = lax.broadcasted_iota(jnp.int32, (KTILE, QTILE), 0)
-    first = spans[0:1, pl.ds(base, QTILE)] - start
+    first = jnp.maximum(spans[0:1, pl.ds(base, QTILE)] - start, floor)
     last = spans[1:2, pl.ds(base, QTILE)] - start
     return (position >= first) & (position < last)
 
 
-def walk(steps, tiles, j, fetch, work):
-    amount = steps[j * (tiles + 1)]
-
-    def tile(i):
-        index = steps[j * (tiles + 1) + 1 + jnp.minimum(i, amount - 1)]
-        start = pl.multiple_of(index * KTILE, KTILE)
-        return start, jnp.where(i < amount, start, -(1 << 24))
-
-    fetch(0, tile(0)[0])
-
-    @pl.loop(0, (amount + 1) // 2)
-    def _(i):
-        here, there, later = tile(2 * i), tile(2 * i + 1), tile(2 * i + 2)
-        fetch(1, there[0])
-        work(0, *here)
-        fetch(0, later[0])
-        work(1, *there)
+class Tiles:
+    def __init__(self, steps, length, j):
+        self.end = length // KSTEP
+        self.span = KTILE // KSTEP
+        self.steps, self.row = steps, j * (self.end + self.span + 1)
+
+    def after(self, step):
+        return self.steps[self.row + step]
+
+    def following(self, step):
+        return self.after(step + self.span)
+
+    def place(self, step):
+        return pl.multiple_of(jnp.minimum(step, self.end - self.span) * KSTEP, KSTEP)
+
+    def floor(self, step):
+        floor = jnp.maximum(step - (self.end - self.span), 0) * KSTEP
+        return jnp.where(step < self.end, floor, KTILE)
+
+
+def walk(tiles, fetch, work):
+    begin = tiles.after(0)
+    fetch(0, tiles.place(begin))
+
+    def body(here):
+        there = tiles.following(here)
+        later = tiles.following(there)
+        fetch(1, tiles.place(there))
+        work(0, tiles.place(here), tiles.floor(here))
+        fetch(0, tiles.place(later))
+        work(1, tiles.place(there), tiles.floor(there))
+        return later
+
+    lax.while_loop(lambda here: here < tiles.end, body, begin)
 
 
 def forward_kernel(where, rows, classes, ids, flags, first_q, last_q, spans, *rest):
@@ -145,18 +185,9 @@
     ]
     length = kv.shape[0]
     tiles = length // KTILE
-    copies = piece_copies(where, ids, pieces, kv, sem, rows, classes)
-    for copy in copies:
-        copy.start()
+    start_pieces(where, ids, pieces, kv, sem, rows, classes)
     order_queries(ids, first_q, last_q, q, rows)
-    for copy in copies:
-        copy.wait()
-
-    @pl.loop(0, tiles)
-    def _(t):
-        start = pl.multiple_of(t * KTILE, KTILE)
-        vt[0:128, pl.ds(start, KTILE)] = kv[pl.ds(start, KTILE), 128:256].T
-        vt[128:256, pl.ds(start, KTILE)] = kv[pl.ds(start, KTILE), 256:384].T
+    turn_pieces(pieces, kv, vt, (1, 2), sem, rows)
 
     v_row = (128, 192, 0)
 
@@ -182,8 +213,8 @@
                     preferred_element_type=jnp.float32,
                 )
 
-        def work(stage, start, position):
-            same = allowed(spans, base, position)
+        def work(stage, start, floor):
+            same = allowed(spans, base, start, floor)
             for head in range(OWN):
                 scores = jnp.where(same, stages[stage][head], masked_value)
                 old = top[head : head + 1, :]
@@ -202,7 +233,7 @@
                     preferred_element_type=jnp.float32,
                 )
 
-        walk(flags, tiles, j, fetch, work)
+        walk(Tiles(flags, length, j), fetch, work)
         outs = [
             accum[64 * head : 64 * head + 64, :] / total[head : head + 1, :] for head in range(OWN)
         ]
@@ -215,7 +246,7 @@
         lse[:, pl.ds(base, QTILE)] = top[...] + jnp.log(total[...])
 
     for chunk in range(GROUPS):
-        o_parts[chunk] = o_low[rows * chunk : rows * chunk + rows, :]
+        o_parts[chunk] = pack(o_low[rows * chunk : rows * chunk + rows, :])
 
 
 def backward_kernel(where, rows, classes, out_where, extra, ids, flags, first_q, last_q, spans, o_first, o_second, lse, *rest):
@@ -226,9 +257,7 @@
     dq, q, grad, kv, kt, qm, dom, stats, dqt, dkv, low_kv, sem = rest[len(out_where) :]
     length = kv.shape[0]
     tiles = length // KTILE
-    copies = piece_copies(where, ids, pieces, kv, sem, rows, classes)
-    for copy in copies:
-        copy.start()
+    start_pieces(where, ids, pieces, kv, sem, rows, classes)
 
     @pl.loop(0, tiles)
     def _(t):
@@ -237,18 +266,12 @@
 
     order_queries(ids, first_q, last_q, q, rows)
     for chunk in range(GROUPS):
+        first, last = unpack(grads[chunk])
         grad[rows * chunk : rows * chunk + rows, :] = jnp.concatenate(
-            [grads[chunk], jnp.zeros((rows, 64), jnp.bfloat16)], axis=1
+            [first, last, jnp.zeros((rows, 64), jnp.bfloat16)], axis=1
         )
 
-    for copy in copies:
-        copy.wait()
-
-    @pl.loop(0, tiles)
-    def _(t):
-        start = pl.multiple_of(t * KTILE, KTILE)
-        kt[0:128, pl.ds(start, KTILE)] = kv[pl.ds(start, KTILE), 0:128].T
-        kt[128:256, pl.ds(start, KTILE)] = kv[pl.ds(start, KTILE), 128:256].T
+    turn_pieces(pieces, kv, kt, (0, 1), sem, rows)
 
     k_row = (0, 64, 192)
 
@@ -277,11 +300,12 @@
             left = kv[place, 128 * block : 128 * block + 128]
             return lax.dot_general(left, right, NT, preferred_element_type=jnp.float32)
 
-        @pl.loop(0, flags[j * (tiles + 1)])
-        def _(i):
-            start = pl.multiple_of(flags[j * (tiles + 1) + 1 + i] * KTILE, KTILE)
+        meets = Tiles(flags, length, j)
+
+        def work(step):
+            start = meets.place(step)
             place = pl.ds(start, KTILE)
-            same = allowed(spans, base, start)
+            same = allowed(spans, base, start, meets.floor(step))
             sums = [None, None, None]
 
             def add(block, left, right):
@@ -303,7 +327,9 @@
                 )
             for block in range(3):
                 dkv[place, 128 * block : 128 * block + 128] += sums[block]
-
+            return meets.following(step)
+
+        lax.while_loop(lambda step: step < meets.end, work, meets.after(0))
         lower = dqt[0:128, :].T * 0.125
         upper = dqt[64:192, :].T * 0.125
         dq[pl.ds(base, QTILE), 0:128] = lower.astype(jnp.bfloat16)
@@ -344,7 +370,7 @@
     return pl.pallas_call(
         functools.partial(forward_kernel, where, rows, classes),
         out_shape=(
-            jax.ShapeDtypeStruct((GROUPS, rows, WIDTH), jnp.bfloat16),
+            jax.ShapeDtypeStruct((GROUPS, rows * 3 // 2, 128), jnp.bfloat16),
             jax.ShapeDtypeStruct((queries, 128), jnp.float32),
             jax.ShapeDtypeStruct((queries, 128), jnp.float32),
             jax.ShapeDtypeStruct((8, queries), jnp.float32),
@@ -466,6 +492,61 @@
         ),
         name="project",
     )(ids, bias, *chunks, *weights)
+
+
+def out_kernel(parts, weight, vectors, tokens, attn, hidden, hidden_low, unit, scale):
+    for g in range(GROUPS):
+        attn[:, WIDTH * g : WIDTH * g + WIDTH] = jnp.concatenate(unpack(parts[g]), axis=1)
+    total = jnp.dot(attn[...], weight[...], preferred_element_type=jnp.float32) + vectors[0:1, :]
+    total = tokens[...].astype(jnp.float32) + total
+    value, normal, spread = norm_forward(total, vectors[1:2, :], vectors[2:3, :])
+    hidden[...] = value
+    hidden_low[...] = value.astype(jnp.bfloat16)
+    unit[...] = normal
+    scale[...] = jnp.broadcast_to(spread, scale.shape)
+
+
+def out_project(parts, weight, vectors, tokens):
+    shape = tokens.shape
+    return pl.pallas_call(
+        out_kernel,
+        out_shape=(
+            jax.ShapeDtypeStruct(shape, jnp.bfloat16),
+            jax.ShapeDtypeStruct(shape, jnp.float32),
+            jax.ShapeDtypeStruct(shape, jnp.bfloat16),
+            jax.ShapeDtypeStruct(shape, jnp.float32),
+            jax.ShapeDtypeStruct((shape[0], 128), jnp.float32),
+        ),
+        in_specs=[VMEM_SPEC] * 4,
+        out_specs=(VMEM_SPEC,) * 5,
+        compiler_params=PARAMS,
+        cost_estimate=pl.CostEstimate(
+            flops=2 * shape[0] * D * D, bytes_accessed=5 << 20, transcendentals=0
+        ),
+        name="out_project",
+    )(parts, weight, vectors, tokens)
+
+
+def out_back_kernel(grad, weight, parts):
+    for g in range(GROUPS):
+        part = lax.dot_general(
+            grad[...], weight[WIDTH * g : WIDTH * g + WIDTH, :], NT, preferred_element_type=jnp.float32
+        )
+        parts[g] = pack(part.astype(jnp.bfloat16))
+
+
+def out_back(grad, weight):
+    return pl.pallas_call(
+        out_back_kernel,
+        out_shape=jax.ShapeDtypeStruct((GROUPS, grad.shape[0] * 3 // 2, 128), jnp.bfloat16),
+        in_specs=[VMEM_SPEC] * 2,
+        out_specs=VMEM_SPEC,
+        compiler_params=PARAMS,
+        cost_estimate=pl.CostEstimate(
+            flops=2 * grad.shape[0] * D * D, bytes_accessed=3 << 20, transcendentals=0
+        ),
+        name="out_back",
+    )(grad, weight)
 
 
 def tn(left, right):
@@ -901,13 +982,14 @@
     spans = jnp.concatenate(
         [begins[None], ends[None], jnp.zeros((6, begins.shape[0]), jnp.int32)], axis=0
     )
-    edges = (jnp.arange(tiles) * KTILE)[None, :, None]
-    meets = (begins.reshape(-1, 1, QTILE) < edges + KTILE) & (ends.reshape(-1, 1, QTILE) > edges)
-    meets = jnp.any(meets, axis=-1).astype(jnp.int32)
-    rank = jnp.cumsum(meets, axis=1)
-    slots = (rank[:, None, :] == jnp.arange(1, tiles + 1)[None, :, None]) & (meets[:, None, :] > 0)
-    listed = jnp.sum(jnp.where(slots, jnp.arange(tiles), 0), axis=-1)
-    flags = jnp.concatenate([rank[:, -1:], listed], axis=1).astype(jnp.int32).reshape(-1)
+    ends_at = length // KSTEP
+    edges = (jnp.arange(ends_at) * KSTEP)[None, :, None]
+    meets = (begins.reshape(-1, 1, QTILE) < edges + KSTEP) & (ends.reshape(-1, 1, QTILE) > edges)
+    meets = jnp.any(meets, axis=-1)
+    steps = jnp.arange(ends_at)
+    starts = jnp.arange(ends_at + KTILE // KSTEP + 1)
+    later = meets[:, None, :] & (steps[None, None, :] >= starts[None, :, None])
+    flags = jnp.min(jnp.where(later, steps, ends_at), axis=-1).astype(jnp.int32).reshape(-1)
 
     last_kv, last_q = project(place_ids, b_group, (fourth,), w_group)
     spread(last_kv, (3,))
@@ -930,10 +1012,14 @@
     def send_back(parts):
         return lax.all_to_all(parts, "h", 0, 0, tiled=True)
 
-    attn_low = jnp.transpose(send_back(o_parts), (1, 0, 2)).reshape(count, D)
-    attended = mm(attn_low, full_out) + bias_out
-    hidden, unit_one, scale_one = norm_forward(widen(inputs) + attended, gain_attn, shift_attn)
-    hidden_low = low(hidden)
+    zeros = jnp.zeros_like(bias_out)
+    attn_low, hidden, hidden_low, unit_one, scale_one = out_project(
+        send_back(o_parts),
+        full_out,
+        jnp.stack([bias_out, gain_attn, shift_attn] + [zeros] * 5),
+        inputs,
+    )
+    scale_one = scale_one[:, :1]
     raised = mm(hidden_low, full_up) + bias_up
     active, slope = gelu_pair(raised)
     active_low = low(active)
@@ -952,9 +1038,8 @@
     )
     grad_attended = low(grad_sum_one)
     grad_b_out = jnp.sum(widen(grad_attended), axis=0)
-    grad_attn = low(back_product(grad_attended, full_out))
-
-    grad_rows = send_back(jnp.transpose(grad_attn.reshape(count, GROUPS, WIDTH), (1, 0, 2)))
+
+    grad_rows = send_back(out_back(grad_attended, full_out))
 
     vectors = jnp.concatenate(
         [grad_b_out, grad_gain_one, grad_shift_one, grad_b_down, grad_gain_two, grad_shift_two, grad_b_up]
@@ -964,7 +1049,7 @@
         vectors = jnp.pad(low(vectors), (0, 9216 - 7680)).reshape(8, 3, 384)
         vectors = jnp.pad(vectors, ((0, 0), (0, 13), (0, 0)))
         near, far = upper_grad(
-            place_ids, hidden_low, grad_raised, attn_low, grad_attended, vectors, by_group
+            place_ids, hidden_low, grad_raised, attn_low, grad_attended, vectors, grad_attended
         )
         shape = (2, 2, 2, 2, 256, 384)
         near, far = near.reshape(shape), swap(far, "c", 1).reshape(shape)
@@ -973,7 +1058,7 @@
         upper, give = fold(near, far, down_sum)
         after = (give,)
         give = swap(give, "m", 1)
-        down_sum = tie(down_sum, grad_rows)
+        down_sum = tie(down_sum, grad_rows, by_group)
         down_sum = lax.psum_scatter(down_sum, ("h", "c"), scatter_dimension=0, tiled=True)
     else:
         grad_w_down = low(outer_sum(active_low, grad_lowered))

time: 402 us -> 392 us (0.975); the launches traced: 403 us -> 388 us
  waiting for transfers between devices: 125 us -> 107 us
  Pallas kernels: 128 us -> 142 us
  local copies, waits for them, and re-layouts: 37.8 us -> 32.6 us
    ppermute x36, waiting for transfers between devices: 110 us -> 101 us  [swap(): return lax.ppermute(array, axis, [(i, i ^ bit) for i in range(size)])]
    pallas_call x0 -> x2, Pallas kernels: none -> 6.99 us  [the longest x1 4.02 us: out_project(): pl.pallas_call(out_kernel, out_shape=(jax.ShapeDtypeStruct(shape, jnp.bfl...]
    all_gather x1, waiting for transfers between devices: 6.47 us -> 0.01 us  [per_device(): by_group = lax.all_gather(by_group, ('wa', 'c'), axis=0, tiled=True)]
    pallas_call x1, Pallas kernels: 42.7 us -> 46.9 us  [attend_backward(): pl.pallas_call(functools.partial(backward_kernel, where, rows, classes, o...]
    dot_general x3 -> x2, matrix products: 13.5 us -> 11.4 us  [mm(): return jnp.dot(left, right, preferred_element_type=jnp.float32)]
    unnamed x110 -> x109, local copies, waits for them, and re-layouts: 8.54 us -> 9.55 us
  transfers between devices with their start and end apart: 46 -> 46, of which waited for: 19 -> 19; matrix products, arithmetic and copies ran while one was open for 17% -> 15% of each run, Pallas kernels for 30% -> 35%
where the time goes in v6:
time: 392 us; the launch traced here: 388 us
  Pallas kernels  142 us (36%)
  waiting for transfers between devices  107 us (27%)
  starting transfers between devices  54.8 us (14%)
  local copies, waits for them, and re-layouts  32.6 us (8%)
  matrix products  16.5 us (4%)
  other arithmetic  15.4 us (4%)
  between operations  15 us (4%)
  blocking collectives  4.44 us (1%)
    ppermute x36, waiting for transfers between devices, swap(): return lax.ppermute(array, axis, [(i, i ^ bit) for i in range(size)])  101 us
    pallas_call x1, Pallas kernels, attend_backward(): pl.pallas_call(functools.partial(backward_kernel, where, rows, classes, o...  46.9 us
    ppermute x36, starting transfers between devices, swap(): return lax.ppermute(array, axis, [(i, i ^ bit) for i in range(size)])  42.5 us
    pallas_call x1, Pallas kernels, attend_forward(): pl.pallas_call(functools.partial(forward_kernel, where, rows, classes), o...  33.5 us
    all_to_all x3, starting transfers between devices, send_back(): return lax.all_to_all(parts, 'h', 0, 0, tiled=True)  11.6 us
    dot_general x2, matrix products, mm(): return jnp.dot(left, right, preferred_element_type=jnp.float32)  11.4 us
    unnamed x109, local copies, waits for them, and re-layouts  9.55 us
    pallas_call x1, Pallas kernels, upper_grad(): pl.pallas_call(upper_grad_kernel, out_shape=(jax.ShapeDtypeStruct((16, 25...  8.68 us
  transfers between devices with their start and end apart: 46, of which 19 were waited for; matrix products, arithmetic and copies ran while one was open for 15% of the time, Pallas kernels for 35%

profile of v6, /device:TPU:0, one launch (start us, length us, event | category | flops | bytes accessed | tf_op | source)
XLA Modules:
  0.0 388.3 jit_solution(7684202715427174747)
XLA Ops:
  7.3 3.1 collective-permute-start
  10.3 2.6 collective-permute-start.1
  13.6 2.7 pick_weights.1.rest_3_.rest_1_
  22.5 2.4 constant_dynamic-slice_fusion.3
  24.9 4.4 %all-gather.1 = bf16[2,1,4608]{2,1,0:T(2,128)(2,1)S(1)} all-gather(bf16[1,1,4608]{2,1,0:T(2,128)(2,1)S(1)} %reshape.330), channel_id=2, replica_groups=mesh['h'=4,'m'=2,'c'=2,'wa'=2] {'wa'}, dimensions={0}, use_global_device_ids=true | all-gather | bytes 27648 | tf_op jit(solution)/shard_map/all_gather | solution.py:931
  29.4 2.8 collective-permute-done.rest_1_.t1
  32.2 2.7 collective-permute-done.1.rest_2_.t2
  37.3 4.2 %project.2 = (bf16[3,320,384]{2,1,0:T(8,128)(2,1)}, bf16[960,256]{1,0:T(8,128)(2,1)}) custom-call(s32[4]{0:T(128)} %pad_add_fusion.4.ids, f32[1,640]{1,0:T(1,128)} %broadcast_in_dim.80.bias, bf16[320,768]{1,0:T(8,128)(2,1)} %bitcast.107, bf16[320,768]{1,0:T(8,128)(2,1)} %copy-done.21, bf16[320,768]{1,0:T(8,128)(2,1)} %collective-permute-done.1.rest_2_.t2, ...), custom_call_target="tpu_custom_call" | custom-call | flops 943718400 | bytes 2097152 | tf_op jit(solution)/shard_map/project/pallas_call | solution.py:481
  52.7 6.2 %collective-permute-done.6 = s32[8,320]{1,0:T(8,128)S(1)} collective-permute-done((s32[8,320]{1,0:T(8,128)S(1)}, s32[8,320]{1,0:T(8,128)S(1)}, u32[]{:S(2)}, u32[]{:S(2)}) %collective-permute-start.6) | collective-permute-done | bytes 10272 | tf_op jit(solution)/shard_map/ppermute | solution.py:79
  60.9 2.9 project.3
  65.3 2.1 collective-permute-done.8.rest_1_.rest_2_
  69.2 2.2 collective-permute-done.11.rest_5_.rest_6_
  74.0 33.5 %attend_forward.1 = (bf16[4,480,128]{2,1,0:T(8,128)(2,1)}, f32[1280,128]{1,0:T(8,128)}, f32[1280,128]{1,0:T(8,128)}, f32[8,1280]{1,0:T(8,128)}) custom-call(s32[2]{0:T(128)} %pad_add_fusion.3.ids, s32[225]{0:T(256)} %reshape.297.flags, bf16[960,256]{1,0:T(8,128)(2,1)} %get-tuple-element.98.first_q, bf16[320,256]{1,0:T(8,128)(2,1)} %get-tuple-element.99.last_q, ...), custom_call_target="tpu_custom_call" | custom-call | flops 5033164800 | bytes 8388608 | tf_op jit(solution)/shard_map/attend_forward/pallas_call | solution.py:370
  107.6 3.8 all-to-all-start
  114.9 3.8 concatenate.45
  122.1 4.0 %out_project.1 = (bf16[320,768]{1,0:T(8,128)(2,1)}, f32[320,768]{1,0:T(8,128)}, bf16[320,768]{1,0:T(8,128)(2,1)}, f32[320,768]{1,0:T(8,128)}, f32[320,128]{1,0:T(8,128)}) custom-call(bf16[4,480,128]{2,1,0:T(8,128)(2,1)} %copy-done.13, bf16[768,768]{1,0:T(8,128)(2,1)} %all-gather.7.cloned.1.call-done.weight, f32[8,768]{1,0:T(8,128)} %stack.102.vectors, ...), custom_call_target="tpu_custom_call" | custom-call | flops 377487360 | bytes 5242880 | tf_op jit(solution)/shard_map/out_project/pallas_call | solution.py:511
  127.2 6.6 %multiply_convert_fusion = (bf16[320,3072]{1,0:T(8,128)(2,1)S(1)}, f32[320,3072]{1,0:T(8,128)}) fusion(f32[3072]{0:T(1024)S(1)} %copy-done.23, bf16[320,768]{1,0:T(8,128)(2,1)} %get-tuple-element.104.hid, bf16[768,3072]{1,0:T(8,128)(2,1)} %all-gather.9.cloned.1.call-done), kind=kOutput, calls=%fused_computation.9 | convolution fusion | flops 1515847680 | bytes 11120640 | tf_op jit(solution)/shard_map/dot_general | solution.py:39
  133.8 4.8 %convolution_add_fusion.2 = f32[320,768]{1,0:T(8,128)S(1)} fusion(bf16[320,3072]{1,0:T(8,128)(2,1)S(1)} %get-tuple-element.225.active, bf16[3072,768]{1,0:T(8,128)(2,1)} %all-gather.11.cloned.1.call-done, f32[768]{0:T(1024)S(1)} %reshape.313), kind=kOutput, calls=%fused_computation.20 | convolution fusion | flops 1510195200 | bytes 7670784 | tf_op jit(solution)/shard_map/dot_general | solution.py:39
  141.8 2.9 fusion.38
  144.8 2.2 multiply_reduce_fusion
  148.4 3.0 out_back.1
  151.4 3.5 all-to-all-start.1
  157.4 8.7 %upper_grad.1 = (bf16[16,256,384]{2,1,0:T(8,128)(2,1)}, bf16[16,256,384]{2,1,0:T(8,128)(2,1)}) custom-call(s32[4]{0:T(128)} %pad_add_fusion.4.ids, bf16[320,768]{1,0:T(8,128)(2,1)} %get-tuple-element.104.hid, bf16[320,3072]{1,0:T(8,128)(2,1)} %copy-done.41, bf16[320,768]{1,0:T(8,128)(2,1)} %get-tuple-element.109.attn, ...), custom_call_target="tpu_custom_call" | custom-call | flops 1887436800 | bytes 12582912 | tf_op jit(solution)/shard_map/upper_grad/pallas_call | solution.py:614
  166.1 8.2 %down_grad.1 = bf16[4,4,384,384]{3,2,1,0:T(8,128)(2,1)} custom-call(bf16[320,3072]{1,0:T(8,128)(2,1)} %copy-done.11, bf16[320,768]{1,0:T(8,128)(2,1)} %copy-done.12, bf16[2,2,2,2,256,384]{5,4,3,2,1,0:T(8,128)(2,1)} %bitcast.97), custom_call_target="tpu_custom_call" | custom-call | flops 1509949440 | bytes 8388608 | tf_op jit(solution)/shard_map/down_grad/pallas_call | solution.py:570
  175.2 5.9 %collective-permute-done.14 = bf16[16,256,384]{2,1,0:T(8,128)(2,1)S(1)} collective-permute-done((bf16[16,256,384]{2,1,0:T(8,128)(2,1)}, bf16[16,256,384]{2,1,0:T(8,128)(2,1)S(1)}, u32[]{:S(2)}, u32[]{:S(2)}) %collective-permute-start.14) | collective-permute-done | bytes 3145760 | tf_op jit(solution)/shard_map/ppermute | solution.py:79
  182.4 5.8 %collective-permute-start.15 = (bf16[2,2,2,256,384]{4,3,2,1,0:T(8,128)(2,1)S(1)}, bf16[2,2,2,256,384]{4,3,2,1,0:T(8,128)(2,1)S(1)}, u32[]{:S(2)}, u32[]{:S(2)}) collective-permute-start(bf16[2,2,2,256,384]{4,3,2,1,0:T(8,128)(2,1)S(1)} %get-tuple-element.186.rest_9_), channel_id=1, source_target_pairs={{0,4},{4,0},{1,5},{5,1},{2,6},{6,2},{3,7},{7,3},{8,12},{12,8},{9,1... | collective-permute-start | bytes 4718600 | tf_op jit(solution)/shard_map/ppermute | solution.py:79
  188.2 46.9 %attend_backward.1 = (bf16[2,4,320,384]{3,2,1,0:T(8,128)(2,1)}, bf16[1,4,320,384]{3,2,1,0:T(8,128)(2,1)}, bf16[1,4,320,384]{3,2,1,0:T(8,128)(2,1)}, bf16[1280,192]{1,0:T(8,128)(2,1)}) custom-call(s32[2]{0:T(128)} %pad_add_fusion.3.ids, s32[225]{0:T(256)} %reshape.297.flags, bf16[960,256]{1,0:T(8,128)(2,1)} %get-tuple-element.98.first_q, ...), custom_call_target="tpu_custom_call" | custom-call | flops 12582912000 | bytes 16777216 | tf_op jit(solution)/shard_map/attend_backward/pallas_call | solution.py:408
  236.0 3.4 collective-permute-start.17
  242.4 20.8 %collective-permute-done.17 = bf16[2,2,256,384]{3,2,1,0:T(8,128)(2,1)} collective-permute-done((bf16[2,2,256,384]{3,2,1,0:T(8,128)(2,1)S(1)}, bf16[2,2,256,384]{3,2,1,0:T(8,128)(2,1)}, u32[]{:S(2)}, u32[]{:S(2)}) %collective-permute-start.17) | collective-permute-done | bytes 786464 | tf_op jit(solution)/shard_map/ppermute | solution.py:79
  264.5 2.3 collective-permute-start.20
  267.8 7.5 %qkv_grads.1 = (bf16[2,208,576]{2,1,0:T(8,128)(2,1)}, bf16[2,208,576]{2,1,0:T(8,128)(2,1)}, bf16[4,320,576]{2,1,0:T(8,128)(2,1)}) custom-call(s32[4]{0:T(128)} %pad_add_fusion.4.ids, bf16[320,768]{1,0:T(8,128)(2,1)} %bitcast.109, bf16[320,768]{1,0:T(8,128)(2,1)} %copy-done.21, bf16[320,768]{1,0:T(8,128)(2,1)} %collective-permute-done.1.rest_2_.t2, ...), custom_call_target="tpu_custom_call" | custom-call | flops 1132462080 | bytes 4194304 | tf_op jit(solution)/shard_map/qkv_grads/pallas_call | solution.py:770
  275.4 3.0 collective-permute-start.22
  279.6 1.9 collective-permute-start.23
  281.4 6.5 %collective-permute-done.22 = bf16[256,384]{1,0:T(8,128)(2,1)S(1)} collective-permute-done((bf16[256,384]{1,0:T(8,128)(2,1)S(1)}, bf16[256,384]{1,0:T(8,128)(2,1)S(1)}, u32[]{:S(2)}, u32[]{:S(2)}) %collective-permute-start.22) | collective-permute-done | bytes 196640 | tf_op jit(solution)/shard_map/ppermute | solution.py:79
  288.0 2.9 collective-permute-start.24
  291.6 13.4 %collective-permute-done.24 = bf16[192,384]{1,0:T(8,128)(2,1)S(1)} collective-permute-done((bf16[192,384]{1,0:T(8,128)(2,1)}, bf16[192,384]{1,0:T(8,128)(2,1)S(1)}, u32[]{:S(2)}, u32[]{:S(2)}) %collective-permute-start.24) | collective-permute-done | bytes 147488 | tf_op jit(solution)/shard_map/ppermute | solution.py:79
  306.1 2.1 collective-permute-start.28
  308.2 7.6 %collective-permute-done.27 = bf16[2,192,384]{2,1,0:T(8,128)(2,1)S(1)} collective-permute-done((bf16[2,192,384]{2,1,0:T(8,128)(2,1)S(1)}, bf16[2,192,384]{2,1,0:T(8,128)(2,1)S(1)}, u32[]{:S(2)}, u32[]{:S(2)}) %collective-permute-start.27) | collective-permute-done | bytes 294944 | tf_op jit(solution)/shard_map/ppermute | solution.py:79
  317.6 10.9 %collective-permute-done.28 = bf16[2,256,384]{2,1,0:T(8,128)(2,1)S(1)} collective-permute-done((bf16[2,256,384]{2,1,0:T(8,128)(2,1)S(1)}, bf16[2,256,384]{2,1,0:T(8,128)(2,1)S(1)}, u32[]{:S(2)}, u32[]{:S(2)}) %collective-permute-start.28) | collective-permute-done | bytes 393248 | tf_op jit(solution)/shard_map/ppermute | solution.py:79
  328.6 1.9 collective-permute-done.29
  332.2 4.4 %all-to-all-start.2 = ((bf16[4,320,576]{2,1,0:T(8,128)(2,1)}), bf16[4,320,576]{2,1,0:T(8,128)(2,1)}, u32[]{:S(2)}, u32[]{:S(2)}) async-start(bf16[4,320,576]{2,1,0:T(8,128)(2,1)} %get-tuple-element.153), calls=%async_computation.5 | async-start | bytes 3276800 | tf_op jit(solution)/shard_map/all_to_all | solution.py:1013
  337.7 10.2 %collective-permute-done.31 = bf16[2,208,576]{2,1,0:T(8,128)(2,1)} collective-permute-done((bf16[2,208,576]{2,1,0:T(8,128)(2,1)}, bf16[2,208,576]{2,1,0:T(8,128)(2,1)}, u32[]{:S(2)}, u32[]{:S(2)}) %collective-permute-start.31) | collective-permute-done | bytes 479264 | tf_op jit(solution)/shard_map/ppermute | solution.py:79
  349.1 5.2 %unpack_down.1 = f32[1536,768]{1,0:T(8,128)} custom-call(s32[4]{0:T(128)} %pad_add_fusion.4.ids, bf16[8,192,384]{2,1,0:T(8,128)(2,1)} %bitcast.102, bf16[8,192,384]{2,1,0:T(8,128)(2,1)} %bitcast.38.block_other), custom_call_target="tpu_custom_call" | custom-call | tf_op jit(solution)/shard_map/unpack_down/pallas_call | solution.py:714
  356.2 4.6 %collective-permute-done.34.other = bf16[4,208,576]{2,1,0:T(8,128)(2,1)} collective-permute-done((bf16[4,208,576]{2,1,0:T(8,128)(2,1)S(1)}, bf16[4,208,576]{2,1,0:T(8,128)(2,1)}, u32[]{:S(2)}, u32[]{:S(2)}) %collective-permute-start.34) | collective-permute-done | bytes 958496 | tf_op jit(solution)/shard_map/ppermute | solution.py:79
  360.8 3.8 unpack_qkv.1
  367.0 6.0 %unpack_upper.1 = (f32[384,3072]{1,0:T(8,128)}, f32[384,768]{1,0:T(8,128)}, f32[384]{0:T(512)}, f32[384]{0:T(512)}, f32[384]{0:T(512)}, /*index=5*/f32[384]{0:T(...) custom-call(s32[4]{0:T(128)} %pad_add_fusion.4.ids, bf16[8,256,384]{2,1,0:T(8,128)(2,1)} %bitcast.101, ...), custom_call_target="tpu_custom_call" | custom-call | tf_op jit(solution)/shard_map/unpack_upper/pallas_call | solution.py:678
  373.0 2.9 all-to-all-done.2.both
  375.9 5.6 %token_grads.1 = f32[320,768]{1,0:T(8,128)} custom-call(f32[320,768]{1,0:T(8,128)} %get-tuple-element.151.base, bf16[4,320,576]{2,1,0:T(8,128)(2,1)} %all-to-all-done.2.both, bf16[768,2560]{1,0:T(8,128)(2,1)} %all-gather.13.cloned.1.call-done.weight), custom_call_target="tpu_custom_call" | custom-call | flops 1132462080 | bytes 8388608 | tf_op jit(solution)/shard_map/token_grads/pallas_call | solution.py:821
  (291 shorter events, 64.7 us)
Async XLA Ops:
  7.2 112.5 %all-gather.7.cloned.1.call-start = ((), (), s32[]{:S(2)}) async-start(), calls=%async_computation.6 | async-start | bytes 1474560 | tf_op jit(solution)/shard_map/all_gather | solution.py:944
  7.3 24.9 %collective-permute-start = (bf16[320,768]{1,0:T(8,128)(2,1)}, bf16[320,768]{1,0:T(8,128)(2,1)S(1)}, u32[]{:S(2)}, u32[]{:S(2)}) collective-permute-start(bf16[320,768]{1,0:T(8,128)(2,1)} %bitcast.105), channel_id=1, source_target_pairs={{0,8},{8,0},{16,24},{24,16},{1,9},{9,1},{17,25},{25,17},{2,10},{10... | collective-permute-start | bytes 1474568 | tf_op jit(solution)/shard_map/ppermute | solution.py:79
  10.3 24.5 %collective-permute-start.1 = (bf16[320,768]{1,0:T(8,128)(2,1)}, bf16[320,768]{1,0:T(8,128)(2,1)}, u32[]{:S(2)}, u32[]{:S(2)}) collective-permute-start(bf16[320,768]{1,0:T(8,128)(2,1)} %bitcast.106), channel_id=1, source_target_pairs={{0,16},{8,24},{16,0},{24,8},{1,17},{9,25},{17,1},{25,9},{2,18},{10... | collective-permute-start | bytes 1474568 | tf_op jit(solution)/shard_map/ppermute | solution.py:79
  16.2 13.1 %collective-permute-start.2 = (bf16[384,640]{1,0:T(8,128)(2,1)}, bf16[384,640]{1,0:T(8,128)(2,1)S(1)}, u32[]{:S(2)}, u32[]{:S(2)}) collective-permute-start(bf16[384,640]{1,0:T(8,128)(2,1)} %pick_weights.1.rest_3_.rest_1_), channel_id=1, source_target_pairs={{0,1},{1,0},{2,3},{3,2},{4,5},{5,4},{6,7},{7,6},{8,9},{9,8},{10,11... | collective-permute-start | bytes 1474568 | tf_op jit(solution)/shard_map/ppermute | solution.py:79
  34.9 92.3 %all-gather.9.cloned.1.call-start = ((), (), s32[]{:S(2)}) async-start(), calls=%async_computation.7 | async-start | bytes 5898240 | tf_op jit(solution)/shard_map/all_gather | solution.py:944
  35.6 98.2 %all-gather.11.cloned.1.call-start = ((), (), s32[]{:S(2)}) async-start(), calls=%async_computation.8 | async-start | bytes 5898240 | tf_op jit(solution)/shard_map/all_gather | solution.py:944
  41.6 1.2 collective-permute-start.3
  42.7 3.7 collective-permute-start.4
  46.4 3.8 collective-permute-start.5
  47.0 13.1 %collective-permute-start.7 = (bf16[320,768]{1,0:T(8,128)(2,1)}, bf16[320,768]{1,0:T(8,128)(2,1)S(1)}, u32[]{:S(2)}, u32[]{:S(2)}) collective-permute-start(bf16[320,768]{1,0:T(8,128)(2,1)} %collective-permute-done.1.rest_2_.t2), channel_id=1, source_target_pairs={{0,8},{8,0},{16,24},{24,16},{1,9},{9,1},{17,25},{25,17},{2,10},{10... | collective-permute-start | bytes 1474568 | tf_op jit(solution)/shard_map/ppermute | solution.py:79
  48.6 18.8 %collective-permute-start.8 = (bf16[3,320,384]{2,1,0:T(8,128)(2,1)}, bf16[3,320,384]{2,1,0:T(8,128)(2,1)S(1)}, u32[]{:S(2)}, u32[]{:S(2)}) collective-permute-start(bf16[3,320,384]{2,1,0:T(8,128)(2,1)} %get-tuple-element.96.rest_0_.rest_1_), channel_id=1, source_target_pairs={{0,4},{4,0},{1,5},{5,1},{2,6},{6,2},{3,7},{7,3},{8,12},{12,8},{9,1... | collective-permute-start | bytes 2211848 | tf_op jit(solution)/shard_map/ppermute | solution.py:79
  50.2 22.0 %collective-permute-start.9 = (bf16[3,320,384]{2,1,0:T(8,128)(2,1)}, bf16[3,320,384]{2,1,0:T(8,128)(2,1)S(1)}, u32[]{:S(2)}, u32[]{:S(2)}) collective-permute-start(bf16[3,320,384]{2,1,0:T(8,128)(2,1)} %get-tuple-element.96.rest_0_.rest_1_), channel_id=1, source_target_pairs={{0,2},{2,0},{1,3},{3,1},{4,6},{6,4},{5,7},{7,5},{8,10},{10,8},{9,1... | collective-permute-start | bytes 2211848 | tf_op jit(solution)/shard_map/ppermute | solution.py:79
  50.2 8.7 %collective-permute-start.6 = (s32[8,320]{1,0:T(8,128)S(1)}, s32[8,320]{1,0:T(8,128)S(1)}, u32[]{:S(2)}, u32[]{:S(2)}) collective-permute-start(s32[8,320]{1,0:T(8,128)S(1)} %pad_add_fusion), channel_id=1, source_target_pairs={{0,16},{8,24},{16,0},{24,8},{1,17},{9,25},{17,1},{25,9},{2,18},{10... | collective-permute-start | bytes 30728 | tf_op jit(solution)/shard_map/ppermute | solution.py:79
  63.8 7.6 %collective-permute-start.11 = (bf16[1,320,384]{2,1,0:T(8,128)(2,1)}, bf16[1,320,384]{2,1,0:T(8,128)(2,1)S(1)}, u32[]{:S(2)}, u32[]{:S(2)}) collective-permute-start(bf16[1,320,384]{2,1,0:T(8,128)(2,1)} %get-tuple-element.100.rest_4_.rest_5_), channel_id=1, source_target_pairs={{0,4},{4,0},{1,5},{5,1},{2,6},{6,2},{3,7},{7,3},{8,12},{12,8},{9,1... | collective-permute-start | bytes 737288 | tf_op jit(solution)/shard_map/ppermute | solution.py:79
  67.5 5.6 %collective-permute-start.10 = (bf16[3,320,384]{2,1,0:T(8,128)(2,1)S(1)}, bf16[3,320,384]{2,1,0:T(8,128)(2,1)S(1)}, u32[]{:S(2)}, u32[]{:S(2)}) collective-permute-start(bf16[3,320,384]{2,1,0:T(8,128)(2,1)S(1)} %collective-permute-done.8.rest_1_.rest_2_), channel_id=1, source_target_pairs={{0,2},{2,0},{1,3},{3,1},{4,6},{6,4},{5,7},{7,5},{8,10},{10,8},{9,1... | collective-permute-start | bytes 2211848 | tf_op jit(solution)/shard_map/ppermute | solution.py:79
  68.7 3.5 collective-permute-start.12
  71.4 1.7 collective-permute-start.13
  74.0 37.4 %copy-start.7 = (bf16[384,768]{1,0:T(8,128)(2,1)S(1)}, bf16[384,768]{1,0:T(8,128)(2,1)}, u32[]{:S(2)}) copy-start(bf16[384,768]{1,0:T(8,128)(2,1)} %w_v.1) | copy-start | bytes 1769476
  107.6 13.7 %all-to-all-start = ((bf16[4,480,128]{2,1,0:T(8,128)(2,1)}), bf16[4,480,128]{2,1,0:T(8,128)(2,1)S(1)}, u32[]{:S(2)}, u32[]{:S(2)}) async-start(bf16[4,480,128]{2,1,0:T(8,128)(2,1)} %get-tuple-element.101), calls=%async_computation | async-start | bytes 983040 | tf_op jit(solution)/shard_map/all_to_all | solution.py:1013
  111.4 63.0 %all-gather.13.cloned.1.call-start = ((), (), s32[]{:S(2)}) async-start(), calls=%async_computation.9 | async-start | bytes 4915200 | tf_op jit(solution)/shard_map/all_gather | solution.py:1010
  151.4 23.0 %all-to-all-start.1 = ((bf16[4,480,128]{2,1,0:T(8,128)(2,1)}), bf16[4,480,128]{2,1,0:T(8,128)(2,1)S(1)}, u32[]{:S(2)}, u32[]{:S(2)}) async-start(bf16[4,480,128]{2,1,0:T(8,128)(2,1)} %out_back.1), calls=%async_computation.1 | async-start | bytes 983040 | tf_op jit(solution)/shard_map/all_to_all | solution.py:1013
  154.9 87.2 %reduce-scatter.4.cloned.1.call-start = ((), (), s32[]{:S(2)}) async-start(), calls=%async_computation.10 | async-start | bytes 5308416 | tf_op jit(solution)/shard_map/reduce_scatter | solution.py:1062
  175.1 100.1 %reduce-scatter.6.cloned.1.call-start = ((), (), s32[]{:S(2)}) async-start(), calls=%async_computation.11 | async-start | bytes 884736 | tf_op jit(solution)/shard_map/reduce_scatter | solution.py:1106
  175.1 5.9 %collective-permute-start.14 = (bf16[16,256,384]{2,1,0:T(8,128)(2,1)}, bf16[16,256,384]{2,1,0:T(8,128)(2,1)S(1)}, u32[]{:S(2)}, u32[]{:S(2)}) collective-permute-start(bf16[16,256,384]{2,1,0:T(8,128)(2,1)} %get-tuple-element.112), channel_id=1, source_target_pairs={{0,2},{2,0},{1,3},{3,1},{4,6},{6,4},{5,7},{7,5},{8,10},{10,8},{9,1... | collective-permute-start | bytes 9437192 | tf_op jit(solution)/shard_map/ppermute | solution.py:79
  182.4 53.2 %collective-permute-start.15 = (bf16[2,2,2,256,384]{4,3,2,1,0:T(8,128)(2,1)S(1)}, bf16[2,2,2,256,384]{4,3,2,1,0:T(8,128)(2,1)S(1)}, u32[]{:S(2)}, u32[]{:S(2)}) collective-permute-start(bf16[2,2,2,256,384]{4,3,2,1,0:T(8,128)(2,1)S(1)} %get-tuple-element.186.rest_9_), channel_id=1, source_target_pairs={{0,4},{4,0},{1,5},{5,1},{2,6},{6,2},{3,7},{7,3},{8,12},{12,8},{9,1... | collective-permute-start | bytes 4718600 | tf_op jit(solution)/shard_map/ppermute | solution.py:79
  235.1 4.4 %collective-permute-start.16 = (bf16[1,4,320,384]{3,2,1,0:T(8,128)(2,1)}, bf16[1,4,320,384]{3,2,1,0:T(8,128)(2,1)S(1)}, u32[]{:S(2)}, u32[]{:S(2)}) collective-permute-start(bf16[1,4,320,384]{3,2,1,0:T(8,128)(2,1)} %get-tuple-element.121), channel_id=1, source_target_pairs={{0,2},{2,0},{1,3},{3,1},{4,6},{6,4},{5,7},{7,5},{8,10},{10,8},{9,1... | collective-permute-start | bytes 2949128 | tf_op jit(solution)/shard_map/ppermute | solution.py:79
  235.2 31.7 %collective-permute-start.18 = (bf16[1,4,320,384]{3,2,1,0:T(8,128)(2,1)}, bf16[1,4,320,384]{3,2,1,0:T(8,128)(2,1)}, u32[]{:S(2)}, u32[]{:S(2)}) collective-permute-start(bf16[1,4,320,384]{3,2,1,0:T(8,128)(2,1)} %get-tuple-element.124), channel_id=1, source_target_pairs={{0,2},{2,0},{1,3},{3,1},{4,6},{6,4},{5,7},{7,5},{8,10},{10,8},{9,1... | collective-permute-start | bytes 2949128 | tf_op jit(solution)/shard_map/ppermute | solution.py:79
  236.0 27.1 %collective-permute-start.17 = (bf16[2,2,256,384]{3,2,1,0:T(8,128)(2,1)S(1)}, bf16[2,2,256,384]{3,2,1,0:T(8,128)(2,1)}, u32[]{:S(2)}, u32[]{:S(2)}) collective-permute-start(bf16[2,2,256,384]{3,2,1,0:T(8,128)(2,1)S(1)} %get-tuple-element.184), channel_id=1, source_target_pairs={{0,1},{1,0},{2,3},{3,2},{4,5},{5,4},{6,7},{7,6},{8,9},{9,8},{10,11... | collective-permute-start | bytes 2359304 | tf_op jit(solution)/shard_map/ppermute | solution.py:79
  240.6 26.2 %collective-permute-start.19 = (bf16[4,320,384]{2,1,0:T(8,128)(2,1)}, bf16[4,320,384]{2,1,0:T(8,128)(2,1)S(1)}, u32[]{:S(2)}, u32[]{:S(2)}) collective-permute-start(bf16[4,320,384]{2,1,0:T(8,128)(2,1)} %fusion.14), channel_id=1, source_target_pairs={{0,4},{4,0},{1,5},{5,1},{2,6},{6,2},{3,7},{7,3},{8,12},{12,8},{9,1... | collective-permute-start | bytes 2949128 | tf_op jit(solution)/shard_map/ppermute | solution.py:79
  242.1 45.9 %reduce-scatter.8.cloned.1.call-start = ((), (), s32[]{:S(2)}) async-start(), calls=%async_computation.12 | async-start | bytes 442368 | tf_op jit(solution)/shard_map/reduce_scatter | solution.py:1131
  264.5 10.8 %collective-permute-start.20 = (bf16[2,256,384]{2,1,0:T(8,128)(2,1)S(1)}, bf16[2,256,384]{2,1,0:T(8,128)(2,1)S(1)}, u32[]{:S(2)}, u32[]{:S(2)}) collective-permute-start(bf16[2,256,384]{2,1,0:T(8,128)(2,1)S(1)} %get-tuple-element.190), channel_id=1, source_target_pairs={{0,8},{8,0},{16,24},{24,16},{1,9},{9,1},{17,25},{25,17},{2,10},{10... | collective-permute-start | bytes 1179656 | tf_op jit(solution)/shard_map/ppermute | solution.py:79
  275.2 3.2 collective-permute-start.21
  275.4 12.5 %collective-permute-start.22 = (bf16[256,384]{1,0:T(8,128)(2,1)S(1)}, bf16[256,384]{1,0:T(8,128)(2,1)S(1)}, u32[]{:S(2)}, u32[]{:S(2)}) collective-permute-start(bf16[256,384]{1,0:T(8,128)(2,1)S(1)} %get-tuple-element.195), channel_id=1, source_target_pairs={{0,16},{8,24},{16,0},{24,8},{1,17},{9,25},{17,1},{25,9},{2,18},{10... | collective-permute-start | bytes 589832 | tf_op jit(solution)/shard_map/ppermute | solution.py:79
  279.6 11.4 %collective-permute-start.23 = (bf16[208,576]{1,0:T(8,128)(2,1)S(1)}, bf16[208,576]{1,0:T(8,128)(2,1)S(1)}, u32[]{:S(2)}, u32[]{:S(2)}) collective-permute-start(bf16[208,576]{1,0:T(8,128)(2,1)S(1)} %get-tuple-element.191), channel_id=1, source_target_pairs={{0,1},{1,0},{2,3},{3,2},{4,5},{5,4},{6,7},{7,6},{8,9},{9,8},{10,11... | collective-permute-start | bytes 718856 | tf_op jit(solution)/shard_map/ppermute | solution.py:79
  287.9 18.1 %collective-permute-start.25 = (bf16[256,384]{1,0:T(8,128)(2,1)S(1)}, bf16[256,384]{1,0:T(8,128)(2,1)S(1)}, u32[]{:S(2)}, u32[]{:S(2)}) collective-permute-start(bf16[256,384]{1,0:T(8,128)(2,1)S(1)} %add_convert_fusion.10), channel_id=1, source_target_pairs={{0,16},{8,24},{16,0},{24,8},{1,17},{9,25},{17,1},{25,9},{2,18},{10... | collective-permute-start | bytes 589832 | tf_op jit(solution)/shard_map/ppermute | solution.py:79
  288.0 17.0 %collective-permute-start.24 = (bf16[192,384]{1,0:T(8,128)(2,1)}, bf16[192,384]{1,0:T(8,128)(2,1)S(1)}, u32[]{:S(2)}, u32[]{:S(2)}) collective-permute-start(bf16[192,384]{1,0:T(8,128)(2,1)} %reduce-scatter.8.cloned.1.call-done), channel_id=1, source_target_pairs={{0,16},{8,24},{16,0},{24,8},{1,17},{9,25},{17,1},{25,9},{2,18},{10... | collective-permute-start | bytes 442376 | tf_op jit(solution)/shard_map/ppermute | solution.py:79
  291.0 17.2 %collective-permute-start.26 = (bf16[208,576]{1,0:T(8,128)(2,1)S(1)}, bf16[208,576]{1,0:T(8,128)(2,1)S(1)}, u32[]{:S(2)}, u32[]{:S(2)}) collective-permute-start(bf16[208,576]{1,0:T(8,128)(2,1)S(1)} %add_convert_fusion.7), channel_id=1, source_target_pairs={{0,4},{4,0},{1,5},{5,1},{2,6},{6,2},{3,7},{7,3},{8,12},{12,8},{9,1... | collective-permute-start | bytes 718856 | tf_op jit(solution)/shard_map/ppermute | solution.py:79
  305.9 9.9 %collective-permute-start.27 = (bf16[2,192,384]{2,1,0:T(8,128)(2,1)S(1)}, bf16[2,192,384]{2,1,0:T(8,128)(2,1)S(1)}, u32[]{:S(2)}, u32[]{:S(2)}) collective-permute-start(bf16[2,192,384]{2,1,0:T(8,128)(2,1)S(1)} %pad_maximum_fusion.6), channel_id=1, source_target_pairs={{0,8},{8,0},{16,24},{24,16},{1,9},{9,1},{17,25},{25,17},{2,10},{10... | collective-permute-start | bytes 884744 | tf_op jit(solution)/shard_map/ppermute | solution.py:79
  306.1 22.4 %collective-permute-start.28 = (bf16[2,256,384]{2,1,0:T(8,128)(2,1)S(1)}, bf16[2,256,384]{2,1,0:T(8,128)(2,1)S(1)}, u32[]{:S(2)}, u32[]{:S(2)}) collective-permute-start(bf16[2,256,384]{2,1,0:T(8,128)(2,1)S(1)} %pad_maximum_fusion.5), channel_id=1, source_target_pairs={{0,8},{8,0},{16,24},{24,16},{1,9},{9,1},{17,25},{25,17},{2,10},{10... | collective-permute-start | bytes 1179656 | tf_op jit(solution)/shard_map/ppermute | solution.py:79
  316.0 15.5 %collective-permute-start.30 = (bf16[2,2,192,384]{3,2,1,0:T(8,128)(2,1)S(1)}, bf16[2,2,192,384]{3,2,1,0:T(8,128)(2,1)S(1)}, u32[]{:S(2)}, u32[]{:S(2)}) collective-permute-start(bf16[2,2,192,384]{3,2,1,0:T(8,128)(2,1)S(1)} %pad_maximum_fusion.3), channel_id=1, source_target_pairs={{0,4},{4,0},{1,5},{5,1},{2,6},{6,2},{3,7},{7,3},{8,12},{12,8},{9,1... | collective-permute-start | bytes 1769480 | tf_op jit(solution)/shard_map/ppermute | solution.py:79
  317.5 13.0 %collective-permute-start.29 = (bf16[208,576]{1,0:T(8,128)(2,1)S(1)}, bf16[208,576]{1,0:T(8,128)(2,1)S(1)}, u32[]{:S(2)}, u32[]{:S(2)}) collective-permute-start(bf16[208,576]{1,0:T(8,128)(2,1)S(1)} %add_convert_fusion.6), channel_id=1, source_target_pairs={{0,16},{8,24},{16,0},{24,8},{1,17},{9,25},{17,1},{25,9},{2,18},{10... | collective-permute-start | bytes 718856 | tf_op jit(solution)/shard_map/ppermute | solution.py:79
  331.6 17.5 %collective-permute-start.32 = (bf16[2,2,2,192,384]{4,3,2,1,0:T(8,128)(2,1)S(1)}, bf16[2,2,2,192,384]{4,3,2,1,0:T(8,128)(2,1)}, u32[]{:S(2)}, u32[]{:S(2)}) collective-permute-start(bf16[2,2,2,192,384]{4,3,2,1,0:T(8,128)(2,1)S(1)} %pad_maximum_fusion.1), channel_id=1, source_target_pairs={{0,2},{2,0},{1,3},{3,1},{4,6},{6,4},{5,7},{7,5},{8,10},{10,8},{9,1... | collective-permute-start | bytes 3538952 | tf_op jit(solution)/shard_map/ppermute | solution.py:79
  331.6 22.7 %collective-permute-start.33 = (bf16[2,2,256,384]{3,2,1,0:T(8,128)(2,1)S(1)}, bf16[2,2,256,384]{3,2,1,0:T(8,128)(2,1)}, u32[]{:S(2)}, u32[]{:S(2)}) collective-permute-start(bf16[2,2,256,384]{3,2,1,0:T(8,128)(2,1)S(1)} %pad_maximum_fusion.2), channel_id=1, source_target_pairs={{0,4},{4,0},{1,5},{5,1},{2,6},{6,2},{3,7},{7,3},{8,12},{12,8},{9,1... | collective-permute-start | bytes 2359304 | tf_op jit(solution)/shard_map/ppermute | solution.py:79
  332.2 15.7 %collective-permute-start.31 = (bf16[2,208,576]{2,1,0:T(8,128)(2,1)}, bf16[2,208,576]{2,1,0:T(8,128)(2,1)}, u32[]{:S(2)}, u32[]{:S(2)}) collective-permute-start(bf16[2,208,576]{2,1,0:T(8,128)(2,1)} %pad_maximum_fusion.4), channel_id=1, source_target_pairs={{0,8},{8,0},{16,24},{24,16},{1,9},{9,1},{17,25},{25,17},{2,10},{10... | collective-permute-start | bytes 1437704 | tf_op jit(solution)/shard_map/ppermute | solution.py:79
  332.2 43.6 %all-to-all-start.2 = ((bf16[4,320,576]{2,1,0:T(8,128)(2,1)}), bf16[4,320,576]{2,1,0:T(8,128)(2,1)}, u32[]{:S(2)}, u32[]{:S(2)}) async-start(bf16[4,320,576]{2,1,0:T(8,128)(2,1)} %get-tuple-element.153), calls=%async_computation.5 | async-start | bytes 3276800 | tf_op jit(solution)/shard_map/all_to_all | solution.py:1013
  355.6 11.4 %copy-start.3 = (bf16[2,2,2,256,384]{4,3,2,1,0:T(8,128)(2,1)}, bf16[2,2,2,256,384]{4,3,2,1,0:T(8,128)(2,1)S(1)}, u32[]{:S(2)}) copy-start(bf16[2,2,2,256,384]{4,3,2,1,0:T(8,128)(2,1)S(1)} %pad_maximum_fusion) | copy-start | bytes 4718596
  355.7 11.4 %collective-permute-start.35 = (bf16[2,2,2,256,384]{4,3,2,1,0:T(8,128)(2,1)S(1)}, bf16[2,2,2,256,384]{4,3,2,1,0:T(8,128)(2,1)}, u32[]{:S(2)}, u32[]{:S(2)}) collective-permute-start(bf16[2,2,2,256,384]{4,3,2,1,0:T(8,128)(2,1)S(1)} %pad_maximum_fusion), channel_id=1, source_target_pairs={{0,2},{2,0},{1,3},{3,1},{4,6},{6,4},{5,7},{7,5},{8,10},{10,8},{9,1... | collective-permute-start | bytes 4718600 | tf_op jit(solution)/shard_map/ppermute | solution.py:79
  355.7 5.0 %collective-permute-start.34 = (bf16[4,208,576]{2,1,0:T(8,128)(2,1)S(1)}, bf16[4,208,576]{2,1,0:T(8,128)(2,1)}, u32[]{:S(2)}, u32[]{:S(2)}) collective-permute-start(bf16[4,208,576]{2,1,0:T(8,128)(2,1)S(1)} %constant_dynamic-update-slice_fusion.own), channel_id=1, source_target_pairs={{0,2},{2,0},{1,3},{3,1},{4,6},{6,4},{5,7},{7,5},{8,10},{10,8},{9,1... | collective-permute-start | bytes 2875400 | tf_op jit(solution)/shard_map/ppermute | solution.py:79
  (42 other events, 192.7 us)
Sparse Core Ops, SparseCore 0:
  35.0 17.5 all-gather.6
  54.7 37.4 all-gather.8
  94.4 37.5 all-gather.10
  133.9 32.9 all-gather.12
  174.5 60.9 reduce-scatter.3
  242.2 22.3 reduce-scatter.5
  275.4 12.0 reduce-scatter.7

commit v7 on v6

--- a/solution.py
+++ b/solution.py
@@ -742,7 +742,11 @@
         own = slice(rows * flip, rows * flip + rows)
         start = pl.multiple_of((flip ^ ids[3]) * rows, 64)
         block = jnp.concatenate([term, dq[pl.ds(start, rows), :]], axis=1)
-        both[flip ^ ids[3]] = block
+        half = rows // 2
+        last = jnp.concatenate([block[:half, 512:], block[half:, 512:]], axis=1)
+        both[flip ^ ids[3]] = jnp.concatenate(
+            [block[:, 128 * n : 128 * n + 128] for n in range(4)] + [last], axis=0
+        )
         whole[own, :] = block
         total = total + jnp.sum(block.astype(jnp.float32), axis=0, keepdims=True)
     first = lax.broadcasted_iota(jnp.int32, (16, 576), 0) == 0
@@ -770,7 +774,7 @@
     return pl.pallas_call(
         qkv_grad_kernel,
         out_shape=(jax.ShapeDtypeStruct((2, 208, 576), jnp.bfloat16),) * 2
-        + (jax.ShapeDtypeStruct((GROUPS, rows, 576), jnp.bfloat16),),
+        + (jax.ShapeDtypeStruct((GROUPS, rows * 9 // 2, 128), jnp.bfloat16),),
         in_specs=[SMEM_SPEC] + [VMEM_SPEC] * 8,
         out_specs=(VMEM_SPEC,) * 3,
         scratch_shapes=[pltpu.VMEM((queries, 576), jnp.bfloat16)],
@@ -813,7 +817,16 @@
     total = base[...]
     for g in range(GROUPS):
         w = weight[:, 640 * g : 640 * g + 576]
-        total = total + lax.dot_general(both[g], w, NT, preferred_element_type=jnp.float32)
+        block = both[g]
+        if block.shape[1] == 128:
+            rows = total.shape[0]
+            last = block[4 * rows :]
+            block = jnp.concatenate(
+                [block[rows * n : rows * n + rows] for n in range(4)]
+                + [jnp.concatenate([last[:, :64], last[:, 64:]], axis=0)],
+                axis=1,
+            )
+        total = total + lax.dot_general(block, w, NT, preferred_element_type=jnp.float32)
     out[...] = total
 
 

time: 392 us -> 391 us (level); the launches traced: 388 us -> 392 us
  waiting for transfers between devices: 107 us -> 119 us
  starting transfers between devices: 54.8 us -> 45.8 us
    ppermute x36, waiting for transfers between devices: 101 us -> 112 us  [swap(): return lax.ppermute(array, axis, [(i, i ^ bit) for i in range(size)])]
    ppermute x36, starting transfers between devices: 42.5 us -> 33.5 us  [swap(): return lax.ppermute(array, axis, [(i, i ^ bit) for i in range(size)])]
where the time goes in v7:
time: 391 us; the launch traced here: 392 us
  Pallas kernels  142 us (36%)
  waiting for transfers between devices  119 us (30%)
  starting transfers between devices  45.8 us (12%)
  local copies, waits for them, and re-layouts  33.3 us (9%)
  matrix products  16.9 us (4%)
  other arithmetic  15.4 us (4%)
  between operations  15 us (4%)
  blocking collectives  4.44 us (1%)
    ppermute x36, waiting for transfers between devices, swap(): return lax.ppermute(array, axis, [(i, i ^ bit) for i in range(size)])  112 us
    pallas_call x1, Pallas kernels, attend_backward(): pl.pallas_call(functools.partial(backward_kernel, where, rows, classes, o...  46.9 us
    pallas_call x1, Pallas kernels, attend_forward(): pl.pallas_call(functools.partial(forward_kernel, where, rows, classes), o...  33.5 us
    ppermute x36, starting transfers between devices, swap(): return lax.ppermute(array, axis, [(i, i ^ bit) for i in range(size)])  33.5 us
    dot_general x2, matrix products, mm(): return jnp.dot(left, right, preferred_element_type=jnp.float32)  11.7 us
    all_to_all x3, starting transfers between devices, send_back(): return lax.all_to_all(parts, 'h', 0, 0, tiled=True)  11.6 us
    unnamed x109, local copies, waits for them, and re-layouts  10.2 us
    pallas_call x1, Pallas kernels, upper_grad(): pl.pallas_call(upper_grad_kernel, out_shape=(jax.ShapeDtypeStruct((16, 25...  8.67 us
  transfers between devices with their start and end apart: 46, of which 19 were waited for; matrix products, arithmetic and copies ran while one was open for 15% of the time, Pallas kernels for 35%

profile of v7, /device:TPU:0, one launch (start us, length us, event | category | flops | bytes accessed | tf_op | source)
XLA Modules:
  0.0 392.1 jit_solution(2579487698915475668)
XLA Ops:
  7.3 3.1 collective-permute-start
  10.3 2.6 collective-permute-start.1
  13.6 2.7 pick_weights.1.rest_3_.rest_1_
  20.8 1.7 constant_dynamic-slice_fusion.4
  22.5 2.4 constant_dynamic-slice_fusion.3
  24.9 4.4 %all-gather.1 = bf16[2,1,4608]{2,1,0:T(2,128)(2,1)S(1)} all-gather(bf16[1,1,4608]{2,1,0:T(2,128)(2,1)S(1)} %reshape.330), channel_id=2, replica_groups=mesh['h'=4,'m'=2,'c'=2,'wa'=2] {'wa'}, dimensions={0}, use_global_device_ids=true | all-gather | bytes 27648 | tf_op jit(solution)/shard_map/all_gather | solution.py:944
  29.4 2.8 collective-permute-done.rest_1_.t1
  32.2 2.7 collective-permute-done.1.rest_2_.t2
  37.3 4.2 %project.2 = (bf16[3,320,384]{2,1,0:T(8,128)(2,1)}, bf16[960,256]{1,0:T(8,128)(2,1)}) custom-call(s32[4]{0:T(128)} %pad_add_fusion.4.ids, f32[1,640]{1,0:T(1,128)} %broadcast_in_dim.80.bias, bf16[320,768]{1,0:T(8,128)(2,1)} %bitcast.107, bf16[320,768]{1,0:T(8,128)(2,1)} %copy-done.21, bf16[320,768]{1,0:T(8,128)(2,1)} %collective-permute-done.1.rest_2_.t2, ...), custom_call_target="tpu_custom_call" | custom-call | flops 943718400 | bytes 2097152 | tf_op jit(solution)/shard_map/project/pallas_call | solution.py:481
  47.0 1.6 collective-permute-start.7
  52.7 6.2 %collective-permute-done.6 = s32[8,320]{1,0:T(8,128)S(1)} collective-permute-done((s32[8,320]{1,0:T(8,128)S(1)}, s32[8,320]{1,0:T(8,128)S(1)}, u32[]{:S(2)}, u32[]{:S(2)}) %collective-permute-start.6) | collective-permute-done | bytes 10272 | tf_op jit(solution)/shard_map/ppermute | solution.py:79
  60.9 2.9 project.3
  65.3 2.1 collective-permute-done.8.rest_1_.rest_2_
  69.2 2.2 collective-permute-done.11.rest_5_.rest_6_
  74.0 33.5 %attend_forward.1 = (bf16[4,480,128]{2,1,0:T(8,128)(2,1)}, f32[1280,128]{1,0:T(8,128)}, f32[1280,128]{1,0:T(8,128)}, f32[8,1280]{1,0:T(8,128)}) custom-call(s32[2]{0:T(128)} %pad_add_fusion.3.ids, s32[225]{0:T(256)} %reshape.297.flags, bf16[960,256]{1,0:T(8,128)(2,1)} %get-tuple-element.98.first_q, bf16[320,256]{1,0:T(8,128)(2,1)} %get-tuple-element.99.last_q, ...), custom_call_target="tpu_custom_call" | custom-call | flops 5033164800 | bytes 8388608 | tf_op jit(solution)/shard_map/attend_forward/pallas_call | solution.py:370
  107.6 3.8 all-to-all-start
  114.9 3.8 concatenate.45
  119.8 5.8 %all-to-all-done.parts = bf16[4,480,128]{2,1,0:T(8,128)(2,1)S(1)} async-done(((bf16[4,480,128]{2,1,0:T(8,128)(2,1)}), bf16[4,480,128]{2,1,0:T(8,128)(2,1)S(1)}, u32[]{:S(2)}, u32[]{:S(2)}) %all-to-all-start) | async-done | bytes 491552 | tf_op jit(solution)/shard_map/all_to_all | solution.py:1026
  126.3 4.0 %out_project.1 = (bf16[320,768]{1,0:T(8,128)(2,1)}, f32[320,768]{1,0:T(8,128)}, bf16[320,768]{1,0:T(8,128)(2,1)}, f32[320,768]{1,0:T(8,128)}, f32[320,128]{1,0:T(8,128)}) custom-call(bf16[4,480,128]{2,1,0:T(8,128)(2,1)} %copy-done.13, bf16[768,768]{1,0:T(8,128)(2,1)} %all-gather.7.cloned.1.call-done.weight, f32[8,768]{1,0:T(8,128)} %stack.102.vectors, ...), custom_call_target="tpu_custom_call" | custom-call | flops 377487360 | bytes 5242880 | tf_op jit(solution)/shard_map/out_project/pallas_call | solution.py:511
  131.4 6.5 %multiply_convert_fusion = (bf16[320,3072]{1,0:T(8,128)(2,1)S(1)}, f32[320,3072]{1,0:T(8,128)}) fusion(f32[3072]{0:T(1024)S(1)} %copy-done.23, bf16[320,768]{1,0:T(8,128)(2,1)} %get-tuple-element.104.hid, bf16[768,3072]{1,0:T(8,128)(2,1)} %all-gather.9.cloned.1.call-done), kind=kOutput, calls=%fused_computation.9 | convolution fusion | flops 1515847680 | bytes 11120640 | tf_op jit(solution)/shard_map/dot_general | solution.py:39
  138.0 5.1 %convolution_add_fusion.2 = f32[320,768]{1,0:T(8,128)S(1)} fusion(bf16[320,3072]{1,0:T(8,128)(2,1)S(1)} %get-tuple-element.225.active, bf16[3072,768]{1,0:T(8,128)(2,1)} %all-gather.11.cloned.1.call-done, f32[768]{0:T(1024)S(1)} %reshape.313), kind=kOutput, calls=%fused_computation.20 | convolution fusion | flops 1510195200 | bytes 7670784 | tf_op jit(solution)/shard_map/dot_general | solution.py:39
  145.9 2.9 fusion.38
  148.9 2.2 multiply_reduce_fusion
  152.6 3.0 out_back.1
  155.6 3.5 all-to-all-start.1
  161.6 8.7 %upper_grad.1 = (bf16[16,256,384]{2,1,0:T(8,128)(2,1)}, bf16[16,256,384]{2,1,0:T(8,128)(2,1)}) custom-call(s32[4]{0:T(128)} %pad_add_fusion.4.ids, bf16[320,768]{1,0:T(8,128)(2,1)} %get-tuple-element.104.hid, bf16[320,3072]{1,0:T(8,128)(2,1)} %copy-done.41, bf16[320,768]{1,0:T(8,128)(2,1)} %get-tuple-element.109.attn, ...), custom_call_target="tpu_custom_call" | custom-call | flops 1887436800 | bytes 12582912 | tf_op jit(solution)/shard_map/upper_grad/pallas_call | solution.py:614
  170.3 8.2 %down_grad.1 = bf16[4,4,384,384]{3,2,1,0:T(8,128)(2,1)} custom-call(bf16[320,3072]{1,0:T(8,128)(2,1)} %copy-done.11, bf16[320,768]{1,0:T(8,128)(2,1)} %copy-done.12, bf16[2,2,2,2,256,384]{5,4,3,2,1,0:T(8,128)(2,1)} %bitcast.97), custom_call_target="tpu_custom_call" | custom-call | flops 1509949440 | bytes 8388608 | tf_op jit(solution)/shard_map/down_grad/pallas_call | solution.py:570
  179.3 5.9 %collective-permute-done.14 = bf16[16,256,384]{2,1,0:T(8,128)(2,1)S(1)} collective-permute-done((bf16[16,256,384]{2,1,0:T(8,128)(2,1)}, bf16[16,256,384]{2,1,0:T(8,128)(2,1)S(1)}, u32[]{:S(2)}, u32[]{:S(2)}) %collective-permute-start.14) | collective-permute-done | bytes 3145760 | tf_op jit(solution)/shard_map/ppermute | solution.py:79
  187.7 46.9 %attend_backward.1 = (bf16[2,4,320,384]{3,2,1,0:T(8,128)(2,1)}, bf16[1,4,320,384]{3,2,1,0:T(8,128)(2,1)}, bf16[1,4,320,384]{3,2,1,0:T(8,128)(2,1)}, bf16[1280,192]{1,0:T(8,128)(2,1)}) custom-call(s32[2]{0:T(128)} %pad_add_fusion.3.ids, s32[225]{0:T(256)} %reshape.297.flags, bf16[960,256]{1,0:T(8,128)(2,1)} %get-tuple-element.98.first_q, ...), custom_call_target="tpu_custom_call" | custom-call | flops 12582912000 | bytes 16777216 | tf_op jit(solution)/shard_map/attend_backward/pallas_call | solution.py:408
  237.3 1.7 collective-permute-done.16
  241.3 21.6 %collective-permute-done.17 = bf16[2,2,256,384]{3,2,1,0:T(8,128)(2,1)} collective-permute-done((bf16[2,2,256,384]{3,2,1,0:T(8,128)(2,1)S(1)}, bf16[2,2,256,384]{3,2,1,0:T(8,128)(2,1)}, u32[]{:S(2)}, u32[]{:S(2)}) %collective-permute-start.17) | collective-permute-done | bytes 786464 | tf_op jit(solution)/shard_map/ppermute | solution.py:79
  264.3 1.8 collective-permute-start.20
  267.0 7.5 %qkv_grads.1 = (bf16[2,208,576]{2,1,0:T(8,128)(2,1)}, bf16[2,208,576]{2,1,0:T(8,128)(2,1)}, bf16[4,1440,128]{2,1,0:T(8,128)(2,1)}) custom-call(s32[4]{0:T(128)} %pad_add_fusion.4.ids, bf16[320,768]{1,0:T(8,128)(2,1)} %bitcast.109, bf16[320,768]{1,0:T(8,128)(2,1)} %copy-done.21, bf16[320,768]{1,0:T(8,128)(2,1)} %collective-permute-done.1.rest_2_.t2, ...), custom_call_target="tpu_custom_call" | custom-call | flops 1132462080 | bytes 4194304 | tf_op jit(solution)/shard_map/qkv_grads/pallas_call | solution.py:774
  275.1 2.9 collective-permute-start.22
  279.4 7.9 %collective-permute-done.22 = bf16[256,384]{1,0:T(8,128)(2,1)S(1)} collective-permute-done((bf16[256,384]{1,0:T(8,128)(2,1)S(1)}, bf16[256,384]{1,0:T(8,128)(2,1)S(1)}, u32[]{:S(2)}, u32[]{:S(2)}) %collective-permute-start.22) | collective-permute-done | bytes 196640 | tf_op jit(solution)/shard_map/ppermute | solution.py:79
  287.4 2.9 collective-permute-start.24
  291.0 13.4 %collective-permute-done.24 = bf16[192,384]{1,0:T(8,128)(2,1)S(1)} collective-permute-done((bf16[192,384]{1,0:T(8,128)(2,1)}, bf16[192,384]{1,0:T(8,128)(2,1)S(1)}, u32[]{:S(2)}, u32[]{:S(2)}) %collective-permute-start.24) | collective-permute-done | bytes 147488 | tf_op jit(solution)/shard_map/ppermute | solution.py:79
  305.6 2.1 collective-permute-start.28
  307.7 7.6 %collective-permute-done.27 = bf16[2,192,384]{2,1,0:T(8,128)(2,1)S(1)} collective-permute-done((bf16[2,192,384]{2,1,0:T(8,128)(2,1)S(1)}, bf16[2,192,384]{2,1,0:T(8,128)(2,1)S(1)}, u32[]{:S(2)}, u32[]{:S(2)}) %collective-permute-start.27) | collective-permute-done | bytes 294944 | tf_op jit(solution)/shard_map/ppermute | solution.py:79
  317.0 11.6 %collective-permute-done.28 = bf16[2,256,384]{2,1,0:T(8,128)(2,1)S(1)} collective-permute-done((bf16[2,256,384]{2,1,0:T(8,128)(2,1)S(1)}, bf16[2,256,384]{2,1,0:T(8,128)(2,1)S(1)}, u32[]{:S(2)}, u32[]{:S(2)}) %collective-permute-start.28) | collective-permute-done | bytes 393248 | tf_op jit(solution)/shard_map/ppermute | solution.py:79
  329.8 1.9 collective-permute-start.33
  331.7 4.3 %all-to-all-start.2 = ((bf16[4,1440,128]{2,1,0:T(8,128)(2,1)}), bf16[4,1440,128]{2,1,0:T(8,128)(2,1)}, u32[]{:S(2)}, u32[]{:S(2)}) async-start(bf16[4,1440,128]{2,1,0:T(8,128)(2,1)} %get-tuple-element.153), calls=%async_computation.5 | async-start | bytes 2949120 | tf_op jit(solution)/shard_map/all_to_all | solution.py:1026
  337.2 17.3 %collective-permute-done.31 = bf16[2,208,576]{2,1,0:T(8,128)(2,1)} collective-permute-done((bf16[2,208,576]{2,1,0:T(8,128)(2,1)}, bf16[2,208,576]{2,1,0:T(8,128)(2,1)}, u32[]{:S(2)}, u32[]{:S(2)}) %collective-permute-start.31) | collective-permute-done | bytes 479264 | tf_op jit(solution)/shard_map/ppermute | solution.py:79
  355.7 5.2 %unpack_down.1 = f32[1536,768]{1,0:T(8,128)} custom-call(s32[4]{0:T(128)} %pad_add_fusion.4.ids, bf16[8,192,384]{2,1,0:T(8,128)(2,1)} %bitcast.102, bf16[8,192,384]{2,1,0:T(8,128)(2,1)} %bitcast.38.block_other), custom_call_target="tpu_custom_call" | custom-call | tf_op jit(solution)/shard_map/unpack_down/pallas_call | solution.py:714
  362.8 4.6 %collective-permute-done.34.other = bf16[4,208,576]{2,1,0:T(8,128)(2,1)} collective-permute-done((bf16[4,208,576]{2,1,0:T(8,128)(2,1)S(1)}, bf16[4,208,576]{2,1,0:T(8,128)(2,1)}, u32[]{:S(2)}, u32[]{:S(2)}) %collective-permute-start.34) | collective-permute-done | bytes 958496 | tf_op jit(solution)/shard_map/ppermute | solution.py:79
  367.3 3.8 unpack_qkv.1
  373.6 6.0 %unpack_upper.1 = (f32[384,3072]{1,0:T(8,128)}, f32[384,768]{1,0:T(8,128)}, f32[384]{0:T(512)}, f32[384]{0:T(512)}, f32[384]{0:T(512)}, /*index=5*/f32[384]{0:T(...) custom-call(s32[4]{0:T(128)} %pad_add_fusion.4.ids, bf16[8,256,384]{2,1,0:T(8,128)(2,1)} %bitcast.101, ...), custom_call_target="tpu_custom_call" | custom-call | tf_op jit(solution)/shard_map/unpack_upper/pallas_call | solution.py:678
  379.6 5.6 %token_grads.1 = f32[320,768]{1,0:T(8,128)} custom-call(f32[320,768]{1,0:T(8,128)} %get-tuple-element.151.base, bf16[4,1440,128]{2,1,0:T(8,128)(2,1)} %all-to-all-done.2.both, bf16[768,2560]{1,0:T(8,128)(2,1)} %all-gather.13.cloned.1.call-done.weight), custom_call_target="tpu_custom_call" | custom-call | flops 1132462080 | bytes 8388608 | tf_op jit(solution)/shard_map/token_grads/pallas_call | solution.py:834
  (291 shorter events, 61.7 us)
Async XLA Ops:
  7.2 112.6 %all-gather.7.cloned.1.call-start = ((), (), s32[]{:S(2)}) async-start(), calls=%async_computation.6 | async-start | bytes 1474560 | tf_op jit(solution)/shard_map/all_gather | solution.py:957
  7.3 24.9 %collective-permute-start = (bf16[320,768]{1,0:T(8,128)(2,1)}, bf16[320,768]{1,0:T(8,128)(2,1)S(1)}, u32[]{:S(2)}, u32[]{:S(2)}) collective-permute-start(bf16[320,768]{1,0:T(8,128)(2,1)} %bitcast.105), channel_id=1, source_target_pairs={{0,8},{8,0},{16,24},{24,16},{1,9},{9,1},{17,25},{25,17},{2,10},{10... | collective-permute-start | bytes 1474568 | tf_op jit(solution)/shard_map/ppermute | solution.py:79
  10.3 24.5 %collective-permute-start.1 = (bf16[320,768]{1,0:T(8,128)(2,1)}, bf16[320,768]{1,0:T(8,128)(2,1)}, u32[]{:S(2)}, u32[]{:S(2)}) collective-permute-start(bf16[320,768]{1,0:T(8,128)(2,1)} %bitcast.106), channel_id=1, source_target_pairs={{0,16},{8,24},{16,0},{24,8},{1,17},{9,25},{17,1},{25,9},{2,18},{10... | collective-permute-start | bytes 1474568 | tf_op jit(solution)/shard_map/ppermute | solution.py:79
  16.2 13.1 %collective-permute-start.2 = (bf16[384,640]{1,0:T(8,128)(2,1)}, bf16[384,640]{1,0:T(8,128)(2,1)S(1)}, u32[]{:S(2)}, u32[]{:S(2)}) collective-permute-start(bf16[384,640]{1,0:T(8,128)(2,1)} %pick_weights.1.rest_3_.rest_1_), channel_id=1, source_target_pairs={{0,1},{1,0},{2,3},{3,2},{4,5},{5,4},{6,7},{7,6},{8,9},{9,8},{10,11... | collective-permute-start | bytes 1474568 | tf_op jit(solution)/shard_map/ppermute | solution.py:79
  34.9 96.5 %all-gather.9.cloned.1.call-start = ((), (), s32[]{:S(2)}) async-start(), calls=%async_computation.7 | async-start | bytes 5898240 | tf_op jit(solution)/shard_map/all_gather | solution.py:957
  35.6 102.4 %all-gather.11.cloned.1.call-start = ((), (), s32[]{:S(2)}) async-start(), calls=%async_computation.8 | async-start | bytes 5898240 | tf_op jit(solution)/shard_map/all_gather | solution.py:957
  41.6 1.2 collective-permute-start.3
  42.7 3.7 collective-permute-start.4
  46.4 3.8 collective-permute-start.5
  47.0 13.1 %collective-permute-start.7 = (bf16[320,768]{1,0:T(8,128)(2,1)}, bf16[320,768]{1,0:T(8,128)(2,1)S(1)}, u32[]{:S(2)}, u32[]{:S(2)}) collective-permute-start(bf16[320,768]{1,0:T(8,128)(2,1)} %collective-permute-done.1.rest_2_.t2), channel_id=1, source_target_pairs={{0,8},{8,0},{16,24},{24,16},{1,9},{9,1},{17,25},{25,17},{2,10},{10... | collective-permute-start | bytes 1474568 | tf_op jit(solution)/shard_map/ppermute | solution.py:79
  48.6 18.8 %collective-permute-start.8 = (bf16[3,320,384]{2,1,0:T(8,128)(2,1)}, bf16[3,320,384]{2,1,0:T(8,128)(2,1)S(1)}, u32[]{:S(2)}, u32[]{:S(2)}) collective-permute-start(bf16[3,320,384]{2,1,0:T(8,128)(2,1)} %get-tuple-element.96.rest_0_.rest_1_), channel_id=1, source_target_pairs={{0,4},{4,0},{1,5},{5,1},{2,6},{6,2},{3,7},{7,3},{8,12},{12,8},{9,1... | collective-permute-start | bytes 2211848 | tf_op jit(solution)/shard_map/ppermute | solution.py:79
  50.2 22.0 %collective-permute-start.9 = (bf16[3,320,384]{2,1,0:T(8,128)(2,1)}, bf16[3,320,384]{2,1,0:T(8,128)(2,1)S(1)}, u32[]{:S(2)}, u32[]{:S(2)}) collective-permute-start(bf16[3,320,384]{2,1,0:T(8,128)(2,1)} %get-tuple-element.96.rest_0_.rest_1_), channel_id=1, source_target_pairs={{0,2},{2,0},{1,3},{3,1},{4,6},{6,4},{5,7},{7,5},{8,10},{10,8},{9,1... | collective-permute-start | bytes 2211848 | tf_op jit(solution)/shard_map/ppermute | solution.py:79
  50.2 8.7 %collective-permute-start.6 = (s32[8,320]{1,0:T(8,128)S(1)}, s32[8,320]{1,0:T(8,128)S(1)}, u32[]{:S(2)}, u32[]{:S(2)}) collective-permute-start(s32[8,320]{1,0:T(8,128)S(1)} %pad_add_fusion), channel_id=1, source_target_pairs={{0,16},{8,24},{16,0},{24,8},{1,17},{9,25},{17,1},{25,9},{2,18},{10... | collective-permute-start | bytes 30728 | tf_op jit(solution)/shard_map/ppermute | solution.py:79
  63.8 7.6 %collective-permute-start.11 = (bf16[1,320,384]{2,1,0:T(8,128)(2,1)}, bf16[1,320,384]{2,1,0:T(8,128)(2,1)S(1)}, u32[]{:S(2)}, u32[]{:S(2)}) collective-permute-start(bf16[1,320,384]{2,1,0:T(8,128)(2,1)} %get-tuple-element.100.rest_4_.rest_5_), channel_id=1, source_target_pairs={{0,4},{4,0},{1,5},{5,1},{2,6},{6,2},{3,7},{7,3},{8,12},{12,8},{9,1... | collective-permute-start | bytes 737288 | tf_op jit(solution)/shard_map/ppermute | solution.py:79
  67.5 5.6 %collective-permute-start.10 = (bf16[3,320,384]{2,1,0:T(8,128)(2,1)S(1)}, bf16[3,320,384]{2,1,0:T(8,128)(2,1)S(1)}, u32[]{:S(2)}, u32[]{:S(2)}) collective-permute-start(bf16[3,320,384]{2,1,0:T(8,128)(2,1)S(1)} %collective-permute-done.8.rest_1_.rest_2_), channel_id=1, source_target_pairs={{0,2},{2,0},{1,3},{3,1},{4,6},{6,4},{5,7},{7,5},{8,10},{10,8},{9,1... | collective-permute-start | bytes 2211848 | tf_op jit(solution)/shard_map/ppermute | solution.py:79
  68.7 3.5 collective-permute-start.12
  71.4 1.7 collective-permute-start.13
  74.0 37.4 %copy-start.7 = (bf16[384,768]{1,0:T(8,128)(2,1)S(1)}, bf16[384,768]{1,0:T(8,128)(2,1)}, u32[]{:S(2)}) copy-start(bf16[384,768]{1,0:T(8,128)(2,1)} %w_v.1) | copy-start | bytes 1769476
  107.6 17.9 %all-to-all-start = ((bf16[4,480,128]{2,1,0:T(8,128)(2,1)}), bf16[4,480,128]{2,1,0:T(8,128)(2,1)S(1)}, u32[]{:S(2)}, u32[]{:S(2)}) async-start(bf16[4,480,128]{2,1,0:T(8,128)(2,1)} %get-tuple-element.101), calls=%async_computation | async-start | bytes 983040 | tf_op jit(solution)/shard_map/all_to_all | solution.py:1026
  111.4 67.2 %all-gather.13.cloned.1.call-start = ((), (), s32[]{:S(2)}) async-start(), calls=%async_computation.9 | async-start | bytes 4915200 | tf_op jit(solution)/shard_map/all_gather | solution.py:1023
  119.7 11.7 %copy-start.23 = (f32[3072]{0:T(1024)S(1)}, f32[3072]{0:T(1024)}, u32[]{:S(2)}) copy-start(f32[3072]{0:T(1024)} %reshape.312) | copy-start | bytes 36868
  155.6 22.9 %all-to-all-start.1 = ((bf16[4,480,128]{2,1,0:T(8,128)(2,1)}), bf16[4,480,128]{2,1,0:T(8,128)(2,1)S(1)}, u32[]{:S(2)}, u32[]{:S(2)}) async-start(bf16[4,480,128]{2,1,0:T(8,128)(2,1)} %out_back.1), calls=%async_computation.1 | async-start | bytes 983040 | tf_op jit(solution)/shard_map/all_to_all | solution.py:1026
  159.1 81.9 %reduce-scatter.4.cloned.1.call-start = ((), (), s32[]{:S(2)}) async-start(), calls=%async_computation.10 | async-start | bytes 5308416 | tf_op jit(solution)/shard_map/reduce_scatter | solution.py:1075
  179.3 95.3 %reduce-scatter.6.cloned.1.call-start = ((), (), s32[]{:S(2)}) async-start(), calls=%async_computation.11 | async-start | bytes 884736 | tf_op jit(solution)/shard_map/reduce_scatter | solution.py:1119
  179.3 5.9 %collective-permute-start.14 = (bf16[16,256,384]{2,1,0:T(8,128)(2,1)}, bf16[16,256,384]{2,1,0:T(8,128)(2,1)S(1)}, u32[]{:S(2)}, u32[]{:S(2)}) collective-permute-start(bf16[16,256,384]{2,1,0:T(8,128)(2,1)} %get-tuple-element.112), channel_id=1, source_target_pairs={{0,2},{2,0},{1,3},{3,1},{4,6},{6,4},{5,7},{7,5},{8,10},{10,8},{9,1... | collective-permute-start | bytes 9437192 | tf_op jit(solution)/shard_map/ppermute | solution.py:79
  186.6 49.6 %collective-permute-start.15 = (bf16[2,2,2,256,384]{4,3,2,1,0:T(8,128)(2,1)S(1)}, bf16[2,2,2,256,384]{4,3,2,1,0:T(8,128)(2,1)S(1)}, u32[]{:S(2)}, u32[]{:S(2)}) collective-permute-start(bf16[2,2,2,256,384]{4,3,2,1,0:T(8,128)(2,1)S(1)} %get-tuple-element.186.rest_9_), channel_id=1, source_target_pairs={{0,4},{4,0},{1,5},{5,1},{2,6},{6,2},{3,7},{7,3},{8,12},{12,8},{9,1... | collective-permute-start | bytes 4718600 | tf_op jit(solution)/shard_map/ppermute | solution.py:79
  234.6 4.4 %collective-permute-start.16 = (bf16[1,4,320,384]{3,2,1,0:T(8,128)(2,1)}, bf16[1,4,320,384]{3,2,1,0:T(8,128)(2,1)S(1)}, u32[]{:S(2)}, u32[]{:S(2)}) collective-permute-start(bf16[1,4,320,384]{3,2,1,0:T(8,128)(2,1)} %get-tuple-element.121), channel_id=1, source_target_pairs={{0,2},{2,0},{1,3},{3,1},{4,6},{6,4},{5,7},{7,5},{8,10},{10,8},{9,1... | collective-permute-start | bytes 2949128 | tf_op jit(solution)/shard_map/ppermute | solution.py:79
  236.1 30.0 %collective-permute-start.18 = (bf16[1,4,320,384]{3,2,1,0:T(8,128)(2,1)}, bf16[1,4,320,384]{3,2,1,0:T(8,128)(2,1)}, u32[]{:S(2)}, u32[]{:S(2)}) collective-permute-start(bf16[1,4,320,384]{3,2,1,0:T(8,128)(2,1)} %get-tuple-element.124), channel_id=1, source_target_pairs={{0,2},{2,0},{1,3},{3,1},{4,6},{6,4},{5,7},{7,5},{8,10},{10,8},{9,1... | collective-permute-start | bytes 2949128 | tf_op jit(solution)/shard_map/ppermute | solution.py:79
  236.6 26.4 %collective-permute-start.17 = (bf16[2,2,256,384]{3,2,1,0:T(8,128)(2,1)S(1)}, bf16[2,2,256,384]{3,2,1,0:T(8,128)(2,1)}, u32[]{:S(2)}, u32[]{:S(2)}) collective-permute-start(bf16[2,2,256,384]{3,2,1,0:T(8,128)(2,1)S(1)} %get-tuple-element.184), channel_id=1, source_target_pairs={{0,1},{1,0},{2,3},{3,2},{4,5},{5,4},{6,7},{7,6},{8,9},{9,8},{10,11... | collective-permute-start | bytes 2359304 | tf_op jit(solution)/shard_map/ppermute | solution.py:79
  240.2 25.9 %collective-permute-start.19 = (bf16[4,320,384]{2,1,0:T(8,128)(2,1)}, bf16[4,320,384]{2,1,0:T(8,128)(2,1)S(1)}, u32[]{:S(2)}, u32[]{:S(2)}) collective-permute-start(bf16[4,320,384]{2,1,0:T(8,128)(2,1)} %fusion.14), channel_id=1, source_target_pairs={{0,4},{4,0},{1,5},{5,1},{2,6},{6,2},{3,7},{7,3},{8,12},{12,8},{9,1... | collective-permute-start | bytes 2949128 | tf_op jit(solution)/shard_map/ppermute | solution.py:79
  241.0 46.3 %reduce-scatter.8.cloned.1.call-start = ((), (), s32[]{:S(2)}) async-start(), calls=%async_computation.12 | async-start | bytes 442368 | tf_op jit(solution)/shard_map/reduce_scatter | solution.py:1144
  264.3 10.7 %collective-permute-start.20 = (bf16[2,256,384]{2,1,0:T(8,128)(2,1)S(1)}, bf16[2,256,384]{2,1,0:T(8,128)(2,1)S(1)}, u32[]{:S(2)}, u32[]{:S(2)}) collective-permute-start(bf16[2,256,384]{2,1,0:T(8,128)(2,1)S(1)} %get-tuple-element.190), channel_id=1, source_target_pairs={{0,8},{8,0},{16,24},{24,16},{1,9},{9,1},{17,25},{25,17},{2,10},{10... | collective-permute-start | bytes 1179656 | tf_op jit(solution)/shard_map/ppermute | solution.py:79
  274.6 3.5 collective-permute-start.21
  275.1 12.1 %collective-permute-start.22 = (bf16[256,384]{1,0:T(8,128)(2,1)S(1)}, bf16[256,384]{1,0:T(8,128)(2,1)S(1)}, u32[]{:S(2)}, u32[]{:S(2)}) collective-permute-start(bf16[256,384]{1,0:T(8,128)(2,1)S(1)} %get-tuple-element.195), channel_id=1, source_target_pairs={{0,16},{8,24},{16,0},{24,8},{1,17},{9,25},{17,1},{25,9},{2,18},{10... | collective-permute-start | bytes 589832 | tf_op jit(solution)/shard_map/ppermute | solution.py:79
  279.2 11.1 %collective-permute-start.23 = (bf16[208,576]{1,0:T(8,128)(2,1)S(1)}, bf16[208,576]{1,0:T(8,128)(2,1)S(1)}, u32[]{:S(2)}, u32[]{:S(2)}) collective-permute-start(bf16[208,576]{1,0:T(8,128)(2,1)S(1)} %get-tuple-element.191), channel_id=1, source_target_pairs={{0,1},{1,0},{2,3},{3,2},{4,5},{5,4},{6,7},{7,6},{8,9},{9,8},{10,11... | collective-permute-start | bytes 718856 | tf_op jit(solution)/shard_map/ppermute | solution.py:79
  287.3 18.2 %collective-permute-start.25 = (bf16[256,384]{1,0:T(8,128)(2,1)S(1)}, bf16[256,384]{1,0:T(8,128)(2,1)S(1)}, u32[]{:S(2)}, u32[]{:S(2)}) collective-permute-start(bf16[256,384]{1,0:T(8,128)(2,1)S(1)} %add_convert_fusion.10), channel_id=1, source_target_pairs={{0,16},{8,24},{16,0},{24,8},{1,17},{9,25},{17,1},{25,9},{2,18},{10... | collective-permute-start | bytes 589832 | tf_op jit(solution)/shard_map/ppermute | solution.py:79
  287.4 17.1 %collective-permute-start.24 = (bf16[192,384]{1,0:T(8,128)(2,1)}, bf16[192,384]{1,0:T(8,128)(2,1)S(1)}, u32[]{:S(2)}, u32[]{:S(2)}) collective-permute-start(bf16[192,384]{1,0:T(8,128)(2,1)} %reduce-scatter.8.cloned.1.call-done), channel_id=1, source_target_pairs={{0,16},{8,24},{16,0},{24,8},{1,17},{9,25},{17,1},{25,9},{2,18},{10... | collective-permute-start | bytes 442376 | tf_op jit(solution)/shard_map/ppermute | solution.py:79
  290.3 17.3 %collective-permute-start.26 = (bf16[208,576]{1,0:T(8,128)(2,1)S(1)}, bf16[208,576]{1,0:T(8,128)(2,1)S(1)}, u32[]{:S(2)}, u32[]{:S(2)}) collective-permute-start(bf16[208,576]{1,0:T(8,128)(2,1)S(1)} %add_convert_fusion.7), channel_id=1, source_target_pairs={{0,4},{4,0},{1,5},{5,1},{2,6},{6,2},{3,7},{7,3},{8,12},{12,8},{9,1... | collective-permute-start | bytes 718856 | tf_op jit(solution)/shard_map/ppermute | solution.py:79
  305.4 9.9 %collective-permute-start.27 = (bf16[2,192,384]{2,1,0:T(8,128)(2,1)S(1)}, bf16[2,192,384]{2,1,0:T(8,128)(2,1)S(1)}, u32[]{:S(2)}, u32[]{:S(2)}) collective-permute-start(bf16[2,192,384]{2,1,0:T(8,128)(2,1)S(1)} %pad_maximum_fusion.6), channel_id=1, source_target_pairs={{0,8},{8,0},{16,24},{24,16},{1,9},{9,1},{17,25},{25,17},{2,10},{10... | collective-permute-start | bytes 884744 | tf_op jit(solution)/shard_map/ppermute | solution.py:79
  305.6 23.0 %collective-permute-start.28 = (bf16[2,256,384]{2,1,0:T(8,128)(2,1)S(1)}, bf16[2,256,384]{2,1,0:T(8,128)(2,1)S(1)}, u32[]{:S(2)}, u32[]{:S(2)}) collective-permute-start(bf16[2,256,384]{2,1,0:T(8,128)(2,1)S(1)} %pad_maximum_fusion.5), channel_id=1, source_target_pairs={{0,8},{8,0},{16,24},{24,16},{1,9},{9,1},{17,25},{25,17},{2,10},{10... | collective-permute-start | bytes 1179656 | tf_op jit(solution)/shard_map/ppermute | solution.py:79
  315.4 14.1 %collective-permute-start.30 = (bf16[2,2,192,384]{3,2,1,0:T(8,128)(2,1)S(1)}, bf16[2,2,192,384]{3,2,1,0:T(8,128)(2,1)S(1)}, u32[]{:S(2)}, u32[]{:S(2)}) collective-permute-start(bf16[2,2,192,384]{3,2,1,0:T(8,128)(2,1)S(1)} %pad_maximum_fusion.3), channel_id=1, source_target_pairs={{0,4},{4,0},{1,5},{5,1},{2,6},{6,2},{3,7},{7,3},{8,12},{12,8},{9,1... | collective-permute-start | bytes 1769480 | tf_op jit(solution)/shard_map/ppermute | solution.py:79
  316.0 12.7 %collective-permute-start.29 = (bf16[208,576]{1,0:T(8,128)(2,1)S(1)}, bf16[208,576]{1,0:T(8,128)(2,1)S(1)}, u32[]{:S(2)}, u32[]{:S(2)}) collective-permute-start(bf16[208,576]{1,0:T(8,128)(2,1)S(1)} %add_convert_fusion.6), channel_id=1, source_target_pairs={{0,16},{8,24},{16,0},{24,8},{1,17},{9,25},{17,1},{25,9},{2,18},{10... | collective-permute-start | bytes 718856 | tf_op jit(solution)/shard_map/ppermute | solution.py:79
  329.7 26.0 %collective-permute-start.32 = (bf16[2,2,2,192,384]{4,3,2,1,0:T(8,128)(2,1)S(1)}, bf16[2,2,2,192,384]{4,3,2,1,0:T(8,128)(2,1)}, u32[]{:S(2)}, u32[]{:S(2)}) collective-permute-start(bf16[2,2,2,192,384]{4,3,2,1,0:T(8,128)(2,1)S(1)} %pad_maximum_fusion.1), channel_id=1, source_target_pairs={{0,2},{2,0},{1,3},{3,1},{4,6},{6,4},{5,7},{7,5},{8,10},{10,8},{9,1... | collective-permute-start | bytes 3538952 | tf_op jit(solution)/shard_map/ppermute | solution.py:79
  329.8 31.1 %collective-permute-start.33 = (bf16[2,2,256,384]{3,2,1,0:T(8,128)(2,1)S(1)}, bf16[2,2,256,384]{3,2,1,0:T(8,128)(2,1)}, u32[]{:S(2)}, u32[]{:S(2)}) collective-permute-start(bf16[2,2,256,384]{3,2,1,0:T(8,128)(2,1)S(1)} %pad_maximum_fusion.2), channel_id=1, source_target_pairs={{0,4},{4,0},{1,5},{5,1},{2,6},{6,2},{3,7},{7,3},{8,12},{12,8},{9,1... | collective-permute-start | bytes 2359304 | tf_op jit(solution)/shard_map/ppermute | solution.py:79
  331.7 22.8 %collective-permute-start.31 = (bf16[2,208,576]{2,1,0:T(8,128)(2,1)}, bf16[2,208,576]{2,1,0:T(8,128)(2,1)}, u32[]{:S(2)}, u32[]{:S(2)}) collective-permute-start(bf16[2,208,576]{2,1,0:T(8,128)(2,1)} %pad_maximum_fusion.4), channel_id=1, source_target_pairs={{0,8},{8,0},{16,24},{24,16},{1,9},{9,1},{17,25},{25,17},{2,10},{10... | collective-permute-start | bytes 1437704 | tf_op jit(solution)/shard_map/ppermute | solution.py:79
  331.7 47.9 %all-to-all-start.2 = ((bf16[4,1440,128]{2,1,0:T(8,128)(2,1)}), bf16[4,1440,128]{2,1,0:T(8,128)(2,1)}, u32[]{:S(2)}, u32[]{:S(2)}) async-start(bf16[4,1440,128]{2,1,0:T(8,128)(2,1)} %get-tuple-element.153), calls=%async_computation.5 | async-start | bytes 2949120 | tf_op jit(solution)/shard_map/all_to_all | solution.py:1026
  362.2 11.4 %collective-permute-start.35 = (bf16[2,2,2,256,384]{4,3,2,1,0:T(8,128)(2,1)S(1)}, bf16[2,2,2,256,384]{4,3,2,1,0:T(8,128)(2,1)}, u32[]{:S(2)}, u32[]{:S(2)}) collective-permute-start(bf16[2,2,2,256,384]{4,3,2,1,0:T(8,128)(2,1)S(1)} %pad_maximum_fusion), channel_id=1, source_target_pairs={{0,2},{2,0},{1,3},{3,1},{4,6},{6,4},{5,7},{7,5},{8,10},{10,8},{9,1... | collective-permute-start | bytes 4718600 | tf_op jit(solution)/shard_map/ppermute | solution.py:79
  362.3 5.0 %collective-permute-start.34 = (bf16[4,208,576]{2,1,0:T(8,128)(2,1)S(1)}, bf16[4,208,576]{2,1,0:T(8,128)(2,1)}, u32[]{:S(2)}, u32[]{:S(2)}) collective-permute-start(bf16[4,208,576]{2,1,0:T(8,128)(2,1)S(1)} %constant_dynamic-update-slice_fusion.own), channel_id=1, source_target_pairs={{0,2},{2,0},{1,3},{3,1},{4,6},{6,4},{5,7},{7,5},{8,10},{10,8},{9,1... | collective-permute-start | bytes 2875400 | tf_op jit(solution)/shard_map/ppermute | solution.py:79
  (42 other events, 189.1 us)
Sparse Core Ops, SparseCore 0:
  35.0 17.5 all-gather.6
  54.7 37.4 all-gather.8
  94.4 37.4 all-gather.10
  133.9 32.9 all-gather.12
  178.7 55.3 reduce-scatter.3
  241.2 22.1 reduce-scatter.5
  274.7 10.9 reduce-scatter.7
